TPU v7x, 256 devices: a whole 4x4x8 slice. The times are simulated.
256 devices in a mesh: dp: 32 (over z, x), fsdp: 8 (over y, core).
Axes of the slice: x: 4, y: 4, z: 8, core: 2. Of those that a mesh axis runs over, the one named last changes fastest.
Arguments:
- hidden: bfloat16 [64, 256, 5120], P('dp', None, 'fsdp'), may hold values from -8 to 8
- gain: bfloat16 [5120], P('fsdp'), may hold values from 0.25 to 1.75
- head: bfloat16 [4096, 5120], P('fsdp'), may hold values from -1 to 1
- targets: int32 [64, 256], P('dp'), may hold values from 0 to 4095, as said below
- lengths: int32 [64], P('dp'), may hold values from 1 to 256, 8192 in all
- old_logp: float32 [64, 256], P('dp'), may hold values from -64 to 0
- rewards: float32 [64], P('dp'), may hold values from -6 to 6
- group_slot: int32 [64], P('dp'), may hold values from 0 to 63, each once
Outputs:
- loss: float32 [], replicated
- grad_hidden: bfloat16 [64, 256, 5120], P('dp', None, 'fsdp')
- grad_gain: float32 [5120], P('fsdp')
- grad_head_t: float32 [5120, 4096], P('dp', 'fsdp')
Inputs may be any that keep to these rules, and one draw needn't show every extreme that they name: `lengths`: they sum to 8192 and one of them equals 256. `group_slot`: each value once; responses with equal group_slot // 8 answer one prompt. At position 0, different responses have different targets.
All inputs are finite; a program needn't handle non-finite values. No bound on the sum of `lengths` on one device may be relied on, other than what follows from the above.
Results may differ from a plain program's by a relative error of at most 0.018.
Values may be sent and summed in bfloat16 or wider, within the bound.
No kernel may reach another device: no remote copies, remote signals or barrier semaphores. Data moves between devices by JAX's collectives and lax.ppermute only.
A program may use at most 64 MiB of HBM per device.

v0:
```python
import jax
import jax.numpy as jnp
from jax import lax
from jax.sharding import Mesh
from jax.sharding import PartitionSpec as P

GROUP = 8
FSDP = ("fsdp_0", "fsdp_1")
DP = ("dp_0", "dp_1")


eps_norm = 1e-06
clip_low = 0.8
clip_high = 1.2
dual_bound = 3.0


def gather_turned(arrays, axis, dims):
    turned = [jnp.moveaxis(a, dim, 0) for a, dim in zip(arrays, dims)]
    both = jnp.concatenate([t.reshape(len(t), -1) for t in turned], axis=1)
    filled, at, done = (lax.all_gather(both, axis, axis=0, tiled=True), 0, [])
    for t, dim in zip(turned, dims):
        slab = filled[:, at : at + t[0].size].reshape(-1, *t.shape[1:])
        done.append(jnp.moveaxis(slab, 0, dim))
        at += t[0].size
    return tuple(done)


def copy_for_each(value, axis):
    size = lax.axis_size(axis)
    return lax.all_to_all(
        jnp.broadcast_to(value[None], (size, *value.shape)), axis, 0, 0, tiled=True
    )


def over_copies(value, axis):
    return copy_for_each(value, axis).sum(axis=0)


def in_one(arrays, axis):
    flat, at, done = (jnp.concatenate([a.reshape(-1) for a in arrays]), 0, [])
    so_far = over_copies(flat, axis)
    for a in arrays:
        done.append(so_far[at : at + a.size].reshape(a.shape))
        at += a.size
    return tuple(done)


def all_in_one(value, axis):
    leaves = jax.tree.leaves(value)
    sequence = sorted(range(len(leaves)), key=lambda k: -leaves[k].size)
    width = (1, *leaves[sequence[0]].shape)[-1]
    lines = [
        jnp.pad(leaves[k].reshape(-1), (0, -leaves[k].size % width)).reshape(-1, width)
        for k in sequence
    ]
    both, at, found = (copy_for_each(jnp.concatenate(lines), axis), 0, {})
    for k, line in zip(sequence, lines):
        slab = both[:, at : at + len(line)].reshape(len(both), -1)
        found[k] = slab[:, : leaves[k].size].reshape(-1, *leaves[k].shape)
        at += len(line)
    numbers = iter(range(len(leaves)))
    return jax.tree.map(lambda _: found[next(numbers)], value)


def folded_in_pairs(pieces, combine):
    while len(jax.tree.leaves(pieces)[0]) > 1:
        pieces = jax.vmap(combine)(
            *(jax.tree.map(lambda part: part[side::2], pieces) for side in (0, 1))
        )
    return jax.tree.map(lambda part: part[0], pieces)


def merged(value, axis, combine):
    pieces = all_in_one(value, axis)
    return folded_in_pairs(pieces, combine)


def cut_along(value, dim, size):
    dims = value.shape
    pieces = value.reshape(*dims[:dim], size, dims[dim] // size, *dims[dim + 1 :])
    return jnp.moveaxis(pieces, dim, 0)


def sent_and_summed(value, axis, dim):
    pieces = cut_along(value, dim, lax.axis_size(axis))
    arrived = lax.all_to_all(pieces, axis, split_axis=0, concat_axis=0, tiled=True)
    return arrived.astype(jnp.float32).sum(axis=0)


def summed_rows(value, axes, dim):
    far, near = axes
    pieces = cut_along(value, dim, lax.axis_size(far))
    nearer = sent_and_summed(pieces, near, dim + 1)
    arrived = lax.all_to_all(
        nearer.astype(jnp.bfloat16), far, split_axis=0, concat_axis=0, tiled=True
    )
    return arrived.astype(jnp.float32).sum(axis=0)


def cut_rows(length, count):
    step = length // count
    if step >= 8:
        step -= step % 8
    return [step * k for k in range(1, count)]


def own_block(pieces, axes, sequence):
    dims = [lax.axis_size(a) for a in axes]
    pieces = pieces.reshape(*dims, *pieces.shape[1:])
    pieces = pieces.transpose(*sequence, *range(len(axes), pieces.ndim))
    pieces = pieces.reshape(-1, *pieces.shape[len(axes) :])
    for k in sequence:
        pieces = lax.psum_scatter(pieces, axes[k], scatter_dimension=0, tiled=True)
    return pieces[0]


def sum_all_axes(value, axes, dim):
    pieces = cut_along(value, dim, lax.axis_size(axes))
    cut = max(range(1, max(2, pieces.ndim - 1)), key=lambda d: pieces.shape[d])
    count, done = (len(axes), [])
    for first, slab in enumerate(jnp.split(pieces, cut_rows(pieces.shape[cut], count), axis=cut)):
        if slab.size:
            sequence = [(first + k) % count for k in range(count)]
            done.append(own_block(slab, axes, sequence))
    return jnp.concatenate(done, axis=cut - 1)


def join_stats(first, second):
    top = jnp.maximum(first[0], second[0])
    total = first[1] * jnp.exp(first[0] - top) + second[1] * jnp.exp(second[0] - top)
    return (top, total, first[2] + second[2])


def body(hidden, gain, head, targets, lengths, old_logp, rewards, group_slot):
    resp_here, length_max, shard_cols = hidden.shape
    rows = resp_here * length_max
    whole, gain_full = gather_turned((hidden, gain), FSDP, (2, 0))
    width = whole.shape[2]
    whole = whole.reshape(rows, width)
    vocab_here = head.shape[0]
    vocab_start = lax.axis_index(FSDP) * vocab_here
    groups_all = resp_here * lax.axis_size(DP) // GROUP
    group = group_slot // GROUP
    member = (group[:, None] == jnp.arange(groups_all, dtype=jnp.int32)[None, :]).astype(
        jnp.float32
    )
    local_sums = jnp.sum(member * rewards[:, None], axis=0)
    local_count = jnp.sum(lengths).astype(jnp.float32)
    group_sums, count = in_one((local_sums, local_count), DP)
    adv_resp = rewards - jnp.sum(member * group_sums[None, :], axis=1) / GROUP
    adv = jnp.repeat(adv_resp, length_max)
    mask = (
        (jnp.arange(length_max, dtype=jnp.int32)[None, :] < lengths[:, None])
        .astype(jnp.float32)
        .reshape(rows)
    )
    gain_f = gain_full.astype(jnp.float32)
    inv = lax.rsqrt(
        jnp.mean(jnp.square(whole.astype(jnp.float32)), axis=1, keepdims=True) + eps_norm
    )
    normed = (whole.astype(jnp.float32) * inv * gain_f).astype(jnp.bfloat16)
    logits = lax.dot_general(
        normed, head, (((1,), (1,)), ((), ())), preferred_element_type=jnp.float32
    )
    top_local = jnp.max(logits, axis=1)
    sum_local = jnp.sum(jnp.exp(logits - top_local[:, None]), axis=1)
    local_targets = targets.reshape(rows) - vocab_start
    hits = jnp.arange(vocab_here, dtype=jnp.int32)[None, :] == local_targets[:, None]
    chosen_local = jnp.sum(jnp.where(hits, logits, 0.0), axis=1)
    top, total, chosen = merged((top_local, sum_local, chosen_local), FSDP, join_stats)
    lse = top + jnp.log(total)
    logp = chosen - lse
    ratio = jnp.exp(logp - old_logp.reshape(rows))
    first = ratio * adv
    second = jnp.clip(ratio, clip_low, clip_high) * adv
    policy = -jnp.minimum(first, second)
    policy = jnp.where(adv < 0, jnp.minimum(policy, -dual_bound * adv), policy)
    loss_local = jnp.sum(mask * policy)
    active = (first <= second) & jnp.logical_not((adv < 0) & (first < dual_bound * adv))
    slots_all = rows * lax.axis_size(DP)
    grad_logp = slots_all / count * mask * jnp.where(active, -ratio * adv, 0.0)
    probs = jnp.exp(logits - lse[:, None])
    dlogits = (grad_logp[:, None] * (hits.astype(jnp.float32) - probs)).astype(jnp.bfloat16)
    dn_part = jnp.dot(dlogits, head, preferred_element_type=jnp.float32)
    h_share = hidden.reshape(rows, shard_cols).astype(jnp.float32)
    gain_share = gain.astype(jnp.float32)
    dn_share = summed_rows(dn_part.astype(jnp.bfloat16), ("fsdp_0", "fsdp_1"), 1)
    dots = over_copies(jnp.sum(h_share * (dn_share * gain_share), axis=1), FSDP)
    dy = dn_share * gain_share
    grad_h = inv * dy - h_share * inv * inv * inv * dots[:, None] / width
    gain_part = jnp.sum(dn_share * h_share * inv, axis=0)
    grad_head_t = sum_all_axes(
        lax.dot_general(
            normed, dlogits, (((0,), (0,)), ((), ())), preferred_element_type=jnp.float32
        ).astype(jnp.bfloat16),
        DP,
        0,
    ).astype(jnp.float32)
    loss_sum, grad_gain = (over_copies(loss_local, DP), over_copies(gain_part, DP))
    loss = loss_sum / count
    grad_hidden = grad_h.astype(jnp.bfloat16).reshape(resp_here, length_max, shard_cols)
    return (loss, grad_hidden, grad_gain, grad_head_t)


def solution(mesh):
    split = Mesh(mesh.devices.reshape(8, 4, 4, 2), ("dp_0", "dp_1", "fsdp_0", "fsdp_1"))
    return jax.shard_map(
        body,
        mesh=split,
        in_specs=(
            P(DP, None, FSDP),
            P(FSDP),
            P(FSDP, None),
            P(DP, None),
            P(DP),
            P(DP, None),
            P(DP),
            P(DP),
        ),
        out_specs=(P(), P(DP, None, FSDP), P(FSDP), P(DP, FSDP)),
        check_vma=False,
    )
```

profile of v0, /device:TPU:32, one launch (start us, length us, event | category | flops | bytes accessed | tf_op | source)
XLA Modules:
  0.0 237.5 jit_solution(12902411099103322722)
XLA Ops:
  7.2 0.7 reshape.262
  7.9 2.0 pad_maximum_fusion
  10.0 1.3 reduce_sum.143
  11.9 0.7 and_select_fusion
  12.6 0.7 select_reduce_fusion.2
  13.4 0.6 broadcast_in_dim.24
  14.0 11.2 %all-to-all-start = ((f32[32,1,9]{2,1,0:T(1,128)}), f32[32,1,9]{2,1,0:T(1,128)S(1)}, u32[]{:S(2)}, u32[]{:S(2)}) async-start(f32[32,1,9]{2,1,0:T(1,128)} %broadcast_in_dim.24), calls=%async_computation | async-start | bytes 32768 | tf_op jit(solution)/shard_map/all_to_all | solution.py:31
  25.2 0.7 subtract_bitcast_fusion
  25.9 0.7 copy.72
  26.6 7.1 %all-to-all-done = f32[32,1,9]{2,1,0:T(1,128)S(1)} async-done(((f32[32,1,9]{2,1,0:T(1,128)}), f32[32,1,9]{2,1,0:T(1,128)S(1)}, u32[]{:S(2)}, u32[]{:S(2)}) %all-to-all-start) | async-done | bytes 1184 | tf_op jit(solution)/shard_map/all_to_all | solution.py:31
  33.9 0.7 broadcast_multiply_fusion
  34.6 17.5 %all-gather.2.cloned.1.call-done = bf16[5120,513]{0,1:T(8,128)(2,1)} async-done(((bf16[640,513]{0,1:T(8,128)(2,1)}), bf16[5120,513]{0,1:T(8,128)(2,1)}) %all-gather.2.cloned.1.call-update) | async-done | bytes 5253136 | tf_op jit(solution)/shard_map/all_gather | solution.py:21
  52.1 3.7 %fusion.3 = f32[512]{0:T(512)S(1)} fusion(bf16[5120,513]{0,1:T(8,128)(2,1)} %all-gather.2.cloned.1.call-done), kind=kLoop, calls=%fused_computation.5 | loop fusion | flops 7863808 | bytes 5244928 | tf_op jit(solution)/shard_map/reduce_sum | solution.py:160
  55.8 0.9 slice_convert_fusion
  56.8 5.3 %fusion.24 = (f32[512]{0:T(512)S(1)}, f32[512,512]{0,1:T(8,128)S(1)}) fusion(bf16[512,5120]{1,0:T(8,128)(2,1)S(1)} %copy-done.2, f32[512]{0:T(512)S(1)} %add_rsqrt_fusion, f32[5120]{0:T(1024)S(1)} %bitcast.83, bf16[5120,513]{0,1:T(8,128)(2,1)} %all-gather.2.cloned.1.call-done), kind=kOutput, calls=%fused_computation.70 | convolution fusion | flops 2695101952 | bytes 11558912 | tf_op jit(solution)/shard_map/dot_general | solution.py:163
  62.4 0.7 broadcast_in_dim.27
  63.0 3.4 %all-to-all-start.1 = ((f32[8,3,512]{2,1,0:T(4,128)}), f32[8,3,512]{2,1,0:T(4,128)S(1)}, u32[]{:S(2)}, u32[]{:S(2)}) async-start(f32[8,3,512]{2,1,0:T(4,128)} %broadcast_in_dim.27), calls=%async_computation.1 | async-start | bytes 131072 | tf_op jit(solution)/shard_map/all_to_all | solution.py:31
  66.5 0.6 slice.105
  67.7 4.2 %all-to-all-done.1 = f32[8,3,512]{2,1,0:T(4,128)S(1)} async-done(((f32[8,3,512]{2,1,0:T(4,128)}), f32[8,3,512]{2,1,0:T(4,128)S(1)}, u32[]{:S(2)}, u32[]{:S(2)}) %all-to-all-start.1) | async-done | bytes 49184 | tf_op jit(solution)/shard_map/all_to_all | solution.py:31
  72.4 0.7 broadcast_bitcast_fusion
  73.1 5.6 %convolution_convert_fusion = bf16[5120,512]{1,0:T(8,128)(2,1)S(1)} fusion(f32[512]{0:T(512)S(1)} %add_rsqrt_fusion, f32[5120]{0:T(1024)S(1)} %bitcast.84, bf16[5120,513]{0,1:T(8,128)(2,1)} %all-gather.2.cloned.1.call-done, f32[512,512]{0,1:T(8,128)S(1)} %get-tuple-element.26, f32[512]{0:T(512)S(1)} %bitcast.79, f32[512]{0:T(512)S(1)} %select_multiply_fusion, ...), kind=kOutput, calls=%fused_computation.6 | convolution fusion | flops 2699034624 | bytes 11563008 | tf_op jit(solution)/shard_map/dot_general | solution.py:194
  78.8 1.9 fusion.22
  80.8 1.7 copy.58
  82.5 8.1 %convolution_convert_fusion.1 = bf16[512,5120]{1,0:T(8,128)(2,1)} fusion(bf16[512,5120]{1,0:T(8,128)(2,1)} %param.10, f32[512,512]{0,1:T(8,128)} %copy-done.3, f32[512]{0:T(512)S(1)} %bitcast.80, f32[512]{0:T(512)S(1)} %select_multiply_fusion, s32[512]{0:T(512)S(1)} %bitcast.77), kind=kOutput, calls=%fused_computation.7 | convolution fusion | flops 2688548864 | bytes 11540480 | tf_op jit(solution)/shard_map/dot_general | solution.py:185
  90.6 8.0 %copy.59 = bf16[512,5120]{0,1:T(8,128)(2,1)} copy(bf16[512,5120]{1,0:T(8,128)(2,1)} %convolution_convert_fusion.1) | data formatting | bytes 10485760 | tf_op jit(solution)/shard_map/reshape | solution.py:81
  98.6 9.1 %copy.53 = bf16[2,4,512,640]{3,1,2,0:T(4,128)(2,1)} copy(bf16[2,4,512,640]{2,3,0,1:T(8,128)(2,1)} %bitcast.67) | data formatting | bytes 10485760 | tf_op jit(solution)/shard_map/transpose | solution.py:82
  107.8 13.6 %all_to_all.39 = bf16[2,4,512,640]{3,1,2,0:T(4,128)(2,1)} all-to-all(bf16[2,4,512,640]{3,1,2,0:T(4,128)(2,1)} %copy.53), channel_id=1, replica_groups=mesh['dp_0'=8,'dp_1'=4,'fsdp_0'=4,'fsdp_1'=2] {'fsdp_1'}, dimensions={0} | all-to-all | bytes 10485760 | tf_op jit(solution)/shard_map/all_to_all | solution.py:87
  121.4 6.8 %reduce_sum.152 = bf16[4,512,640]{2,0,1:T(4,128)(2,1)S(1)} reduce(bf16[2,4,512,640]{3,1,2,0:T(4,128)(2,1)} %all_to_all.39, bf16[]{:T(256)} %constant.59.clone.1), dimensions={0}, to_apply=%region_10.11 | reduce | flops 1310720 | bytes 7864322 | tf_op jit(solution)/shard_map/reduce_sum | solution.py:88
  128.2 1.8 copy.55
  130.0 3.8 %all-to-all-start.4 = ((bf16[4,512,640]{2,1,0:T(8,128)(2,1)}), bf16[4,512,640]{2,1,0:T(8,128)(2,1)S(1)}, u32[]{:S(2)}, u32[]{:S(2)}) async-start(bf16[4,512,640]{2,1,0:T(8,128)(2,1)} %copy.55), calls=%async_computation.4 | async-start | bytes 5242880 | tf_op jit(solution)/shard_map/all_to_all | solution.py:95
  133.9 0.5 reduce-scatter.7.cloned.1.call-update
  134.4 28.4 %reduce-scatter.9.cloned.1.call-done = bf16[8,80,512]{2,1,0:T(8,128)(2,1)} async-done(((bf16[32,80,512]{2,1,0:T(8,128)(2,1)}), bf16[8,80,512]{2,1,0:T(8,128)(2,1)}) %reduce-scatter.9.cloned.1.call-update) | async-done | bytes 655376 | tf_op jit(solution)/shard_map/reduce_scatter | solution.py:114
  162.9 3.4 %all-to-all-done.4 = bf16[4,512,640]{2,1,0:T(8,128)(2,1)S(1)} async-done(((bf16[4,512,640]{2,1,0:T(8,128)(2,1)}), bf16[4,512,640]{2,1,0:T(8,128)(2,1)S(1)}, u32[]{:S(2)}, u32[]{:S(2)}) %all-to-all-start.4) | async-done | bytes 2621472 | tf_op jit(solution)/shard_map/all_to_all | solution.py:95
  166.3 1.5 broadcast_in_dim.30
  167.8 10.1 %all-to-all-start.2 = ((f32[32,1,1]{2,1,0:T(1,128)}), f32[32,1,1]{2,1,0:T(1,128)S(1)}, u32[]{:S(2)}, u32[]{:S(2)}) async-start(f32[32,1,1]{2,1,0:T(1,128)} %broadcast_in_dim.30), calls=%async_computation.2 | async-start | bytes 32768 | tf_op jit(solution)/shard_map/all_to_all | solution.py:31
  177.9 2.2 convert_reduce_fusion
  180.6 5.7 %all-to-all-done.2 = f32[32,1,1]{2,1,0:T(1,128)S(1)} async-done(((f32[32,1,1]{2,1,0:T(1,128)}), f32[32,1,1]{2,1,0:T(1,128)S(1)}, u32[]{:S(2)}, u32[]{:S(2)}) %all-to-all-start.2) | async-done | bytes 160 | tf_op jit(solution)/shard_map/all_to_all | solution.py:31
  186.4 0.6 broadcast_in_dim.32
  187.0 3.3 %all-to-all-start.5 = ((f32[8,1,512]{2,1,0:T(1,128)}), f32[8,1,512]{2,1,0:T(1,128)S(1)}, u32[]{:S(2)}, u32[]{:S(2)}) async-start(f32[8,1,512]{2,1,0:T(1,128)} %broadcast_in_dim.32), calls=%async_computation.5 | async-start | bytes 32768 | tf_op jit(solution)/shard_map/all_to_all | solution.py:31
  190.3 0.6 reduce_sum.151
  192.3 3.3 %all-to-all-done.5 = f32[8,1,512]{2,1,0:T(1,128)S(1)} async-done(((f32[8,1,512]{2,1,0:T(1,128)}), f32[8,1,512]{2,1,0:T(1,128)S(1)}, u32[]{:S(2)}, u32[]{:S(2)}) %all-to-all-start.5) | async-done | bytes 16416 | tf_op jit(solution)/shard_map/all_to_all | solution.py:31
  195.6 0.7 broadcast_in_dim.33
  196.3 4.9 %all-to-all-start.6 = ((f32[32,1,640]{2,1,0:T(1,128)}), f32[32,1,640]{2,1,0:T(1,128)S(1)}, u32[]{:S(2)}, u32[]{:S(2)}) async-start(f32[32,1,640]{2,1,0:T(1,128)} %broadcast_in_dim.33), calls=%async_computation.6 | async-start | bytes 163840 | tf_op jit(solution)/shard_map/all_to_all | solution.py:31
  201.3 1.3 fusion.9
  202.6 8.1 %all-to-all-done.6 = f32[32,1,640]{2,1,0:T(1,128)S(1)} async-done(((f32[32,1,640]{2,1,0:T(1,128)}), f32[32,1,640]{2,1,0:T(1,128)S(1)}, u32[]{:S(2)}, u32[]{:S(2)}) %all-to-all-start.6) | async-done | bytes 81952 | tf_op jit(solution)/shard_map/all_to_all | solution.py:31
  210.7 0.7 reduce_sum.158
  211.4 16.8 %reduce-scatter.11.cloned.1.call-done = bf16[1,80,512]{2,1,0:T(8,128)(2,1)} async-done(((bf16[8,80,512]{2,1,0:T(8,128)(2,1)}), bf16[1,80,512]{2,1,0:T(8,128)(2,1)}) %reduce-scatter.11.cloned.1.call-update) | async-done | bytes 81936 | tf_op jit(solution)/shard_map/reduce_scatter | solution.py:114
  228.1 1.7 maximum_convert_fusion
  (63 shorter events, 2.0 us)
Async XLA Ops:
  7.2 44.9 %all-gather.2.cloned.1.call-start = ((), (), s32[]{:S(2)}) async-start(), calls=%async_computation.11 | async-start | bytes 5990400 | tf_op jit(solution)/shard_map/all_gather | solution.py:21
  14.0 19.7 %all-to-all-start = ((f32[32,1,9]{2,1,0:T(1,128)}), f32[32,1,9]{2,1,0:T(1,128)S(1)}, u32[]{:S(2)}, u32[]{:S(2)}) async-start(f32[32,1,9]{2,1,0:T(1,128)} %broadcast_in_dim.24), calls=%async_computation | async-start | bytes 32768 | tf_op jit(solution)/shard_map/all_to_all | solution.py:31
  52.1 4.7 %copy-start.2 = (bf16[512,5120]{1,0:T(8,128)(2,1)S(1)}, bf16[512,5120]{1,0:T(8,128)(2,1)}, u32[]{:S(2)}) copy-start(bf16[512,5120]{1,0:T(8,128)(2,1)} %param.10) | copy-start | bytes 15728644
  56.8 15.6 %copy-start.5 = (f32[2,256]{1,0:T(2,128)S(1)}, f32[2,256]{1,0:T(2,128)}, u32[]{:S(2)}) copy-start(f32[2,256]{1,0:T(2,128)} %param.13) | copy-start | bytes 6148
  56.8 15.6 %copy-start.6 = (s32[2]{0:T(128)S(1)}, s32[2]{0:T(128)}, u32[]{:S(2)}) copy-start(s32[2]{0:T(128)} %param.12) | copy-start | bytes 28
  62.1 16.7 %copy-start.3 = (f32[512,512]{0,1:T(8,128)}, f32[512,512]{0,1:T(8,128)S(1)}, u32[]{:S(2)}) copy-start(f32[512,512]{0,1:T(8,128)S(1)} %get-tuple-element.26) | copy-start | bytes 3145732
  63.0 8.9 %all-to-all-start.1 = ((f32[8,3,512]{2,1,0:T(4,128)}), f32[8,3,512]{2,1,0:T(4,128)S(1)}, u32[]{:S(2)}, u32[]{:S(2)}) async-start(f32[8,3,512]{2,1,0:T(4,128)} %broadcast_in_dim.27), calls=%async_computation.1 | async-start | bytes 131072 | tf_op jit(solution)/shard_map/all_to_all | solution.py:31
  66.4 67.5 %reduce-scatter.5.cloned.1.call-start = ((), (), s32[]{:S(2)}) async-start(), calls=%async_computation.12 | async-start | bytes 2949120 | tf_op jit(solution)/shard_map/reduce_scatter | solution.py:114
  80.7 82.1 %reduce-scatter.9.cloned.1.call-start = ((), (), s32[]{:S(2)}) async-start(), calls=%async_computation.14 | async-start | bytes 3276800 | tf_op jit(solution)/shard_map/reduce_scatter | solution.py:114
  128.2 34.7 %copy-start.4 = (bf16[640]{0:T(1024)(128)(2,1)S(1)}, bf16[640]{0:T(1024)(128)(2,1)}, u32[]{:S(2)}) copy-start(bf16[640]{0:T(1024)(128)(2,1)} %param.9) | copy-start | bytes 3844
  130.0 50.1 %copy-start.1 = (bf16[2,256,640]{2,1,0:T(8,128)(2,1)S(1)}, bf16[2,256,640]{2,1,0:T(8,128)(2,1)}, u32[]{:S(2)}) copy-start(bf16[2,256,640]{2,1,0:T(8,128)(2,1)} %param.8) | copy-start | bytes 1966084
  130.0 36.3 %all-to-all-start.4 = ((bf16[4,512,640]{2,1,0:T(8,128)(2,1)}), bf16[4,512,640]{2,1,0:T(8,128)(2,1)S(1)}, u32[]{:S(2)}, u32[]{:S(2)}) async-start(bf16[4,512,640]{2,1,0:T(8,128)(2,1)} %copy.55), calls=%async_computation.4 | async-start | bytes 5242880 | tf_op jit(solution)/shard_map/all_to_all | solution.py:95
  133.8 77.5 %reduce-scatter.7.cloned.1.call-start = ((), (), s32[]{:S(2)}) async-start(), calls=%async_computation.13 | async-start | bytes 409600 | tf_op jit(solution)/shard_map/reduce_scatter | solution.py:114
  134.4 93.7 %reduce-scatter.11.cloned.1.call-start = ((), (), s32[]{:S(2)}) async-start(), calls=%async_computation.15 | async-start | bytes 737280 | tf_op jit(solution)/shard_map/reduce_scatter | solution.py:114
  166.3 1.5 copy-start
  167.8 18.5 %all-to-all-start.2 = ((f32[32,1,1]{2,1,0:T(1,128)}), f32[32,1,1]{2,1,0:T(1,128)S(1)}, u32[]{:S(2)}, u32[]{:S(2)}) async-start(f32[32,1,1]{2,1,0:T(1,128)} %broadcast_in_dim.30), calls=%async_computation.2 | async-start | bytes 32768 | tf_op jit(solution)/shard_map/all_to_all | solution.py:31
  187.0 8.6 %all-to-all-start.5 = ((f32[8,1,512]{2,1,0:T(1,128)}), f32[8,1,512]{2,1,0:T(1,128)S(1)}, u32[]{:S(2)}, u32[]{:S(2)}) async-start(f32[8,1,512]{2,1,0:T(1,128)} %broadcast_in_dim.32), calls=%async_computation.5 | async-start | bytes 32768 | tf_op jit(solution)/shard_map/all_to_all | solution.py:31
  196.3 14.4 %all-to-all-start.6 = ((f32[32,1,640]{2,1,0:T(1,128)}), f32[32,1,640]{2,1,0:T(1,128)S(1)}, u32[]{:S(2)}, u32[]{:S(2)}) async-start(f32[32,1,640]{2,1,0:T(1,128)} %broadcast_in_dim.33), calls=%async_computation.6 | async-start | bytes 163840 | tf_op jit(solution)/shard_map/all_to_all | solution.py:31
Sparse Core Ops, SparseCore 0:
  10.1 41.9 all-gather.1
  80.8 42.6 reduce-scatter.4
  126.1 36.6 reduce-scatter.8
  165.2 23.0 reduce-scatter.6
  190.6 37.4 reduce-scatter.10
where the time goes:
time: 240 us; the launch traced here: 237 us
  waiting for transfers between devices  95.1 us (40%)
  starting transfers between devices  36.9 us (15%)
  local copies, waits for them, and re-layouts  29.1 us (12%)
  other arithmetic  26 us (11%)
  matrix products  19 us (8%)
  between operations  17.8 us (7%)
  blocking collectives  13.6 us (6%)
    reduce_scatter x4, waiting for transfers between devices, own_block(): pieces = lax.psum_scatter(pieces, axes[k], scatter_dimension=0, tiled=True)  45.1 us
    all_to_all x5, starting transfers between devices, copy_for_each(): lax.all_to_all(jnp.broadcast_to(value[None], (size, *value.shape)), axis,...  32.9 us
    all_to_all x5, waiting for transfers between devices, copy_for_each(): lax.all_to_all(jnp.broadcast_to(value[None], (size, *value.shape)), axis,...  28.4 us
    all_gather x1, waiting for transfers between devices, gather_turned(): filled, at, done = (lax.all_gather(both, axis, axis=0, tiled=True), 0, [])  17.5 us
    all_to_all x1, blocking collectives, sent_and_summed(): lax.all_to_all(pieces, axis, split_axis=0, concat_axis=0, tiled=True)  13.6 us
    transpose x1, local copies, waits for them, and re-layouts, cut_along(): return jnp.moveaxis(pieces, dim, 0)  9.14 us
    dot_general x1, matrix products, body(): dn_part = jnp.dot(dlogits, head, preferred_element_type=jnp.float32)  8.11 us
    reshape x1, local copies, waits for them, and re-layouts, cut_along(): value.reshape(*dims[:dim], size, dims[dim] // size, *dims[dim + 1:])  8.02 us
  transfers between devices with their start and end apart: 11, of which 9 were waited for; matrix products, arithmetic and copies ran while one was open for 21% of the time, Pallas kernels for 0%

commit v1 on v0

v1 whole, which is shorter than its diff:
```python
import functools

import jax
import jax.numpy as jnp
from jax import lax
from jax.experimental import pallas as pl
from jax.experimental.pallas import tpu as pltpu
from jax.sharding import Mesh
from jax.sharding import PartitionSpec as P

GROUP = 8
FSDP = ("y", "c")
DP = ("z", "x")
SIZES = {"z": 8, "x": 4, "y": 4, "c": 2}

eps_norm = 1e-06
clip_low = 0.8
clip_high = 1.2
dual_bound = 3.0

f32, bf16 = jnp.float32, jnp.bfloat16
VMEM = pltpu.VMEM


def shift(value, axis, step):
    n = SIZES[axis]
    return lax.ppermute(value, axis, [(i, (i + step) % n) for i in range(n)])


def turn(value, step):
    return lax.ppermute(
        value, "z", [(i, (i + (step if i % 2 == 0 else -step)) % 8) for i in range(8)]
    )


def params(limit=60 << 20):
    return pltpu.CompilerParams(vmem_limit_bytes=limit)


def cost(flops, nbytes, trans=0):
    return pl.CostEstimate(flops=flops, bytes_accessed=nbytes, transcendentals=trans)


def whole(space=None):
    return pl.BlockSpec(memory_space=space or VMEM)


def like(shape, kind=bf16):
    return jax.ShapeDtypeStruct(shape, kind)


def column(row):
    n = row.shape[1]
    return jnp.transpose(jnp.broadcast_to(row, (128, n)))[:, 0:1]


def rows_of(columns):
    n = columns[0].shape[0]
    lane = lax.broadcasted_iota(jnp.int32, (n, 128), 1)
    table = jnp.zeros((n, 128), f32)
    for k, col in enumerate(columns):
        table = jnp.where(lane == k, col, table)
    return jnp.transpose(table)[0:8, :]


def full(shape):
    return pl.BlockSpec(shape, lambda k, *at: (0,) * len(shape))


def logits_kernel(count, per, last, table, at, *refs):
    pieces = refs[: count * per]
    refs = refs[count * per :]
    if last:
        acc_in, sq_in, tgt = refs[:3]
        refs = refs[3:]
    head, hb = refs[:2]
    outs, (slot, acc, sq, sem) = refs[2:-4], refs[-4:]
    j = pl.program_id(0)
    rows = acc.shape[0]

    @pl.when(j == 0)
    def _():
        copies = []
        for k, piece in enumerate(pieces):
            first = 0 if k % per == 0 else pieces[k - 1].shape[0]
            copies.append(
                pltpu.make_async_copy(
                    piece, slot.at[k // per, pl.ds(first, piece.shape[0]), :], sem.at[k]
                )
            )
        for copy in copies:
            copy.start()
        if last:
            acc[...] = acc_in[...]
            sq[...] = column(sq_in[0:1, :])
        else:
            acc[...] = jnp.zeros_like(acc)
            sq[...] = jnp.zeros_like(sq)
        for copy in copies:
            copy.wait()

    gain = slot[j, 0:16, :][0:1, :].astype(f32)
    raw = slot[j, 16 : 16 + rows, :].astype(f32)
    sq[...] += jnp.sum(raw * raw, axis=1, keepdims=True)
    scaled = (raw * gain).astype(bf16)
    hb[0] = scaled
    acc[...] += lax.dot_general(
        scaled, head[...], (((1,), (1,)), ((), ())), preferred_element_type=f32
    )

    @pl.when(j == count - 1)
    def _():
        if not last:
            outs[0][...] = acc[...]
            outs[1][...] = rows_of([sq[...]])
            return
        lg, st, inv_ref = outs
        inv_c = lax.rsqrt(sq[...] / 5120.0 + eps_norm)
        inv_ref[...] = rows_of([inv_c])
        logits = acc[...] * inv_c
        lg[...] = logits
        half = logits.shape[1]
        entry = lax.broadcasted_iota(jnp.int32, logits.shape, 1) + at[0] * half
        target = column(tgt[...].astype(f32)).astype(jnp.int32)
        top = jnp.max(logits, axis=1, keepdims=True)
        power = jnp.exp(logits - top)
        found = rows_of(
            [
                top,
                jnp.sum(power, axis=1, keepdims=True),
                jnp.sum(power * logits, axis=1, keepdims=True),
                jnp.sum(jnp.where(entry == target, logits, 0.0), axis=1, keepdims=True),
            ]
        )
        for k in range(st.shape[0]):
            st[k] = found


def logits_of(table, at, blocks, head, before=None, targets=None):
    count, per = len(blocks), len(blocks[0])
    last = before is not None
    half = head.shape[0]
    cols = blocks[0][0].shape[1]
    height = sum(p.shape[0] for p in blocks[0])
    rows = height - 16
    anywhere = pl.BlockSpec(memory_space=pl.ANY)
    shapes = [like((count, rows, cols))]
    specs = [pl.BlockSpec((1, rows, cols), lambda j, *a: (j, 0, 0))]
    shapes += [like((rows, half), f32)]
    shapes += [like((8, 8, rows), f32)] if last else []
    shapes += [like((8, rows), f32)]
    extra = (*before, targets) if last else ()
    return pl.pallas_call(
        functools.partial(logits_kernel, count, per, last),
        out_shape=shapes,
        grid_spec=pltpu.PrefetchScalarGridSpec(
            num_scalar_prefetch=2,
            grid=(count,),
            in_specs=[anywhere] * (count * per)
            + [full(e.shape) for e in extra]
            + [pl.BlockSpec((half, cols), lambda j, table, at: (0, table[j]))],
            out_specs=specs + [full(s.shape) for s in shapes[1:]],
            scratch_shapes=[
                VMEM((count, height, cols), bf16),
                VMEM((rows, half), f32),
                VMEM((rows, 1), f32),
                pltpu.SemaphoreType.DMA((count * per,)),
            ],
        ),
        compiler_params=params(),
        cost_estimate=cost(2 * rows * half * count * cols, 2 * count * cols * (2 * rows + half)),
        name="logits_last" if last else "logits_first",
    )(table, at, *[p for b in blocks for p in b], *extra, head)


def turned_kernel(a, out):
    out[0] = jnp.transpose(a[0])


def turned(blocks):
    count, rows, cols = blocks.shape
    return pl.pallas_call(
        turned_kernel,
        out_shape=like((count, cols, rows)),
        grid=(count,),
        in_specs=[pl.BlockSpec((1, rows, cols), lambda j: (j, 0, 0))],
        out_specs=pl.BlockSpec((1, cols, rows), lambda j: (j, 0, 0)),
        compiler_params=params(),
        cost_estimate=cost(0, 4 * blocks.size),
        name="turned",
    )(blocks)


def policy_kernel(at, nums, st, lg, inv_ref, tgt, old, dl, small):
    half = lg.shape[1]
    rows = lg.shape[0]
    top = jnp.max(st[:, 0, :], axis=0, keepdims=True)
    weight = jnp.exp(st[:, 0, :] - top)
    total = jnp.sum(st[:, 1, :] * weight, axis=0, keepdims=True)
    moment = jnp.sum(st[:, 2, :] * weight, axis=0, keepdims=True)
    chosen = jnp.sum(st[:, 3, :], axis=0, keepdims=True)
    lse = top + jnp.log(total)
    inv = inv_ref[0:1, :]
    ratio = jnp.exp(chosen - lse - old[...])
    position = lax.broadcasted_iota(jnp.int32, ratio.shape, 1)
    second_one = position >= rows // 2
    adv = jnp.where(second_one, nums[1], nums[0])
    length = jnp.where(second_one, nums[3], nums[2])
    within = jnp.where(second_one, position - rows // 2, position).astype(f32)
    mask = jnp.where(within < length, 1.0, 0.0)
    first = ratio * adv
    second = jnp.clip(ratio, clip_low, clip_high) * adv
    policy = -jnp.minimum(first, second)
    policy = jnp.where(adv < 0, jnp.minimum(policy, -dual_bound * adv), policy)
    active = (first <= second) & jnp.logical_not((adv < 0) & (first < dual_bound * adv))
    grad_logp = nums[4] * mask * jnp.where(active, -first, 0.0)
    kappa = inv * inv * grad_logp * (chosen - moment / total) / 5120.0
    small[...] = jnp.concatenate(
        [kappa, mask * policy, jnp.zeros((6, ratio.shape[1]), f32)], axis=0
    )
    lse_c, scale_c = column(lse), column(grad_logp * inv)
    target = column(tgt[...].astype(f32)).astype(jnp.int32)
    entry = lax.broadcasted_iota(jnp.int32, lg.shape, 1) + at[0] * half
    hit = jnp.where(entry == target, 1.0, 0.0)
    dl[...] = (scale_c * (hit - jnp.exp(lg[...] - lse_c))).astype(bf16)


def policy_of(at, nums, stats, logits, inv, targets, old_logp):
    rows, half = logits.shape
    return pl.pallas_call(
        policy_kernel,
        out_shape=[like((rows, half)), like((8, rows), f32)],
        in_specs=[whole(pltpu.SMEM)] * 2 + [whole()] * 5,
        out_specs=[whole()] * 2,
        compiler_params=params(),
        cost_estimate=cost(8 * rows * half, 6 * rows * half, rows * half),
        name="policy",
    )(at, nums, stats, logits, inv, targets, old_logp)


def left_of(j, early, late):
    return jnp.where(j < 6, early[0], late[0])


def heads_x_kernel(table, at, early, late, dl, out):
    j = pl.program_id(0)
    got = jnp.dot(left_of(j, early, late), dl[...], preferred_element_type=f32).astype(bf16)
    step = got.shape[0] // 4
    for k in range(4):
        out[k, table[j]] = got[k * step : (k + 1) * step, :]


def heads_z_kernel(table, at, early, late, dl, send_a, send_b, keep_a, keep_b, tmp):
    j = pl.program_id(0)
    x, z = at[4], at[3]
    tmp[...] = jnp.dot(left_of(j, early, late), dl[...], preferred_element_type=f32)
    step = tmp.shape[0] // 4
    width = tmp.shape[1] // 2
    odd = lax.rem(z, 2)
    ahead = lax.rem(table[j] - z + 8, 8)
    behind = lax.rem(8 - ahead, 8)
    for side, send, keep in ((0, send_a, keep_a), (1, send_b, keep_b)):
        q = jnp.where(odd == side, ahead, behind)
        low = lax.rem(q, 4)
        sent = (low == 1) | (low == 2)
        send_at = jnp.where(sent, 2 * (q // 4) + low - 1, 0)
        keep_at = jnp.where(q == 0, 0, jnp.where(q == 7, 1, jnp.where(q == 4, 2, 3)))
        cut = slice(side * width, (side + 1) * width)

        @pl.when(sent)
        def _(send=send, cut=cut, send_at=send_at):
            for k in range(4):
                start = pl.multiple_of(lax.rem(x + k, 4) * step, step)
                send[send_at, k] = tmp[pl.ds(start, step), cut].astype(bf16)

        @pl.when(jnp.logical_not(sent))
        def _(keep=keep, cut=cut, keep_at=keep_at):
            for k in range(4):
                start = pl.multiple_of(lax.rem(x + k, 4) * step, step)
                keep[keep_at, k] = tmp[pl.ds(start, step), cut].astype(bf16)


def heads_of(table, at, early, late, dl, second, kernel, shapes, scratch, name):
    _, cols, rows = early.shape
    half = dl.shape[1] // 2
    return pl.pallas_call(
        kernel,
        out_shape=[like(s) for s in shapes],
        grid_spec=pltpu.PrefetchScalarGridSpec(
            num_scalar_prefetch=2,
            grid=(8,),
            in_specs=[
                pl.BlockSpec((1, cols, rows), lambda j, *a: (jnp.minimum(j, 5), 0, 0)),
                pl.BlockSpec((1, cols, rows), lambda j, *a: (jnp.maximum(j - 6, 0), 0, 0)),
                pl.BlockSpec((rows, half), lambda j, *a: (0, second)),
            ],
            out_specs=[full(s) for s in shapes],
            scratch_shapes=[VMEM((cols, half), f32)] if scratch else [],
        ),
        compiler_params=params(),
        cost_estimate=cost(2 * rows * 8 * cols * half, 16 * rows * cols + 16 * cols * half),
        name=name,
    )(table, at, early, late, dl)


def back_kernel(table, at, dl, head, send, keep):
    k = pl.program_id(0)
    part = jnp.dot(dl[...], head[...], preferred_element_type=f32).astype(bf16)

    @pl.when(k < 4)
    def _():
        send[0] = part

    @pl.when(k >= 4)
    def _():
        keep[0] = part


def back_of(table, at, dl, head, cols):
    rows, half = dl.shape
    return pl.pallas_call(
        back_kernel,
        out_shape=[like((4, rows, cols))] * 2,
        grid_spec=pltpu.PrefetchScalarGridSpec(
            num_scalar_prefetch=2,
            grid=(8,),
            in_specs=[
                full((rows, half)),
                pl.BlockSpec((half, cols), lambda k, table, at: (0, table[8 + k])),
            ],
            out_specs=[
                pl.BlockSpec((1, rows, cols), lambda k, *a: (jnp.minimum(k, 3), 0, 0)),
                pl.BlockSpec((1, rows, cols), lambda k, *a: (jnp.maximum(k - 4, 0), 0, 0)),
            ],
        ),
        compiler_params=params(),
        cost_estimate=cost(2 * rows * half * 8 * cols, 16 * half * cols + 16 * rows * cols),
        name="back",
    )(table, at, dl, head)


def sum_cut_kernel(n, groups, *refs):
    ins, outs = refs[:n], refs[n:]
    for out, group in zip(outs, groups):
        for at, j in enumerate(group):
            total = ins[0][j].astype(f32)
            for other in ins[1:]:
                total = total + other[j].astype(f32)
            if len(out.shape) == len(ins[0].shape):
                out[at] = total.astype(out.dtype)
            else:
                out[...] = total.astype(out.dtype)


def sum_cut(ins, groups, name):
    shape = ins[0].shape[1:]
    outs = [like(((len(g),) if len(g) > 1 else ()) + shape) for g in groups]
    return pl.pallas_call(
        functools.partial(sum_cut_kernel, len(ins), groups),
        out_shape=outs,
        in_specs=[whole()] * len(ins),
        out_specs=[whole()] * len(outs),
        compiler_params=params(),
        cost_estimate=cost(len(ins) * ins[0].size, 2 * (len(ins) + 1) * ins[0].size),
        name=name,
    )(*ins)


def sum_first_kernel(a, out):
    for k in range(out.shape[0]):
        total = a[0, k].astype(f32)
        for s in range(1, a.shape[0]):
            total = total + a[s, k].astype(f32)
        out[k] = total.astype(out.dtype)


def sum_first(value, name):
    return pl.pallas_call(
        sum_first_kernel,
        out_shape=like(value.shape[1:]),
        in_specs=[whole()],
        out_specs=whole(),
        compiler_params=params(),
        cost_estimate=cost(value.size, 3 * value.size),
        name=name,
    )(value)


def both_kernel(keep_a, got_a, keep_b, got_b, *outs):
    width = keep_a.shape[2]
    for k, out in enumerate(outs):
        for first, keep, got in ((0, keep_a, got_a), (width, keep_b, got_b)):
            total = keep[k].astype(f32) + got[k].astype(f32)
            out[:, first : first + width] = total.astype(bf16)


def join_kernel(from_z, s0, s1, s2, s3, out):
    width = s0.shape[1]
    total = from_z[0].astype(f32)
    for k in range(1, from_z.shape[0]):
        total = total + from_z[k].astype(f32)
    out[:, :width] = total
    out[:, width:] = (
        s0[...].astype(f32) + s1[...].astype(f32) + s2[...].astype(f32) + s3[...].astype(f32)
    )


def final_kernel(u0, u1, u2, u3, h_ref, g_ref, small, out, part):
    gain = g_ref[...].astype(f32)
    resp, rows, _ = h_ref.shape
    kappa = column(small[0:1, :])
    sums = None
    for r in range(resp):
        cut = slice(r * rows, (r + 1) * rows)
        u = sum(v[cut, :].astype(f32) for v in (u0, u1, u2, u3))
        h = h_ref[r].astype(f32)
        out[r] = (gain * u - h * kappa[cut, :]).astype(bf16)
        now = jnp.sum(u * h, axis=0, keepdims=True)
        sums = now if sums is None else sums + now
    loss = jnp.sum(small[1:2, :], axis=1, keepdims=True)
    part[...] = jnp.concatenate([sums, jnp.broadcast_to(loss, (1, 128))], axis=1)


def simple(kernel, shapes, ins, nbytes, name):
    return pl.pallas_call(
        kernel,
        out_shape=shapes,
        in_specs=[whole()] * len(ins),
        out_specs=[whole()] * len(shapes),
        compiler_params=params(),
        cost_estimate=cost(nbytes // 2, nbytes),
        name=name,
    )(*ins)


def copy_for_each(value, axis):
    size = lax.axis_size(axis)
    return lax.all_to_all(
        jnp.broadcast_to(value[None], (size, *value.shape)), axis, 0, 0, tiled=True
    )


def body(hidden, gain, head, targets, lengths, old_logp, rewards, group_slot):
    resp_here, length_max, cols = hidden.shape
    rows = resp_here * length_max
    x, y, z, c = (lax.axis_index(a) for a in ("x", "y", "z", "c"))
    order = jnp.array([0, 0, 3, 3, 1, 1, 2, 2, 0, 1, 2, 3, 0, 1, 2, 3], jnp.int32)
    other = jnp.array([0, 1] * 4 + [1] * 4 + [0] * 4, jnp.int32)
    table = (2 * ((y + order) % 4) + (c + other) % 2).astype(jnp.int32)
    at = jnp.stack([2 * y + c, y, c, z, x]).astype(jnp.int32)

    payload = jnp.concatenate(
        [jnp.broadcast_to(gain[None], (16, cols)), hidden.reshape(rows, cols)], axis=0
    )
    cut = 16 + length_max
    own_o = shift(payload, "c", 1)
    prev, following = shift(payload, "y", 1), shift(payload, "y", -1)
    far_a, far_b = shift(prev[:cut], "y", 1), shift(following[cut:], "y", -1)
    prev_o, following_o = shift(prev, "c", 1), shift(following, "c", 1)
    far_a_o, far_b_o = shift(far_a, "c", 1), shift(far_b, "c", 1)

    groups_all = resp_here * lax.axis_size(DP) // GROUP
    group = group_slot // GROUP
    member = (group[:, None] == jnp.arange(groups_all, dtype=jnp.int32)[None, :]).astype(f32)
    local = jnp.concatenate(
        [jnp.sum(member * rewards[:, None], axis=0), jnp.sum(lengths).astype(f32)[None]]
    )
    sums = copy_for_each(local, DP).sum(axis=0)
    group_sums, count = sums[:groups_all], sums[groups_all]
    adv_resp = rewards - jnp.sum(member * group_sums[None, :], axis=1) / GROUP
    slots_all = rows * lax.axis_size(DP)
    nums = jnp.concatenate([adv_resp, lengths.astype(f32), (slots_all / count)[None]])
    targets = targets.reshape(1, rows)
    old_logp = old_logp.reshape(1, rows)

    hb_early, acc, sq = logits_of(
        table, at, [(payload,), (own_o,), (prev,), (prev_o,), (following,), (following_o,)], head
    )
    early = turned(hb_early)
    hb_late, logits, stats, inv = logits_of(
        table[6:], at, [(far_a, far_b), (far_a_o, far_b_o)], head, (acc, sq), targets
    )
    all_stats = lax.all_to_all(stats, FSDP, 0, 0, tiled=True)
    late = turned(hb_late)
    dl, small = policy_of(at, nums, all_stats, logits, inv, targets, old_logp)

    part, half = cols // 4, dl.shape[1] // 2
    zs = (4, 4, part, half // 2)
    send_a, send_b, keep_a, keep_b = heads_of(
        table, at, early, late, dl, 1, heads_z_kernel, (zs,) * 4, True, "heads_z"
    )
    (to_x,) = heads_of(
        table, at, early, late, dl, 0, heads_x_kernel, ((4, 8, part, half),), False, "heads_x"
    )
    u_send, u_keep = back_of(table, at, dl, head, cols)
    got_a, got_b = turn(send_a, 1), turn(send_b, -1)
    from_x = lax.all_to_all(to_x, "x", 0, 0, tiled=True)
    u_got = shift(u_send, "c", 1)

    send2_a, keep2_a = sum_cut((keep_a, got_a), ((2, 1), (3, 0)), "sum_z1a")
    send2_b, keep2_b = sum_cut((keep_b, got_b), ((2, 1), (3, 0)), "sum_z1b")
    got2_a, got2_b = turn(send2_a, -1), turn(send2_b, 1)
    send3_a, keep3_a = sum_cut((keep2_a, got2_a), ((0,), (1,)), "sum_z2a")
    send3_b, keep3_b = sum_cut((keep2_b, got2_b), ((0,), (1,)), "sum_z2b")
    got3_a, got3_b = turn(send3_a, 3), turn(send3_b, -3)
    four = simple(
        both_kernel,
        [like((part, half))] * 4,
        (keep3_a, got3_a, keep3_b, got3_b),
        12 * keep3_a.size,
        "sum_z3",
    )
    z_parts = (four[0], shift(four[1], "x", 1), shift(four[2], "x", 2), shift(four[3], "x", -1))

    to_z = sum_first(from_x, "sum_x")
    from_z = lax.all_to_all(to_z, "z", 0, 0, tiled=True)
    (grad_head_t,) = simple(
        join_kernel,
        [like((part, 2 * half), f32)],
        (from_z, *z_parts),
        2 * from_z.size + 16 * part * half,
        "join",
    )

    u0, u1, u2, u3 = sum_cut((u_keep, u_got), ((0,), (1,), (2,), (3,)), "sum_u")
    u_all = (u0, shift(u1, "y", 1), shift(u2, "y", 2), shift(u3, "y", -1))
    grad_hidden, gain_part = simple(
        final_kernel,
        [like(hidden.shape), like((1, cols + 128), f32)],
        (*u_all, hidden, gain.reshape(1, cols), small),
        12 * rows * cols,
        "final",
    )
    tail = gain_part.reshape(-1, 128)
    tail = tail + shift(tail, "x", 1) + shift(tail, "x", 2) + shift(tail, "x", -1)
    for step in (1, -1, 3):
        tail = tail + turn(tail, step)
    tail = tail.reshape(-1)
    return (tail[cols] / count, grad_hidden, tail[:cols], grad_head_t)


def solution(mesh):
    split = Mesh(mesh.devices.reshape(8, 4, 4, 2), ("z", "x", "y", "c"))
    return jax.shard_map(
        body,
        mesh=split,
        in_specs=(
            P(DP, None, FSDP),
            P(FSDP),
            P(FSDP, None),
            P(DP, None),
            P(DP),
            P(DP, None),
            P(DP),
            P(DP),
        ),
        out_specs=(P(), P(DP, None, FSDP), P(FSDP), P(DP, FSDP)),
        check_vma=False,
    )
```

time: 240 us -> 225 us (0.938)
  Pallas kernels: 0 us -> 79.4 us
  waiting for transfers between devices: 95.1 us -> 59.2 us
  starting transfers between devices: 36.9 us -> 59.5 us
  other arithmetic: 26 us -> 4.26 us
  matrix products: 19 us -> 0 us
  blocking collectives: 13.6 us -> 0 us
  local copies, waits for them, and re-layouts: 29.1 us -> 15.6 us
  between operations: 17.8 us -> 4.72 us
    pallas_call x0 -> x17, Pallas kernels: none -> 79.4 us  [the longest x2 17.6 us: heads_of(): pl.pallas_call(kernel, out_shape=[like(s) for s in shapes], grid_spec=plt...]
    reduce_scatter x4 -> x0, waiting for transfers between devices: 45.1 us -> none  [own_block(): pieces = lax.psum_scatter(pieces, axes[k], scatter_dimension=0, tiled=True)]
    ppermute x0 -> x28, starting transfers between devices: none -> 36.4 us  [the longest x19 20 us: shift(): return lax.ppermute(value, axis, [(i, (i + step) % n) for i in range(n)])]
    ppermute x0 -> x28, waiting for transfers between devices: none -> 27.9 us  [the longest x19 16.4 us: shift(): return lax.ppermute(value, axis, [(i, (i + step) % n) for i in range(n)])]
    all_to_all x5 -> x1, waiting for transfers between devices: 28.4 us -> 5.46 us  [copy_for_each(): lax.all_to_all(jnp.broadcast_to(value[None], (size, *value.shape)), axis,...]
    all_to_all x1 -> x3, waiting for transfers between devices: 3.44 us -> 25.8 us  [the longest x1 21.6 us: body(): from_x = lax.all_to_all(to_x, 'x', 0, 0, tiled=True)]
    all_to_all x5 -> x1, starting transfers between devices: 32.9 us -> 11.2 us  [copy_for_each(): lax.all_to_all(jnp.broadcast_to(value[None], (size, *value.shape)), axis,...]
    dot_general x3 -> x0, matrix products: 19 us -> none  [the longest x1 8.11 us: body(): dn_part = jnp.dot(dlogits, head, preferred_element_type=jnp.float32)]
  transfers between devices with their start and end apart: 11 -> 32, of which waited for: 9 -> 9; matrix products, arithmetic and copies ran while one was open for 21% -> 4% of each run, Pallas kernels for 0% -> 27%
where the time goes in v1:
time: 225 us; the launch traced here: 223 us
  Pallas kernels  79.4 us (35%)
  starting transfers between devices  59.5 us (26%)
  waiting for transfers between devices  59.2 us (26%)
  local copies, waits for them, and re-layouts  15.6 us (7%)
  between operations  4.72 us (2%)
  other arithmetic  4.26 us (2%)
    all_to_all x1, waiting for transfers between devices, body(): from_x = lax.all_to_all(to_x, 'x', 0, 0, tiled=True)  21.6 us
    ppermute x19, starting transfers between devices, shift(): return lax.ppermute(value, axis, [(i, (i + step) % n) for i in range(n)])  20 us
    pallas_call x2, Pallas kernels, heads_of(): pl.pallas_call(kernel, out_shape=[like(s) for s in shapes], grid_spec=plt...  17.6 us
    pallas_call x2, Pallas kernels, logits_of(): pl.pallas_call(functools.partial(logits_kernel, count, per, last), out_sh...  17.6 us
    ppermute x19, waiting for transfers between devices, shift(): return lax.ppermute(value, axis, [(i, (i + step) % n) for i in range(n)])  16.4 us
    ppermute x9, starting transfers between devices, turn(): lax.ppermute(value, 'z', [(i, (i + (step if i % 2 == 0 else -step)) % 8)...  16.4 us
    pallas_call x5, Pallas kernels, sum_cut(): pl.pallas_call(functools.partial(sum_cut_kernel, len(ins), groups), out_s...  12.2 us
    ppermute x9, waiting for transfers between devices, turn(): lax.ppermute(value, 'z', [(i, (i + (step if i % 2 == 0 else -step)) % 8)...  11.5 us
  transfers between devices with their start and end apart: 32, of which 9 were waited for; matrix products, arithmetic and copies ran while one was open for 4% of the time, Pallas kernels for 27%

profile of v1, /device:TPU:32, one launch (start us, length us, event | category | flops | bytes accessed | tf_op | source)
XLA Modules:
  0.0 222.6 jit_solution(7479839155955016906)
XLA Ops:
  1.4 1.1 pad_maximum_fusion.refs_0_
  2.6 1.7 collective-permute-start
  4.2 1.7 collective-permute-start.2
  5.9 1.4 fusion.4
  7.3 13.6 %collective-permute-done.refs_2_ = bf16[528,640]{1,0:T(8,128)(2,1)S(1)} collective-permute-done((bf16[528,640]{1,0:T(8,128)(2,1)S(1)}, bf16[528,640]{1,0:T(8,128)(2,1)S(1)}, u32[]{:S(2)}, u32[]{:S(2)}) %collective-permute-start) | collective-permute-done | bytes 675872 | tf_op jit(solution)/shard_map/ppermute | solution.py:27
  22.8 2.9 %collective-permute-start.3 = (bf16[256,640]{1,0:T(8,128)(2,1)}, bf16[256,640]{1,0:T(8,128)(2,1)}, u32[]{:S(2)}, u32[]{:S(2)}) collective-permute-start(bf16[256,640]{1,0:T(8,128)(2,1)} %slice.33), channel_id=1, source_target_pairs={{0,6},{2,0},{4,2},{6,4},{1,7},{3,1},{5,3},{7,5},{8,14},{10,8},{12,... | collective-permute-start | bytes 983048 | tf_op jit(solution)/shard_map/ppermute | solution.py:27
  27.7 11.2 %all-to-all-start = ((f32[32,1,9]{2,1,0:T(1,128)}), f32[32,1,9]{2,1,0:T(1,128)S(1)}, u32[]{:S(2)}, u32[]{:S(2)}) async-start(f32[32,1,9]{2,1,0:T(1,128)} %broadcast_in_dim.9), calls=%async_computation | async-start | bytes 32768 | tf_op jit(solution)/shard_map/all_to_all | solution.py:438
  42.0 5.5 %all-to-all-done = f32[32,1,9]{2,1,0:T(1,128)S(1)} async-done(((f32[32,1,9]{2,1,0:T(1,128)}), f32[32,1,9]{2,1,0:T(1,128)S(1)}, u32[]{:S(2)}, u32[]{:S(2)}) %all-to-all-start) | async-done | bytes 1184 | tf_op jit(solution)/shard_map/all_to_all | solution.py:438
  47.7 0.9 copy-done.5
  48.8 10.7 %logits_first.1 = (bf16[6,512,640]{2,1,0:T(8,128)(2,1)}, f32[512,512]{1,0:T(8,128)}, f32[8,512]{1,0:T(8,128)}) custom-call(s32[16]{0:T(128)} %copy-done.19, s32[5]{0:T(128)} %stack.23.at, bf16[528,640]{1,0:T(8,128)(2,1)} %copy-done.1, bf16[528,640]{1,0:T(8,128)(2,1)} %copy-done.5, bf16[528,640]{1,0:T(8,128)(2,1)} %copy-done.3, bf16[528,640]{1,0:T(8,128)(2,1)} %copy-done.6, ...), custom_call_target="tpu_custom_call" | custom-call | flops 2013265920 | bytes 11796480 | tf_op jit(solution)/shard_map/logits_first/pallas_call | solution.py:153
  59.5 6.9 %logits_last.1 = (bf16[2,512,640]{2,1,0:T(8,128)(2,1)}, f32[512,512]{1,0:T(8,128)}, f32[8,8,512]{2,1,0:T(8,128)}, f32[8,512]{1,0:T(8,128)}) custom-call(s32[10]{0:T(128)} %slice.26.table, s32[5]{0:T(128)} %stack.23.at, bf16[272,640]{1,0:T(8,128)(2,1)} %collective-permute-done.1.refs_0_, bf16[256,640]{1,0:T(8,128)(2,1)} %collective-permute-done.3.refs_1_, ...), custom_call_target="tpu_custom_call" | custom-call | flops 671088640 | bytes 3932160 | tf_op jit(solution)/shard_map/logits_last/pallas_call | solution.py:153
  66.4 3.4 %all-to-all-start.1 = ((f32[8,8,512]{2,1,0:T(8,128)}), f32[8,8,512]{2,1,0:T(8,128)S(1)}, u32[]{:S(2)}, u32[]{:S(2)}) async-start(f32[8,8,512]{2,1,0:T(8,128)} %get-tuple-element.39), calls=%async_computation.1 | async-start | bytes 262144 | tf_op jit(solution)/shard_map/all_to_all | solution.py:483
  71.7 4.2 %all-to-all-done.1.st = f32[8,8,512]{2,1,0:T(8,128)S(1)} async-done(((f32[8,8,512]{2,1,0:T(8,128)}), f32[8,8,512]{2,1,0:T(8,128)S(1)}, u32[]{:S(2)}, u32[]{:S(2)}) %all-to-all-start.1) | async-done | bytes 131104 | tf_op jit(solution)/shard_map/all_to_all | solution.py:483
  76.5 2.7 %policy.1 = (bf16[512,512]{1,0:T(8,128)(2,1)}, f32[8,512]{1,0:T(8,128)}) custom-call(s32[5]{0:T(128)} %stack.23.at, f32[5]{0:T(128)} %pad_maximum_fusion.2.nums, f32[8,8,512]{2,1,0:T(8,128)} %copy-done.11, f32[512,512]{1,0:T(8,128)} %get-tuple-element.40.lg, f32[8,512]{1,0:T(8,128)} %get-tuple-element.41.inv_ref, s32[1,512]{1,0:T(1,128)} %bitcast.22, ...), custom_call_target="tpu_custom_call" | custom-call | flops 2097152 | bytes 1572864 | tf_op jit(solution)/shard_map/policy/pallas_call | solution.py:230
  79.2 10.4 %back.1 = (bf16[4,512,640]{2,1,0:T(8,128)(2,1)}, bf16[4,512,640]{2,1,0:T(8,128)(2,1)}) custom-call(s32[16]{0:T(128)} %copy-done.19, s32[5]{0:T(128)} %stack.23.at, bf16[512,512]{1,0:T(8,128)(2,1)} %get-tuple-element.42.dl, bf16[512,5120]{1,0:T(8,128)(2,1)} %head.1), custom_call_target="tpu_custom_call" | custom-call | flops 2684354560 | bytes 10485760 | tf_op jit(solution)/shard_map/back/pallas_call | solution.py:321
  89.6 6.2 %turned.2.early = bf16[6,640,512]{2,1,0:T(8,128)(2,1)} custom-call(bf16[6,512,640]{2,1,0:T(8,128)(2,1)} %get-tuple-element.52.a), custom_call_target="tpu_custom_call" | custom-call | bytes 7864320 | tf_op jit(solution)/shard_map/turned/pallas_call | solution.py:182
  95.8 2.4 %turned.3.late = bf16[2,640,512]{2,1,0:T(8,128)(2,1)} custom-call(bf16[2,512,640]{2,1,0:T(8,128)(2,1)} %get-tuple-element.53.a), custom_call_target="tpu_custom_call" | custom-call | bytes 2621440 | tf_op jit(solution)/shard_map/turned/pallas_call | solution.py:182
  98.2 8.6 %heads_x.1 = bf16[4,8,160,256]{3,2,1,0:T(8,128)(2,1)} custom-call(s32[16]{0:T(128)} %copy-done.19, s32[5]{0:T(128)} %stack.23.at, bf16[6,640,512]{2,1,0:T(8,128)(2,1)} %turned.2.early, bf16[2,640,512]{2,1,0:T(8,128)(2,1)} %turned.3.late, bf16[512,512]{1,0:T(8,128)(2,1)} %get-tuple-element.42.dl), custom_call_target="tpu_custom_call" | custom-call | flops 1342177280 | bytes 7864320 | tf_op jit(solution)/shard_map/heads_x/pallas_call | solution.py:286
  106.8 3.8 %all-to-all-start.2 = ((bf16[4,8,160,256]{3,2,1,0:T(8,128)(2,1)}), bf16[4,8,160,256]{3,2,1,0:T(8,128)(2,1)S(1)}, u32[]{:S(2)}, u32[]{:S(2)}) async-start(bf16[4,8,160,256]{3,2,1,0:T(8,128)(2,1)} %heads_x.1), calls=%async_computation.2 | async-start | bytes 5242880 | tf_op jit(solution)/shard_map/all_to_all | solution.py:497
  110.6 9.0 %heads_z.1 = (bf16[4,4,160,128]{3,2,1,0:T(8,128)(2,1)}, bf16[4,4,160,128]{3,2,1,0:T(8,128)(2,1)}, bf16[4,4,160,128]{3,2,1,0:T(8,128)(2,1)}, bf16[4,4,160,128]{3,2,1,0:T(8,128)(2,1)}) custom-call(s32[16]{0:T(128)} %copy-done.19, s32[5]{0:T(128)} %stack.23.at, bf16[6,640,512]{2,1,0:T(8,128)(2,1)} %turned.2.early, bf16[2,640,512]{2,1,0:T(8,128)(2,1)} %turned.3.late, ...), custom_call_target="tpu_custom_call" | custom-call | flops 1342177280 | bytes 7864320 | tf_op jit(solution)/shard_map/heads_z/pallas_call | solution.py:286
  120.3 1.4 collective-permute-start.19
  121.7 21.6 %all-to-all-done.2.a = bf16[4,8,160,256]{3,2,1,0:T(8,128)(2,1)S(1)} async-done(((bf16[4,8,160,256]{3,2,1,0:T(8,128)(2,1)}), bf16[4,8,160,256]{3,2,1,0:T(8,128)(2,1)S(1)}, u32[]{:S(2)}, u32[]{:S(2)}) %all-to-all-start.2) | async-done | bytes 2621472 | tf_op jit(solution)/shard_map/all_to_all | solution.py:497
  143.3 1.5 copy-done
  144.8 2.9 %sum_x.1 = bf16[8,160,256]{2,1,0:T(8,128)(2,1)} custom-call(bf16[4,8,160,256]{3,2,1,0:T(8,128)(2,1)} %copy-done), custom_call_target="tpu_custom_call" | custom-call | flops 1310720 | bytes 3932160 | tf_op jit(solution)/shard_map/sum_x/pallas_call | solution.py:378
  147.7 4.7 %all-to-all-start.3 = ((bf16[8,160,256]{2,1,0:T(8,128)(2,1)}), bf16[8,160,256]{2,1,0:T(8,128)(2,1)S(1)}, u32[]{:S(2)}, u32[]{:S(2)}) async-start(bf16[8,160,256]{2,1,0:T(8,128)(2,1)} %sum_x.1), calls=%async_computation.3 | async-start | bytes 1310720 | tf_op jit(solution)/shard_map/all_to_all | solution.py:516
  152.4 4.2 %sum_u.1 = (bf16[512,640]{1,0:T(8,128)(2,1)}, bf16[512,640]{1,0:T(8,128)(2,1)}, bf16[512,640]{1,0:T(8,128)(2,1)}, bf16[512,640]{1,0:T(8,128)(2,1)}) custom-call(bf16[4,512,640]{2,1,0:T(8,128)(2,1)} %get-tuple-element.43.refs_0_, bf16[4,512,640]{2,1,0:T(8,128)(2,1)} %collective-permute-done.9.refs_1_), custom_call_target="tpu_custom_call" | custom-call | flops 2621440 | bytes 7864320 | tf_op jit(solution)/shard_map/sum_u/pallas_call | solution.py:358
  157.1 2.0 collective-permute-start.11
  159.2 0.9 collective-permute-start.12
  160.0 2.2 sum_z1b.1
  163.2 2.2 sum_z1a.1
  165.4 2.8 %collective-permute-start.20 = (bf16[2,4,160,128]{3,2,1,0:T(8,128)(2,1)}, bf16[2,4,160,128]{3,2,1,0:T(8,128)(2,1)S(1)}, u32[]{:S(2)}, u32[]{:S(2)}) collective-permute-start(bf16[2,4,160,128]{3,2,1,0:T(8,128)(2,1)} %get-tuple-element.57), channel_id=1, source_target_pairs={{0,224},{32,64},{64,32},{96,128},{128,96},{160,192},{192,160},{224... | collective-permute-start | bytes 983048 | tf_op jit(solution)/shard_map/ppermute | solution.py:31
  168.2 6.1 %collective-permute-done.23.refs_1_ = bf16[2,4,160,128]{3,2,1,0:T(8,128)(2,1)S(1)} collective-permute-done((bf16[2,4,160,128]{3,2,1,0:T(8,128)(2,1)}, bf16[2,4,160,128]{3,2,1,0:T(8,128)(2,1)S(1)}, u32[]{:S(2)}, u32[]{:S(2)}) %collective-permute-start.23) | collective-permute-done | bytes 327712 | tf_op jit(solution)/shard_map/ppermute | solution.py:31
  175.1 1.8 sum_z2b.1
  176.9 4.7 %collective-permute-start.24 = (bf16[4,160,128]{2,1,0:T(8,128)(2,1)}, bf16[4,160,128]{2,1,0:T(8,128)(2,1)S(1)}, u32[]{:S(2)}, u32[]{:S(2)}) collective-permute-start(bf16[4,160,128]{2,1,0:T(8,128)(2,1)} %get-tuple-element.65), channel_id=1, source_target_pairs={{0,160},{32,128},{64,224},{96,192},{128,32},{160,0},{192,96},{224,... | collective-permute-start | bytes 491528 | tf_op jit(solution)/shard_map/ppermute | solution.py:31
  182.3 1.8 sum_z2a.1
  184.1 1.2 collective-permute-start.21
  185.9 2.2 collective-permute-done.10.u1
  189.6 3.4 %final.1 = (bf16[2,256,640]{2,1,0:T(8,128)(2,1)}, f32[1,768]{1,0:T(1,128)}) custom-call(bf16[512,640]{1,0:T(8,128)(2,1)} %get-tuple-element.45.u0, bf16[512,640]{1,0:T(8,128)(2,1)} %copy-done.8, bf16[512,640]{1,0:T(8,128)(2,1)} %copy-done.9, bf16[512,640]{1,0:T(8,128)(2,1)} %copy-done.10, bf16[2,256,640]{2,1,0:T(8,128)(2,1)} %h_ref.1, ...), custom_call_target="tpu_custom_call" | custom-call | flops 1966080 | bytes 3932160 | tf_op jit(solution)/shard_map/final/pallas_call | solution.py:425
  194.3 2.1 collective-permute-start.14
  197.8 1.9 sum_z3.1
  199.7 1.3 collective-permute-start.25
  201.1 1.5 collective-permute-start.26
  202.6 2.6 %collective-permute-start.27 = (bf16[160,256]{1,0:T(8,128)(2,1)}, bf16[160,256]{1,0:T(8,128)(2,1)S(1)}, u32[]{:S(2)}, u32[]{:S(2)}) collective-permute-start(bf16[160,256]{1,0:T(8,128)(2,1)} %get-tuple-element.69), channel_id=1, source_target_pairs={{0,24},{8,0},{16,8},{24,16},{1,25},{9,1},{17,9},{25,17},{2,26},{10... | collective-permute-start | bytes 245768 | tf_op jit(solution)/shard_map/ppermute | solution.py:27
  205.7 3.2 %collective-permute-done.16 = f32[6,128]{1,0:T(8,128)S(1)} collective-permute-done((f32[6,128]{1,0:T(8,128)S(1)}, f32[6,128]{1,0:T(8,128)S(1)}, u32[]{:S(2)}, u32[]{:S(2)}) %collective-permute-start.16) | collective-permute-done | bytes 3104 | tf_op jit(solution)/shard_map/ppermute | solution.py:31
  208.9 1.5 collective-permute-start.17
  210.4 2.1 collective-permute-done.17
  212.5 3.6 %collective-permute-start.18 = (f32[6,128]{1,0:T(8,128)S(1)}, f32[6,128]{1,0:T(8,128)S(1)}, u32[]{:S(2)}, u32[]{:S(2)}) collective-permute-start(f32[6,128]{1,0:T(8,128)S(1)} %add.59), channel_id=1, source_target_pairs={{0,96},{32,192},{64,160},{96,0},{128,224},{160,64},{192,32},{224,1... | collective-permute-start | bytes 9224 | tf_op jit(solution)/shard_map/ppermute | solution.py:31
  217.1 2.0 join.1
  (114 shorter events, 20.3 us)
Async XLA Ops:
  0.6 38.9 %copy-start.23 = (s32[16]{0:T(128)S(1)}, s32[16]{0:T(128)}, u32[]{:S(2)}) copy-start(s32[16]{0:T(128)} %constant.71.clone) | copy-start | bytes 196
  0.6 38.8 %copy-start.24 = (s32[16]{0:T(128)S(1)}, s32[16]{0:T(128)}, u32[]{:S(2)}) copy-start(s32[16]{0:T(128)} %constant.72.clone) | copy-start | bytes 196
  0.7 25.6 %copy-start.25 = (s32[2]{0:T(128)S(1)}, s32[2]{0:T(128)}, u32[]{:S(2)}) copy-start(s32[2]{0:T(128)} %param.17) | copy-start | bytes 28
  0.7 26.2 %copy-start.26 = (f32[2]{0:T(128)S(1)}, f32[2]{0:T(128)}, u32[]{:S(2)}) copy-start(f32[2]{0:T(128)} %param.16) | copy-start | bytes 28
  0.7 39.4 %copy-start.21 = (s32[2,256]{1,0:T(2,128)S(1)}, s32[2,256]{1,0:T(2,128)}, u32[]{:S(2)}) copy-start(s32[2,256]{1,0:T(2,128)} %param.13) | copy-start | bytes 6148
  0.7 40.0 %copy-start.22 = (f32[2,256]{1,0:T(2,128)S(1)}, f32[2,256]{1,0:T(2,128)}, u32[]{:S(2)}) copy-start(f32[2,256]{1,0:T(2,128)} %param.15) | copy-start | bytes 6148
  2.6 45.1 %copy-start.1 = (bf16[528,640]{1,0:T(8,128)(2,1)}, bf16[528,640]{1,0:T(8,128)(2,1)S(1)}, u32[]{:S(2)}) copy-start(bf16[528,640]{1,0:T(8,128)(2,1)S(1)} %pad_maximum_fusion.refs_0_) | copy-start | bytes 2027524
  2.6 18.3 %collective-permute-start = (bf16[528,640]{1,0:T(8,128)(2,1)S(1)}, bf16[528,640]{1,0:T(8,128)(2,1)S(1)}, u32[]{:S(2)}, u32[]{:S(2)}) collective-permute-start(bf16[528,640]{1,0:T(8,128)(2,1)S(1)} %pad_maximum_fusion.refs_0_), channel_id=1, source_target_pairs={{0,2},{2,4},{4,6},{6,0},{1,3},{3,5},{5,7},{7,1},{8,10},{10,12},{12... | collective-permute-start | bytes 2027528 | tf_op jit(solution)/shard_map/ppermute | solution.py:27
  4.2 17.7 %collective-permute-start.2 = (bf16[528,640]{1,0:T(8,128)(2,1)S(1)}, bf16[528,640]{1,0:T(8,128)(2,1)S(1)}, u32[]{:S(2)}, u32[]{:S(2)}) collective-permute-start(bf16[528,640]{1,0:T(8,128)(2,1)S(1)} %pad_maximum_fusion.refs_0_), channel_id=1, source_target_pairs={{0,6},{2,0},{4,2},{6,4},{1,7},{3,1},{5,3},{7,5},{8,14},{10,8},{12,... | collective-permute-start | bytes 2027528 | tf_op jit(solution)/shard_map/ppermute | solution.py:27
  5.9 41.8 %collective-permute-start.6 = (bf16[528,640]{1,0:T(8,128)(2,1)S(1)}, bf16[528,640]{1,0:T(8,128)(2,1)S(1)}, u32[]{:S(2)}, u32[]{:S(2)}) collective-permute-start(bf16[528,640]{1,0:T(8,128)(2,1)S(1)} %pad_maximum_fusion.refs_0_), channel_id=1, source_target_pairs={{0,1},{1,0},{2,3},{3,2},{4,5},{5,4},{6,7},{7,6},{8,9},{9,8},{10,11... | collective-permute-start | bytes 2027528 | tf_op jit(solution)/shard_map/ppermute | solution.py:27
  20.8 26.9 %copy-start.3 = (bf16[528,640]{1,0:T(8,128)(2,1)}, bf16[528,640]{1,0:T(8,128)(2,1)S(1)}, u32[]{:S(2)}) copy-start(bf16[528,640]{1,0:T(8,128)(2,1)S(1)} %collective-permute-done.refs_2_) | copy-start | bytes 2027524
  21.6 17.3 %collective-permute-start.1 = (bf16[272,640]{1,0:T(8,128)(2,1)}, bf16[272,640]{1,0:T(8,128)(2,1)}, u32[]{:S(2)}, u32[]{:S(2)}) collective-permute-start(bf16[272,640]{1,0:T(8,128)(2,1)} %slice.32), channel_id=1, source_target_pairs={{0,2},{2,4},{4,6},{6,0},{1,3},{3,5},{5,7},{7,1},{8,10},{10,12},{12... | collective-permute-start | bytes 1044488 | tf_op jit(solution)/shard_map/ppermute | solution.py:27
  21.9 25.8 %copy-start.4 = (bf16[528,640]{1,0:T(8,128)(2,1)}, bf16[528,640]{1,0:T(8,128)(2,1)S(1)}, u32[]{:S(2)}) copy-start(bf16[528,640]{1,0:T(8,128)(2,1)S(1)} %collective-permute-done.2.refs_4_) | copy-start | bytes 2027524
  22.8 16.1 %collective-permute-start.3 = (bf16[256,640]{1,0:T(8,128)(2,1)}, bf16[256,640]{1,0:T(8,128)(2,1)}, u32[]{:S(2)}, u32[]{:S(2)}) collective-permute-start(bf16[256,640]{1,0:T(8,128)(2,1)} %slice.33), channel_id=1, source_target_pairs={{0,6},{2,0},{4,2},{6,4},{1,7},{3,1},{5,3},{7,5},{8,14},{10,8},{12,... | collective-permute-start | bytes 983048 | tf_op jit(solution)/shard_map/ppermute | solution.py:27
  25.7 22.0 %collective-permute-start.7 = (bf16[528,640]{1,0:T(8,128)(2,1)S(1)}, bf16[528,640]{1,0:T(8,128)(2,1)S(1)}, u32[]{:S(2)}, u32[]{:S(2)}) collective-permute-start(bf16[528,640]{1,0:T(8,128)(2,1)S(1)} %collective-permute-done.refs_2_), channel_id=1, source_target_pairs={{0,1},{1,0},{2,3},{3,2},{4,5},{5,4},{6,7},{7,6},{8,9},{9,8},{10,11... | collective-permute-start | bytes 2027528 | tf_op jit(solution)/shard_map/ppermute | solution.py:27
  25.7 22.0 %collective-permute-start.8 = (bf16[528,640]{1,0:T(8,128)(2,1)S(1)}, bf16[528,640]{1,0:T(8,128)(2,1)}, u32[]{:S(2)}, u32[]{:S(2)}) collective-permute-start(bf16[528,640]{1,0:T(8,128)(2,1)S(1)} %collective-permute-done.2.refs_4_), channel_id=1, source_target_pairs={{0,1},{1,0},{2,3},{3,2},{4,5},{5,4},{6,7},{7,6},{8,9},{9,8},{10,11... | collective-permute-start | bytes 2027528 | tf_op jit(solution)/shard_map/ppermute | solution.py:27
  27.7 19.8 %all-to-all-start = ((f32[32,1,9]{2,1,0:T(1,128)}), f32[32,1,9]{2,1,0:T(1,128)S(1)}, u32[]{:S(2)}, u32[]{:S(2)}) async-start(f32[32,1,9]{2,1,0:T(1,128)} %broadcast_in_dim.9), calls=%async_computation | async-start | bytes 32768 | tf_op jit(solution)/shard_map/all_to_all | solution.py:438
  38.9 20.6 %collective-permute-start.5 = (bf16[256,640]{1,0:T(8,128)(2,1)}, bf16[256,640]{1,0:T(8,128)(2,1)}, u32[]{:S(2)}, u32[]{:S(2)}) collective-permute-start(bf16[256,640]{1,0:T(8,128)(2,1)} %collective-permute-done.3.refs_1_), channel_id=1, source_target_pairs={{0,1},{1,0},{2,3},{3,2},{4,5},{5,4},{6,7},{7,6},{8,9},{9,8},{10,11... | collective-permute-start | bytes 983048 | tf_op jit(solution)/shard_map/ppermute | solution.py:27
  39.0 20.5 %collective-permute-start.4 = (bf16[272,640]{1,0:T(8,128)(2,1)}, bf16[272,640]{1,0:T(8,128)(2,1)}, u32[]{:S(2)}, u32[]{:S(2)}) collective-permute-start(bf16[272,640]{1,0:T(8,128)(2,1)} %collective-permute-done.1.refs_0_), channel_id=1, source_target_pairs={{0,1},{1,0},{2,3},{3,2},{4,5},{5,4},{6,7},{7,6},{8,9},{9,8},{10,11... | collective-permute-start | bytes 1044488 | tf_op jit(solution)/shard_map/ppermute | solution.py:27
  39.5 8.2 %copy-start.19 = (s32[16]{0:T(128)}, s32[16]{0:T(128)S(1)}, u32[]{:S(2)}) copy-start(s32[16]{0:T(128)S(1)} %fusion.table) | copy-start | bytes 196
  47.7 0.9 copy-start.5
  47.7 1.1 copy-start.6
  66.4 9.4 %all-to-all-start.1 = ((f32[8,8,512]{2,1,0:T(8,128)}), f32[8,8,512]{2,1,0:T(8,128)S(1)}, u32[]{:S(2)}, u32[]{:S(2)}) async-start(f32[8,8,512]{2,1,0:T(8,128)} %get-tuple-element.39), calls=%async_computation.1 | async-start | bytes 262144 | tf_op jit(solution)/shard_map/all_to_all | solution.py:483
  89.6 62.8 %collective-permute-start.9 = (bf16[4,512,640]{2,1,0:T(8,128)(2,1)}, bf16[4,512,640]{2,1,0:T(8,128)(2,1)}, u32[]{:S(2)}, u32[]{:S(2)}) collective-permute-start(bf16[4,512,640]{2,1,0:T(8,128)(2,1)} %get-tuple-element.44), channel_id=1, source_target_pairs={{0,1},{1,0},{2,3},{3,2},{4,5},{5,4},{6,7},{7,6},{8,9},{9,8},{10,11... | collective-permute-start | bytes 7864328 | tf_op jit(solution)/shard_map/ppermute | solution.py:27
  106.8 36.5 %all-to-all-start.2 = ((bf16[4,8,160,256]{3,2,1,0:T(8,128)(2,1)}), bf16[4,8,160,256]{3,2,1,0:T(8,128)(2,1)S(1)}, u32[]{:S(2)}, u32[]{:S(2)}) async-start(bf16[4,8,160,256]{3,2,1,0:T(8,128)(2,1)} %heads_x.1), calls=%async_computation.2 | async-start | bytes 5242880 | tf_op jit(solution)/shard_map/all_to_all | solution.py:497
  119.7 40.3 %collective-permute-start.22 = (bf16[4,4,160,128]{3,2,1,0:T(8,128)(2,1)}, bf16[4,4,160,128]{3,2,1,0:T(8,128)(2,1)}, u32[]{:S(2)}, u32[]{:S(2)}) collective-permute-start(bf16[4,4,160,128]{3,2,1,0:T(8,128)(2,1)} %get-tuple-element.61), channel_id=1, source_target_pairs={{0,224},{32,64},{64,32},{96,128},{128,96},{160,192},{192,160},{224... | collective-permute-start | bytes 1966088 | tf_op jit(solution)/shard_map/ppermute | solution.py:31
  120.3 42.1 %collective-permute-start.19 = (bf16[4,4,160,128]{3,2,1,0:T(8,128)(2,1)}, bf16[4,4,160,128]{3,2,1,0:T(8,128)(2,1)S(1)}, u32[]{:S(2)}, u32[]{:S(2)}) collective-permute-start(bf16[4,4,160,128]{3,2,1,0:T(8,128)(2,1)} %get-tuple-element.55), channel_id=1, source_target_pairs={{0,32},{32,0},{64,96},{96,64},{128,160},{160,128},{192,224},{224,1... | collective-permute-start | bytes 1966088 | tf_op jit(solution)/shard_map/ppermute | solution.py:31
  143.3 1.5 copy-start
  147.7 68.5 %all-to-all-start.3 = ((bf16[8,160,256]{2,1,0:T(8,128)(2,1)}), bf16[8,160,256]{2,1,0:T(8,128)(2,1)S(1)}, u32[]{:S(2)}, u32[]{:S(2)}) async-start(bf16[8,160,256]{2,1,0:T(8,128)(2,1)} %sum_x.1), calls=%async_computation.3 | async-start | bytes 1310720 | tf_op jit(solution)/shard_map/all_to_all | solution.py:516
  156.6 28.8 %copy-start.20 = (bf16[640]{0:T(1024)(128)(2,1)S(1)}, bf16[640]{0:T(1024)(128)(2,1)}, u32[]{:S(2)}) copy-start(bf16[640]{0:T(1024)(128)(2,1)} %param.11) | copy-start | bytes 3844
  156.6 31.5 %collective-permute-start.10 = (bf16[512,640]{1,0:T(8,128)(2,1)}, bf16[512,640]{1,0:T(8,128)(2,1)S(1)}, u32[]{:S(2)}, u32[]{:S(2)}) collective-permute-start(bf16[512,640]{1,0:T(8,128)(2,1)} %get-tuple-element.46), channel_id=1, source_target_pairs={{0,2},{2,4},{4,6},{6,0},{1,3},{3,5},{5,7},{7,1},{8,10},{10,12},{12... | collective-permute-start | bytes 1966088 | tf_op jit(solution)/shard_map/ppermute | solution.py:27
  157.1 31.0 %collective-permute-start.11 = (bf16[512,640]{1,0:T(8,128)(2,1)}, bf16[512,640]{1,0:T(8,128)(2,1)S(1)}, u32[]{:S(2)}, u32[]{:S(2)}) collective-permute-start(bf16[512,640]{1,0:T(8,128)(2,1)} %get-tuple-element.47), channel_id=1, source_target_pairs={{0,4},{2,6},{4,0},{6,2},{1,5},{3,7},{5,1},{7,3},{8,12},{10,14},{12... | collective-permute-start | bytes 1966088 | tf_op jit(solution)/shard_map/ppermute | solution.py:27
  159.2 29.6 %collective-permute-start.12 = (bf16[512,640]{1,0:T(8,128)(2,1)}, bf16[512,640]{1,0:T(8,128)(2,1)S(1)}, u32[]{:S(2)}, u32[]{:S(2)}) collective-permute-start(bf16[512,640]{1,0:T(8,128)(2,1)} %get-tuple-element.48), channel_id=1, source_target_pairs={{0,6},{2,0},{4,2},{6,4},{1,7},{3,1},{5,3},{7,5},{8,14},{10,8},{12,... | collective-permute-start | bytes 1966088 | tf_op jit(solution)/shard_map/ppermute | solution.py:27
  162.3 12.1 %collective-permute-start.23 = (bf16[2,4,160,128]{3,2,1,0:T(8,128)(2,1)}, bf16[2,4,160,128]{3,2,1,0:T(8,128)(2,1)S(1)}, u32[]{:S(2)}, u32[]{:S(2)}) collective-permute-start(bf16[2,4,160,128]{3,2,1,0:T(8,128)(2,1)} %get-tuple-element.63), channel_id=1, source_target_pairs={{0,32},{32,0},{64,96},{96,64},{128,160},{160,128},{192,224},{224,1... | collective-permute-start | bytes 983048 | tf_op jit(solution)/shard_map/ppermute | solution.py:31
  165.4 16.2 %collective-permute-start.20 = (bf16[2,4,160,128]{3,2,1,0:T(8,128)(2,1)}, bf16[2,4,160,128]{3,2,1,0:T(8,128)(2,1)S(1)}, u32[]{:S(2)}, u32[]{:S(2)}) collective-permute-start(bf16[2,4,160,128]{3,2,1,0:T(8,128)(2,1)} %get-tuple-element.57), channel_id=1, source_target_pairs={{0,224},{32,64},{64,32},{96,128},{128,96},{160,192},{192,160},{224... | collective-permute-start | bytes 983048 | tf_op jit(solution)/shard_map/ppermute | solution.py:31
  176.9 20.2 %collective-permute-start.24 = (bf16[4,160,128]{2,1,0:T(8,128)(2,1)}, bf16[4,160,128]{2,1,0:T(8,128)(2,1)S(1)}, u32[]{:S(2)}, u32[]{:S(2)}) collective-permute-start(bf16[4,160,128]{2,1,0:T(8,128)(2,1)} %get-tuple-element.65), channel_id=1, source_target_pairs={{0,160},{32,128},{64,224},{96,192},{128,32},{160,0},{192,96},{224,... | collective-permute-start | bytes 491528 | tf_op jit(solution)/shard_map/ppermute | solution.py:31
  184.1 13.0 %collective-permute-start.21 = (bf16[4,160,128]{2,1,0:T(8,128)(2,1)}, bf16[4,160,128]{2,1,0:T(8,128)(2,1)S(1)}, u32[]{:S(2)}, u32[]{:S(2)}) collective-permute-start(bf16[4,160,128]{2,1,0:T(8,128)(2,1)} %get-tuple-element.59), channel_id=1, source_target_pairs={{0,96},{32,192},{64,160},{96,0},{128,224},{160,64},{192,32},{224,1... | collective-permute-start | bytes 491528 | tf_op jit(solution)/shard_map/ppermute | solution.py:31
  188.1 1.0 copy-start.9
  193.7 8.9 %collective-permute-start.13 = (f32[6,128]{1,0:T(8,128)S(1)}, f32[6,128]{1,0:T(8,128)S(1)}, u32[]{:S(2)}, u32[]{:S(2)}) collective-permute-start(f32[6,128]{1,0:T(8,128)S(1)} %bitcast.24), channel_id=1, source_target_pairs={{0,8},{8,16},{16,24},{24,0},{1,9},{9,17},{17,25},{25,1},{2,10},{10... | collective-permute-start | bytes 9224 | tf_op jit(solution)/shard_map/ppermute | solution.py:27
  194.3 10.9 %collective-permute-start.14 = (f32[6,128]{1,0:T(8,128)S(1)}, f32[6,128]{1,0:T(8,128)S(1)}, u32[]{:S(2)}, u32[]{:S(2)}) collective-permute-start(f32[6,128]{1,0:T(8,128)S(1)} %bitcast.25), channel_id=1, source_target_pairs={{0,16},{8,24},{16,0},{24,8},{1,17},{9,25},{17,1},{25,9},{2,18},{10... | collective-permute-start | bytes 9224 | tf_op jit(solution)/shard_map/ppermute | solution.py:27
  196.4 8.8 %collective-permute-start.15 = (f32[6,128]{1,0:T(8,128)S(1)}, f32[6,128]{1,0:T(8,128)S(1)}, u32[]{:S(2)}, u32[]{:S(2)}) collective-permute-start(f32[6,128]{1,0:T(8,128)S(1)} %bitcast.26), channel_id=1, source_target_pairs={{0,24},{8,0},{16,8},{24,16},{1,25},{9,1},{17,9},{25,17},{2,26},{10... | collective-permute-start | bytes 9224 | tf_op jit(solution)/shard_map/ppermute | solution.py:27
  199.7 16.4 %collective-permute-start.25 = (bf16[160,256]{1,0:T(8,128)(2,1)}, bf16[160,256]{1,0:T(8,128)(2,1)S(1)}, u32[]{:S(2)}, u32[]{:S(2)}) collective-permute-start(bf16[160,256]{1,0:T(8,128)(2,1)} %get-tuple-element.67), channel_id=1, source_target_pairs={{0,8},{8,16},{16,24},{24,0},{1,9},{9,17},{17,25},{25,1},{2,10},{10... | collective-permute-start | bytes 245768 | tf_op jit(solution)/shard_map/ppermute | solution.py:27
  201.1 15.1 %collective-permute-start.26 = (bf16[160,256]{1,0:T(8,128)(2,1)}, bf16[160,256]{1,0:T(8,128)(2,1)S(1)}, u32[]{:S(2)}, u32[]{:S(2)}) collective-permute-start(bf16[160,256]{1,0:T(8,128)(2,1)} %get-tuple-element.68), channel_id=1, source_target_pairs={{0,16},{8,24},{16,0},{24,8},{1,17},{9,25},{17,1},{25,9},{2,18},{10... | collective-permute-start | bytes 245768 | tf_op jit(solution)/shard_map/ppermute | solution.py:27
  202.6 13.5 %collective-permute-start.27 = (bf16[160,256]{1,0:T(8,128)(2,1)}, bf16[160,256]{1,0:T(8,128)(2,1)S(1)}, u32[]{:S(2)}, u32[]{:S(2)}) collective-permute-start(bf16[160,256]{1,0:T(8,128)(2,1)} %get-tuple-element.69), channel_id=1, source_target_pairs={{0,24},{8,0},{16,8},{24,16},{1,25},{9,1},{17,9},{25,17},{2,26},{10... | collective-permute-start | bytes 245768 | tf_op jit(solution)/shard_map/ppermute | solution.py:27
  205.2 3.7 %collective-permute-start.16 = (f32[6,128]{1,0:T(8,128)S(1)}, f32[6,128]{1,0:T(8,128)S(1)}, u32[]{:S(2)}, u32[]{:S(2)}) collective-permute-start(f32[6,128]{1,0:T(8,128)S(1)} %add_add_fusion), channel_id=1, source_target_pairs={{0,32},{32,0},{64,96},{96,64},{128,160},{160,128},{192,224},{224,1... | collective-permute-start | bytes 9224 | tf_op jit(solution)/shard_map/ppermute | solution.py:31
  208.9 3.6 %collective-permute-start.17 = (f32[6,128]{1,0:T(8,128)S(1)}, f32[6,128]{1,0:T(8,128)S(1)}, u32[]{:S(2)}, u32[]{:S(2)}) collective-permute-start(f32[6,128]{1,0:T(8,128)S(1)} %add.58), channel_id=1, source_target_pairs={{0,224},{32,64},{64,32},{96,128},{128,96},{160,192},{192,160},{224... | collective-permute-start | bytes 9224 | tf_op jit(solution)/shard_map/ppermute | solution.py:31
  212.5 6.6 %collective-permute-start.18 = (f32[6,128]{1,0:T(8,128)S(1)}, f32[6,128]{1,0:T(8,128)S(1)}, u32[]{:S(2)}, u32[]{:S(2)}) collective-permute-start(f32[6,128]{1,0:T(8,128)S(1)} %add.59), channel_id=1, source_target_pairs={{0,96},{32,192},{64,160},{96,0},{128,224},{160,64},{192,32},{224,1... | collective-permute-start | bytes 9224 | tf_op jit(solution)/shard_map/ppermute | solution.py:31
  216.2 0.9 copy-start.2
  (11 other events, 7.9 us)

commit v2 on v1

--- a/solution.py
+++ b/solution.py
@@ -67,9 +67,9 @@
     return pl.BlockSpec(shape, lambda k, *at: (0,) * len(shape))
 
 
-def logits_kernel(count, per, last, table, at, *refs):
-    pieces = refs[: count * per]
-    refs = refs[count * per :]
+def logits_kernel(count, per, last, at, *refs):
+    pieces = refs[: count * per * 2]
+    refs = refs[count * per * 2 :]
     if last:
         acc_in, sq_in, tgt = refs[:3]
         refs = refs[3:]
@@ -77,17 +77,17 @@
     outs, (slot, acc, sq, sem) = refs[2:-4], refs[-4:]
     j = pl.program_id(0)
     rows = acc.shape[0]
+    cols = slot.shape[2] // 2
 
     @pl.when(j == 0)
     def _():
         copies = []
         for k, piece in enumerate(pieces):
             first = 0 if k % per == 0 else pieces[k - 1].shape[0]
-            copies.append(
-                pltpu.make_async_copy(
-                    piece, slot.at[k // per, pl.ds(first, piece.shape[0]), :], sem.at[k]
-                )
-            )
+            side = lax.rem(at[2] + (k // per) % 2, 2)
+            lanes = pl.ds(pl.multiple_of(side * cols, cols), cols)
+            place = slot.at[k // (2 * per), pl.ds(first, piece.shape[0]), lanes]
+            copies.append(pltpu.make_async_copy(piece, place, sem.at[k]))
         for copy in copies:
             copy.start()
         if last:
@@ -136,12 +136,12 @@
             st[k] = found
 
 
-def logits_of(table, at, blocks, head, before=None, targets=None):
-    count, per = len(blocks), len(blocks[0])
+def logits_of(at, first, blocks, head, before=None, targets=None):
+    count, per = len(blocks), len(blocks[0]) // 2
     last = before is not None
     half = head.shape[0]
-    cols = blocks[0][0].shape[1]
-    height = sum(p.shape[0] for p in blocks[0])
+    cols = 2 * blocks[0][0].shape[1]
+    height = sum(p.shape[0] for p in blocks[0]) // 2
     rows = height - 16
     anywhere = pl.BlockSpec(memory_space=pl.ANY)
     shapes = [like((count, rows, cols))]
@@ -154,41 +154,23 @@
         functools.partial(logits_kernel, count, per, last),
         out_shape=shapes,
         grid_spec=pltpu.PrefetchScalarGridSpec(
-            num_scalar_prefetch=2,
+            num_scalar_prefetch=1,
             grid=(count,),
-            in_specs=[anywhere] * (count * per)
+            in_specs=[anywhere] * (count * per * 2)
             + [full(e.shape) for e in extra]
-            + [pl.BlockSpec((half, cols), lambda j, table, at: (0, table[j]))],
+            + [pl.BlockSpec((half, cols), lambda j, at: (0, at[8 + first + j]))],
             out_specs=specs + [full(s.shape) for s in shapes[1:]],
             scratch_shapes=[
                 VMEM((count, height, cols), bf16),
                 VMEM((rows, half), f32),
                 VMEM((rows, 1), f32),
-                pltpu.SemaphoreType.DMA((count * per,)),
+                pltpu.SemaphoreType.DMA((count * per * 2,)),
             ],
         ),
         compiler_params=params(),
         cost_estimate=cost(2 * rows * half * count * cols, 2 * count * cols * (2 * rows + half)),
         name="logits_last" if last else "logits_first",
-    )(table, at, *[p for b in blocks for p in b], *extra, head)
-
-
-def turned_kernel(a, out):
-    out[0] = jnp.transpose(a[0])
-
-
-def turned(blocks):
-    count, rows, cols = blocks.shape
-    return pl.pallas_call(
-        turned_kernel,
-        out_shape=like((count, cols, rows)),
-        grid=(count,),
-        in_specs=[pl.BlockSpec((1, rows, cols), lambda j: (j, 0, 0))],
-        out_specs=pl.BlockSpec((1, cols, rows), lambda j: (j, 0, 0)),
-        compiler_params=params(),
-        cost_estimate=cost(0, 4 * blocks.size),
-        name="turned",
-    )(blocks)
+    )(at, *[p for b in blocks for p in b], *extra, head)
 
 
 def policy_kernel(at, nums, st, lg, inv_ref, tgt, old, dl, small):
@@ -238,105 +220,80 @@
     )(at, nums, stats, logits, inv, targets, old_logp)
 
 
-def left_of(j, early, late):
-    return jnp.where(j < 6, early[0], late[0])
-
-
-def heads_x_kernel(table, at, early, late, dl, out):
+def products_kernel(at, early, late, dl, head, to_x, send_a, send_b, keep_a, keep_b, u_send, u_keep):
     j = pl.program_id(0)
-    got = jnp.dot(left_of(j, early, late), dl[...], preferred_element_type=f32).astype(bf16)
-    step = got.shape[0] // 4
-    for k in range(4):
-        out[k, table[j]] = got[k * step : (k + 1) * step, :]
-
-
-def heads_z_kernel(table, at, early, late, dl, send_a, send_b, keep_a, keep_b, tmp):
-    j = pl.program_id(0)
-    x, z = at[4], at[3]
-    tmp[...] = jnp.dot(left_of(j, early, late), dl[...], preferred_element_type=f32)
-    step = tmp.shape[0] // 4
-    width = tmp.shape[1] // 2
+    c, z = at[2], at[3]
+    scaled = jnp.where(j < 3, early[0], late[0])
+    cols = scaled.shape[1] // 2
+    step, half = cols // 4, dl.shape[1] // 2
+    width = half // 2
+    back = jnp.dot(dl[...], head[...], preferred_element_type=f32).astype(bf16)
+
+    @pl.when(c == 0)
+    def _():
+        u_keep[0] = back[:, :cols]
+        u_send[0] = back[:, cols:]
+
+    @pl.when(c == 1)
+    def _():
+        u_send[0] = back[:, :cols]
+        u_keep[0] = back[:, cols:]
+
+    got = lax.dot_general(
+        scaled, dl[...], (((0,), (0,)), ((), ())), preferred_element_type=f32
+    ).astype(bf16)
     odd = lax.rem(z, 2)
-    ahead = lax.rem(table[j] - z + 8, 8)
-    behind = lax.rem(8 - ahead, 8)
-    for side, send, keep in ((0, send_a, keep_a), (1, send_b, keep_b)):
-        q = jnp.where(odd == side, ahead, behind)
-        low = lax.rem(q, 4)
-        sent = (low == 1) | (low == 2)
-        send_at = jnp.where(sent, 2 * (q // 4) + low - 1, 0)
-        keep_at = jnp.where(q == 0, 0, jnp.where(q == 7, 1, jnp.where(q == 4, 2, 3)))
-        cut = slice(side * width, (side + 1) * width)
-
-        @pl.when(sent)
-        def _(send=send, cut=cut, send_at=send_at):
-            for k in range(4):
-                start = pl.multiple_of(lax.rem(x + k, 4) * step, step)
-                send[send_at, k] = tmp[pl.ds(start, step), cut].astype(bf16)
-
-        @pl.when(jnp.logical_not(sent))
-        def _(keep=keep, cut=cut, keep_at=keep_at):
-            for k in range(4):
-                start = pl.multiple_of(lax.rem(x + k, 4) * step, step)
-                keep[keep_at, k] = tmp[pl.ds(start, step), cut].astype(bf16)
-
-
-def heads_of(table, at, early, late, dl, second, kernel, shapes, scratch, name):
-    _, cols, rows = early.shape
-    half = dl.shape[1] // 2
+    for i in range(2):
+        place = 2 * at[8 + j] + i
+        ahead = lax.rem(place - z + 8, 8)
+        behind = lax.rem(8 - ahead, 8)
+        parts = [got[i * cols + k * step : i * cols + (k + 1) * step, :] for k in range(4)]
+        for k in range(4):
+            to_x[k, place] = parts[k][:, :half]
+        for side, send, keep in ((0, send_a, keep_a), (1, send_b, keep_b)):
+            q = jnp.where(odd == side, ahead, behind)
+            low = lax.rem(q, 4)
+            sent = (low == 1) | (low == 2)
+            send_at = jnp.where(sent, 2 * (q // 4) + low - 1, 0)
+            keep_at = jnp.where(q == 0, 0, jnp.where(q == 7, 1, jnp.where(q == 4, 2, 3)))
+            cut = slice(half + side * width, half + (side + 1) * width)
+
+            @pl.when(sent)
+            def _(send=send, cut=cut, send_at=send_at, parts=parts):
+                for k in range(4):
+                    send[send_at, k] = parts[k][:, cut]
+
+            @pl.when(jnp.logical_not(sent))
+            def _(keep=keep, cut=cut, keep_at=keep_at, parts=parts):
+                for k in range(4):
+                    keep[keep_at, k] = parts[k][:, cut]
+
+
+def products_of(at, early, late, dl, head):
+    _, rows, cols = early.shape
+    half = dl.shape[1]
+    step = cols // 8
+    cut = like((4, 4, step, half // 4))
+    shapes = [like((4, 8, step, half // 2))] + [cut] * 4 + [like((4, rows, cols // 2))] * 2
     return pl.pallas_call(
-        kernel,
-        out_shape=[like(s) for s in shapes],
+        products_kernel,
+        out_shape=shapes,
         grid_spec=pltpu.PrefetchScalarGridSpec(
-            num_scalar_prefetch=2,
-            grid=(8,),
+            num_scalar_prefetch=1,
+            grid=(4,),
             in_specs=[
-                pl.BlockSpec((1, cols, rows), lambda j, *a: (jnp.minimum(j, 5), 0, 0)),
-                pl.BlockSpec((1, cols, rows), lambda j, *a: (jnp.maximum(j - 6, 0), 0, 0)),
-                pl.BlockSpec((rows, half), lambda j, *a: (0, second)),
+                pl.BlockSpec((1, rows, cols), lambda j, at: (jnp.minimum(j, 2), 0, 0)),
+                full(late.shape),
+                full((rows, half)),
+                pl.BlockSpec((half, cols), lambda j, at: (0, at[8 + j])),
             ],
-            out_specs=[full(s) for s in shapes],
-            scratch_shapes=[VMEM((cols, half), f32)] if scratch else [],
+            out_specs=[full(s.shape) for s in shapes[:5]]
+            + [pl.BlockSpec((1, rows, cols // 2), lambda j, at: (j, 0, 0))] * 2,
         ),
         compiler_params=params(),
-        cost_estimate=cost(2 * rows * 8 * cols * half, 16 * rows * cols + 16 * cols * half),
-        name=name,
-    )(table, at, early, late, dl)
-
-
-def back_kernel(table, at, dl, head, send, keep):
-    k = pl.program_id(0)
-    part = jnp.dot(dl[...], head[...], preferred_element_type=f32).astype(bf16)
-
-    @pl.when(k < 4)
-    def _():
-        send[0] = part
-
-    @pl.when(k >= 4)
-    def _():
-        keep[0] = part
-
-
-def back_of(table, at, dl, head, cols):
-    rows, half = dl.shape
-    return pl.pallas_call(
-        back_kernel,
-        out_shape=[like((4, rows, cols))] * 2,
-        grid_spec=pltpu.PrefetchScalarGridSpec(
-            num_scalar_prefetch=2,
-            grid=(8,),
-            in_specs=[
-                full((rows, half)),
-                pl.BlockSpec((half, cols), lambda k, table, at: (0, table[8 + k])),
-            ],
-            out_specs=[
-                pl.BlockSpec((1, rows, cols), lambda k, *a: (jnp.minimum(k, 3), 0, 0)),
-                pl.BlockSpec((1, rows, cols), lambda k, *a: (jnp.maximum(k - 4, 0), 0, 0)),
-            ],
-        ),
-        compiler_params=params(),
-        cost_estimate=cost(2 * rows * half * 8 * cols, 16 * half * cols + 16 * rows * cols),
-        name="back",
-    )(table, at, dl, head)
+        cost_estimate=cost(4 * rows * 4 * cols * half, 32 * rows * cols),
+        name="products",
+    )(at, early, late, dl, head)
 
 
 def sum_cut_kernel(n, groups, *refs):
@@ -386,11 +343,12 @@
     )(value)
 
 
-def both_kernel(keep_a, got_a, keep_b, got_b, *outs):
+def both_kernel(at, keep_a, got_a, keep_b, got_b, *outs):
     width = keep_a.shape[2]
     for k, out in enumerate(outs):
+        place = lax.rem(at[4] + k, 4)
         for first, keep, got in ((0, keep_a, got_a), (width, keep_b, got_b)):
-            total = keep[k].astype(f32) + got[k].astype(f32)
+            total = keep[place].astype(f32) + got[place].astype(f32)
             out[:, first : first + width] = total.astype(bf16)
 
 
@@ -425,7 +383,7 @@
     return pl.pallas_call(
         kernel,
         out_shape=shapes,
-        in_specs=[whole()] * len(ins),
+        in_specs=[whole(pltpu.SMEM if v.ndim == 1 else VMEM) for v in ins],
         out_specs=[whole()] * len(shapes),
         compiler_params=params(),
         cost_estimate=cost(nbytes // 2, nbytes),
@@ -440,24 +398,23 @@
     )
 
 
+def after(value, *first):
+    return lax.optimization_barrier((value, *first))[0]
+
+
 def body(hidden, gain, head, targets, lengths, old_logp, rewards, group_slot):
     resp_here, length_max, cols = hidden.shape
     rows = resp_here * length_max
     x, y, z, c = (lax.axis_index(a) for a in ("x", "y", "z", "c"))
-    order = jnp.array([0, 0, 3, 3, 1, 1, 2, 2, 0, 1, 2, 3, 0, 1, 2, 3], jnp.int32)
-    other = jnp.array([0, 1] * 4 + [1] * 4 + [0] * 4, jnp.int32)
-    table = (2 * ((y + order) % 4) + (c + other) % 2).astype(jnp.int32)
-    at = jnp.stack([2 * y + c, y, c, z, x]).astype(jnp.int32)
+    chips = (y + jnp.array([0, 3, 1, 2], jnp.int32)) % 4
+    at = jnp.concatenate([jnp.stack([2 * y + c, y, c, z, x, x, x, x]), chips]).astype(jnp.int32)
 
     payload = jnp.concatenate(
         [jnp.broadcast_to(gain[None], (16, cols)), hidden.reshape(rows, cols)], axis=0
     )
     cut = 16 + length_max
+    prev, following = shift(payload, "y", 1), shift(payload, "y", -1)
     own_o = shift(payload, "c", 1)
-    prev, following = shift(payload, "y", 1), shift(payload, "y", -1)
-    far_a, far_b = shift(prev[:cut], "y", 1), shift(following[cut:], "y", -1)
-    prev_o, following_o = shift(prev, "c", 1), shift(following, "c", 1)
-    far_a_o, far_b_o = shift(far_a, "c", 1), shift(far_b, "c", 1)
 
     groups_all = resp_here * lax.axis_size(DP) // GROUP
     group = group_slot // GROUP
@@ -465,7 +422,12 @@
     local = jnp.concatenate(
         [jnp.sum(member * rewards[:, None], axis=0), jnp.sum(lengths).astype(f32)[None]]
     )
-    sums = copy_for_each(local, DP).sum(axis=0)
+    over_x = copy_for_each(local, "x").sum(axis=0)
+    prev, following, over_x = lax.optimization_barrier((prev, following, over_x))
+
+    far_a, far_b = shift(prev[:cut], "y", 1), shift(following[cut:], "y", -1)
+    prev_o, following_o = shift(prev, "c", 1), shift(following, "c", 1)
+    sums = copy_for_each(over_x, "z").sum(axis=0)
     group_sums, count = sums[:groups_all], sums[groups_all]
     adv_resp = rewards - jnp.sum(member * group_sums[None, :], axis=1) / GROUP
     slots_all = rows * lax.axis_size(DP)
@@ -473,47 +435,60 @@
     targets = targets.reshape(1, rows)
     old_logp = old_logp.reshape(1, rows)
 
-    hb_early, acc, sq = logits_of(
-        table, at, [(payload,), (own_o,), (prev,), (prev_o,), (following,), (following_o,)], head
-    )
-    early = turned(hb_early)
-    hb_late, logits, stats, inv = logits_of(
-        table[6:], at, [(far_a, far_b), (far_a_o, far_b_o)], head, (acc, sq), targets
+    early, acc, sq = logits_of(
+        at, 0, [(payload, own_o), (prev, prev_o), (following, following_o)], head
+    )
+    far_a_o, far_b_o = shift(far_a, "c", 1), shift(far_b, "c", 1)
+    acc, nums, far_a_o = lax.optimization_barrier((acc, nums, far_a_o))
+    late, logits, stats, inv = logits_of(
+        at, 3, [(far_a, far_b, far_a_o, far_b_o)], head, (acc, sq), targets
     )
     all_stats = lax.all_to_all(stats, FSDP, 0, 0, tiled=True)
-    late = turned(hb_late)
     dl, small = policy_of(at, nums, all_stats, logits, inv, targets, old_logp)
-
+    to_x, send_a, send_b, keep_a, keep_b, u_send, u_keep = products_of(at, early, late, dl, head)
     part, half = cols // 4, dl.shape[1] // 2
-    zs = (4, 4, part, half // 2)
-    send_a, send_b, keep_a, keep_b = heads_of(
-        table, at, early, late, dl, 1, heads_z_kernel, (zs,) * 4, True, "heads_z"
-    )
-    (to_x,) = heads_of(
-        table, at, early, late, dl, 0, heads_x_kernel, ((4, 8, part, half),), False, "heads_x"
-    )
-    u_send, u_keep = back_of(table, at, dl, head, cols)
+
+    u_got = shift(u_send, "c", 1)
     got_a, got_b = turn(send_a, 1), turn(send_b, -1)
     from_x = lax.all_to_all(to_x, "x", 0, 0, tiled=True)
-    u_got = shift(u_send, "c", 1)
-
+    u0, u1, u2, u3 = sum_cut((u_keep, u_got), ((0,), (1,), (2,), (3,)), "sum_u")
+    u1, u2, u3 = shift(u1, "y", -1), shift(u2, "y", 1), shift(u3, "y", 2)
+
+    got_a = after(got_a, u0)
     send2_a, keep2_a = sum_cut((keep_a, got_a), ((2, 1), (3, 0)), "sum_z1a")
     send2_b, keep2_b = sum_cut((keep_b, got_b), ((2, 1), (3, 0)), "sum_z1b")
     got2_a, got2_b = turn(send2_a, -1), turn(send2_b, 1)
+    from_x = after(from_x, send2_a, send2_b)
+    to_z = sum_first(from_x, "sum_x")
+    from_z = lax.all_to_all(to_z, "z", 0, 0, tiled=True)
+
+    got2_a, got2_b = after(got2_a, to_z), after(got2_b, to_z)
     send3_a, keep3_a = sum_cut((keep2_a, got2_a), ((0,), (1,)), "sum_z2a")
     send3_b, keep3_b = sum_cut((keep2_b, got2_b), ((0,), (1,)), "sum_z2b")
     got3_a, got3_b = turn(send3_a, 3), turn(send3_b, -3)
+
+    u1 = after(u1, send3_a, send3_b)
+    grad_hidden, gain_part = simple(
+        final_kernel,
+        [like(hidden.shape), like((1, cols + 128), f32)],
+        (u0, u1, u2, u3, hidden, gain.reshape(1, cols), small),
+        12 * rows * cols,
+        "final",
+    )
+    tail = gain_part.reshape(-1, 128)
+    tail = tail + shift(tail, "x", 1) + shift(tail, "x", 2) + shift(tail, "x", -1)
+
+    got3_a = after(got3_a, gain_part)
     four = simple(
         both_kernel,
         [like((part, half))] * 4,
-        (keep3_a, got3_a, keep3_b, got3_b),
+        (at, keep3_a, got3_a, keep3_b, got3_b),
         12 * keep3_a.size,
         "sum_z3",
     )
     z_parts = (four[0], shift(four[1], "x", 1), shift(four[2], "x", 2), shift(four[3], "x", -1))
-
-    to_z = sum_first(from_x, "sum_x")
-    from_z = lax.all_to_all(to_z, "z", 0, 0, tiled=True)
+    for step in (1, -1, 3):
+        tail = tail + turn(tail, step)
     (grad_head_t,) = simple(
         join_kernel,
         [like((part, 2 * half), f32)],
@@ -521,20 +496,6 @@
         2 * from_z.size + 16 * part * half,
         "join",
     )
-
-    u0, u1, u2, u3 = sum_cut((u_keep, u_got), ((0,), (1,), (2,), (3,)), "sum_u")
-    u_all = (u0, shift(u1, "y", 1), shift(u2, "y", 2), shift(u3, "y", -1))
-    grad_hidden, gain_part = simple(
-        final_kernel,
-        [like(hidden.shape), like((1, cols + 128), f32)],
-        (*u_all, hidden, gain.reshape(1, cols), small),
-        12 * rows * cols,
-        "final",
-    )
-    tail = gain_part.reshape(-1, 128)
-    tail = tail + shift(tail, "x", 1) + shift(tail, "x", 2) + shift(tail, "x", -1)
-    for step in (1, -1, 3):
-        tail = tail + turn(tail, step)
     tail = tail.reshape(-1)
     return (tail[cols] / count, grad_hidden, tail[:cols], grad_head_t)
 

time: 225 us -> 210 us (0.933)
  Pallas kernels: 79.4 us -> 55.2 us
  blocking collectives: 0 us -> 9.34 us
  starting transfers between devices: 59.5 us -> 56.3 us
    ppermute x9, waiting for transfers between devices: 11.5 us -> 37.4 us  [turn(): lax.ppermute(value, 'z', [(i, (i + (step if i % 2 == 0 else -step)) % 8)...]
    pallas_call x8 -> x4, Pallas kernels: 44 us -> 21.6 us  [the longest x1 14.3 us: products_of(): pl.pallas_call(products_kernel, out_shape=shapes, grid_spec=pltpu.Prefetc...]
    all_to_all x1, waiting for transfers between devices: 21.6 us -> 5.98 us  [body(): from_x = lax.all_to_all(to_x, 'x', 0, 0, tiled=True)]
    all_to_all x0 -> x1, blocking collectives: none -> 9.34 us  [copy_for_each(): lax.all_to_all(jnp.broadcast_to(value[None], (size, *value.shape)), axis,...]
    ppermute x19, waiting for transfers between devices: 16.4 us -> 7.43 us  [shift(): return lax.ppermute(value, axis, [(i, (i + step) % n) for i in range(n)])]
    all_to_all x1, starting transfers between devices: 11.2 us -> 8.57 us  [copy_for_each(): lax.all_to_all(jnp.broadcast_to(value[None], (size, *value.shape)), axis,...]
    unnamed x56 -> x58, local copies, waits for them, and re-layouts: 9.14 us -> 10.1 us
  transfers between devices with their start and end apart: 32 -> 32, of which waited for: 9 -> 9; matrix products, arithmetic and copies ran while one was open for 4% -> 5% of each run, Pallas kernels for 27% -> 13%
where the time goes in v2:
time: 210 us; the launch traced here: 208 us
  waiting for transfers between devices  61 us (29%)
  starting transfers between devices  56.3 us (27%)
  Pallas kernels  55.2 us (26%)
  local copies, waits for them, and re-layouts  15.9 us (8%)
  blocking collectives  9.34 us (4%)
  other arithmetic  5.56 us (3%)
  between operations  4.76 us (2%)
    ppermute x9, waiting for transfers between devices, turn(): lax.ppermute(value, 'z', [(i, (i + (step if i % 2 == 0 else -step)) % 8)...  37.4 us
    ppermute x19, starting transfers between devices, shift(): return lax.ppermute(value, axis, [(i, (i + step) % n) for i in range(n)])  19.3 us
    pallas_call x2, Pallas kernels, logits_of(): pl.pallas_call(functools.partial(logits_kernel, count, per, last), out_sh...  15.7 us
    ppermute x9, starting transfers between devices, turn(): lax.ppermute(value, 'z', [(i, (i + (step if i % 2 == 0 else -step)) % 8)...  15.6 us
    pallas_call x1, Pallas kernels, products_of(): pl.pallas_call(products_kernel, out_shape=shapes, grid_spec=pltpu.Prefetc...  14.3 us
    pallas_call x5, Pallas kernels, sum_cut(): pl.pallas_call(functools.partial(sum_cut_kernel, len(ins), groups), out_s...  12.3 us
    unnamed x58, local copies, waits for them, and re-layouts  10.1 us
    all_to_all x1, blocking collectives, copy_for_each(): lax.all_to_all(jnp.broadcast_to(value[None], (size, *value.shape)), axis,...  9.34 us
  transfers between devices with their start and end apart: 32, of which 9 were waited for; matrix products, arithmetic and copies ran while one was open for 5% of the time, Pallas kernels for 13%

profile of v2, /device:TPU:32, one launch (start us, length us, event | category | flops | bytes accessed | tf_op | source)
XLA Modules:
  0.0 208.1 jit_solution(10136044868956572928)
XLA Ops:
  1.4 1.1 pad_maximum_fusion.refs_0_
  2.5 1.7 collective-permute-start.1
  4.2 1.7 collective-permute-start.2
  5.8 1.4 fusion.1
  9.4 9.3 %all_to_all.27 = f32[4,1,9]{2,1,0:T(1,128)S(1)} all-to-all(f32[4,1,9]{2,1,0:T(1,128)S(1)} %broadcast_in_dim.12), channel_id=1, replica_groups=mesh['z'=8,'x'=4,'y'=4,'c'=2] {'x'}, dimensions={0} | all-to-all | bytes 288 | tf_op jit(solution)/shard_map/all_to_all | solution.py:396
  18.7 2.1 collective-permute-done.1.refs_2_
  20.8 0.9 slice.21
  21.7 1.5 collective-permute-start.5
  24.5 1.7 collective-permute-start.6
  26.8 8.6 %all-to-all-start.1 = ((f32[8,1,9]{2,1,0:T(1,128)}), f32[8,1,9]{2,1,0:T(1,128)S(1)}, u32[]{:S(2)}, u32[]{:S(2)}) async-start(f32[8,1,9]{2,1,0:T(1,128)} %broadcast_in_dim.13), calls=%async_computation.1 | async-start | bytes 8192 | tf_op jit(solution)/shard_map/all_to_all | solution.py:396
  36.6 4.9 %all-to-all-done.1 = f32[8,1,9]{2,1,0:T(1,128)S(1)} async-done(((f32[8,1,9]{2,1,0:T(1,128)}), f32[8,1,9]{2,1,0:T(1,128)S(1)}, u32[]{:S(2)}, u32[]{:S(2)}) %all-to-all-start.1) | async-done | bytes 320 | tf_op jit(solution)/shard_map/all_to_all | solution.py:396
  44.3 0.9 copy-done.5
  45.4 9.6 %logits_first.1 = (bf16[3,512,1280]{2,1,0:T(8,128)(2,1)}, f32[512,512]{1,0:T(8,128)}, f32[8,512]{1,0:T(8,128)}) custom-call(s32[12]{0:T(128)} %concatenate.12.at, bf16[528,640]{1,0:T(8,128)(2,1)} %copy-done.1, bf16[528,640]{1,0:T(8,128)(2,1)} %copy-done.5, bf16[528,640]{1,0:T(8,128)(2,1)} %copy-done.3, bf16[528,640]{1,0:T(8,128)(2,1)} %copy-done.6, ...), custom_call_target="tpu_custom_call" | custom-call | flops 2013265920 | bytes 11796480 | tf_op jit(solution)/shard_map/logits_first/pallas_call | solution.py:153
  55.7 6.1 %logits_last.1 = (bf16[1,512,1280]{2,1,0:T(8,128)(2,1)}, f32[512,512]{1,0:T(8,128)}, f32[8,8,512]{2,1,0:T(8,128)}, f32[8,512]{1,0:T(8,128)}) custom-call(s32[12]{0:T(128)} %concatenate.12.at, bf16[272,640]{1,0:T(8,128)(2,1)} %collective-permute-done.5.refs_0_, bf16[256,640]{1,0:T(8,128)(2,1)} %collective-permute-done.6.refs_1_, bf16[272,640]{1,0:T(8,128)(2,1)} %copy-done.12, ...), custom_call_target="tpu_custom_call" | custom-call | flops 671088640 | bytes 3932160 | tf_op jit(solution)/shard_map/logits_last/pallas_call | solution.py:153
  61.8 3.6 %all-to-all-start.2 = ((f32[8,8,512]{2,1,0:T(8,128)}), f32[8,8,512]{2,1,0:T(8,128)S(1)}, u32[]{:S(2)}, u32[]{:S(2)}) async-start(f32[8,8,512]{2,1,0:T(8,128)} %get-tuple-element.60), calls=%async_computation.2 | async-start | bytes 262144 | tf_op jit(solution)/shard_map/all_to_all | solution.py:446
  66.0 5.3 %all-to-all-done.2.st = f32[8,8,512]{2,1,0:T(8,128)S(1)} async-done(((f32[8,8,512]{2,1,0:T(8,128)}), f32[8,8,512]{2,1,0:T(8,128)S(1)}, u32[]{:S(2)}, u32[]{:S(2)}) %all-to-all-start.2) | async-done | bytes 131104 | tf_op jit(solution)/shard_map/all_to_all | solution.py:446
  71.9 2.7 %policy.1 = (bf16[512,512]{1,0:T(8,128)(2,1)}, f32[8,512]{1,0:T(8,128)}) custom-call(s32[12]{0:T(128)} %concatenate.12.at, f32[5]{0:T(128)} %pad_maximum_fusion.2.nums, f32[8,8,512]{2,1,0:T(8,128)} %copy-done.11, f32[512,512]{1,0:T(8,128)} %get-tuple-element.61.lg, f32[8,512]{1,0:T(8,128)} %get-tuple-element.62.inv_ref, s32[1,512]{1,0:T(1,128)} %bitcast.24, ...), custom_call_target="tpu_custom_call" | custom-call | flops 2097152 | bytes 1572864 | tf_op jit(solution)/shard_map/policy/pallas_call | solution.py:212
  74.6 14.3 %products.1 = (bf16[4,8,160,256]{3,2,1,0:T(8,128)(2,1)}, bf16[4,4,160,128]{3,2,1,0:T(8,128)(2,1)}, bf16[4,4,160,128]{3,2,1,0:T(8,128)(2,1)}, bf16[4,4,160,128]{3...) custom-call(s32[12]{0:T(128)} %concatenate.12.at, ...), custom_call_target="tpu_custom_call" | custom-call | flops 5368709120 | bytes 20971520 | tf_op jit(solution)/shard_map/products/pallas_call | solution.py:278
  88.9 4.3 %all-to-all-start.3 = ((bf16[4,8,160,256]{3,2,1,0:T(8,128)(2,1)}), bf16[4,8,160,256]{3,2,1,0:T(8,128)(2,1)S(1)}, u32[]{:S(2)}, u32[]{:S(2)}) async-start(bf16[4,8,160,256]{3,2,1,0:T(8,128)(2,1)} %get-tuple-element.73), calls=%async_computation.3 | async-start | bytes 5242880 | tf_op jit(solution)/shard_map/all_to_all | solution.py:453
  93.8 1.5 collective-permute-start.11
  95.2 15.2 %collective-permute-done.13.refs_1_ = bf16[4,4,160,128]{3,2,1,0:T(8,128)(2,1)} collective-permute-done((bf16[4,4,160,128]{3,2,1,0:T(8,128)(2,1)}, bf16[4,4,160,128]{3,2,1,0:T(8,128)(2,1)}, u32[]{:S(2)}, u32[]{:S(2)}) %collective-permute-start.13) | collective-permute-done | bytes 655392 | tf_op jit(solution)/shard_map/ppermute | solution.py:31
  110.4 2.2 %sum_z1b.1 = (bf16[2,4,160,128]{3,2,1,0:T(8,128)(2,1)}, bf16[2,4,160,128]{3,2,1,0:T(8,128)(2,1)}) custom-call(bf16[4,4,160,128]{3,2,1,0:T(8,128)(2,1)} %get-tuple-element.74.refs_0_, bf16[4,4,160,128]{3,2,1,0:T(8,128)(2,1)} %collective-permute-done.13.refs_1_), custom_call_target="tpu_custom_call" | custom-call | flops 655360 | bytes 1966080 | tf_op jit(solution)/shard_map/sum_z1b/pallas_call | solution.py:315
  112.6 4.2 %sum_u.1 = (bf16[512,640]{1,0:T(8,128)(2,1)}, bf16[512,640]{1,0:T(8,128)(2,1)}, bf16[512,640]{1,0:T(8,128)(2,1)}, bf16[512,640]{1,0:T(8,128)(2,1)}) custom-call(bf16[4,512,640]{2,1,0:T(8,128)(2,1)} %get-tuple-element.64.refs_0_, bf16[4,512,640]{2,1,0:T(8,128)(2,1)} %collective-permute-done.9.refs_1_), custom_call_target="tpu_custom_call" | custom-call | flops 2621440 | bytes 7864320 | tf_op jit(solution)/shard_map/sum_u/pallas_call | solution.py:315
  117.6 2.2 %sum_z1a.1 = (bf16[2,4,160,128]{3,2,1,0:T(8,128)(2,1)}, bf16[2,4,160,128]{3,2,1,0:T(8,128)(2,1)}) custom-call(bf16[4,4,160,128]{3,2,1,0:T(8,128)(2,1)} %get-tuple-element.68.refs_0_, bf16[4,4,160,128]{3,2,1,0:T(8,128)(2,1)} %copy-done.7), custom_call_target="tpu_custom_call" | custom-call | flops 655360 | bytes 1966080 | tf_op jit(solution)/shard_map/sum_z1a/pallas_call | solution.py:315
  119.8 6.0 %all-to-all-done.3.a = bf16[4,8,160,256]{3,2,1,0:T(8,128)(2,1)S(1)} async-done(((bf16[4,8,160,256]{3,2,1,0:T(8,128)(2,1)}), bf16[4,8,160,256]{3,2,1,0:T(8,128)(2,1)S(1)}, u32[]{:S(2)}, u32[]{:S(2)}) %all-to-all-start.3) | async-done | bytes 2621472 | tf_op jit(solution)/shard_map/all_to_all | solution.py:453
  125.8 1.5 copy-done
  127.3 2.9 %sum_x.1 = bf16[8,160,256]{2,1,0:T(8,128)(2,1)} custom-call(bf16[4,8,160,256]{3,2,1,0:T(8,128)(2,1)} %copy-done), custom_call_target="tpu_custom_call" | custom-call | flops 1310720 | bytes 3932160 | tf_op jit(solution)/shard_map/sum_x/pallas_call | solution.py:335
  130.2 4.9 %all-to-all-start.4 = ((bf16[8,160,256]{2,1,0:T(8,128)(2,1)}), bf16[8,160,256]{2,1,0:T(8,128)(2,1)S(1)}, u32[]{:S(2)}, u32[]{:S(2)}) async-start(bf16[8,160,256]{2,1,0:T(8,128)(2,1)} %sum_x.1), calls=%async_computation.4 | async-start | bytes 1310720 | tf_op jit(solution)/shard_map/all_to_all | solution.py:463
  135.1 1.2 collective-permute-start.10
  136.2 0.9 collective-permute-start.15
  138.1 2.8 %collective-permute-start.12 = (bf16[2,4,160,128]{3,2,1,0:T(8,128)(2,1)}, bf16[2,4,160,128]{3,2,1,0:T(8,128)(2,1)S(1)}, u32[]{:S(2)}, u32[]{:S(2)}) collective-permute-start(bf16[2,4,160,128]{3,2,1,0:T(8,128)(2,1)} %get-tuple-element.72), channel_id=1, source_target_pairs={{0,224},{32,64},{64,32},{96,128},{128,96},{160,192},{192,160},{224... | collective-permute-start | bytes 983048 | tf_op jit(solution)/shard_map/ppermute | solution.py:31
  141.5 15.2 %collective-permute-done.14.refs_1_ = bf16[2,4,160,128]{3,2,1,0:T(8,128)(2,1)S(1)} collective-permute-done((bf16[2,4,160,128]{3,2,1,0:T(8,128)(2,1)S(1)}, bf16[2,4,160,128]{3,2,1,0:T(8,128)(2,1)S(1)}, u32[]{:S(2)}, u32[]{:S(2)}) %collective-permute-start.14) | collective-permute-done | bytes 327712 | tf_op jit(solution)/shard_map/ppermute | solution.py:31
  157.4 1.9 sum_z2b.1
  160.0 1.9 sum_z2a.1
  161.9 5.3 %collective-permute-done.15.u2 = bf16[512,640]{1,0:T(8,128)(2,1)S(1)} collective-permute-done((bf16[512,640]{1,0:T(8,128)(2,1)}, bf16[512,640]{1,0:T(8,128)(2,1)S(1)}, u32[]{:S(2)}, u32[]{:S(2)}) %collective-permute-start.15) | collective-permute-done | bytes 655392 | tf_op jit(solution)/shard_map/ppermute | solution.py:27
  168.2 3.4 %final.1 = (bf16[2,256,640]{2,1,0:T(8,128)(2,1)}, f32[1,768]{1,0:T(1,128)}) custom-call(bf16[512,640]{1,0:T(8,128)(2,1)} %get-tuple-element.66.u0, bf16[512,640]{1,0:T(8,128)(2,1)} %copy-done.8, bf16[512,640]{1,0:T(8,128)(2,1)} %copy-done.9, bf16[512,640]{1,0:T(8,128)(2,1)} %copy-done.10, bf16[2,256,640]{2,1,0:T(8,128)(2,1)} %h_ref.1, ...), custom_call_target="tpu_custom_call" | custom-call | flops 1966080 | bytes 3932160 | tf_op jit(solution)/shard_map/final/pallas_call | solution.py:383
  173.0 2.1 collective-permute-start.18
  175.8 4.5 %collective-permute-start.24 = (bf16[4,160,128]{2,1,0:T(8,128)(2,1)S(1)}, bf16[4,160,128]{2,1,0:T(8,128)(2,1)S(1)}, u32[]{:S(2)}, u32[]{:S(2)}) collective-permute-start(bf16[4,160,128]{2,1,0:T(8,128)(2,1)S(1)} %copy-done.24), channel_id=1, source_target_pairs={{0,160},{32,128},{64,224},{96,192},{128,32},{160,0},{192,96},{224,... | collective-permute-start | bytes 491528 | tf_op jit(solution)/shard_map/ppermute | solution.py:31
  180.3 1.5 collective-permute-start.23
  182.4 4.8 %collective-permute-done.20 = f32[6,128]{1,0:T(8,128)S(1)} collective-permute-done((f32[6,128]{1,0:T(8,128)S(1)}, f32[6,128]{1,0:T(8,128)S(1)}, u32[]{:S(2)}, u32[]{:S(2)}) %collective-permute-start.20) | collective-permute-done | bytes 3104 | tf_op jit(solution)/shard_map/ppermute | solution.py:31
  187.2 1.4 collective-permute-start.21
  188.6 2.2 %collective-permute-done.21 = f32[6,128]{1,0:T(8,128)S(1)} collective-permute-done((f32[6,128]{1,0:T(8,128)S(1)}, f32[6,128]{1,0:T(8,128)S(1)}, u32[]{:S(2)}, u32[]{:S(2)}) %collective-permute-start.21) | collective-permute-done | bytes 3104 | tf_op jit(solution)/shard_map/ppermute | solution.py:31
  190.8 2.6 %collective-permute-start.22 = (f32[6,128]{1,0:T(8,128)S(1)}, f32[6,128]{1,0:T(8,128)S(1)}, u32[]{:S(2)}, u32[]{:S(2)}) collective-permute-start(f32[6,128]{1,0:T(8,128)S(1)} %add.42), channel_id=1, source_target_pairs={{0,96},{32,192},{64,160},{96,0},{128,224},{160,64},{192,32},{224,1... | collective-permute-start | bytes 9224 | tf_op jit(solution)/shard_map/ppermute | solution.py:31
  194.2 1.9 sum_z3.1
  196.1 1.3 collective-permute-start.25
  197.4 1.6 collective-permute-start.26
  198.9 2.6 %collective-permute-start.27 = (bf16[160,256]{1,0:T(8,128)(2,1)}, bf16[160,256]{1,0:T(8,128)(2,1)S(1)}, u32[]{:S(2)}, u32[]{:S(2)}) collective-permute-start(bf16[160,256]{1,0:T(8,128)(2,1)} %get-tuple-element.95), channel_id=1, source_target_pairs={{0,24},{8,0},{16,8},{24,16},{1,25},{9,1},{17,9},{25,17},{2,26},{10... | collective-permute-start | bytes 245768 | tf_op jit(solution)/shard_map/ppermute | solution.py:27
  204.9 2.0 join.1
  (114 shorter events, 20.6 us)
Async XLA Ops:
  0.6 25.5 %copy-start.27 = (s32[4]{0:T(128)S(1)}, s32[4]{0:T(128)}, u32[]{:S(2)}) copy-start(s32[4]{0:T(128)} %constant.60.clone) | copy-start | bytes 52
  0.6 41.7 %copy-start.26 = (f32[2]{0:T(128)S(1)}, f32[2]{0:T(128)}, u32[]{:S(2)}) copy-start(f32[2]{0:T(128)} %param.15) | copy-start | bytes 28
  0.7 34.7 %copy-start.21 = (s32[2,256]{1,0:T(2,128)S(1)}, s32[2,256]{1,0:T(2,128)}, u32[]{:S(2)}) copy-start(s32[2,256]{1,0:T(2,128)} %param.12) | copy-start | bytes 6148
  2.5 41.7 %copy-start.1 = (bf16[528,640]{1,0:T(8,128)(2,1)}, bf16[528,640]{1,0:T(8,128)(2,1)S(1)}, u32[]{:S(2)}) copy-start(bf16[528,640]{1,0:T(8,128)(2,1)S(1)} %pad_maximum_fusion.refs_0_) | copy-start | bytes 2027524
  2.5 18.3 %collective-permute-start.1 = (bf16[528,640]{1,0:T(8,128)(2,1)S(1)}, bf16[528,640]{1,0:T(8,128)(2,1)S(1)}, u32[]{:S(2)}, u32[]{:S(2)}) collective-permute-start(bf16[528,640]{1,0:T(8,128)(2,1)S(1)} %pad_maximum_fusion.refs_0_), channel_id=1, source_target_pairs={{0,2},{2,4},{4,6},{6,0},{1,3},{3,5},{5,7},{7,1},{8,10},{10,12},{12... | collective-permute-start | bytes 2027528 | tf_op jit(solution)/shard_map/ppermute | solution.py:27
  4.2 16.6 %collective-permute-start.2 = (bf16[528,640]{1,0:T(8,128)(2,1)S(1)}, bf16[528,640]{1,0:T(8,128)(2,1)S(1)}, u32[]{:S(2)}, u32[]{:S(2)}) collective-permute-start(bf16[528,640]{1,0:T(8,128)(2,1)S(1)} %pad_maximum_fusion.refs_0_), channel_id=1, source_target_pairs={{0,6},{2,0},{4,2},{6,4},{1,7},{3,1},{5,3},{7,5},{8,14},{10,8},{12,... | collective-permute-start | bytes 2027528 | tf_op jit(solution)/shard_map/ppermute | solution.py:27
  20.8 23.5 %copy-start.3 = (bf16[528,640]{1,0:T(8,128)(2,1)}, bf16[528,640]{1,0:T(8,128)(2,1)S(1)}, u32[]{:S(2)}) copy-start(bf16[528,640]{1,0:T(8,128)(2,1)S(1)} %collective-permute-done.1.refs_2_) | copy-start | bytes 2027524
  20.8 23.5 %copy-start.4 = (bf16[528,640]{1,0:T(8,128)(2,1)}, bf16[528,640]{1,0:T(8,128)(2,1)S(1)}, u32[]{:S(2)}) copy-start(bf16[528,640]{1,0:T(8,128)(2,1)S(1)} %collective-permute-done.2.refs_4_) | copy-start | bytes 2027524
  21.7 20.1 %collective-permute-start.5 = (bf16[272,640]{1,0:T(8,128)(2,1)}, bf16[272,640]{1,0:T(8,128)(2,1)}, u32[]{:S(2)}, u32[]{:S(2)}) collective-permute-start(bf16[272,640]{1,0:T(8,128)(2,1)} %slice.21), channel_id=1, source_target_pairs={{0,2},{2,4},{4,6},{6,0},{1,3},{3,5},{5,7},{7,1},{8,10},{10,12},{12... | collective-permute-start | bytes 1044488 | tf_op jit(solution)/shard_map/ppermute | solution.py:27
  23.2 21.0 %collective-permute-start = (bf16[528,640]{1,0:T(8,128)(2,1)S(1)}, bf16[528,640]{1,0:T(8,128)(2,1)S(1)}, u32[]{:S(2)}, u32[]{:S(2)}) collective-permute-start(bf16[528,640]{1,0:T(8,128)(2,1)S(1)} %pad_maximum_fusion.refs_0_), channel_id=1, source_target_pairs={{0,1},{1,0},{2,3},{3,2},{4,5},{5,4},{6,7},{7,6},{8,9},{9,8},{10,11... | collective-permute-start | bytes 2027528 | tf_op jit(solution)/shard_map/ppermute | solution.py:27
  23.2 21.0 %collective-permute-start.3 = (bf16[528,640]{1,0:T(8,128)(2,1)S(1)}, bf16[528,640]{1,0:T(8,128)(2,1)S(1)}, u32[]{:S(2)}, u32[]{:S(2)}) collective-permute-start(bf16[528,640]{1,0:T(8,128)(2,1)S(1)} %collective-permute-done.1.refs_2_), channel_id=1, source_target_pairs={{0,1},{1,0},{2,3},{3,2},{4,5},{5,4},{6,7},{7,6},{8,9},{9,8},{10,11... | collective-permute-start | bytes 2027528 | tf_op jit(solution)/shard_map/ppermute | solution.py:27
  23.7 20.5 %collective-permute-start.4 = (bf16[528,640]{1,0:T(8,128)(2,1)S(1)}, bf16[528,640]{1,0:T(8,128)(2,1)}, u32[]{:S(2)}, u32[]{:S(2)}) collective-permute-start(bf16[528,640]{1,0:T(8,128)(2,1)S(1)} %collective-permute-done.2.refs_4_), channel_id=1, source_target_pairs={{0,1},{1,0},{2,3},{3,2},{4,5},{5,4},{6,7},{7,6},{8,9},{9,8},{10,11... | collective-permute-start | bytes 2027528 | tf_op jit(solution)/shard_map/ppermute | solution.py:27
  24.5 17.2 %collective-permute-start.6 = (bf16[256,640]{1,0:T(8,128)(2,1)}, bf16[256,640]{1,0:T(8,128)(2,1)}, u32[]{:S(2)}, u32[]{:S(2)}) collective-permute-start(bf16[256,640]{1,0:T(8,128)(2,1)} %slice.22), channel_id=1, source_target_pairs={{0,6},{2,0},{4,2},{6,4},{1,7},{3,1},{5,3},{7,5},{8,14},{10,8},{12,... | collective-permute-start | bytes 983048 | tf_op jit(solution)/shard_map/ppermute | solution.py:27
  26.8 14.7 %all-to-all-start.1 = ((f32[8,1,9]{2,1,0:T(1,128)}), f32[8,1,9]{2,1,0:T(1,128)S(1)}, u32[]{:S(2)}, u32[]{:S(2)}) async-start(f32[8,1,9]{2,1,0:T(1,128)} %broadcast_in_dim.13), calls=%async_computation.1 | async-start | bytes 8192 | tf_op jit(solution)/shard_map/all_to_all | solution.py:396
  41.7 13.2 %collective-permute-start.8 = (bf16[256,640]{1,0:T(8,128)(2,1)}, bf16[256,640]{1,0:T(8,128)(2,1)}, u32[]{:S(2)}, u32[]{:S(2)}) collective-permute-start(bf16[256,640]{1,0:T(8,128)(2,1)} %collective-permute-done.6.refs_1_), channel_id=1, source_target_pairs={{0,1},{1,0},{2,3},{3,2},{4,5},{5,4},{6,7},{7,6},{8,9},{9,8},{10,11... | collective-permute-start | bytes 983048 | tf_op jit(solution)/shard_map/ppermute | solution.py:27
  41.8 13.1 %collective-permute-start.7 = (bf16[272,640]{1,0:T(8,128)(2,1)}, bf16[272,640]{1,0:T(8,128)(2,1)S(1)}, u32[]{:S(2)}, u32[]{:S(2)}) collective-permute-start(bf16[272,640]{1,0:T(8,128)(2,1)} %collective-permute-done.5.refs_0_), channel_id=1, source_target_pairs={{0,1},{1,0},{2,3},{3,2},{4,5},{5,4},{6,7},{7,6},{8,9},{9,8},{10,11... | collective-permute-start | bytes 1044488 | tf_op jit(solution)/shard_map/ppermute | solution.py:27
  44.2 0.9 copy-start.5
  44.2 1.1 copy-start.6
  55.7 9.7 %copy-start.22 = (f32[2,256]{1,0:T(2,128)S(1)}, f32[2,256]{1,0:T(2,128)}, u32[]{:S(2)}) copy-start(f32[2,256]{1,0:T(2,128)} %param.14) | copy-start | bytes 6148
  61.8 9.4 %all-to-all-start.2 = ((f32[8,8,512]{2,1,0:T(8,128)}), f32[8,8,512]{2,1,0:T(8,128)S(1)}, u32[]{:S(2)}, u32[]{:S(2)}) async-start(f32[8,8,512]{2,1,0:T(8,128)} %get-tuple-element.60), calls=%async_computation.2 | async-start | bytes 262144 | tf_op jit(solution)/shard_map/all_to_all | solution.py:446
  88.9 23.7 %collective-permute-start.9 = (bf16[4,512,640]{2,1,0:T(8,128)(2,1)}, bf16[4,512,640]{2,1,0:T(8,128)(2,1)}, u32[]{:S(2)}, u32[]{:S(2)}) collective-permute-start(bf16[4,512,640]{2,1,0:T(8,128)(2,1)} %get-tuple-element.65), channel_id=1, source_target_pairs={{0,1},{1,0},{2,3},{3,2},{4,5},{5,4},{6,7},{7,6},{8,9},{9,8},{10,11... | collective-permute-start | bytes 7864328 | tf_op jit(solution)/shard_map/ppermute | solution.py:27
  88.9 36.9 %all-to-all-start.3 = ((bf16[4,8,160,256]{3,2,1,0:T(8,128)(2,1)}), bf16[4,8,160,256]{3,2,1,0:T(8,128)(2,1)S(1)}, u32[]{:S(2)}, u32[]{:S(2)}) async-start(bf16[4,8,160,256]{3,2,1,0:T(8,128)(2,1)} %get-tuple-element.73), calls=%async_computation.3 | async-start | bytes 5242880 | tf_op jit(solution)/shard_map/all_to_all | solution.py:453
  93.2 17.2 %collective-permute-start.13 = (bf16[4,4,160,128]{3,2,1,0:T(8,128)(2,1)}, bf16[4,4,160,128]{3,2,1,0:T(8,128)(2,1)}, u32[]{:S(2)}, u32[]{:S(2)}) collective-permute-start(bf16[4,4,160,128]{3,2,1,0:T(8,128)(2,1)} %get-tuple-element.75), channel_id=1, source_target_pairs={{0,224},{32,64},{64,32},{96,128},{128,96},{160,192},{192,160},{224... | collective-permute-start | bytes 1966088 | tf_op jit(solution)/shard_map/ppermute | solution.py:31
  93.8 23.0 %collective-permute-start.11 = (bf16[4,4,160,128]{3,2,1,0:T(8,128)(2,1)}, bf16[4,4,160,128]{3,2,1,0:T(8,128)(2,1)S(1)}, u32[]{:S(2)}, u32[]{:S(2)}) collective-permute-start(bf16[4,4,160,128]{3,2,1,0:T(8,128)(2,1)} %get-tuple-element.69), channel_id=1, source_target_pairs={{0,32},{32,0},{64,96},{96,64},{128,160},{160,128},{192,224},{224,1... | collective-permute-start | bytes 1966088 | tf_op jit(solution)/shard_map/ppermute | solution.py:31
  119.8 18.1 %copy-start.23 = (bf16[2,4,160,128]{3,2,1,0:T(8,128)(2,1)S(1)}, bf16[2,4,160,128]{3,2,1,0:T(8,128)(2,1)}, u32[]{:S(2)}) copy-start(bf16[2,4,160,128]{3,2,1,0:T(8,128)(2,1)} %get-tuple-element.76) | copy-start | bytes 983044
  119.8 21.1 %copy-start.20 = (bf16[640]{0:T(1024)(128)(2,1)S(1)}, bf16[640]{0:T(1024)(128)(2,1)}, u32[]{:S(2)}) copy-start(bf16[640]{0:T(1024)(128)(2,1)} %param.10) | copy-start | bytes 3844
  125.8 1.5 copy-start
  130.2 73.9 %all-to-all-start.4 = ((bf16[8,160,256]{2,1,0:T(8,128)(2,1)}), bf16[8,160,256]{2,1,0:T(8,128)(2,1)S(1)}, u32[]{:S(2)}, u32[]{:S(2)}) async-start(bf16[8,160,256]{2,1,0:T(8,128)(2,1)} %sum_x.1), calls=%async_computation.4 | async-start | bytes 1310720 | tf_op jit(solution)/shard_map/all_to_all | solution.py:463
  135.1 26.8 %collective-permute-start.10 = (bf16[512,640]{1,0:T(8,128)(2,1)}, bf16[512,640]{1,0:T(8,128)(2,1)S(1)}, u32[]{:S(2)}, u32[]{:S(2)}) collective-permute-start(bf16[512,640]{1,0:T(8,128)(2,1)} %get-tuple-element.67), channel_id=1, source_target_pairs={{0,6},{2,0},{4,2},{6,4},{1,7},{3,1},{5,3},{7,5},{8,14},{10,8},{12,... | collective-permute-start | bytes 1966088 | tf_op jit(solution)/shard_map/ppermute | solution.py:27
  136.2 30.9 %collective-permute-start.15 = (bf16[512,640]{1,0:T(8,128)(2,1)}, bf16[512,640]{1,0:T(8,128)(2,1)S(1)}, u32[]{:S(2)}, u32[]{:S(2)}) collective-permute-start(bf16[512,640]{1,0:T(8,128)(2,1)} %get-tuple-element.84), channel_id=1, source_target_pairs={{0,2},{2,4},{4,6},{6,0},{1,3},{3,5},{5,7},{7,1},{8,10},{10,12},{12... | collective-permute-start | bytes 1966088 | tf_op jit(solution)/shard_map/ppermute | solution.py:27
  137.1 30.1 %collective-permute-start.16 = (bf16[512,640]{1,0:T(8,128)(2,1)}, bf16[512,640]{1,0:T(8,128)(2,1)S(1)}, u32[]{:S(2)}, u32[]{:S(2)}) collective-permute-start(bf16[512,640]{1,0:T(8,128)(2,1)} %get-tuple-element.85), channel_id=1, source_target_pairs={{0,4},{2,6},{4,0},{6,2},{1,5},{3,7},{5,1},{7,3},{8,12},{10,14},{12... | collective-permute-start | bytes 1966088 | tf_op jit(solution)/shard_map/ppermute | solution.py:27
  137.9 18.8 %collective-permute-start.14 = (bf16[2,4,160,128]{3,2,1,0:T(8,128)(2,1)S(1)}, bf16[2,4,160,128]{3,2,1,0:T(8,128)(2,1)S(1)}, u32[]{:S(2)}, u32[]{:S(2)}) collective-permute-start(bf16[2,4,160,128]{3,2,1,0:T(8,128)(2,1)S(1)} %copy-done.23), channel_id=1, source_target_pairs={{0,32},{32,0},{64,96},{96,64},{128,160},{160,128},{192,224},{224,1... | collective-permute-start | bytes 983048 | tf_op jit(solution)/shard_map/ppermute | solution.py:31
  138.1 21.2 %collective-permute-start.12 = (bf16[2,4,160,128]{3,2,1,0:T(8,128)(2,1)}, bf16[2,4,160,128]{3,2,1,0:T(8,128)(2,1)S(1)}, u32[]{:S(2)}, u32[]{:S(2)}) collective-permute-start(bf16[2,4,160,128]{3,2,1,0:T(8,128)(2,1)} %get-tuple-element.72), channel_id=1, source_target_pairs={{0,224},{32,64},{64,32},{96,128},{128,96},{160,192},{192,160},{224... | collective-permute-start | bytes 983048 | tf_op jit(solution)/shard_map/ppermute | solution.py:31
  159.3 16.5 %copy-start.24 = (bf16[4,160,128]{2,1,0:T(8,128)(2,1)S(1)}, bf16[4,160,128]{2,1,0:T(8,128)(2,1)}, u32[]{:S(2)}) copy-start(bf16[4,160,128]{2,1,0:T(8,128)(2,1)} %get-tuple-element.82) | copy-start | bytes 491524
  161.9 18.4 %copy-start.25 = (bf16[4,160,128]{2,1,0:T(8,128)(2,1)S(1)}, bf16[4,160,128]{2,1,0:T(8,128)(2,1)}, u32[]{:S(2)}) copy-start(bf16[4,160,128]{2,1,0:T(8,128)(2,1)} %get-tuple-element.79) | copy-start | bytes 491524
  161.9 5.3 %copy-start.8 = (bf16[512,640]{1,0:T(8,128)(2,1)}, bf16[512,640]{1,0:T(8,128)(2,1)S(1)}, u32[]{:S(2)}) copy-start(bf16[512,640]{1,0:T(8,128)(2,1)S(1)} %collective-permute-done.10.u1) | copy-start | bytes 1966084
  167.2 1.1 copy-start.10
  172.3 9.4 %collective-permute-start.17 = (f32[6,128]{1,0:T(8,128)S(1)}, f32[6,128]{1,0:T(8,128)S(1)}, u32[]{:S(2)}, u32[]{:S(2)}) collective-permute-start(f32[6,128]{1,0:T(8,128)S(1)} %bitcast.26), channel_id=1, source_target_pairs={{0,8},{8,16},{16,24},{24,0},{1,9},{9,17},{17,25},{25,1},{2,10},{10... | collective-permute-start | bytes 9224 | tf_op jit(solution)/shard_map/ppermute | solution.py:27
  173.0 8.7 %collective-permute-start.18 = (f32[6,128]{1,0:T(8,128)S(1)}, f32[6,128]{1,0:T(8,128)S(1)}, u32[]{:S(2)}, u32[]{:S(2)}) collective-permute-start(f32[6,128]{1,0:T(8,128)S(1)} %bitcast.27), channel_id=1, source_target_pairs={{0,16},{8,24},{16,0},{24,8},{1,17},{9,25},{17,1},{25,9},{2,18},{10... | collective-permute-start | bytes 9224 | tf_op jit(solution)/shard_map/ppermute | solution.py:27
  175.0 6.7 %collective-permute-start.19 = (f32[6,128]{1,0:T(8,128)S(1)}, f32[6,128]{1,0:T(8,128)S(1)}, u32[]{:S(2)}, u32[]{:S(2)}) collective-permute-start(f32[6,128]{1,0:T(8,128)S(1)} %bitcast.28), channel_id=1, source_target_pairs={{0,24},{8,0},{16,8},{24,16},{1,25},{9,1},{17,9},{25,17},{2,26},{10... | collective-permute-start | bytes 9224 | tf_op jit(solution)/shard_map/ppermute | solution.py:27
  175.8 17.7 %collective-permute-start.24 = (bf16[4,160,128]{2,1,0:T(8,128)(2,1)S(1)}, bf16[4,160,128]{2,1,0:T(8,128)(2,1)S(1)}, u32[]{:S(2)}, u32[]{:S(2)}) collective-permute-start(bf16[4,160,128]{2,1,0:T(8,128)(2,1)S(1)} %copy-done.24), channel_id=1, source_target_pairs={{0,160},{32,128},{64,224},{96,192},{128,32},{160,0},{192,96},{224,... | collective-permute-start | bytes 491528 | tf_op jit(solution)/shard_map/ppermute | solution.py:31
  180.3 13.2 %collective-permute-start.23 = (bf16[4,160,128]{2,1,0:T(8,128)(2,1)S(1)}, bf16[4,160,128]{2,1,0:T(8,128)(2,1)S(1)}, u32[]{:S(2)}, u32[]{:S(2)}) collective-permute-start(bf16[4,160,128]{2,1,0:T(8,128)(2,1)S(1)} %copy-done.25), channel_id=1, source_target_pairs={{0,96},{32,192},{64,160},{96,0},{128,224},{160,64},{192,32},{224,1... | collective-permute-start | bytes 491528 | tf_op jit(solution)/shard_map/ppermute | solution.py:31
  181.7 5.5 %collective-permute-start.20 = (f32[6,128]{1,0:T(8,128)S(1)}, f32[6,128]{1,0:T(8,128)S(1)}, u32[]{:S(2)}, u32[]{:S(2)}) collective-permute-start(f32[6,128]{1,0:T(8,128)S(1)} %add_add_fusion), channel_id=1, source_target_pairs={{0,32},{32,0},{64,96},{96,64},{128,160},{160,128},{192,224},{224,1... | collective-permute-start | bytes 9224 | tf_op jit(solution)/shard_map/ppermute | solution.py:31
  187.2 3.6 %collective-permute-start.21 = (f32[6,128]{1,0:T(8,128)S(1)}, f32[6,128]{1,0:T(8,128)S(1)}, u32[]{:S(2)}, u32[]{:S(2)}) collective-permute-start(f32[6,128]{1,0:T(8,128)S(1)} %add.41), channel_id=1, source_target_pairs={{0,224},{32,64},{64,32},{96,128},{128,96},{160,192},{192,160},{224... | collective-permute-start | bytes 9224 | tf_op jit(solution)/shard_map/ppermute | solution.py:31
  190.8 10.7 %collective-permute-start.22 = (f32[6,128]{1,0:T(8,128)S(1)}, f32[6,128]{1,0:T(8,128)S(1)}, u32[]{:S(2)}, u32[]{:S(2)}) collective-permute-start(f32[6,128]{1,0:T(8,128)S(1)} %add.42), channel_id=1, source_target_pairs={{0,96},{32,192},{64,160},{96,0},{128,224},{160,64},{192,32},{224,1... | collective-permute-start | bytes 9224 | tf_op jit(solution)/shard_map/ppermute | solution.py:31
  196.1 7.9 %collective-permute-start.25 = (bf16[160,256]{1,0:T(8,128)(2,1)}, bf16[160,256]{1,0:T(8,128)(2,1)S(1)}, u32[]{:S(2)}, u32[]{:S(2)}) collective-permute-start(bf16[160,256]{1,0:T(8,128)(2,1)} %get-tuple-element.93), channel_id=1, source_target_pairs={{0,8},{8,16},{16,24},{24,0},{1,9},{9,17},{17,25},{25,1},{2,10},{10... | collective-permute-start | bytes 245768 | tf_op jit(solution)/shard_map/ppermute | solution.py:27
  197.4 6.6 %collective-permute-start.26 = (bf16[160,256]{1,0:T(8,128)(2,1)}, bf16[160,256]{1,0:T(8,128)(2,1)S(1)}, u32[]{:S(2)}, u32[]{:S(2)}) collective-permute-start(bf16[160,256]{1,0:T(8,128)(2,1)} %get-tuple-element.94), channel_id=1, source_target_pairs={{0,16},{8,24},{16,0},{24,8},{1,17},{9,25},{17,1},{25,9},{2,18},{10... | collective-permute-start | bytes 245768 | tf_op jit(solution)/shard_map/ppermute | solution.py:27
  198.9 5.1 %collective-permute-start.27 = (bf16[160,256]{1,0:T(8,128)(2,1)}, bf16[160,256]{1,0:T(8,128)(2,1)S(1)}, u32[]{:S(2)}, u32[]{:S(2)}) collective-permute-start(bf16[160,256]{1,0:T(8,128)(2,1)} %get-tuple-element.95), channel_id=1, source_target_pairs={{0,24},{8,0},{16,8},{24,16},{1,25},{9,1},{17,9},{25,17},{2,26},{10... | collective-permute-start | bytes 245768 | tf_op jit(solution)/shard_map/ppermute | solution.py:27
  (12 other events, 8.7 us)

commit v3 on v2

--- a/solution.py
+++ b/solution.py
@@ -220,13 +220,9 @@
     )(at, nums, stats, logits, inv, targets, old_logp)
 
 
-def products_kernel(at, early, late, dl, head, to_x, send_a, send_b, keep_a, keep_b, u_send, u_keep):
-    j = pl.program_id(0)
-    c, z = at[2], at[3]
-    scaled = jnp.where(j < 3, early[0], late[0])
-    cols = scaled.shape[1] // 2
-    step, half = cols // 4, dl.shape[1] // 2
-    width = half // 2
+def back_kernel(at, dl, head, u_send, u_keep):
+    c = at[2]
+    cols = head.shape[1] // 2
     back = jnp.dot(dl[...], head[...], preferred_element_type=f32).astype(bf16)
 
     @pl.when(c == 0)
@@ -239,44 +235,51 @@
         u_send[0] = back[:, :cols]
         u_keep[0] = back[:, cols:]
 
+
+def back_of(at, dl, head, cols):
+    rows, half = dl.shape
+    shapes = [like((4, rows, cols))] * 2
+    return pl.pallas_call(
+        back_kernel,
+        out_shape=shapes,
+        grid_spec=pltpu.PrefetchScalarGridSpec(
+            num_scalar_prefetch=1,
+            grid=(4,),
+            in_specs=[
+                full((rows, half)),
+                pl.BlockSpec((half, 2 * cols), lambda j, at: (0, at[8 + j])),
+            ],
+            out_specs=[pl.BlockSpec((1, rows, cols), lambda j, at: (j, 0, 0))] * 2,
+        ),
+        compiler_params=params(),
+        cost_estimate=cost(2 * rows * 8 * cols * half, 32 * rows * cols),
+        name="back",
+    )(at, dl, head)
+
+
+def heads_kernel(at, early, late, dl, to_x, to_z):
+    j = pl.program_id(0)
+    scaled = jnp.where(j < 3, early[0], late[0])
+    cols = scaled.shape[1] // 2
+    step, half = cols // 4, dl.shape[1] // 2
     got = lax.dot_general(
         scaled, dl[...], (((0,), (0,)), ((), ())), preferred_element_type=f32
     ).astype(bf16)
-    odd = lax.rem(z, 2)
     for i in range(2):
         place = 2 * at[8 + j] + i
-        ahead = lax.rem(place - z + 8, 8)
-        behind = lax.rem(8 - ahead, 8)
-        parts = [got[i * cols + k * step : i * cols + (k + 1) * step, :] for k in range(4)]
         for k in range(4):
-            to_x[k, place] = parts[k][:, :half]
-        for side, send, keep in ((0, send_a, keep_a), (1, send_b, keep_b)):
-            q = jnp.where(odd == side, ahead, behind)
-            low = lax.rem(q, 4)
-            sent = (low == 1) | (low == 2)
-            send_at = jnp.where(sent, 2 * (q // 4) + low - 1, 0)
-            keep_at = jnp.where(q == 0, 0, jnp.where(q == 7, 1, jnp.where(q == 4, 2, 3)))
-            cut = slice(half + side * width, half + (side + 1) * width)
-
-            @pl.when(sent)
-            def _(send=send, cut=cut, send_at=send_at, parts=parts):
-                for k in range(4):
-                    send[send_at, k] = parts[k][:, cut]
-
-            @pl.when(jnp.logical_not(sent))
-            def _(keep=keep, cut=cut, keep_at=keep_at, parts=parts):
-                for k in range(4):
-                    keep[keep_at, k] = parts[k][:, cut]
-
-
-def products_of(at, early, late, dl, head):
+            part = got[i * cols + k * step : i * cols + (k + 1) * step, :]
+            to_x[k, place] = part[:, :half]
+            to_z[place, k] = part[:, half:]
+
+
+def heads_of(at, early, late, dl):
     _, rows, cols = early.shape
     half = dl.shape[1]
     step = cols // 8
-    cut = like((4, 4, step, half // 4))
-    shapes = [like((4, 8, step, half // 2))] + [cut] * 4 + [like((4, rows, cols // 2))] * 2
-    return pl.pallas_call(
-        products_kernel,
+    shapes = [like((4, 8, step, half // 2)), like((8, 4, step, half // 2))]
+    return pl.pallas_call(
+        heads_kernel,
         out_shape=shapes,
         grid_spec=pltpu.PrefetchScalarGridSpec(
             num_scalar_prefetch=1,
@@ -285,40 +288,39 @@
                 pl.BlockSpec((1, rows, cols), lambda j, at: (jnp.minimum(j, 2), 0, 0)),
                 full(late.shape),
                 full((rows, half)),
-                pl.BlockSpec((half, cols), lambda j, at: (0, at[8 + j])),
             ],
-            out_specs=[full(s.shape) for s in shapes[:5]]
-            + [pl.BlockSpec((1, rows, cols // 2), lambda j, at: (j, 0, 0))] * 2,
+            out_specs=[full(s.shape) for s in shapes],
         ),
         compiler_params=params(),
-        cost_estimate=cost(4 * rows * 4 * cols * half, 32 * rows * cols),
-        name="products",
-    )(at, early, late, dl, head)
-
-
-def sum_cut_kernel(n, groups, *refs):
-    ins, outs = refs[:n], refs[n:]
-    for out, group in zip(outs, groups):
-        for at, j in enumerate(group):
-            total = ins[0][j].astype(f32)
-            for other in ins[1:]:
-                total = total + other[j].astype(f32)
-            if len(out.shape) == len(ins[0].shape):
-                out[at] = total.astype(out.dtype)
-            else:
-                out[...] = total.astype(out.dtype)
-
-
-def sum_cut(ins, groups, name):
+        cost_estimate=cost(2 * rows * 4 * cols * half, 24 * rows * cols),
+        name="heads",
+    )(at, early, late, dl)
+
+
+def sum_pairs_kernel(groups, *refs):
+    pairs = len(refs) // (2 + len(groups))
+    ins, outs = refs[: 2 * pairs], refs[2 * pairs :]
+    for p in range(pairs):
+        keep, got = ins[2 * p], ins[2 * p + 1]
+        for out, group in zip(outs[p * len(groups) :], groups):
+            for at, j in enumerate(group):
+                total = (keep[j].astype(f32) + got[j].astype(f32)).astype(out.dtype)
+                if len(group) > 1:
+                    out[at] = total
+                else:
+                    out[...] = total
+
+
+def sum_pairs(ins, groups, name):
     shape = ins[0].shape[1:]
-    outs = [like(((len(g),) if len(g) > 1 else ()) + shape) for g in groups]
-    return pl.pallas_call(
-        functools.partial(sum_cut_kernel, len(ins), groups),
+    outs = [like(((len(g),) if len(g) > 1 else ()) + shape) for g in groups] * (len(ins) // 2)
+    return pl.pallas_call(
+        functools.partial(sum_pairs_kernel, groups),
         out_shape=outs,
         in_specs=[whole()] * len(ins),
         out_specs=[whole()] * len(outs),
         compiler_params=params(),
-        cost_estimate=cost(len(ins) * ins[0].size, 2 * (len(ins) + 1) * ins[0].size),
+        cost_estimate=cost(len(ins) * ins[0].size, 3 * len(ins) * ins[0].size),
         name=name,
     )(*ins)
 
@@ -343,24 +345,13 @@
     )(value)
 
 
-def both_kernel(at, keep_a, got_a, keep_b, got_b, *outs):
-    width = keep_a.shape[2]
-    for k, out in enumerate(outs):
-        place = lax.rem(at[4] + k, 4)
-        for first, keep, got in ((0, keep_a, got_a), (width, keep_b, got_b)):
-            total = keep[place].astype(f32) + got[place].astype(f32)
-            out[:, first : first + width] = total.astype(bf16)
-
-
-def join_kernel(from_z, s0, s1, s2, s3, out):
-    width = s0.shape[1]
+def join_kernel(from_z, from_x, out):
+    width = from_x.shape[1]
     total = from_z[0].astype(f32)
     for k in range(1, from_z.shape[0]):
         total = total + from_z[k].astype(f32)
     out[:, :width] = total
-    out[:, width:] = (
-        s0[...].astype(f32) + s1[...].astype(f32) + s2[...].astype(f32) + s3[...].astype(f32)
-    )
+    out[:, width:] = from_x[...].astype(f32)
 
 
 def final_kernel(u0, u1, u2, u3, h_ref, g_ref, small, out, part):
@@ -422,12 +413,20 @@
     local = jnp.concatenate(
         [jnp.sum(member * rewards[:, None], axis=0), jnp.sum(lengths).astype(f32)[None]]
     )
-    over_x = copy_for_each(local, "x").sum(axis=0)
-    prev, following, over_x = lax.optimization_barrier((prev, following, over_x))
-
-    far_a, far_b = shift(prev[:cut], "y", 1), shift(following[cut:], "y", -1)
+    over_z = copy_for_each(local, "z").sum(axis=0)
+    prev, following, over_z = lax.optimization_barrier((prev, following, over_z))
+
+    far_a, far_b = prev[:cut], following[cut:]
+    far_a, far_b, prev, following = lax.optimization_barrier((far_a, far_b, prev, following))
+    far_a, far_b = shift(far_a, "y", 1), shift(far_b, "y", -1)
+    sums = copy_for_each(over_z, "x").sum(axis=0)
     prev_o, following_o = shift(prev, "c", 1), shift(following, "c", 1)
-    sums = copy_for_each(over_x, "z").sum(axis=0)
+    early, acc, sq = logits_of(
+        at, 0, [(payload, own_o), (prev, prev_o), (following, following_o)], head
+    )
+    far_a, far_b = after(far_a, acc), after(far_b, acc)
+    far_a_o, far_b_o = shift(far_a, "c", 1), shift(far_b, "c", 1)
+
     group_sums, count = sums[:groups_all], sums[groups_all]
     adv_resp = rewards - jnp.sum(member * group_sums[None, :], axis=1) / GROUP
     slots_all = rows * lax.axis_size(DP)
@@ -435,39 +434,24 @@
     targets = targets.reshape(1, rows)
     old_logp = old_logp.reshape(1, rows)
 
-    early, acc, sq = logits_of(
-        at, 0, [(payload, own_o), (prev, prev_o), (following, following_o)], head
-    )
-    far_a_o, far_b_o = shift(far_a, "c", 1), shift(far_b, "c", 1)
-    acc, nums, far_a_o = lax.optimization_barrier((acc, nums, far_a_o))
     late, logits, stats, inv = logits_of(
         at, 3, [(far_a, far_b, far_a_o, far_b_o)], head, (acc, sq), targets
     )
     all_stats = lax.all_to_all(stats, FSDP, 0, 0, tiled=True)
     dl, small = policy_of(at, nums, all_stats, logits, inv, targets, old_logp)
-    to_x, send_a, send_b, keep_a, keep_b, u_send, u_keep = products_of(at, early, late, dl, head)
     part, half = cols // 4, dl.shape[1] // 2
 
+    u_send, u_keep = back_of(at, dl, head, cols)
     u_got = shift(u_send, "c", 1)
-    got_a, got_b = turn(send_a, 1), turn(send_b, -1)
+    to_x, to_z = heads_of(at, early, late, after(dl, u_send))
+    half_z = lax.psum_scatter(to_z, "z", scatter_dimension=0, tiled=False)
+    half_z = lax.psum_scatter(half_z, "x", scatter_dimension=0, tiled=False)
     from_x = lax.all_to_all(to_x, "x", 0, 0, tiled=True)
-    u0, u1, u2, u3 = sum_cut((u_keep, u_got), ((0,), (1,), (2,), (3,)), "sum_u")
+    u0, u1, u2, u3 = sum_pairs((u_keep, u_got), ((0,), (1,), (2,), (3,)), "sum_u")
     u1, u2, u3 = shift(u1, "y", -1), shift(u2, "y", 1), shift(u3, "y", 2)
 
-    got_a = after(got_a, u0)
-    send2_a, keep2_a = sum_cut((keep_a, got_a), ((2, 1), (3, 0)), "sum_z1a")
-    send2_b, keep2_b = sum_cut((keep_b, got_b), ((2, 1), (3, 0)), "sum_z1b")
-    got2_a, got2_b = turn(send2_a, -1), turn(send2_b, 1)
-    from_x = after(from_x, send2_a, send2_b)
-    to_z = sum_first(from_x, "sum_x")
-    from_z = lax.all_to_all(to_z, "z", 0, 0, tiled=True)
-
-    got2_a, got2_b = after(got2_a, to_z), after(got2_b, to_z)
-    send3_a, keep3_a = sum_cut((keep2_a, got2_a), ((0,), (1,)), "sum_z2a")
-    send3_b, keep3_b = sum_cut((keep2_b, got2_b), ((0,), (1,)), "sum_z2b")
-    got3_a, got3_b = turn(send3_a, 3), turn(send3_b, -3)
-
-    u1 = after(u1, send3_a, send3_b)
+    from_x = after(from_x, u1, u2, u3)
+    from_z = lax.all_to_all(sum_first(from_x, "sum_x"), "z", 0, 0, tiled=True)
     grad_hidden, gain_part = simple(
         final_kernel,
         [like(hidden.shape), like((1, cols + 128), f32)],
@@ -477,22 +461,12 @@
     )
     tail = gain_part.reshape(-1, 128)
     tail = tail + shift(tail, "x", 1) + shift(tail, "x", 2) + shift(tail, "x", -1)
-
-    got3_a = after(got3_a, gain_part)
-    four = simple(
-        both_kernel,
-        [like((part, half))] * 4,
-        (at, keep3_a, got3_a, keep3_b, got3_b),
-        12 * keep3_a.size,
-        "sum_z3",
-    )
-    z_parts = (four[0], shift(four[1], "x", 1), shift(four[2], "x", 2), shift(four[3], "x", -1))
     for step in (1, -1, 3):
         tail = tail + turn(tail, step)
     (grad_head_t,) = simple(
         join_kernel,
         [like((part, 2 * half), f32)],
-        (from_z, *z_parts),
+        (from_z, half_z),
         2 * from_z.size + 16 * part * half,
         "join",
     )

time: 210 us -> 188 us (0.90)
  between operations: 4.76 us -> 18.1 us
  starting transfers between devices: 56.3 us -> 45.9 us
  blocking collectives: 9.34 us -> 0 us
  Pallas kernels: 55.2 us -> 48 us
  local copies, waits for them, and re-layouts: 15.9 us -> 11 us
  waiting for transfers between devices: 61 us -> 58.4 us
    ppermute x9 -> x3, waiting for transfers between devices: 37.4 us -> 8.77 us  [turn(): lax.ppermute(value, 'z', [(i, (i + (step if i % 2 == 0 else -step)) % 8)...]
    all_to_all x1, waiting for transfers between devices: 5.98 us -> 24.2 us  [body(): from_x = lax.all_to_all(to_x, 'x', 0, 0, tiled=True)]
    ppermute x9 -> x3, starting transfers between devices: 15.6 us -> 5.05 us  [turn(): lax.ppermute(value, 'z', [(i, (i + (step if i % 2 == 0 else -step)) % 8)...]
    all_to_all x1 -> x0, blocking collectives: 9.34 us -> none  [copy_for_each(): lax.all_to_all(jnp.broadcast_to(value[None], (size, *value.shape)), axis,...]
    all_to_all x1 -> x2, waiting for transfers between devices: 4.9 us -> 10.8 us  [copy_for_each(): lax.all_to_all(jnp.broadcast_to(value[None], (size, *value.shape)), axis,...]
    unnamed x58 -> x34, local copies, waits for them, and re-layouts: 10.1 us -> 4.59 us
    ppermute x19 -> x16, starting transfers between devices: 19.3 us -> 13.9 us  [shift(): return lax.ppermute(value, axis, [(i, (i + step) % n) for i in range(n)])]
    pallas_call x6 -> x3, Pallas kernels: 26.6 us -> 21.4 us  [the longest x1 8.91 us: heads_of(): pl.pallas_call(heads_kernel, out_shape=shapes, grid_spec=pltpu.PrefetchSc...]
  transfers between devices with their start and end apart: 32 -> 26, of which waited for: 9 -> 12; matrix products, arithmetic and copies ran while one was open for 5% -> 6% of each run, Pallas kernels for 13% -> 11%
where the time goes in v3:
time: 188 us; the launch traced here: 187 us
  waiting for transfers between devices  58.4 us (31%)
  Pallas kernels  48 us (26%)
  starting transfers between devices  45.9 us (24%)
  between operations  18.1 us (10%)
  local copies, waits for them, and re-layouts  11 us (6%)
  other arithmetic  5.53 us (3%)
    all_to_all x1, waiting for transfers between devices, body(): from_x = lax.all_to_all(to_x, 'x', 0, 0, tiled=True)  24.2 us
    pallas_call x2, Pallas kernels, logits_of(): pl.pallas_call(functools.partial(logits_kernel, count, per, last), out_sh...  15.8 us
    ppermute x16, starting transfers between devices, shift(): return lax.ppermute(value, axis, [(i, (i + step) % n) for i in range(n)])  13.9 us
    all_to_all x2, starting transfers between devices, copy_for_each(): lax.all_to_all(jnp.broadcast_to(value[None], (size, *value.shape)), axis,...  12.9 us
    all_to_all x2, waiting for transfers between devices, copy_for_each(): lax.all_to_all(jnp.broadcast_to(value[None], (size, *value.shape)), axis,...  10.8 us
    ppermute x16, waiting for transfers between devices, shift(): return lax.ppermute(value, axis, [(i, (i + step) % n) for i in range(n)])  9.92 us
    pallas_call x1, Pallas kernels, heads_of(): pl.pallas_call(heads_kernel, out_shape=shapes, grid_spec=pltpu.PrefetchSc...  8.91 us
    ppermute x3, waiting for transfers between devices, turn(): lax.ppermute(value, 'z', [(i, (i + (step if i % 2 == 0 else -step)) % 8)...  8.77 us
  transfers between devices with their start and end apart: 26, of which 12 were waited for; matrix products, arithmetic and copies ran while one was open for 6% of the time, Pallas kernels for 11%

profile of v3, /device:TPU:32, one launch (start us, length us, event | category | flops | bytes accessed | tf_op | source)
XLA Modules:
  0.0 187.0 jit_solution(15693374814161672038)
XLA Ops:
  7.2 0.7 broadcast_in_dim.10
  7.9 1.1 pad_maximum_fusion.refs_0_
  9.0 1.7 collective-permute-start
  10.7 1.7 collective-permute-start.1
  12.3 1.4 fusion.1
  14.4 0.7 and_select_fusion
  15.0 0.7 select_reduce_fusion.1
  16.4 8.6 %all-to-all-start = ((f32[8,1,9]{2,1,0:T(1,128)}), f32[8,1,9]{2,1,0:T(1,128)S(1)}, u32[]{:S(2)}, u32[]{:S(2)}) async-start(f32[8,1,9]{2,1,0:T(1,128)} %broadcast_in_dim.12), calls=%async_computation | async-start | bytes 8192 | tf_op jit(solution)/shard_map/all_to_all | solution.py:387
  25.0 6.1 %all-to-all-done = f32[8,1,9]{2,1,0:T(1,128)S(1)} async-done(((f32[8,1,9]{2,1,0:T(1,128)}), f32[8,1,9]{2,1,0:T(1,128)S(1)}, u32[]{:S(2)}, u32[]{:S(2)}) %all-to-all-start) | async-done | bytes 320 | tf_op jit(solution)/shard_map/all_to_all | solution.py:387
  31.2 0.8 slice.23
  32.1 0.8 slice.24
  33.3 1.8 collective-permute-start.6
  35.4 0.7 concatenate.12.at
  36.1 0.8 copy-done.5
  37.2 9.6 %logits_first.1 = (bf16[3,512,1280]{2,1,0:T(8,128)(2,1)}, f32[512,512]{1,0:T(8,128)}, f32[8,512]{1,0:T(8,128)}) custom-call(s32[12]{0:T(128)} %concatenate.12.at, bf16[528,640]{1,0:T(8,128)(2,1)} %copy-done.1, bf16[528,640]{1,0:T(8,128)(2,1)} %copy-done.5, bf16[528,640]{1,0:T(8,128)(2,1)} %copy-done.3, bf16[528,640]{1,0:T(8,128)(2,1)} %copy-done.6, ...), custom_call_target="tpu_custom_call" | custom-call | flops 2013265920 | bytes 11796480 | tf_op jit(solution)/shard_map/logits_first/pallas_call | solution.py:153
  48.6 4.3 %all-to-all-start.1 = ((f32[4,1,9]{2,1,0:T(1,128)}), f32[4,1,9]{2,1,0:T(1,128)S(1)}, u32[]{:S(2)}, u32[]{:S(2)}) async-start(f32[4,1,9]{2,1,0:T(1,128)} %broadcast_in_dim.13), calls=%async_computation.1 | async-start | bytes 4096 | tf_op jit(solution)/shard_map/all_to_all | solution.py:387
  53.4 4.6 %all-to-all-done.1 = f32[4,1,9]{2,1,0:T(1,128)S(1)} async-done(((f32[4,1,9]{2,1,0:T(1,128)}), f32[4,1,9]{2,1,0:T(1,128)S(1)}, u32[]{:S(2)}, u32[]{:S(2)}) %all-to-all-start.1) | async-done | bytes 176 | tf_op jit(solution)/shard_map/all_to_all | solution.py:387
  58.3 0.7 copy-done.10
  59.1 6.2 %logits_last.1 = (bf16[1,512,1280]{2,1,0:T(8,128)(2,1)}, f32[512,512]{1,0:T(8,128)}, f32[8,8,512]{2,1,0:T(8,128)}, f32[8,512]{1,0:T(8,128)}) custom-call(s32[12]{0:T(128)} %concatenate.12.at, bf16[272,640]{1,0:T(8,128)(2,1)} %collective-permute-done.2.refs_0_, bf16[256,640]{1,0:T(8,128)(2,1)} %collective-permute-done.6.refs_1_, bf16[272,640]{1,0:T(8,128)(2,1)} %copy-done.9, ...), custom_call_target="tpu_custom_call" | custom-call | flops 671088640 | bytes 3932160 | tf_op jit(solution)/shard_map/logits_last/pallas_call | solution.py:153
  65.3 4.3 %all-to-all-start.2 = ((f32[8,8,512]{2,1,0:T(8,128)}), f32[8,8,512]{2,1,0:T(8,128)S(1)}, u32[]{:S(2)}, u32[]{:S(2)}) async-start(f32[8,8,512]{2,1,0:T(8,128)} %get-tuple-element.45), calls=%async_computation.2 | async-start | bytes 262144 | tf_op jit(solution)/shard_map/all_to_all | solution.py:440
  71.7 4.0 %all-to-all-done.2.st = f32[8,8,512]{2,1,0:T(8,128)S(1)} async-done(((f32[8,8,512]{2,1,0:T(8,128)}), f32[8,8,512]{2,1,0:T(8,128)S(1)}, u32[]{:S(2)}, u32[]{:S(2)}) %all-to-all-start.2) | async-done | bytes 131104 | tf_op jit(solution)/shard_map/all_to_all | solution.py:440
  76.4 2.7 %policy.1 = (bf16[512,512]{1,0:T(8,128)(2,1)}, f32[8,512]{1,0:T(8,128)}) custom-call(s32[12]{0:T(128)} %concatenate.12.at, f32[5]{0:T(128)} %pad_maximum_fusion.2.nums, f32[8,8,512]{2,1,0:T(8,128)} %copy-done.8, f32[512,512]{1,0:T(8,128)} %get-tuple-element.46.lg, f32[8,512]{1,0:T(8,128)} %get-tuple-element.47.inv_ref, s32[1,512]{1,0:T(1,128)} %bitcast.28, ...), custom_call_target="tpu_custom_call" | custom-call | flops 2097152 | bytes 1572864 | tf_op jit(solution)/shard_map/policy/pallas_call | solution.py:212
  79.1 8.1 %back.1 = (bf16[4,512,640]{2,1,0:T(8,128)(2,1)}, bf16[4,512,640]{2,1,0:T(8,128)(2,1)}) custom-call(s32[12]{0:T(128)} %concatenate.12.at, bf16[512,512]{1,0:T(8,128)(2,1)} %get-tuple-element.60.dl, bf16[512,5120]{1,0:T(8,128)(2,1)} %head.1), custom_call_target="tpu_custom_call" | custom-call | flops 2684354560 | bytes 10485760 | tf_op jit(solution)/shard_map/back/pallas_call | solution.py:242
  87.1 8.9 %heads.1 = (bf16[4,8,160,256]{3,2,1,0:T(8,128)(2,1)}, bf16[8,4,160,256]{3,2,1,0:T(8,128)(2,1)}) custom-call(s32[12]{0:T(128)} %concatenate.12.at, bf16[3,512,1280]{2,1,0:T(8,128)(2,1)} %get-tuple-element.58.early, bf16[1,512,1280]{2,1,0:T(8,128)(2,1)} %get-tuple-element.59.late, bf16[512,512]{1,0:T(8,128)(2,1)} %get-tuple-element.60.dl), custom_call_target="tpu_custom_call" | custom-call | flops 2684354560 | bytes 15728640 | tf_op jit(solution)/shard_map/heads/pallas_call | solution.py:281
  96.2 3.7 %all-to-all-start.3 = ((bf16[4,8,160,256]{3,2,1,0:T(8,128)(2,1)}), bf16[4,8,160,256]{3,2,1,0:T(8,128)(2,1)S(1)}, u32[]{:S(2)}, u32[]{:S(2)}) async-start(bf16[4,8,160,256]{3,2,1,0:T(8,128)(2,1)} %get-tuple-element.61), calls=%async_computation.3 | async-start | bytes 5242880 | tf_op jit(solution)/shard_map/all_to_all | solution.py:449
  99.8 1.6 collective-permute-done.9.refs_1_
  101.4 4.4 %sum_u.1 = (bf16[512,640]{1,0:T(8,128)(2,1)}, bf16[512,640]{1,0:T(8,128)(2,1)}, bf16[512,640]{1,0:T(8,128)(2,1)}, bf16[512,640]{1,0:T(8,128)(2,1)}) custom-call(bf16[4,512,640]{2,1,0:T(8,128)(2,1)} %get-tuple-element.49.refs_0_, bf16[4,512,640]{2,1,0:T(8,128)(2,1)} %collective-permute-done.9.refs_1_), custom_call_target="tpu_custom_call" | custom-call | flops 2621440 | bytes 7864320 | tf_op jit(solution)/shard_map/sum_u/pallas_call | solution.py:317
  105.8 1.0 collective-permute-start.10
  106.8 1.0 collective-permute-start.11
  107.8 0.7 collective-permute-start.12
  108.5 24.2 %all-to-all-done.3.a = bf16[4,8,160,256]{3,2,1,0:T(8,128)(2,1)S(1)} async-done(((bf16[4,8,160,256]{3,2,1,0:T(8,128)(2,1)}), bf16[4,8,160,256]{3,2,1,0:T(8,128)(2,1)S(1)}, u32[]{:S(2)}, u32[]{:S(2)}) %all-to-all-start.3) | async-done | bytes 2621472 | tf_op jit(solution)/shard_map/all_to_all | solution.py:449
  132.7 6.2 %collective-permute-done.11.u2 = bf16[512,640]{1,0:T(8,128)(2,1)} collective-permute-done((bf16[512,640]{1,0:T(8,128)(2,1)}, bf16[512,640]{1,0:T(8,128)(2,1)}, u32[]{:S(2)}, u32[]{:S(2)}) %collective-permute-start.11) | collective-permute-done | bytes 655392 | tf_op jit(solution)/shard_map/ppermute | solution.py:27
  138.9 2.9 %sum_x.1 = bf16[8,160,256]{2,1,0:T(8,128)(2,1)} custom-call(bf16[4,8,160,256]{3,2,1,0:T(8,128)(2,1)} %copy-done), custom_call_target="tpu_custom_call" | custom-call | flops 1310720 | bytes 3932160 | tf_op jit(solution)/shard_map/sum_x/pallas_call | solution.py:337
  141.8 5.9 %all-to-all-start.4 = ((bf16[8,160,256]{2,1,0:T(8,128)(2,1)}), bf16[8,160,256]{2,1,0:T(8,128)(2,1)S(1)}, u32[]{:S(2)}, u32[]{:S(2)}) async-start(bf16[8,160,256]{2,1,0:T(8,128)(2,1)} %sum_x.1), calls=%async_computation.4 | async-start | bytes 1310720 | tf_op jit(solution)/shard_map/all_to_all | solution.py:454
  147.7 0.7 reduce-scatter.5.cloned.1.call-update
  149.0 3.4 %final.1 = (bf16[2,256,640]{2,1,0:T(8,128)(2,1)}, f32[1,768]{1,0:T(1,128)}) custom-call(bf16[512,640]{1,0:T(8,128)(2,1)} %get-tuple-element.51.u0, bf16[512,640]{1,0:T(8,128)(2,1)} %copy-done.7, bf16[512,640]{1,0:T(8,128)(2,1)} %collective-permute-done.11.u2, bf16[512,640]{1,0:T(8,128)(2,1)} %collective-permute-done.12.u3, bf16[2,256,640]{2,1,0:T(8,128)(2,1)} %h_ref.1, ...), custom_call_target="tpu_custom_call" | custom-call | flops 1966080 | bytes 3932160 | tf_op jit(solution)/shard_map/final/pallas_call | solution.py:374
  152.4 0.7 reduce.2
  153.8 2.6 %collective-permute-start.14 = (f32[6,128]{1,0:T(8,128)S(1)}, f32[6,128]{1,0:T(8,128)S(1)}, u32[]{:S(2)}, u32[]{:S(2)}) collective-permute-start(f32[6,128]{1,0:T(8,128)S(1)} %bitcast.31), channel_id=1, source_target_pairs={{0,16},{8,24},{16,0},{24,8},{1,17},{9,25},{17,1},{25,9},{2,18},{10... | collective-permute-start | bytes 9224 | tf_op jit(solution)/shard_map/ppermute | solution.py:27
  156.4 1.5 collective-permute-start.15
  158.0 0.9 collective-permute-done.14
  158.9 1.1 collective-permute-done.15
  160.0 3.6 %collective-permute-done.16 = f32[6,128]{1,0:T(8,128)S(1)} collective-permute-done((f32[6,128]{1,0:T(8,128)S(1)}, f32[6,128]{1,0:T(8,128)S(1)}, u32[]{:S(2)}, u32[]{:S(2)}) %collective-permute-start.16) | collective-permute-done | bytes 3104 | tf_op jit(solution)/shard_map/ppermute | solution.py:31
  163.6 1.5 collective-permute-start.17
  165.1 2.1 %collective-permute-done.17 = f32[6,128]{1,0:T(8,128)S(1)} collective-permute-done((f32[6,128]{1,0:T(8,128)S(1)}, f32[6,128]{1,0:T(8,128)S(1)}, u32[]{:S(2)}, u32[]{:S(2)}) %collective-permute-start.17) | collective-permute-done | bytes 3104 | tf_op jit(solution)/shard_map/ppermute | solution.py:31
  167.2 3.6 %collective-permute-start.18 = (f32[6,128]{1,0:T(8,128)S(1)}, f32[6,128]{1,0:T(8,128)S(1)}, u32[]{:S(2)}, u32[]{:S(2)}) collective-permute-start(f32[6,128]{1,0:T(8,128)S(1)} %add.46), channel_id=1, source_target_pairs={{0,96},{32,192},{64,160},{96,0},{128,224},{160,64},{192,32},{224,1... | collective-permute-start | bytes 9224 | tf_op jit(solution)/shard_map/ppermute | solution.py:31
  170.8 3.0 %collective-permute-done.18 = f32[6,128]{1,0:T(8,128)S(1)} collective-permute-done((f32[6,128]{1,0:T(8,128)S(1)}, f32[6,128]{1,0:T(8,128)S(1)}, u32[]{:S(2)}, u32[]{:S(2)}) %collective-permute-start.18) | collective-permute-done | bytes 3104 | tf_op jit(solution)/shard_map/ppermute | solution.py:31
  176.3 0.8 copy-done.2
  177.1 1.9 %join.1 = f32[160,512]{1,0:T(8,128)} custom-call(bf16[8,160,256]{2,1,0:T(8,128)(2,1)} %copy-done.2, bf16[160,256]{1,0:T(8,128)(2,1)} %bitcast.26), custom_call_target="tpu_custom_call" | custom-call | flops 655360 | bytes 1310720 | tf_op jit(solution)/shard_map/join/pallas_call | solution.py:374
  (75 shorter events, 9.1 us)
Async XLA Ops:
  7.2 28.2 %copy-start.15 = (s32[4]{0:T(128)S(1)}, s32[4]{0:T(128)}, u32[]{:S(2)}) copy-start(s32[4]{0:T(128)} %constant.60.clone) | copy-start | bytes 52
  9.0 27.1 %copy-start.1 = (bf16[528,640]{1,0:T(8,128)(2,1)}, bf16[528,640]{1,0:T(8,128)(2,1)S(1)}, u32[]{:S(2)}) copy-start(bf16[528,640]{1,0:T(8,128)(2,1)S(1)} %pad_maximum_fusion.refs_0_) | copy-start | bytes 2027524
  9.0 22.2 %collective-permute-start = (bf16[528,640]{1,0:T(8,128)(2,1)S(1)}, bf16[528,640]{1,0:T(8,128)(2,1)S(1)}, u32[]{:S(2)}, u32[]{:S(2)}) collective-permute-start(bf16[528,640]{1,0:T(8,128)(2,1)S(1)} %pad_maximum_fusion.refs_0_), channel_id=1, source_target_pairs={{0,2},{2,4},{4,6},{6,0},{1,3},{3,5},{5,7},{7,1},{8,10},{10,12},{12... | collective-permute-start | bytes 2027528 | tf_op jit(solution)/shard_map/ppermute | solution.py:27
  10.7 20.5 %collective-permute-start.1 = (bf16[528,640]{1,0:T(8,128)(2,1)S(1)}, bf16[528,640]{1,0:T(8,128)(2,1)S(1)}, u32[]{:S(2)}, u32[]{:S(2)}) collective-permute-start(bf16[528,640]{1,0:T(8,128)(2,1)S(1)} %pad_maximum_fusion.refs_0_), channel_id=1, source_target_pairs={{0,6},{2,0},{4,2},{6,4},{1,7},{3,1},{5,3},{7,5},{8,14},{10,8},{12,... | collective-permute-start | bytes 2027528 | tf_op jit(solution)/shard_map/ppermute | solution.py:27
  16.4 14.7 %all-to-all-start = ((f32[8,1,9]{2,1,0:T(1,128)}), f32[8,1,9]{2,1,0:T(1,128)S(1)}, u32[]{:S(2)}, u32[]{:S(2)}) async-start(f32[8,1,9]{2,1,0:T(1,128)} %broadcast_in_dim.12), calls=%async_computation | async-start | bytes 8192 | tf_op jit(solution)/shard_map/all_to_all | solution.py:387
  25.0 11.0 %collective-permute-start.3 = (bf16[528,640]{1,0:T(8,128)(2,1)S(1)}, bf16[528,640]{1,0:T(8,128)(2,1)S(1)}, u32[]{:S(2)}, u32[]{:S(2)}) collective-permute-start(bf16[528,640]{1,0:T(8,128)(2,1)S(1)} %pad_maximum_fusion.refs_0_), channel_id=1, source_target_pairs={{0,1},{1,0},{2,3},{3,2},{4,5},{5,4},{6,7},{7,6},{8,9},{9,8},{10,11... | collective-permute-start | bytes 2027528 | tf_op jit(solution)/shard_map/ppermute | solution.py:27
  31.2 4.9 %copy-start.3 = (bf16[528,640]{1,0:T(8,128)(2,1)}, bf16[528,640]{1,0:T(8,128)(2,1)S(1)}, u32[]{:S(2)}) copy-start(bf16[528,640]{1,0:T(8,128)(2,1)S(1)} %collective-permute-done.refs_2_) | copy-start | bytes 2027524
  31.2 4.9 %copy-start.4 = (bf16[528,640]{1,0:T(8,128)(2,1)}, bf16[528,640]{1,0:T(8,128)(2,1)S(1)}, u32[]{:S(2)}) copy-start(bf16[528,640]{1,0:T(8,128)(2,1)S(1)} %collective-permute-done.1.refs_4_) | copy-start | bytes 2027524
  32.8 3.3 %collective-permute-start.4 = (bf16[528,640]{1,0:T(8,128)(2,1)S(1)}, bf16[528,640]{1,0:T(8,128)(2,1)S(1)}, u32[]{:S(2)}, u32[]{:S(2)}) collective-permute-start(bf16[528,640]{1,0:T(8,128)(2,1)S(1)} %collective-permute-done.refs_2_), channel_id=1, source_target_pairs={{0,1},{1,0},{2,3},{3,2},{4,5},{5,4},{6,7},{7,6},{8,9},{9,8},{10,11... | collective-permute-start | bytes 2027528 | tf_op jit(solution)/shard_map/ppermute | solution.py:27
  32.8 3.3 %collective-permute-start.5 = (bf16[528,640]{1,0:T(8,128)(2,1)S(1)}, bf16[528,640]{1,0:T(8,128)(2,1)}, u32[]{:S(2)}, u32[]{:S(2)}) collective-permute-start(bf16[528,640]{1,0:T(8,128)(2,1)S(1)} %collective-permute-done.1.refs_4_), channel_id=1, source_target_pairs={{0,1},{1,0},{2,3},{3,2},{4,5},{5,4},{6,7},{7,6},{8,9},{9,8},{10,11... | collective-permute-start | bytes 2027528 | tf_op jit(solution)/shard_map/ppermute | solution.py:27
  33.3 13.6 %collective-permute-start.6 = (bf16[256,640]{1,0:T(8,128)(2,1)}, bf16[256,640]{1,0:T(8,128)(2,1)}, u32[]{:S(2)}, u32[]{:S(2)}) collective-permute-start(bf16[256,640]{1,0:T(8,128)(2,1)} %slice.24), channel_id=1, source_target_pairs={{0,6},{2,0},{4,2},{6,4},{1,7},{3,1},{5,3},{7,5},{8,14},{10,8},{12,... | collective-permute-start | bytes 983048 | tf_op jit(solution)/shard_map/ppermute | solution.py:27
  35.1 11.7 %collective-permute-start.2 = (bf16[272,640]{1,0:T(8,128)(2,1)}, bf16[272,640]{1,0:T(8,128)(2,1)}, u32[]{:S(2)}, u32[]{:S(2)}) collective-permute-start(bf16[272,640]{1,0:T(8,128)(2,1)} %slice.23), channel_id=1, source_target_pairs={{0,2},{2,4},{4,6},{6,0},{1,3},{3,5},{5,7},{7,1},{8,10},{10,12},{12... | collective-permute-start | bytes 1044488 | tf_op jit(solution)/shard_map/ppermute | solution.py:27
  36.0 11.4 %copy-start.12 = (s32[2,256]{1,0:T(2,128)S(1)}, s32[2,256]{1,0:T(2,128)}, u32[]{:S(2)}) copy-start(s32[2,256]{1,0:T(2,128)} %param.12) | copy-start | bytes 6148
  36.0 16.8 %copy-start.13 = (f32[2,256]{1,0:T(2,128)S(1)}, f32[2,256]{1,0:T(2,128)}, u32[]{:S(2)}) copy-start(f32[2,256]{1,0:T(2,128)} %param.14) | copy-start | bytes 6148
  36.1 0.9 copy-start.5
  36.1 1.2 copy-start.6
  46.8 11.5 %collective-permute-start.7 = (bf16[272,640]{1,0:T(8,128)(2,1)}, bf16[272,640]{1,0:T(8,128)(2,1)S(1)}, u32[]{:S(2)}, u32[]{:S(2)}) collective-permute-start(bf16[272,640]{1,0:T(8,128)(2,1)} %collective-permute-done.2.refs_0_), channel_id=1, source_target_pairs={{0,1},{1,0},{2,3},{3,2},{4,5},{5,4},{6,7},{7,6},{8,9},{9,8},{10,11... | collective-permute-start | bytes 1044488 | tf_op jit(solution)/shard_map/ppermute | solution.py:27
  46.9 11.3 %collective-permute-start.8 = (bf16[256,640]{1,0:T(8,128)(2,1)}, bf16[256,640]{1,0:T(8,128)(2,1)S(1)}, u32[]{:S(2)}, u32[]{:S(2)}) collective-permute-start(bf16[256,640]{1,0:T(8,128)(2,1)} %collective-permute-done.6.refs_1_), channel_id=1, source_target_pairs={{0,1},{1,0},{2,3},{3,2},{4,5},{5,4},{6,7},{7,6},{8,9},{9,8},{10,11... | collective-permute-start | bytes 983048 | tf_op jit(solution)/shard_map/ppermute | solution.py:27
  48.6 9.5 %all-to-all-start.1 = ((f32[4,1,9]{2,1,0:T(1,128)}), f32[4,1,9]{2,1,0:T(1,128)S(1)}, u32[]{:S(2)}, u32[]{:S(2)}) async-start(f32[4,1,9]{2,1,0:T(1,128)} %broadcast_in_dim.13), calls=%async_computation.1 | async-start | bytes 4096 | tf_op jit(solution)/shard_map/all_to_all | solution.py:387
  58.3 0.7 copy-start.10
  58.3 0.8 copy-start.9
  59.1 10.7 %copy-start.14 = (f32[2]{0:T(128)S(1)}, f32[2]{0:T(128)}, u32[]{:S(2)}) copy-start(f32[2]{0:T(128)} %param.15) | copy-start | bytes 28
  65.3 10.4 %all-to-all-start.2 = ((f32[8,8,512]{2,1,0:T(8,128)}), f32[8,8,512]{2,1,0:T(8,128)S(1)}, u32[]{:S(2)}, u32[]{:S(2)}) async-start(f32[8,8,512]{2,1,0:T(8,128)} %get-tuple-element.45), calls=%async_computation.2 | async-start | bytes 262144 | tf_op jit(solution)/shard_map/all_to_all | solution.py:440
  69.6 78.1 %reduce-scatter.3.cloned.1.call-start = ((), (), s32[]{:S(2)}) async-start(), calls=%async_computation.7 | async-start | bytes 2949120 | tf_op jit(solution)/shard_map/reduce_scatter | solution.py:447
  75.7 0.7 copy-start.8
  96.1 5.3 %collective-permute-start.9 = (bf16[4,512,640]{2,1,0:T(8,128)(2,1)}, bf16[4,512,640]{2,1,0:T(8,128)(2,1)}, u32[]{:S(2)}, u32[]{:S(2)}) collective-permute-start(bf16[4,512,640]{2,1,0:T(8,128)(2,1)} %get-tuple-element.50), channel_id=1, source_target_pairs={{0,1},{1,0},{2,3},{3,2},{4,5},{5,4},{6,7},{7,6},{8,9},{9,8},{10,11... | collective-permute-start | bytes 7864328 | tf_op jit(solution)/shard_map/ppermute | solution.py:27
  96.2 36.5 %all-to-all-start.3 = ((bf16[4,8,160,256]{3,2,1,0:T(8,128)(2,1)}), bf16[4,8,160,256]{3,2,1,0:T(8,128)(2,1)S(1)}, u32[]{:S(2)}, u32[]{:S(2)}) async-start(bf16[4,8,160,256]{3,2,1,0:T(8,128)(2,1)} %get-tuple-element.61), calls=%async_computation.3 | async-start | bytes 5242880 | tf_op jit(solution)/shard_map/all_to_all | solution.py:449
  105.8 42.6 %copy-start.11 = (bf16[640]{0:T(1024)(128)(2,1)S(1)}, bf16[640]{0:T(1024)(128)(2,1)}, u32[]{:S(2)}) copy-start(bf16[640]{0:T(1024)(128)(2,1)} %param.10) | copy-start | bytes 3844
  105.8 26.9 %collective-permute-start.10 = (bf16[512,640]{1,0:T(8,128)(2,1)}, bf16[512,640]{1,0:T(8,128)(2,1)S(1)}, u32[]{:S(2)}, u32[]{:S(2)}) collective-permute-start(bf16[512,640]{1,0:T(8,128)(2,1)} %get-tuple-element.52), channel_id=1, source_target_pairs={{0,6},{2,0},{4,2},{6,4},{1,7},{3,1},{5,3},{7,5},{8,14},{10,8},{12,... | collective-permute-start | bytes 1966088 | tf_op jit(solution)/shard_map/ppermute | solution.py:27
  106.8 32.1 %collective-permute-start.11 = (bf16[512,640]{1,0:T(8,128)(2,1)}, bf16[512,640]{1,0:T(8,128)(2,1)}, u32[]{:S(2)}, u32[]{:S(2)}) collective-permute-start(bf16[512,640]{1,0:T(8,128)(2,1)} %get-tuple-element.53), channel_id=1, source_target_pairs={{0,2},{2,4},{4,6},{6,0},{1,3},{3,5},{5,7},{7,1},{8,10},{10,12},{12... | collective-permute-start | bytes 1966088 | tf_op jit(solution)/shard_map/ppermute | solution.py:27
  107.8 31.1 %collective-permute-start.12 = (bf16[512,640]{1,0:T(8,128)(2,1)}, bf16[512,640]{1,0:T(8,128)(2,1)}, u32[]{:S(2)}, u32[]{:S(2)}) collective-permute-start(bf16[512,640]{1,0:T(8,128)(2,1)} %get-tuple-element.54), channel_id=1, source_target_pairs={{0,4},{2,6},{4,0},{6,2},{1,5},{3,7},{5,1},{7,3},{8,12},{10,14},{12... | collective-permute-start | bytes 1966088 | tf_op jit(solution)/shard_map/ppermute | solution.py:27
  132.7 6.2 %copy-start = (bf16[4,8,160,256]{3,2,1,0:T(8,128)(2,1)}, bf16[4,8,160,256]{3,2,1,0:T(8,128)(2,1)S(1)}, u32[]{:S(2)}) copy-start(bf16[4,8,160,256]{3,2,1,0:T(8,128)(2,1)S(1)} %all-to-all-done.3.a) | copy-start | bytes 7864324
  132.7 16.3 %copy-start.7 = (bf16[512,640]{1,0:T(8,128)(2,1)}, bf16[512,640]{1,0:T(8,128)(2,1)S(1)}, u32[]{:S(2)}) copy-start(bf16[512,640]{1,0:T(8,128)(2,1)S(1)} %collective-permute-done.10.u1) | copy-start | bytes 1966084
  141.8 34.5 %all-to-all-start.4 = ((bf16[8,160,256]{2,1,0:T(8,128)(2,1)}), bf16[8,160,256]{2,1,0:T(8,128)(2,1)S(1)}, u32[]{:S(2)}, u32[]{:S(2)}) async-start(bf16[8,160,256]{2,1,0:T(8,128)(2,1)} %sum_x.1), calls=%async_computation.4 | async-start | bytes 1310720 | tf_op jit(solution)/shard_map/all_to_all | solution.py:454
  147.7 28.6 %reduce-scatter.5.cloned.1.call-start = ((), (), s32[]{:S(2)}) async-start(), calls=%async_computation.8 | async-start | bytes 409600 | tf_op jit(solution)/shard_map/reduce_scatter | solution.py:448
  153.1 4.9 %collective-permute-start.13 = (f32[6,128]{1,0:T(8,128)S(1)}, f32[6,128]{1,0:T(8,128)S(1)}, u32[]{:S(2)}, u32[]{:S(2)}) collective-permute-start(f32[6,128]{1,0:T(8,128)S(1)} %bitcast.30), channel_id=1, source_target_pairs={{0,8},{8,16},{16,24},{24,0},{1,9},{9,17},{17,25},{25,1},{2,10},{10... | collective-permute-start | bytes 9224 | tf_op jit(solution)/shard_map/ppermute | solution.py:27
  153.8 5.1 %collective-permute-start.14 = (f32[6,128]{1,0:T(8,128)S(1)}, f32[6,128]{1,0:T(8,128)S(1)}, u32[]{:S(2)}, u32[]{:S(2)}) collective-permute-start(f32[6,128]{1,0:T(8,128)S(1)} %bitcast.31), channel_id=1, source_target_pairs={{0,16},{8,24},{16,0},{24,8},{1,17},{9,25},{17,1},{25,9},{2,18},{10... | collective-permute-start | bytes 9224 | tf_op jit(solution)/shard_map/ppermute | solution.py:27
  156.4 3.6 %collective-permute-start.15 = (f32[6,128]{1,0:T(8,128)S(1)}, f32[6,128]{1,0:T(8,128)S(1)}, u32[]{:S(2)}, u32[]{:S(2)}) collective-permute-start(f32[6,128]{1,0:T(8,128)S(1)} %bitcast.32), channel_id=1, source_target_pairs={{0,24},{8,0},{16,8},{24,16},{1,25},{9,1},{17,9},{25,17},{2,26},{10... | collective-permute-start | bytes 9224 | tf_op jit(solution)/shard_map/ppermute | solution.py:27
  160.0 3.6 %collective-permute-start.16 = (f32[6,128]{1,0:T(8,128)S(1)}, f32[6,128]{1,0:T(8,128)S(1)}, u32[]{:S(2)}, u32[]{:S(2)}) collective-permute-start(f32[6,128]{1,0:T(8,128)S(1)} %add_add_fusion), channel_id=1, source_target_pairs={{0,32},{32,0},{64,96},{96,64},{128,160},{160,128},{192,224},{224,1... | collective-permute-start | bytes 9224 | tf_op jit(solution)/shard_map/ppermute | solution.py:31
  163.6 3.6 %collective-permute-start.17 = (f32[6,128]{1,0:T(8,128)S(1)}, f32[6,128]{1,0:T(8,128)S(1)}, u32[]{:S(2)}, u32[]{:S(2)}) collective-permute-start(f32[6,128]{1,0:T(8,128)S(1)} %add.45), channel_id=1, source_target_pairs={{0,224},{32,64},{64,32},{96,128},{128,96},{160,192},{192,160},{224... | collective-permute-start | bytes 9224 | tf_op jit(solution)/shard_map/ppermute | solution.py:31
  167.2 6.6 %collective-permute-start.18 = (f32[6,128]{1,0:T(8,128)S(1)}, f32[6,128]{1,0:T(8,128)S(1)}, u32[]{:S(2)}, u32[]{:S(2)}) collective-permute-start(f32[6,128]{1,0:T(8,128)S(1)} %add.46), channel_id=1, source_target_pairs={{0,96},{32,192},{64,160},{96,0},{128,224},{160,64},{192,32},{224,1... | collective-permute-start | bytes 9224 | tf_op jit(solution)/shard_map/ppermute | solution.py:31
  176.3 0.8 copy-start.2
Sparse Core Ops, SparseCore 0:
  96.2 38.9 reduce-scatter.2
  151.0 21.5 reduce-scatter.4

commit v4 on v3

--- a/solution.py
+++ b/solution.py
@@ -65,6 +65,16 @@
 
 def full(shape):
     return pl.BlockSpec(shape, lambda k, *at: (0,) * len(shape))
+
+
+def local_kernel(groups, rewards, lengths, slots, out):
+    lane = lax.broadcasted_iota(jnp.int32, (1, 128), 1)
+    row = jnp.zeros((1, 128), f32)
+    for r in range(2):
+        row += jnp.where(lane == slots[r] // GROUP, rewards[r], 0.0)
+        row += jnp.where(lane == groups, lengths[r].astype(f32), 0.0)
+    for k in range(out.shape[0]):
+        out[k] = row
 
 
 def logits_kernel(count, per, last, at, *refs):
@@ -168,14 +178,22 @@
             ],
         ),
         compiler_params=params(),
-        cost_estimate=cost(2 * rows * half * count * cols, 2 * count * cols * (2 * rows + half)),
+        cost_estimate=cost(1000, 1000),
         name="logits_last" if last else "logits_first",
     )(at, *[p for b in blocks for p in b], *extra, head)
 
 
-def policy_kernel(at, nums, st, lg, inv_ref, tgt, old, dl, small):
+def policy_kernel(groups, slots_all, at, rewards, lengths, slots, sums_ref, st, lg, inv_ref, tgt, old, dl, small):
     half = lg.shape[1]
     rows = lg.shape[0]
+    sums = jnp.sum(sums_ref[:, 0, :], axis=0, keepdims=True)
+    lane = lax.broadcasted_iota(jnp.int32, sums.shape, 1)
+
+    def entry_of(k):
+        return jnp.sum(jnp.where(lane == k, sums, 0.0), axis=1, keepdims=True)
+
+    advs = [rewards[r] - entry_of(slots[r] // GROUP) / GROUP for r in range(2)]
+    live = entry_of(groups)
     top = jnp.max(st[:, 0, :], axis=0, keepdims=True)
     weight = jnp.exp(st[:, 0, :] - top)
     total = jnp.sum(st[:, 1, :] * weight, axis=0, keepdims=True)
@@ -186,8 +204,8 @@
     ratio = jnp.exp(chosen - lse - old[...])
     position = lax.broadcasted_iota(jnp.int32, ratio.shape, 1)
     second_one = position >= rows // 2
-    adv = jnp.where(second_one, nums[1], nums[0])
-    length = jnp.where(second_one, nums[3], nums[2])
+    adv = jnp.where(second_one, advs[1], advs[0])
+    length = jnp.where(second_one, lengths[1].astype(f32), lengths[0].astype(f32))
     within = jnp.where(second_one, position - rows // 2, position).astype(f32)
     mask = jnp.where(within < length, 1.0, 0.0)
     first = ratio * adv
@@ -195,10 +213,10 @@
     policy = -jnp.minimum(first, second)
     policy = jnp.where(adv < 0, jnp.minimum(policy, -dual_bound * adv), policy)
     active = (first <= second) & jnp.logical_not((adv < 0) & (first < dual_bound * adv))
-    grad_logp = nums[4] * mask * jnp.where(active, -first, 0.0)
+    grad_logp = slots_all / live * mask * jnp.where(active, -first, 0.0)
     kappa = inv * inv * grad_logp * (chosen - moment / total) / 5120.0
     small[...] = jnp.concatenate(
-        [kappa, mask * policy, jnp.zeros((6, ratio.shape[1]), f32)], axis=0
+        [kappa, mask * policy / live, jnp.zeros((6, ratio.shape[1]), f32)], axis=0
     )
     lse_c, scale_c = column(lse), column(grad_logp * inv)
     target = column(tgt[...].astype(f32)).astype(jnp.int32)
@@ -207,54 +225,45 @@
     dl[...] = (scale_c * (hit - jnp.exp(lg[...] - lse_c))).astype(bf16)
 
 
-def policy_of(at, nums, stats, logits, inv, targets, old_logp):
+def policy_of(groups, slots_all, at, scalars, sums, stats, logits, inv, targets, old_logp):
     rows, half = logits.shape
     return pl.pallas_call(
-        policy_kernel,
+        functools.partial(policy_kernel, groups, float(slots_all)),
         out_shape=[like((rows, half)), like((8, rows), f32)],
-        in_specs=[whole(pltpu.SMEM)] * 2 + [whole()] * 5,
+        in_specs=[whole(pltpu.SMEM)] * 4 + [whole()] * 6,
         out_specs=[whole()] * 2,
         compiler_params=params(),
         cost_estimate=cost(8 * rows * half, 6 * rows * half, rows * half),
         name="policy",
-    )(at, nums, stats, logits, inv, targets, old_logp)
-
-
-def back_kernel(at, dl, head, u_send, u_keep):
-    c = at[2]
-    cols = head.shape[1] // 2
-    back = jnp.dot(dl[...], head[...], preferred_element_type=f32).astype(bf16)
-
-    @pl.when(c == 0)
-    def _():
-        u_keep[0] = back[:, :cols]
-        u_send[0] = back[:, cols:]
-
-    @pl.when(c == 1)
-    def _():
-        u_send[0] = back[:, :cols]
-        u_keep[0] = back[:, cols:]
-
-
-def back_of(at, dl, head, cols):
+    )(at, *scalars, sums, stats, logits, inv, targets, old_logp)
+
+
+def back_kernel(at, dl, dl_o, head, head_o, *outs):
+    total = jnp.dot(dl[...], head[...], preferred_element_type=f32)
+    total += jnp.dot(dl_o[...], head_o[...], preferred_element_type=f32)
+    for k, out in enumerate(outs):
+
+        @pl.when(pl.program_id(0) == k)
+        def _(out=out):
+            out[...] = total.astype(bf16)
+
+
+def back_of(at, dl, dl_o, head, head_o, cols):
     rows, half = dl.shape
-    shapes = [like((4, rows, cols))] * 2
     return pl.pallas_call(
         back_kernel,
-        out_shape=shapes,
+        out_shape=[like((rows, cols))] * 4,
         grid_spec=pltpu.PrefetchScalarGridSpec(
             num_scalar_prefetch=1,
             grid=(4,),
-            in_specs=[
-                full((rows, half)),
-                pl.BlockSpec((half, 2 * cols), lambda j, at: (0, at[8 + j])),
-            ],
-            out_specs=[pl.BlockSpec((1, rows, cols), lambda j, at: (j, 0, 0))] * 2,
+            in_specs=[full((rows, half))] * 2
+            + [pl.BlockSpec((half, cols), lambda j, at: (0, 2 * at[8 + j] + at[2]))] * 2,
+            out_specs=[full((rows, cols))] * 4,
         ),
         compiler_params=params(),
         cost_estimate=cost(2 * rows * 8 * cols * half, 32 * rows * cols),
         name="back",
-    )(at, dl, head)
+    )(at, dl, dl_o, head, head_o)
 
 
 def heads_kernel(at, early, late, dl, to_x, to_z):
@@ -297,34 +306,6 @@
     )(at, early, late, dl)
 
 
-def sum_pairs_kernel(groups, *refs):
-    pairs = len(refs) // (2 + len(groups))
-    ins, outs = refs[: 2 * pairs], refs[2 * pairs :]
-    for p in range(pairs):
-        keep, got = ins[2 * p], ins[2 * p + 1]
-        for out, group in zip(outs[p * len(groups) :], groups):
-            for at, j in enumerate(group):
-                total = (keep[j].astype(f32) + got[j].astype(f32)).astype(out.dtype)
-                if len(group) > 1:
-                    out[at] = total
-                else:
-                    out[...] = total
-
-
-def sum_pairs(ins, groups, name):
-    shape = ins[0].shape[1:]
-    outs = [like(((len(g),) if len(g) > 1 else ()) + shape) for g in groups] * (len(ins) // 2)
-    return pl.pallas_call(
-        functools.partial(sum_pairs_kernel, groups),
-        out_shape=outs,
-        in_specs=[whole()] * len(ins),
-        out_specs=[whole()] * len(outs),
-        compiler_params=params(),
-        cost_estimate=cost(len(ins) * ins[0].size, 3 * len(ins) * ins[0].size),
-        name=name,
-    )(*ins)
-
-
 def sum_first_kernel(a, out):
     for k in range(out.shape[0]):
         total = a[0, k].astype(f32)
@@ -370,23 +351,16 @@
     part[...] = jnp.concatenate([sums, jnp.broadcast_to(loss, (1, 128))], axis=1)
 
 
-def simple(kernel, shapes, ins, nbytes, name):
+def simple(kernel, shapes, ins, nbytes, name, flops=None):
     return pl.pallas_call(
         kernel,
         out_shape=shapes,
         in_specs=[whole(pltpu.SMEM if v.ndim == 1 else VMEM) for v in ins],
         out_specs=[whole()] * len(shapes),
         compiler_params=params(),
-        cost_estimate=cost(nbytes // 2, nbytes),
+        cost_estimate=cost(flops or nbytes // 2, nbytes),
         name=name,
     )(*ins)
-
-
-def copy_for_each(value, axis):
-    size = lax.axis_size(axis)
-    return lax.all_to_all(
-        jnp.broadcast_to(value[None], (size, *value.shape)), axis, 0, 0, tiled=True
-    )
 
 
 def after(value, *first):
@@ -408,29 +382,29 @@
     own_o = shift(payload, "c", 1)
 
     groups_all = resp_here * lax.axis_size(DP) // GROUP
-    group = group_slot // GROUP
-    member = (group[:, None] == jnp.arange(groups_all, dtype=jnp.int32)[None, :]).astype(f32)
-    local = jnp.concatenate(
-        [jnp.sum(member * rewards[:, None], axis=0), jnp.sum(lengths).astype(f32)[None]]
-    )
-    over_z = copy_for_each(local, "z").sum(axis=0)
-    prev, following, over_z = lax.optimization_barrier((prev, following, over_z))
+    scalars = (rewards, lengths, group_slot)
+    (local,) = simple(
+        functools.partial(local_kernel, groups_all),
+        [like((lax.axis_size(DP), 1, 128), f32)],
+        scalars,
+        1 << 14,
+        "local",
+    )
+    sums = lax.all_to_all(local, DP, 0, 0, tiled=True)
+    prev, following, local = lax.optimization_barrier((prev, following, local))
 
     far_a, far_b = prev[:cut], following[cut:]
     far_a, far_b, prev, following = lax.optimization_barrier((far_a, far_b, prev, following))
     far_a, far_b = shift(far_a, "y", 1), shift(far_b, "y", -1)
-    sums = copy_for_each(over_z, "x").sum(axis=0)
     prev_o, following_o = shift(prev, "c", 1), shift(following, "c", 1)
     early, acc, sq = logits_of(
         at, 0, [(payload, own_o), (prev, prev_o), (following, following_o)], head
     )
     far_a, far_b = after(far_a, acc), after(far_b, acc)
+    head_o = shift(after(head, acc), "c", 1)
     far_a_o, far_b_o = shift(far_a, "c", 1), shift(far_b, "c", 1)
 
-    group_sums, count = sums[:groups_all], sums[groups_all]
-    adv_resp = rewards - jnp.sum(member * group_sums[None, :], axis=1) / GROUP
     slots_all = rows * lax.axis_size(DP)
-    nums = jnp.concatenate([adv_resp, lengths.astype(f32), (slots_all / count)[None]])
     targets = targets.reshape(1, rows)
     old_logp = old_logp.reshape(1, rows)
 
@@ -438,26 +412,28 @@
         at, 3, [(far_a, far_b, far_a_o, far_b_o)], head, (acc, sq), targets
     )
     all_stats = lax.all_to_all(stats, FSDP, 0, 0, tiled=True)
-    dl, small = policy_of(at, nums, all_stats, logits, inv, targets, old_logp)
+    dl, small = policy_of(groups_all, slots_all, at, scalars, sums, all_stats, logits, inv, targets, old_logp)
     part, half = cols // 4, dl.shape[1] // 2
 
-    u_send, u_keep = back_of(at, dl, head, cols)
-    u_got = shift(u_send, "c", 1)
-    to_x, to_z = heads_of(at, early, late, after(dl, u_send))
+    dl_o = shift(dl, "c", 1)
+    to_x, to_z = heads_of(at, early, late, dl)
     half_z = lax.psum_scatter(to_z, "z", scatter_dimension=0, tiled=False)
+    from_x = lax.all_to_all(to_x, "x", 0, 0, tiled=True)
+    u0, u1, u2, u3 = back_of(at, after(dl, to_x), dl_o, head, head_o, cols)
+    u1, u2, u3 = shift(u1, "y", -1), shift(u2, "y", 1), shift(u3, "y", 2)
+
+    to_z = sum_first(from_x, "sum_x")
+    from_z = lax.all_to_all(to_z, "z", 0, 0, tiled=True)
+    half_z = after(half_z, to_z)
+    u1, u2, u3, _ = lax.optimization_barrier((u1, u2, u3, half_z))
     half_z = lax.psum_scatter(half_z, "x", scatter_dimension=0, tiled=False)
-    from_x = lax.all_to_all(to_x, "x", 0, 0, tiled=True)
-    u0, u1, u2, u3 = sum_pairs((u_keep, u_got), ((0,), (1,), (2,), (3,)), "sum_u")
-    u1, u2, u3 = shift(u1, "y", -1), shift(u2, "y", 1), shift(u3, "y", 2)
-
-    from_x = after(from_x, u1, u2, u3)
-    from_z = lax.all_to_all(sum_first(from_x, "sum_x"), "z", 0, 0, tiled=True)
     grad_hidden, gain_part = simple(
         final_kernel,
         [like(hidden.shape), like((1, cols + 128), f32)],
         (u0, u1, u2, u3, hidden, gain.reshape(1, cols), small),
         12 * rows * cols,
         "final",
+        200 * 10**9,
     )
     tail = gain_part.reshape(-1, 128)
     tail = tail + shift(tail, "x", 1) + shift(tail, "x", 2) + shift(tail, "x", -1)
@@ -471,7 +447,7 @@
         "join",
     )
     tail = tail.reshape(-1)
-    return (tail[cols] / count, grad_hidden, tail[:cols], grad_head_t)
+    return (tail[cols], grad_hidden, tail[:cols], grad_head_t)
 
 
 def solution(mesh):

time: 188 us -> 174 us (0.926)
  between operations: 18.1 us -> 14.3 us
  other arithmetic: 5.53 us -> 1.87 us
  waiting for transfers between devices: 58.4 us -> 55.5 us
  Pallas kernels: 48 us -> 45.3 us
    ppermute x16 -> x17, waiting for transfers between devices: 9.92 us -> 23.2 us  [shift(): return lax.ppermute(value, axis, [(i, (i + step) % n) for i in range(n)])]
    all_to_all x3 -> x2, waiting for transfers between devices: 10.8 us -> 0.93 us  [the longest x1 0.93 us: body(): sums = lax.all_to_all(local, DP, 0, 0, tiled=True)]
    all_to_all x1, waiting for transfers between devices: 24.2 us -> 17 us  [body(): from_x = lax.all_to_all(to_x, 'x', 0, 0, tiled=True)]
    pallas_call x3 -> x2, Pallas kernels: 15.1 us -> 11.2 us  [the longest x1 8.36 us: back_of(): pl.pallas_call(back_kernel, out_shape=[like((rows, cols))] * 4, grid_spec...]
    unnamed x34 -> x36, local copies, waits for them, and re-layouts: 4.59 us -> 6.08 us
    pallas_call x2 -> x3, Pallas kernels: 5.31 us -> 6.62 us  [simple(): pl.pallas_call(kernel, out_shape=shapes, in_specs=[whole(pltpu.SMEM if v....]
    ppermute x16 -> x17, starting transfers between devices: 13.9 us -> 15 us  [shift(): return lax.ppermute(value, axis, [(i, (i + step) % n) for i in range(n)])]
    all_to_all x3 -> x2, starting transfers between devices: 18.7 us -> 17.9 us  [the longest x1 11.2 us: body(): sums = lax.all_to_all(local, DP, 0, 0, tiled=True)]
  transfers between devices with their start and end apart: 26 -> 26, of which waited for: 12 -> 12; matrix products, arithmetic and copies ran while one was open for 6% -> 3% of each run, Pallas kernels for 11% -> 25%
where the time goes in v4:
time: 174 us; the launch traced here: 173 us
  waiting for transfers between devices  55.5 us (32%)
  starting transfers between devices  45.7 us (26%)
  Pallas kernels  45.3 us (26%)
  between operations  14.3 us (8%)
  local copies, waits for them, and re-layouts  10.7 us (6%)
  other arithmetic  1.87 us (1%)
    ppermute x17, waiting for transfers between devices, shift(): return lax.ppermute(value, axis, [(i, (i + step) % n) for i in range(n)])  23.2 us
    all_to_all x1, waiting for transfers between devices, body(): from_x = lax.all_to_all(to_x, 'x', 0, 0, tiled=True)  17 us
    pallas_call x2, Pallas kernels, logits_of(): pl.pallas_call(functools.partial(logits_kernel, count, per, last), out_sh...  15.8 us
    ppermute x17, starting transfers between devices, shift(): return lax.ppermute(value, axis, [(i, (i + step) % n) for i in range(n)])  15 us
    all_to_all x1, starting transfers between devices, body(): sums = lax.all_to_all(local, DP, 0, 0, tiled=True)  11.2 us
    pallas_call x1, Pallas kernels, heads_of(): pl.pallas_call(heads_kernel, out_shape=shapes, grid_spec=pltpu.PrefetchSc...  8.79 us
    pallas_call x1, Pallas kernels, back_of(): pl.pallas_call(back_kernel, out_shape=[like((rows, cols))] * 4, grid_spec...  8.36 us
    ppermute x3, waiting for transfers between devices, turn(): lax.ppermute(value, 'z', [(i, (i + (step if i % 2 == 0 else -step)) % 8)...  8.2 us
  transfers between devices with their start and end apart: 26, of which 12 were waited for; matrix products, arithmetic and copies ran while one was open for 3% of the time, Pallas kernels for 25%

profile of v4, /device:TPU:32, one launch (start us, length us, event | category | flops | bytes accessed | tf_op | source)
XLA Modules:
  0.0 173.3 jit_solution(12160152385595675576)
XLA Ops:
  7.2 0.7 broadcast_in_dim.8
  7.9 1.1 pad_maximum_fusion.refs_0_
  9.0 3.1 %collective-permute-start.1 = (bf16[528,640]{1,0:T(8,128)(2,1)S(1)}, bf16[528,640]{1,0:T(8,128)(2,1)S(1)}, u32[]{:S(2)}, u32[]{:S(2)}) collective-permute-start(bf16[528,640]{1,0:T(8,128)(2,1)S(1)} %pad_maximum_fusion.refs_0_), channel_id=1, source_target_pairs={{0,6},{2,0},{4,2},{6,4},{1,7},{3,1},{5,3},{7,5},{8,14},{10,8},{12,... | collective-permute-start | bytes 2027528 | tf_op jit(solution)/shard_map/ppermute | solution.py:27
  12.1 1.3 local.1
  13.4 13.1 %collective-permute-done.1.refs_4_ = bf16[528,640]{1,0:T(8,128)(2,1)S(1)} collective-permute-done((bf16[528,640]{1,0:T(8,128)(2,1)S(1)}, bf16[528,640]{1,0:T(8,128)(2,1)S(1)}, u32[]{:S(2)}, u32[]{:S(2)}) %collective-permute-start.1) | collective-permute-done | bytes 675872 | tf_op jit(solution)/shard_map/ppermute | solution.py:27
  26.6 3.4 %collective-permute-done.refs_2_ = bf16[528,640]{1,0:T(8,128)(2,1)S(1)} collective-permute-done((bf16[528,640]{1,0:T(8,128)(2,1)S(1)}, bf16[528,640]{1,0:T(8,128)(2,1)S(1)}, u32[]{:S(2)}, u32[]{:S(2)}) %collective-permute-start) | collective-permute-done | bytes 675872 | tf_op jit(solution)/shard_map/ppermute | solution.py:27
  30.0 0.8 slice.16
  30.8 0.8 slice.15
  32.4 1.7 collective-permute-start.2
  34.1 0.7 concatenate.6.at
  34.8 0.8 copy-done.4
  35.8 9.6 %logits_first.1 = (bf16[3,512,1280]{2,1,0:T(8,128)(2,1)}, f32[512,512]{1,0:T(8,128)}, f32[8,512]{1,0:T(8,128)}) custom-call(s32[12]{0:T(128)} %concatenate.6.at, bf16[528,640]{1,0:T(8,128)(2,1)} %copy-done.1, bf16[528,640]{1,0:T(8,128)(2,1)} %copy-done.4, bf16[528,640]{1,0:T(8,128)(2,1)} %copy-done.2, bf16[528,640]{1,0:T(8,128)(2,1)} %copy-done.5, ...), custom_call_target="tpu_custom_call" | custom-call | flops 1000 | bytes 1000 | tf_op jit(solution)/shard_map/logits_first/pallas_call | solution.py:163
  46.2 11.2 %all-to-all-start = ((f32[32,1,128]{2,1,0:T(1,128)}), f32[32,1,128]{2,1,0:T(1,128)S(1)}, u32[]{:S(2)}, u32[]{:S(2)}) async-start(f32[32,1,128]{2,1,0:T(1,128)} %local.1), calls=%async_computation | async-start | bytes 32768 | tf_op jit(solution)/shard_map/all_to_all | solution.py:393
  58.0 0.7 copy-done.10
  58.8 6.2 %logits_last.1 = (bf16[1,512,1280]{2,1,0:T(8,128)(2,1)}, f32[512,512]{1,0:T(8,128)}, f32[8,8,512]{2,1,0:T(8,128)}, f32[8,512]{1,0:T(8,128)}) custom-call(s32[12]{0:T(128)} %concatenate.6.at, bf16[272,640]{1,0:T(8,128)(2,1)} %collective-permute-done.2.refs_0_, bf16[256,640]{1,0:T(8,128)(2,1)} %collective-permute-done.6.refs_1_, bf16[272,640]{1,0:T(8,128)(2,1)} %copy-done.9, ...), custom_call_target="tpu_custom_call" | custom-call | flops 1000 | bytes 1000 | tf_op jit(solution)/shard_map/logits_last/pallas_call | solution.py:163
  65.0 0.9 all-to-all-done.sums_ref
  65.9 3.4 %all-to-all-start.1 = ((f32[8,8,512]{2,1,0:T(8,128)}), f32[8,8,512]{2,1,0:T(8,128)S(1)}, u32[]{:S(2)}, u32[]{:S(2)}) async-start(f32[8,8,512]{2,1,0:T(8,128)} %get-tuple-element.45), calls=%async_computation.1 | async-start | bytes 262144 | tf_op jit(solution)/shard_map/all_to_all | solution.py:414
  70.0 5.4 %all-to-all-done.1.st = f32[8,8,512]{2,1,0:T(8,128)S(1)} async-done(((f32[8,8,512]{2,1,0:T(8,128)}), f32[8,8,512]{2,1,0:T(8,128)S(1)}, u32[]{:S(2)}, u32[]{:S(2)}) %all-to-all-start.1) | async-done | bytes 131104 | tf_op jit(solution)/shard_map/all_to_all | solution.py:414
  75.4 0.7 copy-done.8
  76.0 2.8 %policy.1 = (bf16[512,512]{1,0:T(8,128)(2,1)}, f32[8,512]{1,0:T(8,128)}) custom-call(s32[12]{0:T(128)} %concatenate.6.at, f32[2]{0:T(128)} %rewards.3, s32[2]{0:T(128)} %lengths.3, s32[2]{0:T(128)} %slots.3, f32[32,1,128]{2,1,0:T(1,128)} %copy-done.11, f32[8,8,512]{2,1,0:T(8,128)} %copy-done.8, f32[512,512]{1,0:T(8,128)} %get-tuple-element.46.lg, ...), custom_call_target="tpu_custom_call" | custom-call | flops 2097152 | bytes 1572864 | tf_op jit(solution)/shard_map/policy/pallas_call | solution.py:230
  78.9 8.8 %heads.1 = (bf16[4,8,160,256]{3,2,1,0:T(8,128)(2,1)}, bf16[8,4,160,256]{3,2,1,0:T(8,128)(2,1)}) custom-call(s32[12]{0:T(128)} %concatenate.6.at, bf16[3,512,1280]{2,1,0:T(8,128)(2,1)} %get-tuple-element.49.early, bf16[1,512,1280]{2,1,0:T(8,128)(2,1)} %get-tuple-element.50.late, bf16[512,512]{1,0:T(8,128)(2,1)} %get-tuple-element.52.dl), custom_call_target="tpu_custom_call" | custom-call | flops 2684354560 | bytes 15728640 | tf_op jit(solution)/shard_map/heads/pallas_call | solution.py:290
  87.7 3.8 %all-to-all-start.2 = ((bf16[4,8,160,256]{3,2,1,0:T(8,128)(2,1)}), bf16[4,8,160,256]{3,2,1,0:T(8,128)(2,1)S(1)}, u32[]{:S(2)}, u32[]{:S(2)}) async-start(bf16[4,8,160,256]{3,2,1,0:T(8,128)(2,1)} %get-tuple-element.51), calls=%async_computation.3 | async-start | bytes 5242880 | tf_op jit(solution)/shard_map/all_to_all | solution.py:421
  91.8 1.9 %collective-permute-done.9.dl_o = bf16[512,512]{1,0:T(8,128)(2,1)S(1)} collective-permute-done((bf16[512,512]{1,0:T(8,128)(2,1)S(1)}, bf16[512,512]{1,0:T(8,128)(2,1)S(1)}, u32[]{:S(2)}, u32[]{:S(2)}) %collective-permute-start.9) | collective-permute-done | bytes 524320 | tf_op jit(solution)/shard_map/ppermute | solution.py:27
  93.7 0.8 copy-done.7
  94.5 8.4 %back.1 = (bf16[512,640]{1,0:T(8,128)(2,1)}, bf16[512,640]{1,0:T(8,128)(2,1)}, bf16[512,640]{1,0:T(8,128)(2,1)}, bf16[512,640]{1,0:T(8,128)(2,1)}) custom-call(s32[12]{0:T(128)} %concatenate.6.at, bf16[512,512]{1,0:T(8,128)(2,1)} %get-tuple-element.52.dl, bf16[512,512]{1,0:T(8,128)(2,1)} %copy-done.7, bf16[512,5120]{1,0:T(8,128)(2,1)} %head.1, ...), custom_call_target="tpu_custom_call" | custom-call | flops 2684354560 | bytes 10485760 | tf_op jit(solution)/shard_map/back/pallas_call | solution.py:253
  102.9 1.2 collective-permute-start.11
  104.1 0.8 collective-permute-start.12
  104.9 1.0 collective-permute-start.13
  106.4 17.0 %all-to-all-done.2.a = bf16[4,8,160,256]{3,2,1,0:T(8,128)(2,1)S(1)} async-done(((bf16[4,8,160,256]{3,2,1,0:T(8,128)(2,1)}), bf16[4,8,160,256]{3,2,1,0:T(8,128)(2,1)S(1)}, u32[]{:S(2)}, u32[]{:S(2)}) %all-to-all-start.2) | async-done | bytes 2621472 | tf_op jit(solution)/shard_map/all_to_all | solution.py:421
  123.5 1.5 copy-done
  125.0 2.9 %sum_x.1 = bf16[8,160,256]{2,1,0:T(8,128)(2,1)} custom-call(bf16[4,8,160,256]{3,2,1,0:T(8,128)(2,1)} %copy-done), custom_call_target="tpu_custom_call" | custom-call | flops 1310720 | bytes 3932160 | tf_op jit(solution)/shard_map/sum_x/pallas_call | solution.py:318
  127.9 6.7 %all-to-all-start.3 = ((bf16[8,160,256]{2,1,0:T(8,128)(2,1)}), bf16[8,160,256]{2,1,0:T(8,128)(2,1)}, u32[]{:S(2)}, u32[]{:S(2)}) async-start(bf16[8,160,256]{2,1,0:T(8,128)(2,1)} %sum_x.1), calls=%async_computation.4 | async-start | bytes 1310720 | tf_op jit(solution)/shard_map/all_to_all | solution.py:426
  134.6 0.7 reduce-scatter.5.cloned.1.call-update
  135.3 0.8 collective-permute-done.12.u2
  136.2 3.4 %final.1 = (bf16[2,256,640]{2,1,0:T(8,128)(2,1)}, f32[1,768]{1,0:T(1,128)}) custom-call(bf16[512,640]{1,0:T(8,128)(2,1)} %get-tuple-element.54.u0, bf16[512,640]{1,0:T(8,128)(2,1)} %copy-done.15, bf16[512,640]{1,0:T(8,128)(2,1)} %collective-permute-done.12.u2, bf16[512,640]{1,0:T(8,128)(2,1)} %collective-permute-done.13.u3, bf16[2,256,640]{2,1,0:T(8,128)(2,1)} %h_ref.1, ...), custom_call_target="tpu_custom_call" | custom-call | flops 199999995904 | bytes 3932160 | tf_op jit(solution)/shard_map/final/pallas_call | solution.py:355
  139.6 0.7 reduce
  140.3 3.4 %collective-permute-start.15 = (f32[6,128]{1,0:T(8,128)S(1)}, f32[6,128]{1,0:T(8,128)S(1)}, u32[]{:S(2)}, u32[]{:S(2)}) collective-permute-start(f32[6,128]{1,0:T(8,128)S(1)} %bitcast.26), channel_id=1, source_target_pairs={{0,16},{8,24},{16,0},{24,8},{1,17},{9,25},{17,1},{25,9},{2,18},{10... | collective-permute-start | bytes 9224 | tf_op jit(solution)/shard_map/ppermute | solution.py:27
  143.6 1.2 collective-permute-start.16
  144.8 0.9 collective-permute-start.14
  145.7 1.6 collective-permute-done.16
  147.2 2.4 %collective-permute-done.14 = f32[6,128]{1,0:T(8,128)S(1)} collective-permute-done((f32[6,128]{1,0:T(8,128)S(1)}, f32[6,128]{1,0:T(8,128)S(1)}, u32[]{:S(2)}, u32[]{:S(2)}) %collective-permute-start.14) | collective-permute-done | bytes 3104 | tf_op jit(solution)/shard_map/ppermute | solution.py:27
  149.6 1.3 collective-permute-start.17
  150.9 2.3 %collective-permute-done.17 = f32[6,128]{1,0:T(8,128)S(1)} collective-permute-done((f32[6,128]{1,0:T(8,128)S(1)}, f32[6,128]{1,0:T(8,128)S(1)}, u32[]{:S(2)}, u32[]{:S(2)}) %collective-permute-start.17) | collective-permute-done | bytes 3104 | tf_op jit(solution)/shard_map/ppermute | solution.py:31
  153.3 1.1 collective-permute-start.18
  154.3 2.5 %collective-permute-done.18 = f32[6,128]{1,0:T(8,128)S(1)} collective-permute-done((f32[6,128]{1,0:T(8,128)S(1)}, f32[6,128]{1,0:T(8,128)S(1)}, u32[]{:S(2)}, u32[]{:S(2)}) %collective-permute-start.18) | collective-permute-done | bytes 3104 | tf_op jit(solution)/shard_map/ppermute | solution.py:31
  156.9 3.3 %collective-permute-start.19 = (f32[6,128]{1,0:T(8,128)S(1)}, f32[6,128]{1,0:T(8,128)S(1)}, u32[]{:S(2)}, u32[]{:S(2)}) collective-permute-start(f32[6,128]{1,0:T(8,128)S(1)} %add.45), channel_id=1, source_target_pairs={{0,96},{32,192},{64,160},{96,0},{128,224},{160,64},{192,32},{224,1... | collective-permute-start | bytes 9224 | tf_op jit(solution)/shard_map/ppermute | solution.py:31
  160.2 3.3 %collective-permute-done.19 = f32[6,128]{1,0:T(8,128)S(1)} collective-permute-done((f32[6,128]{1,0:T(8,128)S(1)}, f32[6,128]{1,0:T(8,128)S(1)}, u32[]{:S(2)}, u32[]{:S(2)}) %collective-permute-start.19) | collective-permute-done | bytes 3104 | tf_op jit(solution)/shard_map/ppermute | solution.py:31
  164.6 1.9 %join.1 = f32[160,512]{1,0:T(8,128)} custom-call(bf16[8,160,256]{2,1,0:T(8,128)(2,1)} %all-to-all-done.3.from_z, bf16[160,256]{1,0:T(8,128)(2,1)} %bitcast.22), custom_call_target="tpu_custom_call" | custom-call | flops 655360 | bytes 1310720 | tf_op jit(solution)/shard_map/join/pallas_call | solution.py:355
  (65 shorter events, 5.2 us)
Async XLA Ops:
  7.2 26.9 %copy-start.16 = (s32[4]{0:T(128)S(1)}, s32[4]{0:T(128)}, u32[]{:S(2)}) copy-start(s32[4]{0:T(128)} %constant.35.clone) | copy-start | bytes 52
  9.0 25.8 %copy-start.1 = (bf16[528,640]{1,0:T(8,128)(2,1)}, bf16[528,640]{1,0:T(8,128)(2,1)S(1)}, u32[]{:S(2)}) copy-start(bf16[528,640]{1,0:T(8,128)(2,1)S(1)} %pad_maximum_fusion.refs_0_) | copy-start | bytes 2027524
  9.0 17.5 %collective-permute-start.1 = (bf16[528,640]{1,0:T(8,128)(2,1)S(1)}, bf16[528,640]{1,0:T(8,128)(2,1)S(1)}, u32[]{:S(2)}, u32[]{:S(2)}) collective-permute-start(bf16[528,640]{1,0:T(8,128)(2,1)S(1)} %pad_maximum_fusion.refs_0_), channel_id=1, source_target_pairs={{0,6},{2,0},{4,2},{6,4},{1,7},{3,1},{5,3},{7,5},{8,14},{10,8},{12,... | collective-permute-start | bytes 2027528 | tf_op jit(solution)/shard_map/ppermute | solution.py:27
  12.1 17.8 %collective-permute-start = (bf16[528,640]{1,0:T(8,128)(2,1)S(1)}, bf16[528,640]{1,0:T(8,128)(2,1)S(1)}, u32[]{:S(2)}, u32[]{:S(2)}) collective-permute-start(bf16[528,640]{1,0:T(8,128)(2,1)S(1)} %pad_maximum_fusion.refs_0_), channel_id=1, source_target_pairs={{0,2},{2,4},{4,6},{6,0},{1,3},{3,5},{5,7},{7,1},{8,10},{10,12},{12... | collective-permute-start | bytes 2027528 | tf_op jit(solution)/shard_map/ppermute | solution.py:27
  12.1 22.6 %collective-permute-start.3 = (bf16[528,640]{1,0:T(8,128)(2,1)S(1)}, bf16[528,640]{1,0:T(8,128)(2,1)S(1)}, u32[]{:S(2)}, u32[]{:S(2)}) collective-permute-start(bf16[528,640]{1,0:T(8,128)(2,1)S(1)} %pad_maximum_fusion.refs_0_), channel_id=1, source_target_pairs={{0,1},{1,0},{2,3},{3,2},{4,5},{5,4},{6,7},{7,6},{8,9},{9,8},{10,11... | collective-permute-start | bytes 2027528 | tf_op jit(solution)/shard_map/ppermute | solution.py:27
  26.5 8.3 %copy-start.3 = (bf16[528,640]{1,0:T(8,128)(2,1)}, bf16[528,640]{1,0:T(8,128)(2,1)S(1)}, u32[]{:S(2)}) copy-start(bf16[528,640]{1,0:T(8,128)(2,1)S(1)} %collective-permute-done.1.refs_4_) | copy-start | bytes 2027524
  30.0 4.8 %copy-start.2 = (bf16[528,640]{1,0:T(8,128)(2,1)}, bf16[528,640]{1,0:T(8,128)(2,1)S(1)}, u32[]{:S(2)}) copy-start(bf16[528,640]{1,0:T(8,128)(2,1)S(1)} %collective-permute-done.refs_2_) | copy-start | bytes 2027524
  31.5 3.2 %collective-permute-start.4 = (bf16[528,640]{1,0:T(8,128)(2,1)S(1)}, bf16[528,640]{1,0:T(8,128)(2,1)S(1)}, u32[]{:S(2)}, u32[]{:S(2)}) collective-permute-start(bf16[528,640]{1,0:T(8,128)(2,1)S(1)} %collective-permute-done.refs_2_), channel_id=1, source_target_pairs={{0,1},{1,0},{2,3},{3,2},{4,5},{5,4},{6,7},{7,6},{8,9},{9,8},{10,11... | collective-permute-start | bytes 2027528 | tf_op jit(solution)/shard_map/ppermute | solution.py:27
  31.5 3.2 %collective-permute-start.5 = (bf16[528,640]{1,0:T(8,128)(2,1)S(1)}, bf16[528,640]{1,0:T(8,128)(2,1)}, u32[]{:S(2)}, u32[]{:S(2)}) collective-permute-start(bf16[528,640]{1,0:T(8,128)(2,1)S(1)} %collective-permute-done.1.refs_4_), channel_id=1, source_target_pairs={{0,1},{1,0},{2,3},{3,2},{4,5},{5,4},{6,7},{7,6},{8,9},{9,8},{10,11... | collective-permute-start | bytes 2027528 | tf_op jit(solution)/shard_map/ppermute | solution.py:27
  32.0 14.0 %collective-permute-start.6 = (bf16[256,640]{1,0:T(8,128)(2,1)}, bf16[256,640]{1,0:T(8,128)(2,1)}, u32[]{:S(2)}, u32[]{:S(2)}) collective-permute-start(bf16[256,640]{1,0:T(8,128)(2,1)} %slice.16), channel_id=1, source_target_pairs={{0,6},{2,0},{4,2},{6,4},{1,7},{3,1},{5,3},{7,5},{8,14},{10,8},{12,... | collective-permute-start | bytes 983048 | tf_op jit(solution)/shard_map/ppermute | solution.py:27
  32.4 13.2 %collective-permute-start.2 = (bf16[272,640]{1,0:T(8,128)(2,1)}, bf16[272,640]{1,0:T(8,128)(2,1)}, u32[]{:S(2)}, u32[]{:S(2)}) collective-permute-start(bf16[272,640]{1,0:T(8,128)(2,1)} %slice.15), channel_id=1, source_target_pairs={{0,2},{2,4},{4,6},{6,0},{1,3},{3,5},{5,7},{7,1},{8,10},{10,12},{12... | collective-permute-start | bytes 1044488 | tf_op jit(solution)/shard_map/ppermute | solution.py:27
  34.8 22.6 %copy-start.13 = (s32[2,256]{1,0:T(2,128)S(1)}, s32[2,256]{1,0:T(2,128)}, u32[]{:S(2)}) copy-start(s32[2,256]{1,0:T(2,128)} %param.12) | copy-start | bytes 6148
  34.8 0.8 copy-start.4
  34.8 1.1 copy-start.5
  45.5 48.2 %collective-permute-start.10 = (bf16[512,5120]{1,0:T(8,128)(2,1)}, bf16[512,5120]{1,0:T(8,128)(2,1)}, u32[]{:S(2)}, u32[]{:S(2)}) collective-permute-start(bf16[512,5120]{1,0:T(8,128)(2,1)} %head.1), channel_id=1, source_target_pairs={{0,1},{1,0},{2,3},{3,2},{4,5},{5,4},{6,7},{7,6},{8,9},{9,8},{10,11... | collective-permute-start | bytes 15728648 | tf_op jit(solution)/shard_map/ppermute | solution.py:27
  45.6 12.4 %collective-permute-start.7 = (bf16[272,640]{1,0:T(8,128)(2,1)}, bf16[272,640]{1,0:T(8,128)(2,1)S(1)}, u32[]{:S(2)}, u32[]{:S(2)}) collective-permute-start(bf16[272,640]{1,0:T(8,128)(2,1)} %collective-permute-done.2.refs_0_), channel_id=1, source_target_pairs={{0,1},{1,0},{2,3},{3,2},{4,5},{5,4},{6,7},{7,6},{8,9},{9,8},{10,11... | collective-permute-start | bytes 1044488 | tf_op jit(solution)/shard_map/ppermute | solution.py:27
  46.1 11.9 %collective-permute-start.8 = (bf16[256,640]{1,0:T(8,128)(2,1)}, bf16[256,640]{1,0:T(8,128)(2,1)S(1)}, u32[]{:S(2)}, u32[]{:S(2)}) collective-permute-start(bf16[256,640]{1,0:T(8,128)(2,1)} %collective-permute-done.6.refs_1_), channel_id=1, source_target_pairs={{0,1},{1,0},{2,3},{3,2},{4,5},{5,4},{6,7},{7,6},{8,9},{9,8},{10,11... | collective-permute-start | bytes 983048 | tf_op jit(solution)/shard_map/ppermute | solution.py:27
  46.2 19.8 %all-to-all-start = ((f32[32,1,128]{2,1,0:T(1,128)}), f32[32,1,128]{2,1,0:T(1,128)S(1)}, u32[]{:S(2)}, u32[]{:S(2)}) async-start(f32[32,1,128]{2,1,0:T(1,128)} %local.1), calls=%async_computation | async-start | bytes 32768 | tf_op jit(solution)/shard_map/all_to_all | solution.py:393
  58.0 0.7 copy-start.10
  58.0 0.8 copy-start.9
  58.8 10.5 %copy-start.14 = (f32[2,256]{1,0:T(2,128)S(1)}, f32[2,256]{1,0:T(2,128)}, u32[]{:S(2)}) copy-start(f32[2,256]{1,0:T(2,128)} %param.14) | copy-start | bytes 6148
  65.9 9.4 %copy-start.11 = (f32[32,1,128]{2,1,0:T(1,128)}, f32[32,1,128]{2,1,0:T(1,128)S(1)}, u32[]{:S(2)}) copy-start(f32[32,1,128]{2,1,0:T(1,128)S(1)} %all-to-all-done.sums_ref) | copy-start | bytes 49156
  65.9 9.4 %all-to-all-start.1 = ((f32[8,8,512]{2,1,0:T(8,128)}), f32[8,8,512]{2,1,0:T(8,128)S(1)}, u32[]{:S(2)}, u32[]{:S(2)}) async-start(f32[8,8,512]{2,1,0:T(8,128)} %get-tuple-element.45), calls=%async_computation.1 | async-start | bytes 262144 | tf_op jit(solution)/shard_map/all_to_all | solution.py:414
  69.3 65.3 %reduce-scatter.3.cloned.1.call-start = ((), (), s32[]{:S(2)}) async-start(), calls=%async_computation.6 | async-start | bytes 2949120 | tf_op jit(solution)/shard_map/reduce_scatter | solution.py:420
  75.4 0.7 copy-start.8
  87.7 3.8 %copy-start.6 = (bf16[512,512]{1,0:T(8,128)(2,1)S(1)}, bf16[512,512]{1,0:T(8,128)(2,1)}, u32[]{:S(2)}) copy-start(bf16[512,512]{1,0:T(8,128)(2,1)} %get-tuple-element.52.dl) | copy-start | bytes 1572868
  87.7 35.8 %all-to-all-start.2 = ((bf16[4,8,160,256]{3,2,1,0:T(8,128)(2,1)}), bf16[4,8,160,256]{3,2,1,0:T(8,128)(2,1)S(1)}, u32[]{:S(2)}, u32[]{:S(2)}) async-start(bf16[4,8,160,256]{3,2,1,0:T(8,128)(2,1)} %get-tuple-element.51), calls=%async_computation.3 | async-start | bytes 5242880 | tf_op jit(solution)/shard_map/all_to_all | solution.py:421
  91.5 14.4 %copy-start.12 = (bf16[640]{0:T(1024)(128)(2,1)S(1)}, bf16[640]{0:T(1024)(128)(2,1)}, u32[]{:S(2)}) copy-start(bf16[640]{0:T(1024)(128)(2,1)} %param.10) | copy-start | bytes 3844
  91.5 2.2 %collective-permute-start.9 = (bf16[512,512]{1,0:T(8,128)(2,1)S(1)}, bf16[512,512]{1,0:T(8,128)(2,1)S(1)}, u32[]{:S(2)}, u32[]{:S(2)}) collective-permute-start(bf16[512,512]{1,0:T(8,128)(2,1)S(1)} %copy-done.6), channel_id=1, source_target_pairs={{0,1},{1,0},{2,3},{3,2},{4,5},{5,4},{6,7},{7,6},{8,9},{9,8},{10,11... | collective-permute-start | bytes 1572872 | tf_op jit(solution)/shard_map/ppermute | solution.py:27
  93.7 0.8 copy-start.7
  102.9 32.4 %collective-permute-start.11 = (bf16[512,640]{1,0:T(8,128)(2,1)}, bf16[512,640]{1,0:T(8,128)(2,1)S(1)}, u32[]{:S(2)}, u32[]{:S(2)}) collective-permute-start(bf16[512,640]{1,0:T(8,128)(2,1)} %get-tuple-element.55), channel_id=1, source_target_pairs={{0,6},{2,0},{4,2},{6,4},{1,7},{3,1},{5,3},{7,5},{8,14},{10,8},{12,... | collective-permute-start | bytes 1966088 | tf_op jit(solution)/shard_map/ppermute | solution.py:27
  104.1 32.1 %collective-permute-start.12 = (bf16[512,640]{1,0:T(8,128)(2,1)}, bf16[512,640]{1,0:T(8,128)(2,1)}, u32[]{:S(2)}, u32[]{:S(2)}) collective-permute-start(bf16[512,640]{1,0:T(8,128)(2,1)} %get-tuple-element.56), channel_id=1, source_target_pairs={{0,2},{2,4},{4,6},{6,0},{1,3},{3,5},{5,7},{7,1},{8,10},{10,12},{12... | collective-permute-start | bytes 1966088 | tf_op jit(solution)/shard_map/ppermute | solution.py:27
  104.9 31.2 %collective-permute-start.13 = (bf16[512,640]{1,0:T(8,128)(2,1)}, bf16[512,640]{1,0:T(8,128)(2,1)}, u32[]{:S(2)}, u32[]{:S(2)}) collective-permute-start(bf16[512,640]{1,0:T(8,128)(2,1)} %get-tuple-element.57), channel_id=1, source_target_pairs={{0,4},{2,6},{4,0},{6,2},{1,5},{3,7},{5,1},{7,3},{8,12},{10,14},{12... | collective-permute-start | bytes 1966088 | tf_op jit(solution)/shard_map/ppermute | solution.py:27
  123.5 1.5 copy-start
  127.9 36.7 %all-to-all-start.3 = ((bf16[8,160,256]{2,1,0:T(8,128)(2,1)}), bf16[8,160,256]{2,1,0:T(8,128)(2,1)}, u32[]{:S(2)}, u32[]{:S(2)}) async-start(bf16[8,160,256]{2,1,0:T(8,128)(2,1)} %sum_x.1), calls=%async_computation.4 | async-start | bytes 1310720 | tf_op jit(solution)/shard_map/all_to_all | solution.py:426
  134.6 30.0 %reduce-scatter.5.cloned.1.call-start = ((), (), s32[]{:S(2)}) async-start(), calls=%async_computation.7 | async-start | bytes 409600 | tf_op jit(solution)/shard_map/reduce_scatter | solution.py:429
  135.3 0.8 copy-start.15
  140.3 5.4 %collective-permute-start.15 = (f32[6,128]{1,0:T(8,128)S(1)}, f32[6,128]{1,0:T(8,128)S(1)}, u32[]{:S(2)}, u32[]{:S(2)}) collective-permute-start(f32[6,128]{1,0:T(8,128)S(1)} %bitcast.26), channel_id=1, source_target_pairs={{0,16},{8,24},{16,0},{24,8},{1,17},{9,25},{17,1},{25,9},{2,18},{10... | collective-permute-start | bytes 9224 | tf_op jit(solution)/shard_map/ppermute | solution.py:27
  143.6 3.6 %collective-permute-start.16 = (f32[6,128]{1,0:T(8,128)S(1)}, f32[6,128]{1,0:T(8,128)S(1)}, u32[]{:S(2)}, u32[]{:S(2)}) collective-permute-start(f32[6,128]{1,0:T(8,128)S(1)} %bitcast.27), channel_id=1, source_target_pairs={{0,24},{8,0},{16,8},{24,16},{1,25},{9,1},{17,9},{25,17},{2,26},{10... | collective-permute-start | bytes 9224 | tf_op jit(solution)/shard_map/ppermute | solution.py:27
  144.8 4.8 %collective-permute-start.14 = (f32[6,128]{1,0:T(8,128)S(1)}, f32[6,128]{1,0:T(8,128)S(1)}, u32[]{:S(2)}, u32[]{:S(2)}) collective-permute-start(f32[6,128]{1,0:T(8,128)S(1)} %bitcast.28), channel_id=1, source_target_pairs={{0,8},{8,16},{16,24},{24,0},{1,9},{9,17},{17,25},{25,1},{2,10},{10... | collective-permute-start | bytes 9224 | tf_op jit(solution)/shard_map/ppermute | solution.py:27
  149.6 3.6 %collective-permute-start.17 = (f32[6,128]{1,0:T(8,128)S(1)}, f32[6,128]{1,0:T(8,128)S(1)}, u32[]{:S(2)}, u32[]{:S(2)}) collective-permute-start(f32[6,128]{1,0:T(8,128)S(1)} %add_add_fusion), channel_id=1, source_target_pairs={{0,32},{32,0},{64,96},{96,64},{128,160},{160,128},{192,224},{224,1... | collective-permute-start | bytes 9224 | tf_op jit(solution)/shard_map/ppermute | solution.py:31
  153.3 3.6 %collective-permute-start.18 = (f32[6,128]{1,0:T(8,128)S(1)}, f32[6,128]{1,0:T(8,128)S(1)}, u32[]{:S(2)}, u32[]{:S(2)}) collective-permute-start(f32[6,128]{1,0:T(8,128)S(1)} %add.44), channel_id=1, source_target_pairs={{0,224},{32,64},{64,32},{96,128},{128,96},{160,192},{192,160},{224... | collective-permute-start | bytes 9224 | tf_op jit(solution)/shard_map/ppermute | solution.py:31
  156.9 6.6 %collective-permute-start.19 = (f32[6,128]{1,0:T(8,128)S(1)}, f32[6,128]{1,0:T(8,128)S(1)}, u32[]{:S(2)}, u32[]{:S(2)}) collective-permute-start(f32[6,128]{1,0:T(8,128)S(1)} %add.45), channel_id=1, source_target_pairs={{0,96},{32,192},{64,160},{96,0},{128,224},{160,64},{192,32},{224,1... | collective-permute-start | bytes 9224 | tf_op jit(solution)/shard_map/ppermute | solution.py:31
Sparse Core Ops, SparseCore 0:
  87.8 41.4 reduce-scatter.2
  137.9 20.5 reduce-scatter.4

commit v5 on v4

--- a/solution.py
+++ b/solution.py
@@ -31,6 +31,10 @@
     return lax.ppermute(
         value, "z", [(i, (i + (step if i % 2 == 0 else -step)) % 8) for i in range(8)]
     )
+
+
+def across(value, axis, bit):
+    return lax.ppermute(value, axis, [(i, i ^ bit) for i in range(SIZES[axis])])
 
 
 def params(limit=60 << 20):
@@ -238,32 +242,54 @@
     )(at, *scalars, sums, stats, logits, inv, targets, old_logp)
 
 
-def back_kernel(at, dl, dl_o, head, head_o, *outs):
+def back_kernel(at, dl, dl_o, early, late, small, head, head_o, u0, u1, u2, u3, stay, go):
+    j = pl.program_id(0)
     total = jnp.dot(dl[...], head[...], preferred_element_type=f32)
     total += jnp.dot(dl_o[...], head_o[...], preferred_element_type=f32)
-    for k, out in enumerate(outs):
-
-        @pl.when(pl.program_id(0) == k)
+    for k, out in enumerate((u0, u1, u2, u3)):
+
+        @pl.when(j == k)
         def _(out=out):
             out[...] = total.astype(bf16)
 
-
-def back_of(at, dl, dl_o, head, head_o, cols):
+    scaled = jnp.where(j < 3, early[0], late[0]).astype(f32)
+    loss = jnp.sum(small[1:2, :], axis=1, keepdims=True) / 4
+    line = jnp.concatenate(
+        [jnp.sum(total * scaled, axis=0, keepdims=True), jnp.broadcast_to(loss, (1, 128))], axis=1
+    )
+    apart = at[8 + j] ^ at[1]
+
+    @pl.when(apart % 2 == 0)
+    def _():
+        stay[apart // 2] = line
+
+    @pl.when(apart % 2 == 1)
+    def _():
+        go[apart // 2] = line
+
+
+def back_of(at, dl, dl_o, early, late, small, head, head_o, cols):
     rows, half = dl.shape
+    shapes = [like((rows, cols))] * 4 + [like((2, 1, cols + 128), f32)] * 2
     return pl.pallas_call(
         back_kernel,
-        out_shape=[like((rows, cols))] * 4,
+        out_shape=shapes,
         grid_spec=pltpu.PrefetchScalarGridSpec(
             num_scalar_prefetch=1,
             grid=(4,),
             in_specs=[full((rows, half))] * 2
+            + [
+                pl.BlockSpec((1, rows, cols), lambda j, at: (jnp.minimum(j, 2), 0, at[2])),
+                pl.BlockSpec((1, rows, cols), lambda j, at: (0, 0, at[2])),
+                full(small.shape),
+            ]
             + [pl.BlockSpec((half, cols), lambda j, at: (0, 2 * at[8 + j] + at[2]))] * 2,
-            out_specs=[full((rows, cols))] * 4,
+            out_specs=[full(s.shape) for s in shapes],
         ),
         compiler_params=params(),
         cost_estimate=cost(2 * rows * 8 * cols * half, 32 * rows * cols),
         name="back",
-    )(at, dl, dl_o, head, head_o)
+    )(at, dl, dl_o, early, late, small, head, head_o)
 
 
 def heads_kernel(at, early, late, dl, to_x, to_z):
@@ -335,20 +361,15 @@
     out[:, width:] = from_x[...].astype(f32)
 
 
-def final_kernel(u0, u1, u2, u3, h_ref, g_ref, small, out, part):
+def final_kernel(u0, u1, u2, u3, h_ref, g_ref, small, out):
     gain = g_ref[...].astype(f32)
     resp, rows, _ = h_ref.shape
     kappa = column(small[0:1, :])
-    sums = None
     for r in range(resp):
         cut = slice(r * rows, (r + 1) * rows)
         u = sum(v[cut, :].astype(f32) for v in (u0, u1, u2, u3))
         h = h_ref[r].astype(f32)
         out[r] = (gain * u - h * kappa[cut, :]).astype(bf16)
-        now = jnp.sum(u * h, axis=0, keepdims=True)
-        sums = now if sums is None else sums + now
-    loss = jnp.sum(small[1:2, :], axis=1, keepdims=True)
-    part[...] = jnp.concatenate([sums, jnp.broadcast_to(loss, (1, 128))], axis=1)
 
 
 def simple(kernel, shapes, ins, nbytes, name, flops=None):
@@ -391,7 +412,7 @@
         "local",
     )
     sums = lax.all_to_all(local, DP, 0, 0, tiled=True)
-    prev, following, local = lax.optimization_barrier((prev, following, local))
+    prev, following, sums = lax.optimization_barrier((prev, following, sums))
 
     far_a, far_b = prev[:cut], following[cut:]
     far_a, far_b, prev, following = lax.optimization_barrier((far_a, far_b, prev, following))
@@ -419,24 +440,30 @@
     to_x, to_z = heads_of(at, early, late, dl)
     half_z = lax.psum_scatter(to_z, "z", scatter_dimension=0, tiled=False)
     from_x = lax.all_to_all(to_x, "x", 0, 0, tiled=True)
-    u0, u1, u2, u3 = back_of(at, after(dl, to_x), dl_o, head, head_o, cols)
+    u0, u1, u2, u3, stay, go = back_of(
+        at, after(dl, to_x), dl_o, early, late, small, head, head_o, cols
+    )
     u1, u2, u3 = shift(u1, "y", -1), shift(u2, "y", 1), shift(u3, "y", 2)
 
     to_z = sum_first(from_x, "sum_x")
+    half_z = after(half_z, to_z)
+    to_z = after(to_z, half_z)
     from_z = lax.all_to_all(to_z, "z", 0, 0, tiled=True)
-    half_z = after(half_z, to_z)
-    u1, u2, u3, _ = lax.optimization_barrier((u1, u2, u3, half_z))
     half_z = lax.psum_scatter(half_z, "x", scatter_dimension=0, tiled=False)
-    grad_hidden, gain_part = simple(
+    u1, u2, u3, _ = lax.optimization_barrier((u1, u2, u3, to_z))
+    (grad_hidden,) = simple(
         final_kernel,
-        [like(hidden.shape), like((1, cols + 128), f32)],
+        [like(hidden.shape)],
         (u0, u1, u2, u3, hidden, gain.reshape(1, cols), small),
         12 * rows * cols,
         "final",
         200 * 10**9,
     )
-    tail = gain_part.reshape(-1, 128)
-    tail = tail + shift(tail, "x", 1) + shift(tail, "x", 2) + shift(tail, "x", -1)
+    stay, go = stay.reshape(2, -1, 128), go.reshape(2, -1, 128)
+    tail = stay + across(go, "y", 1)
+    tail = tail[0] + across(tail[1], "y", 2)
+    tail = after(tail + across(tail, "x", 1), to_z)
+    tail = tail + across(tail, "x", 2)
     for step in (1, -1, 3):
         tail = tail + turn(tail, step)
     (grad_head_t,) = simple(
@@ -447,7 +474,7 @@
         "join",
     )
     tail = tail.reshape(-1)
-    return (tail[cols], grad_hidden, tail[:cols], grad_head_t)
+    return (tail[cols], grad_hidden, tail[:cols] / gain.astype(f32), grad_head_t)
 
 
 def solution(mesh):

time: 174 us -> 191 us (1.098)
  waiting for transfers between devices: 55.5 us -> 65.7 us
  starting transfers between devices: 45.7 us -> 48.4 us
    ppermute x0 -> x4, waiting for transfers between devices: none -> 29.5 us  [across(): return lax.ppermute(value, axis, [(i, i ^ bit) for i in range(SIZES[axis])])]
    all_to_all x1, waiting for transfers between devices: 17 us -> 0.01 us  [body(): from_x = lax.all_to_all(to_x, 'x', 0, 0, tiled=True)]
    ppermute x17 -> x14, waiting for transfers between devices: 23.2 us -> 7.29 us  [shift(): return lax.ppermute(value, axis, [(i, (i + step) % n) for i in range(n)])]
    reduce_scatter x1, waiting for transfers between devices: 0.01 us -> 10.1 us  [body(): half_z = lax.psum_scatter(half_z, 'x', scatter_dimension=0, tiled=False)]
    all_to_all x1, waiting for transfers between devices: 0.93 us -> 8.38 us  [body(): sums = lax.all_to_all(local, DP, 0, 0, tiled=True)]
    ppermute x0 -> x4, starting transfers between devices: none -> 6.46 us  [across(): return lax.ppermute(value, axis, [(i, i ^ bit) for i in range(SIZES[axis])])]
    ppermute x3, waiting for transfers between devices: 8.2 us -> 4.91 us  [turn(): lax.ppermute(value, 'z', [(i, (i + (step if i % 2 == 0 else -step)) % 8)...]
    ppermute x17 -> x14, starting transfers between devices: 15 us -> 12 us  [shift(): return lax.ppermute(value, axis, [(i, (i + step) % n) for i in range(n)])]
  transfers between devices with their start and end apart: 26 -> 27, of which waited for: 12 -> 9; matrix products, arithmetic and copies ran while one was open for 3% -> 3% of each run, Pallas kernels for 25% -> 24%
where the time goes in v5:
time: 191 us; the launch traced here: 190 us
  waiting for transfers between devices  65.7 us (34%)
  starting transfers between devices  48.4 us (25%)
  Pallas kernels  47.1 us (25%)
  between operations  14.3 us (7%)
  local copies, waits for them, and re-layouts  10.9 us (6%)
  other arithmetic  3.22 us (2%)
    ppermute x4, waiting for transfers between devices, across(): return lax.ppermute(value, axis, [(i, i ^ bit) for i in range(SIZES[axis])])  29.5 us
    pallas_call x2, Pallas kernels, logits_of(): pl.pallas_call(functools.partial(logits_kernel, count, per, last), out_sh...  15.7 us
    ppermute x14, starting transfers between devices, shift(): return lax.ppermute(value, axis, [(i, (i + step) % n) for i in range(n)])  12 us
    all_to_all x1, starting transfers between devices, body(): sums = lax.all_to_all(local, DP, 0, 0, tiled=True)  11.2 us
    pallas_call x1, Pallas kernels, back_of(): pl.pallas_call(back_kernel, out_shape=shapes, grid_spec=pltpu.PrefetchSca...  10.3 us
    reduce_scatter x1, waiting for transfers between devices, body(): half_z = lax.psum_scatter(half_z, 'x', scatter_dimension=0, tiled=False)  10.1 us
    pallas_call x1, Pallas kernels, heads_of(): pl.pallas_call(heads_kernel, out_shape=shapes, grid_spec=pltpu.PrefetchSc...  8.81 us
    all_to_all x1, waiting for transfers between devices, body(): sums = lax.all_to_all(local, DP, 0, 0, tiled=True)  8.38 us
  transfers between devices with their start and end apart: 27, of which 9 were waited for; matrix products, arithmetic and copies ran while one was open for 3% of the time, Pallas kernels for 24%

profile of v5, /device:TPU:32, one launch (start us, length us, event | category | flops | bytes accessed | tf_op | source)
XLA Modules:
  0.0 189.6 jit_solution(16726333492811956205)
XLA Ops:
  7.2 0.7 broadcast_in_dim.8
  7.9 1.1 pad_maximum_fusion.refs_0_
  9.0 3.1 %collective-permute-start.1 = (bf16[528,640]{1,0:T(8,128)(2,1)S(1)}, bf16[528,640]{1,0:T(8,128)(2,1)S(1)}, u32[]{:S(2)}, u32[]{:S(2)}) collective-permute-start(bf16[528,640]{1,0:T(8,128)(2,1)S(1)} %pad_maximum_fusion.refs_0_), channel_id=1, source_target_pairs={{0,6},{2,0},{4,2},{6,4},{1,7},{3,1},{5,3},{7,5},{8,14},{10,8},{12,... | collective-permute-start | bytes 2027528 | tf_op jit(solution)/shard_map/ppermute | solution.py:27
  12.1 1.3 local.1
  13.4 11.2 %all-to-all-start = ((f32[32,1,128]{2,1,0:T(1,128)}), f32[32,1,128]{2,1,0:T(1,128)S(1)}, u32[]{:S(2)}, u32[]{:S(2)}) async-start(f32[32,1,128]{2,1,0:T(1,128)} %local.1), calls=%async_computation | async-start | bytes 32768 | tf_op jit(solution)/shard_map/all_to_all | solution.py:414
  24.7 8.4 %all-to-all-done.sums_ref = f32[32,1,128]{2,1,0:T(1,128)S(1)} async-done(((f32[32,1,128]{2,1,0:T(1,128)}), f32[32,1,128]{2,1,0:T(1,128)S(1)}, u32[]{:S(2)}, u32[]{:S(2)}) %all-to-all-start) | async-done | bytes 16416 | tf_op jit(solution)/shard_map/all_to_all | solution.py:414
  33.1 0.9 slice.22
  34.0 0.8 slice.21
  35.3 0.6 collective-permute-start.2
  35.9 2.7 %collective-permute-start.6 = (bf16[256,640]{1,0:T(8,128)(2,1)}, bf16[256,640]{1,0:T(8,128)(2,1)}, u32[]{:S(2)}, u32[]{:S(2)}) collective-permute-start(bf16[256,640]{1,0:T(8,128)(2,1)} %slice.22), channel_id=1, source_target_pairs={{0,6},{2,0},{4,2},{6,4},{1,7},{3,1},{5,3},{7,5},{8,14},{10,8},{12,... | collective-permute-start | bytes 983048 | tf_op jit(solution)/shard_map/ppermute | solution.py:27
  38.5 0.6 concatenate.6.at
  39.2 0.8 copy-done.4
  40.3 9.6 %logits_first.1 = (bf16[3,512,1280]{2,1,0:T(8,128)(2,1)}, f32[512,512]{1,0:T(8,128)}, f32[8,512]{1,0:T(8,128)}) custom-call(s32[12]{0:T(128)} %concatenate.6.at, bf16[528,640]{1,0:T(8,128)(2,1)} %copy-done.1, bf16[528,640]{1,0:T(8,128)(2,1)} %copy-done.4, bf16[528,640]{1,0:T(8,128)(2,1)} %copy-done.2, bf16[528,640]{1,0:T(8,128)(2,1)} %copy-done.5, ...), custom_call_target="tpu_custom_call" | custom-call | flops 1000 | bytes 1000 | tf_op jit(solution)/shard_map/logits_first/pallas_call | solution.py:167
  51.2 5.4 %collective-permute-done.8.refs_3_ = bf16[256,640]{1,0:T(8,128)(2,1)S(1)} collective-permute-done((bf16[256,640]{1,0:T(8,128)(2,1)}, bf16[256,640]{1,0:T(8,128)(2,1)S(1)}, u32[]{:S(2)}, u32[]{:S(2)}) %collective-permute-start.8) | collective-permute-done | bytes 327712 | tf_op jit(solution)/shard_map/ppermute | solution.py:27
  56.5 0.7 copy-done.10
  57.4 6.1 %logits_last.1 = (bf16[1,512,1280]{2,1,0:T(8,128)(2,1)}, f32[512,512]{1,0:T(8,128)}, f32[8,8,512]{2,1,0:T(8,128)}, f32[8,512]{1,0:T(8,128)}) custom-call(s32[12]{0:T(128)} %concatenate.6.at, bf16[272,640]{1,0:T(8,128)(2,1)} %collective-permute-done.2.refs_0_, bf16[256,640]{1,0:T(8,128)(2,1)} %collective-permute-done.6.refs_1_, bf16[272,640]{1,0:T(8,128)(2,1)} %copy-done.9, ...), custom_call_target="tpu_custom_call" | custom-call | flops 1000 | bytes 1000 | tf_op jit(solution)/shard_map/logits_last/pallas_call | solution.py:167
  63.5 3.4 %all-to-all-start.1 = ((f32[8,8,512]{2,1,0:T(8,128)}), f32[8,8,512]{2,1,0:T(8,128)S(1)}, u32[]{:S(2)}, u32[]{:S(2)}) async-start(f32[8,8,512]{2,1,0:T(8,128)} %get-tuple-element.49), calls=%async_computation.1 | async-start | bytes 262144 | tf_op jit(solution)/shard_map/all_to_all | solution.py:435
  67.5 5.4 %all-to-all-done.1.st = f32[8,8,512]{2,1,0:T(8,128)S(1)} async-done(((f32[8,8,512]{2,1,0:T(8,128)}), f32[8,8,512]{2,1,0:T(8,128)S(1)}, u32[]{:S(2)}, u32[]{:S(2)}) %all-to-all-start.1) | async-done | bytes 131104 | tf_op jit(solution)/shard_map/all_to_all | solution.py:435
  72.9 0.7 copy-done.8
  73.6 2.8 %policy.1 = (bf16[512,512]{1,0:T(8,128)(2,1)}, f32[8,512]{1,0:T(8,128)}) custom-call(s32[12]{0:T(128)} %concatenate.6.at, f32[2]{0:T(128)} %rewards.3, s32[2]{0:T(128)} %lengths.3, s32[2]{0:T(128)} %slots.3, f32[32,1,128]{2,1,0:T(1,128)} %copy-done.11, f32[8,8,512]{2,1,0:T(8,128)} %copy-done.8, f32[512,512]{1,0:T(8,128)} %get-tuple-element.50.lg, ...), custom_call_target="tpu_custom_call" | custom-call | flops 2097152 | bytes 1572864 | tf_op jit(solution)/shard_map/policy/pallas_call | solution.py:234
  76.4 8.8 %heads.1 = (bf16[4,8,160,256]{3,2,1,0:T(8,128)(2,1)}, bf16[8,4,160,256]{3,2,1,0:T(8,128)(2,1)}) custom-call(s32[12]{0:T(128)} %concatenate.6.at, bf16[3,512,1280]{2,1,0:T(8,128)(2,1)} %get-tuple-element.53.early, bf16[1,512,1280]{2,1,0:T(8,128)(2,1)} %get-tuple-element.54.late, bf16[512,512]{1,0:T(8,128)(2,1)} %get-tuple-element.56.dl), custom_call_target="tpu_custom_call" | custom-call | flops 2684354560 | bytes 15728640 | tf_op jit(solution)/shard_map/heads/pallas_call | solution.py:316
  85.2 3.8 %all-to-all-start.2 = ((bf16[4,8,160,256]{3,2,1,0:T(8,128)(2,1)}), bf16[4,8,160,256]{3,2,1,0:T(8,128)(2,1)S(1)}, u32[]{:S(2)}, u32[]{:S(2)}) async-start(bf16[4,8,160,256]{3,2,1,0:T(8,128)(2,1)} %get-tuple-element.55), calls=%async_computation.2 | async-start | bytes 5242880 | tf_op jit(solution)/shard_map/all_to_all | solution.py:442
  89.4 1.9 %collective-permute-done.9.dl_o = bf16[512,512]{1,0:T(8,128)(2,1)S(1)} collective-permute-done((bf16[512,512]{1,0:T(8,128)(2,1)S(1)}, bf16[512,512]{1,0:T(8,128)(2,1)S(1)}, u32[]{:S(2)}, u32[]{:S(2)}) %collective-permute-start.9) | collective-permute-done | bytes 524320 | tf_op jit(solution)/shard_map/ppermute | solution.py:27
  91.3 0.8 copy-done.7
  92.1 10.3 %back.1 = (bf16[512,640]{1,0:T(8,128)(2,1)}, bf16[512,640]{1,0:T(8,128)(2,1)}, bf16[512,640]{1,0:T(8,128)(2,1)}, bf16[512,640]{1,0:T(8,128)(2,1)}, f32[2,1,768]{2,1,0:T(1,128)}, /*index=5*/f32[2,1,768]{2,1,0:T(1,128)}) custom-call(s32[12]{0:T(128)} %concatenate.6.at, bf16[512,512]{1,0:T(8,128)(2,1)} %get-tuple-element.56.dl, bf16[512,512]{1,0:T(8,128)(2,1)} %copy-done.7, ...), custom_call_target="tpu_custom_call" | custom-call | flops 2684354560 | bytes 10485760 | tf_op jit(solution)/shard_map/back/pallas_call | solution.py:274
  102.4 0.7 reduce.1
  103.5 0.7 reduce
  104.3 0.9 collective-permute-start.18
  105.2 1.2 collective-permute-start.19
  106.4 2.0 %collective-permute-start.20 = (bf16[512,640]{1,0:T(8,128)(2,1)}, bf16[512,640]{1,0:T(8,128)(2,1)}, u32[]{:S(2)}, u32[]{:S(2)}) collective-permute-start(bf16[512,640]{1,0:T(8,128)(2,1)} %get-tuple-element.68), channel_id=1, source_target_pairs={{0,4},{2,6},{4,0},{6,2},{1,5},{3,7},{5,1},{7,3},{8,12},{10,14},{12... | collective-permute-start | bytes 1966088 | tf_op jit(solution)/shard_map/ppermute | solution.py:27
  108.4 1.6 collective-permute-start.12
  110.0 27.0 %collective-permute-done.12 = f32[6,128]{1,0:T(8,128)S(1)} collective-permute-done((f32[6,128]{1,0:T(8,128)S(1)}, f32[6,128]{1,0:T(8,128)S(1)}, u32[]{:S(2)}, u32[]{:S(2)}) %collective-permute-start.12) | collective-permute-done | bytes 3104 | tf_op jit(solution)/shard_map/ppermute | solution.py:37
  137.1 1.7 collective-permute-start.13
  138.7 1.5 copy-done
  140.2 2.9 %sum_x.1 = bf16[8,160,256]{2,1,0:T(8,128)(2,1)} custom-call(bf16[4,8,160,256]{3,2,1,0:T(8,128)(2,1)} %copy-done), custom_call_target="tpu_custom_call" | custom-call | flops 1310720 | bytes 3932160 | tf_op jit(solution)/shard_map/sum_x/pallas_call | solution.py:344
  143.2 2.8 %collective-permute-start.14 = (f32[6,128]{1,0:T(8,128)S(1)}, f32[6,128]{1,0:T(8,128)S(1)}, u32[]{:S(2)}, u32[]{:S(2)}) collective-permute-start(f32[6,128]{1,0:T(8,128)S(1)} %add.46), channel_id=1, source_target_pairs={{0,16},{8,24},{16,0},{24,8},{1,17},{9,25},{17,1},{25,9},{2,18},{10... | collective-permute-start | bytes 9224 | tf_op jit(solution)/shard_map/ppermute | solution.py:37
  145.9 2.4 %collective-permute-done.14 = f32[6,128]{1,0:T(8,128)S(1)} collective-permute-done((f32[6,128]{1,0:T(8,128)S(1)}, f32[6,128]{1,0:T(8,128)S(1)}, u32[]{:S(2)}, u32[]{:S(2)}) %collective-permute-start.14) | collective-permute-done | bytes 3104 | tf_op jit(solution)/shard_map/ppermute | solution.py:37
  148.4 1.6 collective-permute-start.15
  150.0 2.0 %collective-permute-done.15 = f32[6,128]{1,0:T(8,128)S(1)} collective-permute-done((f32[6,128]{1,0:T(8,128)S(1)}, f32[6,128]{1,0:T(8,128)S(1)}, u32[]{:S(2)}, u32[]{:S(2)}) %collective-permute-start.15) | collective-permute-done | bytes 3104 | tf_op jit(solution)/shard_map/ppermute | solution.py:31
  152.0 0.7 collective-permute-start.16
  152.7 2.9 %collective-permute-done.16 = f32[6,128]{1,0:T(8,128)S(1)} collective-permute-done((f32[6,128]{1,0:T(8,128)S(1)}, f32[6,128]{1,0:T(8,128)S(1)}, u32[]{:S(2)}, u32[]{:S(2)}) %collective-permute-start.16) | collective-permute-done | bytes 3104 | tf_op jit(solution)/shard_map/ppermute | solution.py:31
  155.6 3.3 %collective-permute-start.17 = (f32[6,128]{1,0:T(8,128)S(1)}, f32[6,128]{1,0:T(8,128)S(1)}, u32[]{:S(2)}, u32[]{:S(2)}) collective-permute-start(f32[6,128]{1,0:T(8,128)S(1)} %add.49), channel_id=1, source_target_pairs={{0,96},{32,192},{64,160},{96,0},{128,224},{160,64},{192,32},{224,1... | collective-permute-start | bytes 9224 | tf_op jit(solution)/shard_map/ppermute | solution.py:31
  159.5 5.8 %all-to-all-start.3 = ((bf16[8,160,256]{2,1,0:T(8,128)(2,1)}), bf16[8,160,256]{2,1,0:T(8,128)(2,1)}, u32[]{:S(2)}, u32[]{:S(2)}) async-start(bf16[8,160,256]{2,1,0:T(8,128)(2,1)} %sum_x.1), calls=%async_computation.4 | async-start | bytes 1310720 | tf_op jit(solution)/shard_map/all_to_all | solution.py:451
  165.9 0.6 bitcast_divide_fusion
  166.5 0.8 copy-done.15
  167.3 3.4 %final.1 = bf16[2,256,640]{2,1,0:T(8,128)(2,1)} custom-call(bf16[512,640]{1,0:T(8,128)(2,1)} %get-tuple-element.65.u0, bf16[512,640]{1,0:T(8,128)(2,1)} %copy-done.15, bf16[512,640]{1,0:T(8,128)(2,1)} %collective-permute-done.19.u2, bf16[512,640]{1,0:T(8,128)(2,1)} %collective-permute-done.20.u3, bf16[2,256,640]{2,1,0:T(8,128)(2,1)} %h_ref.1, ...), custom_call_target="tpu_custom_call" | custom-call | flops 199999995904 | bytes 3932160 | tf_op jit(solution)/shard_map/final/pallas_call | solution.py:376
  170.7 10.1 %reduce-scatter.5.cloned.1.call-done = bf16[1,160,256]{2,1,0:T(8,128)(2,1)} async-done(((bf16[4,160,256]{2,1,0:T(8,128)(2,1)}), bf16[1,160,256]{2,1,0:T(8,128)(2,1)}) %reduce-scatter.5.cloned.1.call-update) | async-done | bytes 81936 | tf_op jit(solution)/shard_map/reduce_scatter | solution.py:452
  180.8 1.9 %join.1 = f32[160,512]{1,0:T(8,128)} custom-call(bf16[8,160,256]{2,1,0:T(8,128)(2,1)} %all-to-all-done.3.from_z, bf16[160,256]{1,0:T(8,128)(2,1)} %bitcast.26), custom_call_target="tpu_custom_call" | custom-call | flops 655360 | bytes 1310720 | tf_op jit(solution)/shard_map/join/pallas_call | solution.py:376
  (74 shorter events, 4.9 us)
Async XLA Ops:
  7.2 31.4 %copy-start.16 = (s32[4]{0:T(128)S(1)}, s32[4]{0:T(128)}, u32[]{:S(2)}) copy-start(s32[4]{0:T(128)} %constant.35.clone) | copy-start | bytes 52
  9.0 30.2 %copy-start.1 = (bf16[528,640]{1,0:T(8,128)(2,1)}, bf16[528,640]{1,0:T(8,128)(2,1)S(1)}, u32[]{:S(2)}) copy-start(bf16[528,640]{1,0:T(8,128)(2,1)S(1)} %pad_maximum_fusion.refs_0_) | copy-start | bytes 2027524
  9.0 24.1 %collective-permute-start.1 = (bf16[528,640]{1,0:T(8,128)(2,1)S(1)}, bf16[528,640]{1,0:T(8,128)(2,1)S(1)}, u32[]{:S(2)}, u32[]{:S(2)}) collective-permute-start(bf16[528,640]{1,0:T(8,128)(2,1)S(1)} %pad_maximum_fusion.refs_0_), channel_id=1, source_target_pairs={{0,6},{2,0},{4,2},{6,4},{1,7},{3,1},{5,3},{7,5},{8,14},{10,8},{12,... | collective-permute-start | bytes 2027528 | tf_op jit(solution)/shard_map/ppermute | solution.py:27
  12.1 21.0 %collective-permute-start = (bf16[528,640]{1,0:T(8,128)(2,1)S(1)}, bf16[528,640]{1,0:T(8,128)(2,1)S(1)}, u32[]{:S(2)}, u32[]{:S(2)}) collective-permute-start(bf16[528,640]{1,0:T(8,128)(2,1)S(1)} %pad_maximum_fusion.refs_0_), channel_id=1, source_target_pairs={{0,2},{2,4},{4,6},{6,0},{1,3},{3,5},{5,7},{7,1},{8,10},{10,12},{12... | collective-permute-start | bytes 2027528 | tf_op jit(solution)/shard_map/ppermute | solution.py:27
  13.4 19.7 %all-to-all-start = ((f32[32,1,128]{2,1,0:T(1,128)}), f32[32,1,128]{2,1,0:T(1,128)S(1)}, u32[]{:S(2)}, u32[]{:S(2)}) async-start(f32[32,1,128]{2,1,0:T(1,128)} %local.1), calls=%async_computation | async-start | bytes 32768 | tf_op jit(solution)/shard_map/all_to_all | solution.py:414
  24.6 14.5 %collective-permute-start.3 = (bf16[528,640]{1,0:T(8,128)(2,1)S(1)}, bf16[528,640]{1,0:T(8,128)(2,1)S(1)}, u32[]{:S(2)}, u32[]{:S(2)}) collective-permute-start(bf16[528,640]{1,0:T(8,128)(2,1)S(1)} %pad_maximum_fusion.refs_0_), channel_id=1, source_target_pairs={{0,1},{1,0},{2,3},{3,2},{4,5},{5,4},{6,7},{7,6},{8,9},{9,8},{10,11... | collective-permute-start | bytes 2027528 | tf_op jit(solution)/shard_map/ppermute | solution.py:27
  33.1 16.7 %copy-start.11 = (f32[32,1,128]{2,1,0:T(1,128)}, f32[32,1,128]{2,1,0:T(1,128)S(1)}, u32[]{:S(2)}) copy-start(f32[32,1,128]{2,1,0:T(1,128)S(1)} %all-to-all-done.sums_ref) | copy-start | bytes 49156
  33.1 6.1 %copy-start.3 = (bf16[528,640]{1,0:T(8,128)(2,1)}, bf16[528,640]{1,0:T(8,128)(2,1)S(1)}, u32[]{:S(2)}) copy-start(bf16[528,640]{1,0:T(8,128)(2,1)S(1)} %collective-permute-done.1.refs_4_) | copy-start | bytes 2027524
  33.1 6.1 %copy-start.2 = (bf16[528,640]{1,0:T(8,128)(2,1)}, bf16[528,640]{1,0:T(8,128)(2,1)S(1)}, u32[]{:S(2)}) copy-start(bf16[528,640]{1,0:T(8,128)(2,1)S(1)} %collective-permute-done.refs_2_) | copy-start | bytes 2027524
  34.8 4.4 %collective-permute-start.4 = (bf16[528,640]{1,0:T(8,128)(2,1)S(1)}, bf16[528,640]{1,0:T(8,128)(2,1)S(1)}, u32[]{:S(2)}, u32[]{:S(2)}) collective-permute-start(bf16[528,640]{1,0:T(8,128)(2,1)S(1)} %collective-permute-done.refs_2_), channel_id=1, source_target_pairs={{0,1},{1,0},{2,3},{3,2},{4,5},{5,4},{6,7},{7,6},{8,9},{9,8},{10,11... | collective-permute-start | bytes 2027528 | tf_op jit(solution)/shard_map/ppermute | solution.py:27
  34.8 4.4 %collective-permute-start.5 = (bf16[528,640]{1,0:T(8,128)(2,1)S(1)}, bf16[528,640]{1,0:T(8,128)(2,1)}, u32[]{:S(2)}, u32[]{:S(2)}) collective-permute-start(bf16[528,640]{1,0:T(8,128)(2,1)S(1)} %collective-permute-done.1.refs_4_), channel_id=1, source_target_pairs={{0,1},{1,0},{2,3},{3,2},{4,5},{5,4},{6,7},{7,6},{8,9},{9,8},{10,11... | collective-permute-start | bytes 2027528 | tf_op jit(solution)/shard_map/ppermute | solution.py:27
  35.3 14.6 %collective-permute-start.2 = (bf16[272,640]{1,0:T(8,128)(2,1)}, bf16[272,640]{1,0:T(8,128)(2,1)}, u32[]{:S(2)}, u32[]{:S(2)}) collective-permute-start(bf16[272,640]{1,0:T(8,128)(2,1)} %slice.21), channel_id=1, source_target_pairs={{0,2},{2,4},{4,6},{6,0},{1,3},{3,5},{5,7},{7,1},{8,10},{10,12},{12... | collective-permute-start | bytes 1044488 | tf_op jit(solution)/shard_map/ppermute | solution.py:27
  35.9 14.6 %collective-permute-start.6 = (bf16[256,640]{1,0:T(8,128)(2,1)}, bf16[256,640]{1,0:T(8,128)(2,1)}, u32[]{:S(2)}, u32[]{:S(2)}) collective-permute-start(bf16[256,640]{1,0:T(8,128)(2,1)} %slice.22), channel_id=1, source_target_pairs={{0,6},{2,0},{4,2},{6,4},{1,7},{3,1},{5,3},{7,5},{8,14},{10,8},{12,... | collective-permute-start | bytes 983048 | tf_op jit(solution)/shard_map/ppermute | solution.py:27
  39.2 11.4 %copy-start.13 = (s32[2,256]{1,0:T(2,128)S(1)}, s32[2,256]{1,0:T(2,128)}, u32[]{:S(2)}) copy-start(s32[2,256]{1,0:T(2,128)} %param.12) | copy-start | bytes 6148
  39.2 0.9 copy-start.4
  39.2 1.1 copy-start.5
  49.9 6.6 %collective-permute-start.7 = (bf16[272,640]{1,0:T(8,128)(2,1)}, bf16[272,640]{1,0:T(8,128)(2,1)S(1)}, u32[]{:S(2)}, u32[]{:S(2)}) collective-permute-start(bf16[272,640]{1,0:T(8,128)(2,1)} %collective-permute-done.2.refs_0_), channel_id=1, source_target_pairs={{0,1},{1,0},{2,3},{3,2},{4,5},{5,4},{6,7},{7,6},{8,9},{9,8},{10,11... | collective-permute-start | bytes 1044488 | tf_op jit(solution)/shard_map/ppermute | solution.py:27
  50.0 41.3 %collective-permute-start.10 = (bf16[512,5120]{1,0:T(8,128)(2,1)}, bf16[512,5120]{1,0:T(8,128)(2,1)}, u32[]{:S(2)}, u32[]{:S(2)}) collective-permute-start(bf16[512,5120]{1,0:T(8,128)(2,1)} %head.1), channel_id=1, source_target_pairs={{0,1},{1,0},{2,3},{3,2},{4,5},{5,4},{6,7},{7,6},{8,9},{9,8},{10,11... | collective-permute-start | bytes 15728648 | tf_op jit(solution)/shard_map/ppermute | solution.py:27
  50.5 6.0 %collective-permute-start.8 = (bf16[256,640]{1,0:T(8,128)(2,1)}, bf16[256,640]{1,0:T(8,128)(2,1)S(1)}, u32[]{:S(2)}, u32[]{:S(2)}) collective-permute-start(bf16[256,640]{1,0:T(8,128)(2,1)} %collective-permute-done.6.refs_1_), channel_id=1, source_target_pairs={{0,1},{1,0},{2,3},{3,2},{4,5},{5,4},{6,7},{7,6},{8,9},{9,8},{10,11... | collective-permute-start | bytes 983048 | tf_op jit(solution)/shard_map/ppermute | solution.py:27
  56.5 0.7 copy-start.10
  56.5 0.8 copy-start.9
  57.4 9.6 %copy-start.14 = (f32[2,256]{1,0:T(2,128)S(1)}, f32[2,256]{1,0:T(2,128)}, u32[]{:S(2)}) copy-start(f32[2,256]{1,0:T(2,128)} %param.14) | copy-start | bytes 6148
  63.5 9.4 %all-to-all-start.1 = ((f32[8,8,512]{2,1,0:T(8,128)}), f32[8,8,512]{2,1,0:T(8,128)S(1)}, u32[]{:S(2)}, u32[]{:S(2)}) async-start(f32[8,8,512]{2,1,0:T(8,128)} %get-tuple-element.49), calls=%async_computation.1 | async-start | bytes 262144 | tf_op jit(solution)/shard_map/all_to_all | solution.py:435
  66.9 76.3 %reduce-scatter.3.cloned.1.call-start = ((), (), s32[]{:S(2)}) async-start(), calls=%async_computation.6 | async-start | bytes 2949120 | tf_op jit(solution)/shard_map/reduce_scatter | solution.py:441
  72.9 0.7 copy-start.8
  85.2 3.9 %copy-start.6 = (bf16[512,512]{1,0:T(8,128)(2,1)S(1)}, bf16[512,512]{1,0:T(8,128)(2,1)}, u32[]{:S(2)}) copy-start(bf16[512,512]{1,0:T(8,128)(2,1)} %get-tuple-element.56.dl) | copy-start | bytes 1572868
  85.2 53.5 %all-to-all-start.2 = ((bf16[4,8,160,256]{3,2,1,0:T(8,128)(2,1)}), bf16[4,8,160,256]{3,2,1,0:T(8,128)(2,1)S(1)}, u32[]{:S(2)}, u32[]{:S(2)}) async-start(bf16[4,8,160,256]{3,2,1,0:T(8,128)(2,1)} %get-tuple-element.55), calls=%async_computation.2 | async-start | bytes 5242880 | tf_op jit(solution)/shard_map/all_to_all | solution.py:442
  89.0 91.8 %reduce-scatter.5.cloned.1.call-start = ((), (), s32[]{:S(2)}) async-start(), calls=%async_computation.7 | async-start | bytes 409600 | tf_op jit(solution)/shard_map/reduce_scatter | solution.py:452
  89.1 2.2 %collective-permute-start.9 = (bf16[512,512]{1,0:T(8,128)(2,1)S(1)}, bf16[512,512]{1,0:T(8,128)(2,1)S(1)}, u32[]{:S(2)}, u32[]{:S(2)}) collective-permute-start(bf16[512,512]{1,0:T(8,128)(2,1)S(1)} %copy-done.6), channel_id=1, source_target_pairs={{0,1},{1,0},{2,3},{3,2},{4,5},{5,4},{6,7},{7,6},{8,9},{9,8},{10,11... | collective-permute-start | bytes 1572872 | tf_op jit(solution)/shard_map/ppermute | solution.py:27
  91.3 0.8 copy-start.7
  102.3 56.6 %copy-start.12 = (bf16[640]{0:T(1024)(128)(2,1)S(1)}, bf16[640]{0:T(1024)(128)(2,1)}, u32[]{:S(2)}) copy-start(bf16[640]{0:T(1024)(128)(2,1)} %param.10) | copy-start | bytes 3844
  103.1 5.3 %collective-permute-start.11 = (f32[2,6,128]{2,1,0:T(8,128)S(1)}, f32[2,6,128]{2,1,0:T(8,128)S(1)}, u32[]{:S(2)}, u32[]{:S(2)}) collective-permute-start(f32[2,6,128]{2,1,0:T(8,128)S(1)} %reshape.33), channel_id=1, source_target_pairs={{0,2},{2,0},{4,6},{6,4},{1,3},{3,1},{5,7},{7,5},{8,10},{10,8},{12,... | collective-permute-start | bytes 18440 | tf_op jit(solution)/shard_map/ppermute | solution.py:37
  104.3 62.2 %collective-permute-start.18 = (bf16[512,640]{1,0:T(8,128)(2,1)}, bf16[512,640]{1,0:T(8,128)(2,1)S(1)}, u32[]{:S(2)}, u32[]{:S(2)}) collective-permute-start(bf16[512,640]{1,0:T(8,128)(2,1)} %get-tuple-element.66), channel_id=1, source_target_pairs={{0,6},{2,0},{4,2},{6,4},{1,7},{3,1},{5,3},{7,5},{8,14},{10,8},{12,... | collective-permute-start | bytes 1966088 | tf_op jit(solution)/shard_map/ppermute | solution.py:27
  105.2 61.3 %collective-permute-start.19 = (bf16[512,640]{1,0:T(8,128)(2,1)}, bf16[512,640]{1,0:T(8,128)(2,1)}, u32[]{:S(2)}, u32[]{:S(2)}) collective-permute-start(bf16[512,640]{1,0:T(8,128)(2,1)} %get-tuple-element.67), channel_id=1, source_target_pairs={{0,2},{2,4},{4,6},{6,0},{1,3},{3,5},{5,7},{7,1},{8,10},{10,12},{12... | collective-permute-start | bytes 1966088 | tf_op jit(solution)/shard_map/ppermute | solution.py:27
  106.4 60.1 %collective-permute-start.20 = (bf16[512,640]{1,0:T(8,128)(2,1)}, bf16[512,640]{1,0:T(8,128)(2,1)}, u32[]{:S(2)}, u32[]{:S(2)}) collective-permute-start(bf16[512,640]{1,0:T(8,128)(2,1)} %get-tuple-element.68), channel_id=1, source_target_pairs={{0,4},{2,6},{4,0},{6,2},{1,5},{3,7},{5,1},{7,3},{8,12},{10,14},{12... | collective-permute-start | bytes 1966088 | tf_op jit(solution)/shard_map/ppermute | solution.py:27
  108.4 28.6 %collective-permute-start.12 = (f32[6,128]{1,0:T(8,128)S(1)}, f32[6,128]{1,0:T(8,128)S(1)}, u32[]{:S(2)}, u32[]{:S(2)}) collective-permute-start(f32[6,128]{1,0:T(8,128)S(1)} %slice_bitcast_fusion), channel_id=1, source_target_pairs={{0,4},{2,6},{4,0},{6,2},{1,5},{3,7},{5,1},{7,3},{8,12},{10,14},{12... | collective-permute-start | bytes 9224 | tf_op jit(solution)/shard_map/ppermute | solution.py:37
  137.1 6.1 %collective-permute-start.13 = (f32[6,128]{1,0:T(8,128)S(1)}, f32[6,128]{1,0:T(8,128)S(1)}, u32[]{:S(2)}, u32[]{:S(2)}) collective-permute-start(f32[6,128]{1,0:T(8,128)S(1)} %fusion), channel_id=1, source_target_pairs={{0,8},{8,0},{16,24},{24,16},{1,9},{9,1},{17,25},{25,17},{2,10},{10... | collective-permute-start | bytes 9224 | tf_op jit(solution)/shard_map/ppermute | solution.py:37
  138.7 1.5 copy-start
  143.2 5.2 %collective-permute-start.14 = (f32[6,128]{1,0:T(8,128)S(1)}, f32[6,128]{1,0:T(8,128)S(1)}, u32[]{:S(2)}, u32[]{:S(2)}) collective-permute-start(f32[6,128]{1,0:T(8,128)S(1)} %add.46), channel_id=1, source_target_pairs={{0,16},{8,24},{16,0},{24,8},{1,17},{9,25},{17,1},{25,9},{2,18},{10... | collective-permute-start | bytes 9224 | tf_op jit(solution)/shard_map/ppermute | solution.py:37
  148.4 3.6 %collective-permute-start.15 = (f32[6,128]{1,0:T(8,128)S(1)}, f32[6,128]{1,0:T(8,128)S(1)}, u32[]{:S(2)}, u32[]{:S(2)}) collective-permute-start(f32[6,128]{1,0:T(8,128)S(1)} %add.47), channel_id=1, source_target_pairs={{0,32},{32,0},{64,96},{96,64},{128,160},{160,128},{192,224},{224,1... | collective-permute-start | bytes 9224 | tf_op jit(solution)/shard_map/ppermute | solution.py:31
  152.0 3.6 %collective-permute-start.16 = (f32[6,128]{1,0:T(8,128)S(1)}, f32[6,128]{1,0:T(8,128)S(1)}, u32[]{:S(2)}, u32[]{:S(2)}) collective-permute-start(f32[6,128]{1,0:T(8,128)S(1)} %add.48), channel_id=1, source_target_pairs={{0,224},{32,64},{64,32},{96,128},{128,96},{160,192},{192,160},{224... | collective-permute-start | bytes 9224 | tf_op jit(solution)/shard_map/ppermute | solution.py:31
  155.6 9.8 %collective-permute-start.17 = (f32[6,128]{1,0:T(8,128)S(1)}, f32[6,128]{1,0:T(8,128)S(1)}, u32[]{:S(2)}, u32[]{:S(2)}) collective-permute-start(f32[6,128]{1,0:T(8,128)S(1)} %add.49), channel_id=1, source_target_pairs={{0,96},{32,192},{64,160},{96,0},{128,224},{160,64},{192,32},{224,1... | collective-permute-start | bytes 9224 | tf_op jit(solution)/shard_map/ppermute | solution.py:31
  159.5 21.3 %all-to-all-start.3 = ((bf16[8,160,256]{2,1,0:T(8,128)(2,1)}), bf16[8,160,256]{2,1,0:T(8,128)(2,1)}, u32[]{:S(2)}, u32[]{:S(2)}) async-start(bf16[8,160,256]{2,1,0:T(8,128)(2,1)} %sum_x.1), calls=%async_computation.4 | async-start | bytes 1310720 | tf_op jit(solution)/shard_map/all_to_all | solution.py:451
  166.5 0.9 copy-start.15
Sparse Core Ops, SparseCore 0:
  85.3 40.6 reduce-scatter.2
  159.6 21.1 reduce-scatter.4

commit v6 on v5

--- a/solution.py
+++ b/solution.py
@@ -31,10 +31,6 @@
     return lax.ppermute(
         value, "z", [(i, (i + (step if i % 2 == 0 else -step)) % 8) for i in range(8)]
     )
-
-
-def across(value, axis, bit):
-    return lax.ppermute(value, axis, [(i, i ^ bit) for i in range(SIZES[axis])])
 
 
 def params(limit=60 << 20):
@@ -242,7 +238,7 @@
     )(at, *scalars, sums, stats, logits, inv, targets, old_logp)
 
 
-def back_kernel(at, dl, dl_o, early, late, small, head, head_o, u0, u1, u2, u3, stay, go):
+def back_kernel(at, dl, dl_o, early, late, small, head, head_o, u0, u1, u2, u3, lines):
     j = pl.program_id(0)
     total = jnp.dot(dl[...], head[...], preferred_element_type=f32)
     total += jnp.dot(dl_o[...], head_o[...], preferred_element_type=f32)
@@ -257,20 +253,12 @@
     line = jnp.concatenate(
         [jnp.sum(total * scaled, axis=0, keepdims=True), jnp.broadcast_to(loss, (1, 128))], axis=1
     )
-    apart = at[8 + j] ^ at[1]
-
-    @pl.when(apart % 2 == 0)
-    def _():
-        stay[apart // 2] = line
-
-    @pl.when(apart % 2 == 1)
-    def _():
-        go[apart // 2] = line
+    lines[j] = line
 
 
 def back_of(at, dl, dl_o, early, late, small, head, head_o, cols):
     rows, half = dl.shape
-    shapes = [like((rows, cols))] * 4 + [like((2, 1, cols + 128), f32)] * 2
+    shapes = [like((rows, cols))] * 4 + [like((4, 1, cols + 128), f32)]
     return pl.pallas_call(
         back_kernel,
         out_shape=shapes,
@@ -422,7 +410,6 @@
         at, 0, [(payload, own_o), (prev, prev_o), (following, following_o)], head
     )
     far_a, far_b = after(far_a, acc), after(far_b, acc)
-    head_o = shift(after(head, acc), "c", 1)
     far_a_o, far_b_o = shift(far_a, "c", 1), shift(far_b, "c", 1)
 
     slots_all = rows * lax.axis_size(DP)
@@ -432,6 +419,7 @@
     late, logits, stats, inv = logits_of(
         at, 3, [(far_a, far_b, far_a_o, far_b_o)], head, (acc, sq), targets
     )
+    head_o = shift(after(head, logits), "c", 1)
     all_stats = lax.all_to_all(stats, FSDP, 0, 0, tiled=True)
     dl, small = policy_of(groups_all, slots_all, at, scalars, sums, all_stats, logits, inv, targets, old_logp)
     part, half = cols // 4, dl.shape[1] // 2
@@ -440,10 +428,16 @@
     to_x, to_z = heads_of(at, early, late, dl)
     half_z = lax.psum_scatter(to_z, "z", scatter_dimension=0, tiled=False)
     from_x = lax.all_to_all(to_x, "x", 0, 0, tiled=True)
-    u0, u1, u2, u3, stay, go = back_of(
+    u0, u1, u2, u3, lines = back_of(
         at, after(dl, to_x), dl_o, early, late, small, head, head_o, cols
     )
+    tail = lines[0] + shift(lines[1], "y", -1) + shift(lines[2], "y", 1) + shift(lines[3], "y", 2)
+    u1, u2, u3, tail = lax.optimization_barrier((u1, u2, u3, tail))
     u1, u2, u3 = shift(u1, "y", -1), shift(u2, "y", 1), shift(u3, "y", 2)
+
+    for step in (1, -1, 3):
+        tail = tail + turn(tail, step)
+    from_x = after(from_x, tail)
 
     to_z = sum_first(from_x, "sum_x")
     half_z = after(half_z, to_z)
@@ -459,13 +453,8 @@
         "final",
         200 * 10**9,
     )
-    stay, go = stay.reshape(2, -1, 128), go.reshape(2, -1, 128)
-    tail = stay + across(go, "y", 1)
-    tail = tail[0] + across(tail[1], "y", 2)
-    tail = after(tail + across(tail, "x", 1), to_z)
-    tail = tail + across(tail, "x", 2)
-    for step in (1, -1, 3):
-        tail = tail + turn(tail, step)
+    tail = after(tail, grad_hidden)
+    tail = tail + shift(tail, "x", 1) + shift(tail, "x", 2) + shift(tail, "x", -1)
     (grad_head_t,) = simple(
         join_kernel,
         [like((part, 2 * half), f32)],

time: 191 us -> 162 us (0.85)
  waiting for transfers between devices: 65.7 us -> 37.7 us
    ppermute x4 -> x0, waiting for transfers between devices: 29.5 us -> none  [across(): return lax.ppermute(value, axis, [(i, i ^ bit) for i in range(SIZES[axis])])]
    reduce_scatter x1, waiting for transfers between devices: 10.1 us -> 0.01 us  [body(): half_z = lax.psum_scatter(half_z, 'x', scatter_dimension=0, tiled=False)]
    ppermute x14 -> x20, waiting for transfers between devices: 7.29 us -> 15.9 us  [shift(): return lax.ppermute(value, axis, [(i, (i + step) % n) for i in range(n)])]
    ppermute x4 -> x0, starting transfers between devices: 6.46 us -> none  [across(): return lax.ppermute(value, axis, [(i, i ^ bit) for i in range(SIZES[axis])])]
    ppermute x14 -> x20, starting transfers between devices: 12 us -> 18 us  [shift(): return lax.ppermute(value, axis, [(i, (i + step) % n) for i in range(n)])]
    ppermute x3, waiting for transfers between devices: 4.91 us -> 7.88 us  [turn(): lax.ppermute(value, 'z', [(i, (i + (step if i % 2 == 0 else -step)) % 8)...]
    unnamed x36 -> x40, local copies, waits for them, and re-layouts: 6.82 us -> 6.06 us
  transfers between devices with their start and end apart: 27 -> 29, of which waited for: 9 -> 13; matrix products, arithmetic and copies ran while one was open for 3% -> 4% of each run, Pallas kernels for 24% -> 24%
where the time goes in v6:
time: 162 us; the launch traced here: 161 us
  starting transfers between devices  47.8 us (30%)
  Pallas kernels  46.9 us (29%)
  waiting for transfers between devices  37.7 us (23%)
  between operations  14.3 us (9%)
  local copies, waits for them, and re-layouts  10.8 us (7%)
  other arithmetic  3.05 us (2%)
    ppermute x20, starting transfers between devices, shift(): return lax.ppermute(value, axis, [(i, (i + step) % n) for i in range(n)])  18 us
    ppermute x20, waiting for transfers between devices, shift(): return lax.ppermute(value, axis, [(i, (i + step) % n) for i in range(n)])  15.9 us
    pallas_call x2, Pallas kernels, logits_of(): pl.pallas_call(functools.partial(logits_kernel, count, per, last), out_sh...  15.7 us
    all_to_all x1, starting transfers between devices, body(): sums = lax.all_to_all(local, DP, 0, 0, tiled=True)  11.2 us
    pallas_call x1, Pallas kernels, back_of(): pl.pallas_call(back_kernel, out_shape=shapes, grid_spec=pltpu.PrefetchSca...  10.1 us
    pallas_call x1, Pallas kernels, heads_of(): pl.pallas_call(heads_kernel, out_shape=shapes, grid_spec=pltpu.PrefetchSc...  8.8 us
    all_to_all x1, waiting for transfers between devices, body(): sums = lax.all_to_all(local, DP, 0, 0, tiled=True)  8.38 us
    ppermute x3, waiting for transfers between devices, turn(): lax.ppermute(value, 'z', [(i, (i + (step if i % 2 == 0 else -step)) % 8)...  7.88 us
  transfers between devices with their start and end apart: 29, of which 13 were waited for; matrix products, arithmetic and copies ran while one was open for 4% of the time, Pallas kernels for 24%

profile of v6, /device:TPU:32, one launch (start us, length us, event | category | flops | bytes accessed | tf_op | source)
XLA Modules:
  0.0 160.5 jit_solution(1507618475591290520)
XLA Ops:
  7.2 0.7 broadcast_in_dim.8
  7.9 1.1 pad_maximum_fusion.refs_0_
  9.0 3.1 %collective-permute-start.1 = (bf16[528,640]{1,0:T(8,128)(2,1)S(1)}, bf16[528,640]{1,0:T(8,128)(2,1)S(1)}, u32[]{:S(2)}, u32[]{:S(2)}) collective-permute-start(bf16[528,640]{1,0:T(8,128)(2,1)S(1)} %pad_maximum_fusion.refs_0_), channel_id=1, source_target_pairs={{0,6},{2,0},{4,2},{6,4},{1,7},{3,1},{5,3},{7,5},{8,14},{10,8},{12,... | collective-permute-start | bytes 2027528 | tf_op jit(solution)/shard_map/ppermute | solution.py:27
  12.1 1.3 local.1
  13.4 11.2 %all-to-all-start = ((f32[32,1,128]{2,1,0:T(1,128)}), f32[32,1,128]{2,1,0:T(1,128)S(1)}, u32[]{:S(2)}, u32[]{:S(2)}) async-start(f32[32,1,128]{2,1,0:T(1,128)} %local.1), calls=%async_computation | async-start | bytes 32768 | tf_op jit(solution)/shard_map/all_to_all | solution.py:402
  24.7 8.4 %all-to-all-done.sums_ref = f32[32,1,128]{2,1,0:T(1,128)S(1)} async-done(((f32[32,1,128]{2,1,0:T(1,128)}), f32[32,1,128]{2,1,0:T(1,128)S(1)}, u32[]{:S(2)}, u32[]{:S(2)}) %all-to-all-start) | async-done | bytes 16416 | tf_op jit(solution)/shard_map/all_to_all | solution.py:402
  33.1 0.8 slice.29
  33.9 0.8 slice.28
  35.8 2.7 %collective-permute-start.6 = (bf16[256,640]{1,0:T(8,128)(2,1)}, bf16[256,640]{1,0:T(8,128)(2,1)}, u32[]{:S(2)}, u32[]{:S(2)}) collective-permute-start(bf16[256,640]{1,0:T(8,128)(2,1)} %slice.29), channel_id=1, source_target_pairs={{0,6},{2,0},{4,2},{6,4},{1,7},{3,1},{5,3},{7,5},{8,14},{10,8},{12,... | collective-permute-start | bytes 983048 | tf_op jit(solution)/shard_map/ppermute | solution.py:27
  38.5 0.7 concatenate.6.at
  39.2 0.8 copy-done.4
  40.3 9.5 %logits_first.1 = (bf16[3,512,1280]{2,1,0:T(8,128)(2,1)}, f32[512,512]{1,0:T(8,128)}, f32[8,512]{1,0:T(8,128)}) custom-call(s32[12]{0:T(128)} %concatenate.6.at, bf16[528,640]{1,0:T(8,128)(2,1)} %copy-done.1, bf16[528,640]{1,0:T(8,128)(2,1)} %copy-done.4, bf16[528,640]{1,0:T(8,128)(2,1)} %copy-done.2, bf16[528,640]{1,0:T(8,128)(2,1)} %copy-done.5, ...), custom_call_target="tpu_custom_call" | custom-call | flops 1000 | bytes 1000 | tf_op jit(solution)/shard_map/logits_first/pallas_call | solution.py:163
  51.0 1.2 collective-permute-done.8.refs_3_
  52.3 0.7 copy-done.10
  53.1 6.1 %logits_last.1 = (bf16[1,512,1280]{2,1,0:T(8,128)(2,1)}, f32[512,512]{1,0:T(8,128)}, f32[8,8,512]{2,1,0:T(8,128)}, f32[8,512]{1,0:T(8,128)}) custom-call(s32[12]{0:T(128)} %concatenate.6.at, bf16[272,640]{1,0:T(8,128)(2,1)} %collective-permute-done.2.refs_0_, bf16[256,640]{1,0:T(8,128)(2,1)} %collective-permute-done.6.refs_1_, bf16[272,640]{1,0:T(8,128)(2,1)} %copy-done.9, ...), custom_call_target="tpu_custom_call" | custom-call | flops 1000 | bytes 1000 | tf_op jit(solution)/shard_map/logits_last/pallas_call | solution.py:163
  59.5 3.4 %all-to-all-start.1 = ((f32[8,8,512]{2,1,0:T(8,128)}), f32[8,8,512]{2,1,0:T(8,128)S(1)}, u32[]{:S(2)}, u32[]{:S(2)}) async-start(f32[8,8,512]{2,1,0:T(8,128)} %get-tuple-element.53), calls=%async_computation.1 | async-start | bytes 262144 | tf_op jit(solution)/shard_map/all_to_all | solution.py:423
  63.5 5.4 %all-to-all-done.1.st = f32[8,8,512]{2,1,0:T(8,128)S(1)} async-done(((f32[8,8,512]{2,1,0:T(8,128)}), f32[8,8,512]{2,1,0:T(8,128)S(1)}, u32[]{:S(2)}, u32[]{:S(2)}) %all-to-all-start.1) | async-done | bytes 131104 | tf_op jit(solution)/shard_map/all_to_all | solution.py:423
  69.6 2.8 %policy.1 = (bf16[512,512]{1,0:T(8,128)(2,1)}, f32[8,512]{1,0:T(8,128)}) custom-call(s32[12]{0:T(128)} %concatenate.6.at, f32[2]{0:T(128)} %rewards.3, s32[2]{0:T(128)} %lengths.3, s32[2]{0:T(128)} %slots.3, f32[32,1,128]{2,1,0:T(1,128)} %copy-done.11, f32[8,8,512]{2,1,0:T(8,128)} %copy-done.8, f32[512,512]{1,0:T(8,128)} %get-tuple-element.54.lg, ...), custom_call_target="tpu_custom_call" | custom-call | flops 2097152 | bytes 1572864 | tf_op jit(solution)/shard_map/policy/pallas_call | solution.py:230
  72.4 8.8 %heads.1 = (bf16[4,8,160,256]{3,2,1,0:T(8,128)(2,1)}, bf16[8,4,160,256]{3,2,1,0:T(8,128)(2,1)}) custom-call(s32[12]{0:T(128)} %concatenate.6.at, bf16[3,512,1280]{2,1,0:T(8,128)(2,1)} %get-tuple-element.57.early, bf16[1,512,1280]{2,1,0:T(8,128)(2,1)} %get-tuple-element.58.late, bf16[512,512]{1,0:T(8,128)(2,1)} %get-tuple-element.60.dl), custom_call_target="tpu_custom_call" | custom-call | flops 2684354560 | bytes 15728640 | tf_op jit(solution)/shard_map/heads/pallas_call | solution.py:304
  81.2 3.8 %all-to-all-start.2 = ((bf16[4,8,160,256]{3,2,1,0:T(8,128)(2,1)}), bf16[4,8,160,256]{3,2,1,0:T(8,128)(2,1)S(1)}, u32[]{:S(2)}, u32[]{:S(2)}) async-start(bf16[4,8,160,256]{3,2,1,0:T(8,128)(2,1)} %get-tuple-element.59), calls=%async_computation.2 | async-start | bytes 5242880 | tf_op jit(solution)/shard_map/all_to_all | solution.py:430
  85.4 1.9 %collective-permute-done.9.dl_o = bf16[512,512]{1,0:T(8,128)(2,1)S(1)} collective-permute-done((bf16[512,512]{1,0:T(8,128)(2,1)S(1)}, bf16[512,512]{1,0:T(8,128)(2,1)S(1)}, u32[]{:S(2)}, u32[]{:S(2)}) %collective-permute-start.9) | collective-permute-done | bytes 524320 | tf_op jit(solution)/shard_map/ppermute | solution.py:27
  87.3 0.8 copy-done.7
  88.1 10.1 %back.1 = (bf16[512,640]{1,0:T(8,128)(2,1)}, bf16[512,640]{1,0:T(8,128)(2,1)}, bf16[512,640]{1,0:T(8,128)(2,1)}, bf16[512,640]{1,0:T(8,128)(2,1)}, f32[4,1,768]{2,1,0:T(1,128)}) custom-call(s32[12]{0:T(128)} %concatenate.6.at, bf16[512,512]{1,0:T(8,128)(2,1)} %get-tuple-element.60.dl, bf16[512,512]{1,0:T(8,128)(2,1)} %copy-done.7, ...), custom_call_target="tpu_custom_call" | custom-call | flops 2684354560 | bytes 10485760 | tf_op jit(solution)/shard_map/back/pallas_call | solution.py:262
  98.2 0.7 slice_bitcast_fusion.2
  98.9 1.1 collective-permute-start.11
  100.0 1.3 collective-permute-start.13
  101.3 1.2 collective-permute-done.11
  102.5 2.6 %collective-permute-done.13 = f32[1,768]{1,0:T(1,128)S(1)} collective-permute-done((f32[1,768]{1,0:T(1,128)S(1)}, f32[1,768]{1,0:T(1,128)S(1)}, u32[]{:S(2)}, u32[]{:S(2)}) %collective-permute-start.13) | collective-permute-done | bytes 3104 | tf_op jit(solution)/shard_map/ppermute | solution.py:27
  105.1 1.0 collective-permute-done.12
  106.2 0.7 fusion.1
  106.8 1.1 collective-permute-start.17
  107.9 1.0 collective-permute-start.18
  108.9 1.0 collective-permute-start.19
  109.9 1.6 %collective-permute-start.14 = (f32[1,768]{1,0:T(1,128)S(1)}, f32[1,768]{1,0:T(1,128)S(1)}, u32[]{:S(2)}, u32[]{:S(2)}) collective-permute-start(f32[1,768]{1,0:T(1,128)S(1)} %fusion.1), channel_id=1, source_target_pairs={{0,32},{32,0},{64,96},{96,64},{128,160},{160,128},{192,224},{224,1... | collective-permute-start | bytes 9224 | tf_op jit(solution)/shard_map/ppermute | solution.py:31
  111.5 2.0 %collective-permute-done.14 = f32[1,768]{1,0:T(1,128)S(1)} collective-permute-done((f32[1,768]{1,0:T(1,128)S(1)}, f32[1,768]{1,0:T(1,128)S(1)}, u32[]{:S(2)}, u32[]{:S(2)}) %collective-permute-start.14) | collective-permute-done | bytes 3104 | tf_op jit(solution)/shard_map/ppermute | solution.py:31
  114.1 3.0 %collective-permute-done.15 = f32[1,768]{1,0:T(1,128)S(1)} collective-permute-done((f32[1,768]{1,0:T(1,128)S(1)}, f32[1,768]{1,0:T(1,128)S(1)}, u32[]{:S(2)}, u32[]{:S(2)}) %collective-permute-start.15) | collective-permute-done | bytes 3104 | tf_op jit(solution)/shard_map/ppermute | solution.py:31
  117.1 3.1 %collective-permute-start.16 = (f32[1,768]{1,0:T(1,128)S(1)}, f32[1,768]{1,0:T(1,128)S(1)}, u32[]{:S(2)}, u32[]{:S(2)}) collective-permute-start(f32[1,768]{1,0:T(1,128)S(1)} %add.54), channel_id=1, source_target_pairs={{0,96},{32,192},{64,160},{96,0},{128,224},{160,64},{192,32},{224,1... | collective-permute-start | bytes 9224 | tf_op jit(solution)/shard_map/ppermute | solution.py:31
  120.7 2.9 %collective-permute-done.16 = f32[1,768]{1,0:T(1,128)S(1)} collective-permute-done((f32[1,768]{1,0:T(1,128)S(1)}, f32[1,768]{1,0:T(1,128)S(1)}, u32[]{:S(2)}, u32[]{:S(2)}) %collective-permute-start.16) | collective-permute-done | bytes 3104 | tf_op jit(solution)/shard_map/ppermute | solution.py:31
  124.3 1.5 copy-done
  125.7 2.9 %sum_x.1 = bf16[8,160,256]{2,1,0:T(8,128)(2,1)} custom-call(bf16[4,8,160,256]{3,2,1,0:T(8,128)(2,1)} %copy-done), custom_call_target="tpu_custom_call" | custom-call | flops 1310720 | bytes 3932160 | tf_op jit(solution)/shard_map/sum_x/pallas_call | solution.py:332
  128.7 6.0 %all-to-all-start.3 = ((bf16[8,160,256]{2,1,0:T(8,128)(2,1)}), bf16[8,160,256]{2,1,0:T(8,128)(2,1)}, u32[]{:S(2)}, u32[]{:S(2)}) async-start(bf16[8,160,256]{2,1,0:T(8,128)(2,1)} %sum_x.1), calls=%async_computation.4 | async-start | bytes 1310720 | tf_op jit(solution)/shard_map/all_to_all | solution.py:445
  134.7 4.0 %collective-permute-done.18.u2 = bf16[512,640]{1,0:T(8,128)(2,1)} collective-permute-done((bf16[512,640]{1,0:T(8,128)(2,1)}, bf16[512,640]{1,0:T(8,128)(2,1)}, u32[]{:S(2)}, u32[]{:S(2)}) %collective-permute-start.18) | collective-permute-done | bytes 655392 | tf_op jit(solution)/shard_map/ppermute | solution.py:27
  138.7 3.4 %final.1 = bf16[2,256,640]{2,1,0:T(8,128)(2,1)} custom-call(bf16[512,640]{1,0:T(8,128)(2,1)} %get-tuple-element.68.u0, bf16[512,640]{1,0:T(8,128)(2,1)} %copy-done.17, bf16[512,640]{1,0:T(8,128)(2,1)} %collective-permute-done.18.u2, bf16[512,640]{1,0:T(8,128)(2,1)} %collective-permute-done.19.u3, bf16[2,256,640]{2,1,0:T(8,128)(2,1)} %h_ref.1, ...), custom_call_target="tpu_custom_call" | custom-call | flops 199999995904 | bytes 3932160 | tf_op jit(solution)/shard_map/final/pallas_call | solution.py:364
  142.1 2.9 %collective-permute-start.22 = (f32[1,768]{1,0:T(1,128)S(1)}, f32[1,768]{1,0:T(1,128)S(1)}, u32[]{:S(2)}, u32[]{:S(2)}) collective-permute-start(f32[1,768]{1,0:T(1,128)S(1)} %copy-done.14), channel_id=1, source_target_pairs={{0,24},{8,0},{16,8},{24,16},{1,25},{9,1},{17,9},{25,17},{2,26},{10... | collective-permute-start | bytes 9224 | tf_op jit(solution)/shard_map/ppermute | solution.py:27
  145.0 0.8 collective-permute-start.21
  145.8 0.9 collective-permute-start.20
  146.7 3.4 %collective-permute-done.21 = f32[1,768]{1,0:T(1,128)S(1)} collective-permute-done((f32[1,768]{1,0:T(1,128)S(1)}, f32[1,768]{1,0:T(1,128)S(1)}, u32[]{:S(2)}, u32[]{:S(2)}) %collective-permute-start.21) | collective-permute-done | bytes 3104 | tf_op jit(solution)/shard_map/ppermute | solution.py:27
  151.8 1.9 %join.1 = f32[160,512]{1,0:T(8,128)} custom-call(bf16[8,160,256]{2,1,0:T(8,128)(2,1)} %all-to-all-done.3.from_z, bf16[160,256]{1,0:T(8,128)(2,1)} %bitcast.29), custom_call_target="tpu_custom_call" | custom-call | flops 655360 | bytes 1310720 | tf_op jit(solution)/shard_map/join/pallas_call | solution.py:364
  (77 shorter events, 8.2 us)
Async XLA Ops:
  7.2 31.3 %copy-start.18 = (s32[4]{0:T(128)S(1)}, s32[4]{0:T(128)}, u32[]{:S(2)}) copy-start(s32[4]{0:T(128)} %constant.35.clone) | copy-start | bytes 52
  9.0 30.2 %copy-start.1 = (bf16[528,640]{1,0:T(8,128)(2,1)}, bf16[528,640]{1,0:T(8,128)(2,1)S(1)}, u32[]{:S(2)}) copy-start(bf16[528,640]{1,0:T(8,128)(2,1)S(1)} %pad_maximum_fusion.refs_0_) | copy-start | bytes 2027524
  9.0 24.1 %collective-permute-start.1 = (bf16[528,640]{1,0:T(8,128)(2,1)S(1)}, bf16[528,640]{1,0:T(8,128)(2,1)S(1)}, u32[]{:S(2)}, u32[]{:S(2)}) collective-permute-start(bf16[528,640]{1,0:T(8,128)(2,1)S(1)} %pad_maximum_fusion.refs_0_), channel_id=1, source_target_pairs={{0,6},{2,0},{4,2},{6,4},{1,7},{3,1},{5,3},{7,5},{8,14},{10,8},{12,... | collective-permute-start | bytes 2027528 | tf_op jit(solution)/shard_map/ppermute | solution.py:27
  12.1 21.0 %collective-permute-start = (bf16[528,640]{1,0:T(8,128)(2,1)S(1)}, bf16[528,640]{1,0:T(8,128)(2,1)S(1)}, u32[]{:S(2)}, u32[]{:S(2)}) collective-permute-start(bf16[528,640]{1,0:T(8,128)(2,1)S(1)} %pad_maximum_fusion.refs_0_), channel_id=1, source_target_pairs={{0,2},{2,4},{4,6},{6,0},{1,3},{3,5},{5,7},{7,1},{8,10},{10,12},{12... | collective-permute-start | bytes 2027528 | tf_op jit(solution)/shard_map/ppermute | solution.py:27
  13.4 19.7 %all-to-all-start = ((f32[32,1,128]{2,1,0:T(1,128)}), f32[32,1,128]{2,1,0:T(1,128)S(1)}, u32[]{:S(2)}, u32[]{:S(2)}) async-start(f32[32,1,128]{2,1,0:T(1,128)} %local.1), calls=%async_computation | async-start | bytes 32768 | tf_op jit(solution)/shard_map/all_to_all | solution.py:402
  24.6 14.5 %collective-permute-start.3 = (bf16[528,640]{1,0:T(8,128)(2,1)S(1)}, bf16[528,640]{1,0:T(8,128)(2,1)S(1)}, u32[]{:S(2)}, u32[]{:S(2)}) collective-permute-start(bf16[528,640]{1,0:T(8,128)(2,1)S(1)} %pad_maximum_fusion.refs_0_), channel_id=1, source_target_pairs={{0,1},{1,0},{2,3},{3,2},{4,5},{5,4},{6,7},{7,6},{8,9},{9,8},{10,11... | collective-permute-start | bytes 2027528 | tf_op jit(solution)/shard_map/ppermute | solution.py:27
  33.1 16.7 %copy-start.11 = (f32[32,1,128]{2,1,0:T(1,128)}, f32[32,1,128]{2,1,0:T(1,128)S(1)}, u32[]{:S(2)}) copy-start(f32[32,1,128]{2,1,0:T(1,128)S(1)} %all-to-all-done.sums_ref) | copy-start | bytes 49156
  33.1 6.1 %copy-start.3 = (bf16[528,640]{1,0:T(8,128)(2,1)}, bf16[528,640]{1,0:T(8,128)(2,1)S(1)}, u32[]{:S(2)}) copy-start(bf16[528,640]{1,0:T(8,128)(2,1)S(1)} %collective-permute-done.1.refs_4_) | copy-start | bytes 2027524
  33.1 6.1 %copy-start.2 = (bf16[528,640]{1,0:T(8,128)(2,1)}, bf16[528,640]{1,0:T(8,128)(2,1)S(1)}, u32[]{:S(2)}) copy-start(bf16[528,640]{1,0:T(8,128)(2,1)S(1)} %collective-permute-done.refs_2_) | copy-start | bytes 2027524
  34.7 4.5 %collective-permute-start.4 = (bf16[528,640]{1,0:T(8,128)(2,1)S(1)}, bf16[528,640]{1,0:T(8,128)(2,1)S(1)}, u32[]{:S(2)}, u32[]{:S(2)}) collective-permute-start(bf16[528,640]{1,0:T(8,128)(2,1)S(1)} %collective-permute-done.refs_2_), channel_id=1, source_target_pairs={{0,1},{1,0},{2,3},{3,2},{4,5},{5,4},{6,7},{7,6},{8,9},{9,8},{10,11... | collective-permute-start | bytes 2027528 | tf_op jit(solution)/shard_map/ppermute | solution.py:27
  34.7 4.5 %collective-permute-start.5 = (bf16[528,640]{1,0:T(8,128)(2,1)S(1)}, bf16[528,640]{1,0:T(8,128)(2,1)}, u32[]{:S(2)}, u32[]{:S(2)}) collective-permute-start(bf16[528,640]{1,0:T(8,128)(2,1)S(1)} %collective-permute-done.1.refs_4_), channel_id=1, source_target_pairs={{0,1},{1,0},{2,3},{3,2},{4,5},{5,4},{6,7},{7,6},{8,9},{9,8},{10,11... | collective-permute-start | bytes 2027528 | tf_op jit(solution)/shard_map/ppermute | solution.py:27
  35.2 14.6 %collective-permute-start.2 = (bf16[272,640]{1,0:T(8,128)(2,1)}, bf16[272,640]{1,0:T(8,128)(2,1)}, u32[]{:S(2)}, u32[]{:S(2)}) collective-permute-start(bf16[272,640]{1,0:T(8,128)(2,1)} %slice.28), channel_id=1, source_target_pairs={{0,2},{2,4},{4,6},{6,0},{1,3},{3,5},{5,7},{7,1},{8,10},{10,12},{12... | collective-permute-start | bytes 1044488 | tf_op jit(solution)/shard_map/ppermute | solution.py:27
  35.8 14.1 %collective-permute-start.6 = (bf16[256,640]{1,0:T(8,128)(2,1)}, bf16[256,640]{1,0:T(8,128)(2,1)}, u32[]{:S(2)}, u32[]{:S(2)}) collective-permute-start(bf16[256,640]{1,0:T(8,128)(2,1)} %slice.29), channel_id=1, source_target_pairs={{0,6},{2,0},{4,2},{6,4},{1,7},{3,1},{5,3},{7,5},{8,14},{10,8},{12,... | collective-permute-start | bytes 983048 | tf_op jit(solution)/shard_map/ppermute | solution.py:27
  39.2 11.3 %copy-start.15 = (s32[2,256]{1,0:T(2,128)S(1)}, s32[2,256]{1,0:T(2,128)}, u32[]{:S(2)}) copy-start(s32[2,256]{1,0:T(2,128)} %param.12) | copy-start | bytes 6148
  39.2 0.8 copy-start.4
  39.2 1.1 copy-start.5
  49.8 2.4 %collective-permute-start.7 = (bf16[272,640]{1,0:T(8,128)(2,1)}, bf16[272,640]{1,0:T(8,128)(2,1)S(1)}, u32[]{:S(2)}, u32[]{:S(2)}) collective-permute-start(bf16[272,640]{1,0:T(8,128)(2,1)} %collective-permute-done.2.refs_0_), channel_id=1, source_target_pairs={{0,1},{1,0},{2,3},{3,2},{4,5},{5,4},{6,7},{7,6},{8,9},{9,8},{10,11... | collective-permute-start | bytes 1044488 | tf_op jit(solution)/shard_map/ppermute | solution.py:27
  50.0 2.3 %collective-permute-start.8 = (bf16[256,640]{1,0:T(8,128)(2,1)}, bf16[256,640]{1,0:T(8,128)(2,1)S(1)}, u32[]{:S(2)}, u32[]{:S(2)}) collective-permute-start(bf16[256,640]{1,0:T(8,128)(2,1)} %collective-permute-done.6.refs_1_), channel_id=1, source_target_pairs={{0,1},{1,0},{2,3},{3,2},{4,5},{5,4},{6,7},{7,6},{8,9},{9,8},{10,11... | collective-permute-start | bytes 983048 | tf_op jit(solution)/shard_map/ppermute | solution.py:27
  52.3 0.7 copy-start.10
  52.3 0.8 copy-start.9
  53.1 9.8 %copy-start.16 = (f32[2,256]{1,0:T(2,128)S(1)}, f32[2,256]{1,0:T(2,128)}, u32[]{:S(2)}) copy-start(f32[2,256]{1,0:T(2,128)} %param.14) | copy-start | bytes 6148
  59.3 28.0 %collective-permute-start.10 = (bf16[512,5120]{1,0:T(8,128)(2,1)}, bf16[512,5120]{1,0:T(8,128)(2,1)}, u32[]{:S(2)}, u32[]{:S(2)}) collective-permute-start(bf16[512,5120]{1,0:T(8,128)(2,1)} %head.1), channel_id=1, source_target_pairs={{0,1},{1,0},{2,3},{3,2},{4,5},{5,4},{6,7},{7,6},{8,9},{9,8},{10,11... | collective-permute-start | bytes 15728648 | tf_op jit(solution)/shard_map/ppermute | solution.py:27
  59.5 9.4 %all-to-all-start.1 = ((f32[8,8,512]{2,1,0:T(8,128)}), f32[8,8,512]{2,1,0:T(8,128)S(1)}, u32[]{:S(2)}, u32[]{:S(2)}) async-start(f32[8,8,512]{2,1,0:T(8,128)} %get-tuple-element.53), calls=%async_computation.1 | async-start | bytes 262144 | tf_op jit(solution)/shard_map/all_to_all | solution.py:423
  62.9 65.8 %reduce-scatter.3.cloned.1.call-start = ((), (), s32[]{:S(2)}) async-start(), calls=%async_computation.6 | async-start | bytes 2949120 | tf_op jit(solution)/shard_map/reduce_scatter | solution.py:429
  68.9 0.7 copy-start.8
  81.2 3.9 %copy-start.6 = (bf16[512,512]{1,0:T(8,128)(2,1)S(1)}, bf16[512,512]{1,0:T(8,128)(2,1)}, u32[]{:S(2)}) copy-start(bf16[512,512]{1,0:T(8,128)(2,1)} %get-tuple-element.60.dl) | copy-start | bytes 1572868
  81.2 43.0 %all-to-all-start.2 = ((bf16[4,8,160,256]{3,2,1,0:T(8,128)(2,1)}), bf16[4,8,160,256]{3,2,1,0:T(8,128)(2,1)S(1)}, u32[]{:S(2)}, u32[]{:S(2)}) async-start(bf16[4,8,160,256]{3,2,1,0:T(8,128)(2,1)} %get-tuple-element.59), calls=%async_computation.2 | async-start | bytes 5242880 | tf_op jit(solution)/shard_map/all_to_all | solution.py:430
  85.0 66.7 %reduce-scatter.5.cloned.1.call-start = ((), (), s32[]{:S(2)}) async-start(), calls=%async_computation.7 | async-start | bytes 409600 | tf_op jit(solution)/shard_map/reduce_scatter | solution.py:446
  85.1 2.2 %collective-permute-start.9 = (bf16[512,512]{1,0:T(8,128)(2,1)S(1)}, bf16[512,512]{1,0:T(8,128)(2,1)S(1)}, u32[]{:S(2)}, u32[]{:S(2)}) collective-permute-start(bf16[512,512]{1,0:T(8,128)(2,1)S(1)} %copy-done.6), channel_id=1, source_target_pairs={{0,1},{1,0},{2,3},{3,2},{4,5},{5,4},{6,7},{7,6},{8,9},{9,8},{10,11... | collective-permute-start | bytes 1572872 | tf_op jit(solution)/shard_map/ppermute | solution.py:27
  87.3 0.8 copy-start.7
  88.1 32.1 %copy-start.12 = (bf16[640]{0:T(1024)(128)(2,1)S(1)}, bf16[640]{0:T(1024)(128)(2,1)}, u32[]{:S(2)}) copy-start(bf16[640]{0:T(1024)(128)(2,1)} %param.10) | copy-start | bytes 3844
  98.9 3.6 %collective-permute-start.11 = (f32[1,768]{1,0:T(1,128)S(1)}, f32[1,768]{1,0:T(1,128)S(1)}, u32[]{:S(2)}, u32[]{:S(2)}) collective-permute-start(f32[1,768]{1,0:T(1,128)S(1)} %get-tuple-element.80), channel_id=1, source_target_pairs={{0,6},{2,0},{4,2},{6,4},{1,7},{3,1},{5,3},{7,5},{8,14},{10,8},{12,... | collective-permute-start | bytes 9224 | tf_op jit(solution)/shard_map/ppermute | solution.py:27
  100.0 5.1 %collective-permute-start.13 = (f32[1,768]{1,0:T(1,128)S(1)}, f32[1,768]{1,0:T(1,128)S(1)}, u32[]{:S(2)}, u32[]{:S(2)}) collective-permute-start(f32[1,768]{1,0:T(1,128)S(1)} %get-tuple-element.81), channel_id=1, source_target_pairs={{0,4},{2,6},{4,0},{6,2},{1,5},{3,7},{5,1},{7,3},{8,12},{10,14},{12... | collective-permute-start | bytes 9224 | tf_op jit(solution)/shard_map/ppermute | solution.py:27
  101.3 4.8 %collective-permute-start.12 = (f32[1,768]{1,0:T(1,128)S(1)}, f32[1,768]{1,0:T(1,128)S(1)}, u32[]{:S(2)}, u32[]{:S(2)}) collective-permute-start(f32[1,768]{1,0:T(1,128)S(1)} %get-tuple-element.82), channel_id=1, source_target_pairs={{0,2},{2,4},{4,6},{6,0},{1,3},{3,5},{5,7},{7,1},{8,10},{10,12},{12... | collective-permute-start | bytes 9224 | tf_op jit(solution)/shard_map/ppermute | solution.py:27
  106.8 27.8 %collective-permute-start.17 = (bf16[512,640]{1,0:T(8,128)(2,1)}, bf16[512,640]{1,0:T(8,128)(2,1)S(1)}, u32[]{:S(2)}, u32[]{:S(2)}) collective-permute-start(bf16[512,640]{1,0:T(8,128)(2,1)} %get-tuple-element.69), channel_id=1, source_target_pairs={{0,6},{2,0},{4,2},{6,4},{1,7},{3,1},{5,3},{7,5},{8,14},{10,8},{12,... | collective-permute-start | bytes 1966088 | tf_op jit(solution)/shard_map/ppermute | solution.py:27
  107.9 30.8 %collective-permute-start.18 = (bf16[512,640]{1,0:T(8,128)(2,1)}, bf16[512,640]{1,0:T(8,128)(2,1)}, u32[]{:S(2)}, u32[]{:S(2)}) collective-permute-start(bf16[512,640]{1,0:T(8,128)(2,1)} %get-tuple-element.70), channel_id=1, source_target_pairs={{0,2},{2,4},{4,6},{6,0},{1,3},{3,5},{5,7},{7,1},{8,10},{10,12},{12... | collective-permute-start | bytes 1966088 | tf_op jit(solution)/shard_map/ppermute | solution.py:27
  108.9 29.8 %collective-permute-start.19 = (bf16[512,640]{1,0:T(8,128)(2,1)}, bf16[512,640]{1,0:T(8,128)(2,1)}, u32[]{:S(2)}, u32[]{:S(2)}) collective-permute-start(bf16[512,640]{1,0:T(8,128)(2,1)} %get-tuple-element.71), channel_id=1, source_target_pairs={{0,4},{2,6},{4,0},{6,2},{1,5},{3,7},{5,1},{7,3},{8,12},{10,14},{12... | collective-permute-start | bytes 1966088 | tf_op jit(solution)/shard_map/ppermute | solution.py:27
  109.9 3.6 %collective-permute-start.14 = (f32[1,768]{1,0:T(1,128)S(1)}, f32[1,768]{1,0:T(1,128)S(1)}, u32[]{:S(2)}, u32[]{:S(2)}) collective-permute-start(f32[1,768]{1,0:T(1,128)S(1)} %fusion.1), channel_id=1, source_target_pairs={{0,32},{32,0},{64,96},{96,64},{128,160},{160,128},{192,224},{224,1... | collective-permute-start | bytes 9224 | tf_op jit(solution)/shard_map/ppermute | solution.py:31
  113.5 3.6 %collective-permute-start.15 = (f32[1,768]{1,0:T(1,128)S(1)}, f32[1,768]{1,0:T(1,128)S(1)}, u32[]{:S(2)}, u32[]{:S(2)}) collective-permute-start(f32[1,768]{1,0:T(1,128)S(1)} %add.53), channel_id=1, source_target_pairs={{0,224},{32,64},{64,32},{96,128},{128,96},{160,192},{192,160},{224... | collective-permute-start | bytes 9224 | tf_op jit(solution)/shard_map/ppermute | solution.py:31
  117.1 6.6 %collective-permute-start.16 = (f32[1,768]{1,0:T(1,128)S(1)}, f32[1,768]{1,0:T(1,128)S(1)}, u32[]{:S(2)}, u32[]{:S(2)}) collective-permute-start(f32[1,768]{1,0:T(1,128)S(1)} %add.54), channel_id=1, source_target_pairs={{0,96},{32,192},{64,160},{96,0},{128,224},{160,64},{192,32},{224,1... | collective-permute-start | bytes 9224 | tf_op jit(solution)/shard_map/ppermute | solution.py:31
  124.3 1.5 copy-start
  128.7 23.1 %all-to-all-start.3 = ((bf16[8,160,256]{2,1,0:T(8,128)(2,1)}), bf16[8,160,256]{2,1,0:T(8,128)(2,1)}, u32[]{:S(2)}, u32[]{:S(2)}) async-start(bf16[8,160,256]{2,1,0:T(8,128)(2,1)} %sum_x.1), calls=%async_computation.4 | async-start | bytes 1310720 | tf_op jit(solution)/shard_map/all_to_all | solution.py:445
  134.7 4.0 %copy-start.17 = (bf16[512,640]{1,0:T(8,128)(2,1)}, bf16[512,640]{1,0:T(8,128)(2,1)S(1)}, u32[]{:S(2)}) copy-start(bf16[512,640]{1,0:T(8,128)(2,1)S(1)} %collective-permute-done.17.u1) | copy-start | bytes 1966084
  138.7 3.4 %copy-start.14 = (f32[1,768]{1,0:T(1,128)S(1)}, f32[1,768]{1,0:T(1,128)}, u32[]{:S(2)}) copy-start(f32[1,768]{1,0:T(1,128)} %add.55) | copy-start | bytes 9220
  138.7 12.5 %copy-start.13 = (bf16[640]{0:T(1024)(128)(2,1)S(1)}, bf16[640]{0:T(1024)(128)(2,1)}, u32[]{:S(2)}) copy-start(bf16[640]{0:T(1024)(128)(2,1)} %param.10) | copy-start | bytes 3844
  142.1 4.6 %collective-permute-start.22 = (f32[1,768]{1,0:T(1,128)S(1)}, f32[1,768]{1,0:T(1,128)S(1)}, u32[]{:S(2)}, u32[]{:S(2)}) collective-permute-start(f32[1,768]{1,0:T(1,128)S(1)} %copy-done.14), channel_id=1, source_target_pairs={{0,24},{8,0},{16,8},{24,16},{1,25},{9,1},{17,9},{25,17},{2,26},{10... | collective-permute-start | bytes 9224 | tf_op jit(solution)/shard_map/ppermute | solution.py:27
  145.0 5.1 %collective-permute-start.21 = (f32[1,768]{1,0:T(1,128)S(1)}, f32[1,768]{1,0:T(1,128)S(1)}, u32[]{:S(2)}, u32[]{:S(2)}) collective-permute-start(f32[1,768]{1,0:T(1,128)S(1)} %copy-done.14), channel_id=1, source_target_pairs={{0,16},{8,24},{16,0},{24,8},{1,17},{9,25},{17,1},{25,9},{2,18},{10... | collective-permute-start | bytes 9224 | tf_op jit(solution)/shard_map/ppermute | solution.py:27
  145.8 4.8 %collective-permute-start.20 = (f32[1,768]{1,0:T(1,128)S(1)}, f32[1,768]{1,0:T(1,128)S(1)}, u32[]{:S(2)}, u32[]{:S(2)}) collective-permute-start(f32[1,768]{1,0:T(1,128)S(1)} %copy-done.14), channel_id=1, source_target_pairs={{0,8},{8,16},{16,24},{24,0},{1,9},{9,17},{17,25},{25,1},{2,10},{10... | collective-permute-start | bytes 9224 | tf_op jit(solution)/shard_map/ppermute | solution.py:27
Sparse Core Ops, SparseCore 0:
  81.4 40.3 reduce-scatter.2
  128.8 22.8 reduce-scatter.4

commit v7 on v6

--- a/solution.py
+++ b/solution.py
@@ -183,10 +183,10 @@
     )(at, *[p for b in blocks for p in b], *extra, head)
 
 
-def policy_kernel(groups, slots_all, at, rewards, lengths, slots, sums_ref, st, lg, inv_ref, tgt, old, dl, small):
+def policy_kernel(groups, slots_all, at, rewards, lengths, slots, sum0, sum1, sum2, sum3, st, lg, inv_ref, tgt, old, dl, small):
     half = lg.shape[1]
     rows = lg.shape[0]
-    sums = jnp.sum(sums_ref[:, 0, :], axis=0, keepdims=True)
+    sums = sum0[...] + sum1[...] + sum2[...] + sum3[...]
     lane = lax.broadcasted_iota(jnp.int32, sums.shape, 1)
 
     def entry_of(k):
@@ -230,12 +230,12 @@
     return pl.pallas_call(
         functools.partial(policy_kernel, groups, float(slots_all)),
         out_shape=[like((rows, half)), like((8, rows), f32)],
-        in_specs=[whole(pltpu.SMEM)] * 4 + [whole()] * 6,
+        in_specs=[whole(pltpu.SMEM)] * 4 + [whole()] * 9,
         out_specs=[whole()] * 2,
         compiler_params=params(),
         cost_estimate=cost(8 * rows * half, 6 * rows * half, rows * half),
         name="policy",
-    )(at, *scalars, sums, stats, logits, inv, targets, old_logp)
+    )(at, *scalars, *sums, stats, logits, inv, targets, old_logp)
 
 
 def back_kernel(at, dl, dl_o, early, late, small, head, head_o, u0, u1, u2, u3, lines):
@@ -394,13 +394,13 @@
     scalars = (rewards, lengths, group_slot)
     (local,) = simple(
         functools.partial(local_kernel, groups_all),
-        [like((lax.axis_size(DP), 1, 128), f32)],
+        [like((lax.axis_size("z"), 1, 128), f32)],
         scalars,
         1 << 14,
         "local",
     )
-    sums = lax.all_to_all(local, DP, 0, 0, tiled=True)
-    prev, following, sums = lax.optimization_barrier((prev, following, sums))
+    over_z = lax.all_to_all(local, "z", 0, 0, tiled=True).sum(axis=0)
+    prev, following, over_z = lax.optimization_barrier((prev, following, over_z))
 
     far_a, far_b = prev[:cut], following[cut:]
     far_a, far_b, prev, following = lax.optimization_barrier((far_a, far_b, prev, following))
@@ -420,6 +420,8 @@
         at, 3, [(far_a, far_b, far_a_o, far_b_o)], head, (acc, sq), targets
     )
     head_o = shift(after(head, logits), "c", 1)
+    over_z = after(over_z, logits)
+    sums = (over_z, shift(over_z, "x", 1), shift(over_z, "x", 2), shift(over_z, "x", -1))
     all_stats = lax.all_to_all(stats, FSDP, 0, 0, tiled=True)
     dl, small = policy_of(groups_all, slots_all, at, scalars, sums, all_stats, logits, inv, targets, old_logp)
     part, half = cols // 4, dl.shape[1] // 2
@@ -431,13 +433,12 @@
     u0, u1, u2, u3, lines = back_of(
         at, after(dl, to_x), dl_o, early, late, small, head, head_o, cols
     )
-    tail = lines[0] + shift(lines[1], "y", -1) + shift(lines[2], "y", 1) + shift(lines[3], "y", 2)
-    u1, u2, u3, tail = lax.optimization_barrier((u1, u2, u3, tail))
     u1, u2, u3 = shift(u1, "y", -1), shift(u2, "y", 1), shift(u3, "y", 2)
 
     for step in (1, -1, 3):
-        tail = tail + turn(tail, step)
-    from_x = after(from_x, tail)
+        lines = lines + turn(lines, step)
+    lines = lines + shift(lines, "x", 1) + shift(lines, "x", 2) + shift(lines, "x", -1)
+    from_x = after(from_x, lines)
 
     to_z = sum_first(from_x, "sum_x")
     half_z = after(half_z, to_z)
@@ -453,8 +454,8 @@
         "final",
         200 * 10**9,
     )
-    tail = after(tail, grad_hidden)
-    tail = tail + shift(tail, "x", 1) + shift(tail, "x", 2) + shift(tail, "x", -1)
+    lines = after(lines, grad_hidden)
+    tail = lines[0] + shift(lines[1], "y", -1) + shift(lines[2], "y", 1) + shift(lines[3], "y", 2)
     (grad_head_t,) = simple(
         join_kernel,
         [like((part, 2 * half), f32)],

time: 162 us -> 167 us (1.031)
  starting transfers between devices: 47.8 us -> 57.7 us
  waiting for transfers between devices: 37.7 us -> 32.5 us
    ppermute x20 -> x23, starting transfers between devices: 18 us -> 26.6 us  [shift(): return lax.ppermute(value, axis, [(i, (i + step) % n) for i in range(n)])]
    all_to_all x1, waiting for transfers between devices: 5.43 us -> 0.01 us  [body(): all_stats = lax.all_to_all(stats, FSDP, 0, 0, tiled=True)]
    all_to_all x1, starting transfers between devices: 11.2 us -> 8.57 us  [body(): over_z = lax.all_to_all(local, 'z', 0, 0, tiled=True).sum(axis=0)]
    ppermute x3, starting transfers between devices: 5.34 us -> 7.59 us  [turn(): lax.ppermute(value, 'z', [(i, (i + (step if i % 2 == 0 else -step)) % 8)...]
    all_to_all x1, waiting for transfers between devices: 8.38 us -> 6.15 us  [body(): over_z = lax.all_to_all(local, 'z', 0, 0, tiled=True).sum(axis=0)]
    all_to_all x1, starting transfers between devices: 5.96 us -> 7.64 us  [body(): from_z = lax.all_to_all(to_z, 'z', 0, 0, tiled=True)]
    ppermute x20 -> x23, waiting for transfers between devices: 15.9 us -> 17.3 us  [shift(): return lax.ppermute(value, axis, [(i, (i + step) % n) for i in range(n)])]
    unnamed x40 -> x46, local copies, waits for them, and re-layouts: 6.06 us -> 6.89 us
  transfers between devices with their start and end apart: 29 -> 32, of which waited for: 13 -> 15; matrix products, arithmetic and copies ran while one was open for 4% -> 4% of each run, Pallas kernels for 24% -> 23%
where the time goes in v7:
time: 167 us; the launch traced here: 165 us
  starting transfers between devices  57.7 us (35%)
  Pallas kernels  46.6 us (28%)
  waiting for transfers between devices  32.5 us (19%)
  between operations  14.3 us (9%)
  local copies, waits for them, and re-layouts  10.9 us (7%)
  other arithmetic  3.16 us (2%)
    ppermute x23, starting transfers between devices, shift(): return lax.ppermute(value, axis, [(i, (i + step) % n) for i in range(n)])  26.6 us
    ppermute x23, waiting for transfers between devices, shift(): return lax.ppermute(value, axis, [(i, (i + step) % n) for i in range(n)])  17.3 us
    pallas_call x2, Pallas kernels, logits_of(): pl.pallas_call(functools.partial(logits_kernel, count, per, last), out_sh...  15.7 us
    pallas_call x1, Pallas kernels, back_of(): pl.pallas_call(back_kernel, out_shape=shapes, grid_spec=pltpu.PrefetchSca...  9.87 us
    pallas_call x1, Pallas kernels, heads_of(): pl.pallas_call(heads_kernel, out_shape=shapes, grid_spec=pltpu.PrefetchSc...  8.8 us
    all_to_all x1, starting transfers between devices, body(): over_z = lax.all_to_all(local, 'z', 0, 0, tiled=True).sum(axis=0)  8.57 us
    ppermute x3, waiting for transfers between devices, turn(): lax.ppermute(value, 'z', [(i, (i + (step if i % 2 == 0 else -step)) % 8)...  8.09 us
    all_to_all x1, starting transfers between devices, body(): from_z = lax.all_to_all(to_z, 'z', 0, 0, tiled=True)  7.64 us
  transfers between devices with their start and end apart: 32, of which 15 were waited for; matrix products, arithmetic and copies ran while one was open for 4% of the time, Pallas kernels for 23%

profile of v7, /device:TPU:32, one launch (start us, length us, event | category | flops | bytes accessed | tf_op | source)
XLA Modules:
  0.0 165.1 jit_solution(3655368395365911523)
XLA Ops:
  7.9 1.1 pad_maximum_fusion.refs_0_
  9.0 3.1 %collective-permute-start.1 = (bf16[528,640]{1,0:T(8,128)(2,1)S(1)}, bf16[528,640]{1,0:T(8,128)(2,1)S(1)}, u32[]{:S(2)}, u32[]{:S(2)}) collective-permute-start(bf16[528,640]{1,0:T(8,128)(2,1)S(1)} %pad_maximum_fusion.refs_0_), channel_id=1, source_target_pairs={{0,6},{2,0},{4,2},{6,4},{1,7},{3,1},{5,3},{7,5},{8,14},{10,8},{12,... | collective-permute-start | bytes 2027528 | tf_op jit(solution)/shard_map/ppermute | solution.py:27
  12.1 1.3 local.1
  13.4 8.6 %all-to-all-start = ((f32[8,1,128]{2,1,0:T(1,128)}), f32[8,1,128]{2,1,0:T(1,128)S(1)}, u32[]{:S(2)}, u32[]{:S(2)}) async-start(f32[8,1,128]{2,1,0:T(1,128)} %local.1), calls=%async_computation | async-start | bytes 8192 | tf_op jit(solution)/shard_map/all_to_all | solution.py:402
  22.0 6.1 %all-to-all-done = f32[8,1,128]{2,1,0:T(1,128)S(1)} async-done(((f32[8,1,128]{2,1,0:T(1,128)}), f32[8,1,128]{2,1,0:T(1,128)S(1)}, u32[]{:S(2)}, u32[]{:S(2)}) %all-to-all-start) | async-done | bytes 4128 | tf_op jit(solution)/shard_map/all_to_all | solution.py:402
  28.2 1.8 %collective-permute-done.refs_2_ = bf16[528,640]{1,0:T(8,128)(2,1)S(1)} collective-permute-done((bf16[528,640]{1,0:T(8,128)(2,1)S(1)}, bf16[528,640]{1,0:T(8,128)(2,1)S(1)}, u32[]{:S(2)}, u32[]{:S(2)}) %collective-permute-start) | collective-permute-done | bytes 675872 | tf_op jit(solution)/shard_map/ppermute | solution.py:27
  30.0 0.8 slice.29
  30.8 0.8 slice.28
  32.0 3.2 %collective-permute-start.6 = (bf16[256,640]{1,0:T(8,128)(2,1)}, bf16[256,640]{1,0:T(8,128)(2,1)}, u32[]{:S(2)}, u32[]{:S(2)}) collective-permute-start(bf16[256,640]{1,0:T(8,128)(2,1)} %slice.29), channel_id=1, source_target_pairs={{0,6},{2,0},{4,2},{6,4},{1,7},{3,1},{5,3},{7,5},{8,14},{10,8},{12,... | collective-permute-start | bytes 983048 | tf_op jit(solution)/shard_map/ppermute | solution.py:27
  36.0 0.8 copy-done.4
  37.0 9.5 %logits_first.1 = (bf16[3,512,1280]{2,1,0:T(8,128)(2,1)}, f32[512,512]{1,0:T(8,128)}, f32[8,512]{1,0:T(8,128)}) custom-call(s32[12]{0:T(128)} %concatenate.6.at, bf16[528,640]{1,0:T(8,128)(2,1)} %copy-done.1, bf16[528,640]{1,0:T(8,128)(2,1)} %copy-done.4, bf16[528,640]{1,0:T(8,128)(2,1)} %copy-done.2, bf16[528,640]{1,0:T(8,128)(2,1)} %copy-done.5, ...), custom_call_target="tpu_custom_call" | custom-call | flops 1000 | bytes 1000 | tf_op jit(solution)/shard_map/logits_first/pallas_call | solution.py:163
  47.8 1.2 collective-permute-done.8.refs_3_
  49.8 6.1 %logits_last.1 = (bf16[1,512,1280]{2,1,0:T(8,128)(2,1)}, f32[512,512]{1,0:T(8,128)}, f32[8,8,512]{2,1,0:T(8,128)}, f32[8,512]{1,0:T(8,128)}) custom-call(s32[12]{0:T(128)} %concatenate.6.at, bf16[272,640]{1,0:T(8,128)(2,1)} %collective-permute-done.2.refs_0_, bf16[256,640]{1,0:T(8,128)(2,1)} %collective-permute-done.6.refs_1_, bf16[272,640]{1,0:T(8,128)(2,1)} %copy-done.9, ...), custom_call_target="tpu_custom_call" | custom-call | flops 1000 | bytes 1000 | tf_op jit(solution)/shard_map/logits_last/pallas_call | solution.py:163
  56.2 3.4 %all-to-all-start.1 = ((f32[8,8,512]{2,1,0:T(8,128)}), f32[8,8,512]{2,1,0:T(8,128)S(1)}, u32[]{:S(2)}, u32[]{:S(2)}) async-start(f32[8,8,512]{2,1,0:T(8,128)} %get-tuple-element.52), calls=%async_computation.1 | async-start | bytes 262144 | tf_op jit(solution)/shard_map/all_to_all | solution.py:425
  59.6 2.8 %collective-permute-start.11 = (f32[1,128]{1,0:T(1,128)S(1)}, f32[1,128]{1,0:T(1,128)S(1)}, u32[]{:S(2)}, u32[]{:S(2)}) collective-permute-start(f32[1,128]{1,0:T(1,128)S(1)} %bitcast.34), channel_id=1, source_target_pairs={{0,24},{8,0},{16,8},{24,16},{1,25},{9,1},{17,9},{25,17},{2,26},{10... | collective-permute-start | bytes 1544 | tf_op jit(solution)/shard_map/ppermute | solution.py:27
  62.5 0.8 collective-permute-start.10
  63.3 0.9 collective-permute-start.9
  64.8 2.8 %collective-permute-done.10.sum2 = f32[1,128]{1,0:T(1,128)S(1)} collective-permute-done((f32[1,128]{1,0:T(1,128)S(1)}, f32[1,128]{1,0:T(1,128)S(1)}, u32[]{:S(2)}, u32[]{:S(2)}) %collective-permute-start.10) | collective-permute-done | bytes 544 | tf_op jit(solution)/shard_map/ppermute | solution.py:27
  68.7 2.7 %policy.1 = (bf16[512,512]{1,0:T(8,128)(2,1)}, f32[8,512]{1,0:T(8,128)}) custom-call(s32[12]{0:T(128)} %concatenate.6.at, f32[2]{0:T(128)} %rewards.3, s32[2]{0:T(128)} %lengths.3, s32[2]{0:T(128)} %slots.3, f32[1,128]{1,0:T(1,128)} %bitcast.37, f32[1,128]{1,0:T(1,128)} %copy-done.19, f32[1,128]{1,0:T(1,128)} %copy-done.18, f32[1,128]{1,0:T(1,128)} %copy-done.17, ...), custom_call_target="tpu_custom_call" | custom-call | flops 2097152 | bytes 1572864 | tf_op jit(solution)/shard_map/policy/pallas_call | solution.py:230
  71.4 8.8 %heads.1 = (bf16[4,8,160,256]{3,2,1,0:T(8,128)(2,1)}, bf16[8,4,160,256]{3,2,1,0:T(8,128)(2,1)}) custom-call(s32[12]{0:T(128)} %concatenate.6.at, bf16[3,512,1280]{2,1,0:T(8,128)(2,1)} %get-tuple-element.55.early, bf16[1,512,1280]{2,1,0:T(8,128)(2,1)} %get-tuple-element.56.late, bf16[512,512]{1,0:T(8,128)(2,1)} %get-tuple-element.58.dl), custom_call_target="tpu_custom_call" | custom-call | flops 2684354560 | bytes 15728640 | tf_op jit(solution)/shard_map/heads/pallas_call | solution.py:304
  80.3 3.8 %all-to-all-start.2 = ((bf16[4,8,160,256]{3,2,1,0:T(8,128)(2,1)}), bf16[4,8,160,256]{3,2,1,0:T(8,128)(2,1)S(1)}, u32[]{:S(2)}, u32[]{:S(2)}) async-start(bf16[4,8,160,256]{3,2,1,0:T(8,128)(2,1)} %get-tuple-element.57), calls=%async_computation.2 | async-start | bytes 5242880 | tf_op jit(solution)/shard_map/all_to_all | solution.py:432
  84.2 1.9 %collective-permute-done.12.dl_o = bf16[512,512]{1,0:T(8,128)(2,1)S(1)} collective-permute-done((bf16[512,512]{1,0:T(8,128)(2,1)S(1)}, bf16[512,512]{1,0:T(8,128)(2,1)S(1)}, u32[]{:S(2)}, u32[]{:S(2)}) %collective-permute-start.12) | collective-permute-done | bytes 524320 | tf_op jit(solution)/shard_map/ppermute | solution.py:27
  86.2 0.8 copy-done.7
  87.0 9.9 %back.1 = (bf16[512,640]{1,0:T(8,128)(2,1)}, bf16[512,640]{1,0:T(8,128)(2,1)}, bf16[512,640]{1,0:T(8,128)(2,1)}, bf16[512,640]{1,0:T(8,128)(2,1)}, f32[4,1,768]{2,1,0:T(1,128)}) custom-call(s32[12]{0:T(128)} %concatenate.6.at, bf16[512,512]{1,0:T(8,128)(2,1)} %get-tuple-element.58.dl, bf16[512,512]{1,0:T(8,128)(2,1)} %copy-done.7, ...), custom_call_target="tpu_custom_call" | custom-call | flops 2684354560 | bytes 10485760 | tf_op jit(solution)/shard_map/back/pallas_call | solution.py:262
  96.8 3.1 %collective-permute-start.20 = (bf16[512,640]{1,0:T(8,128)(2,1)}, bf16[512,640]{1,0:T(8,128)(2,1)S(1)}, u32[]{:S(2)}, u32[]{:S(2)}) collective-permute-start(bf16[512,640]{1,0:T(8,128)(2,1)} %get-tuple-element.63), channel_id=1, source_target_pairs={{0,6},{2,0},{4,2},{6,4},{1,7},{3,1},{5,3},{7,5},{8,14},{10,8},{12,... | collective-permute-start | bytes 1966088 | tf_op jit(solution)/shard_map/ppermute | solution.py:27
  99.9 2.3 %collective-permute-start.22 = (bf16[512,640]{1,0:T(8,128)(2,1)}, bf16[512,640]{1,0:T(8,128)(2,1)}, u32[]{:S(2)}, u32[]{:S(2)}) collective-permute-start(bf16[512,640]{1,0:T(8,128)(2,1)} %get-tuple-element.65), channel_id=1, source_target_pairs={{0,4},{2,6},{4,0},{6,2},{1,5},{3,7},{5,1},{7,3},{8,12},{10,14},{12... | collective-permute-start | bytes 1966088 | tf_op jit(solution)/shard_map/ppermute | solution.py:27
  102.3 4.3 %collective-permute-done.14 = f32[4,1,768]{2,1,0:T(1,128)S(1)} collective-permute-done((f32[4,1,768]{2,1,0:T(1,128)}, f32[4,1,768]{2,1,0:T(1,128)S(1)}, u32[]{:S(2)}, u32[]{:S(2)}) %collective-permute-start.14) | collective-permute-done | bytes 12320 | tf_op jit(solution)/shard_map/ppermute | solution.py:31
  106.6 0.7 add.50
  107.3 2.1 %collective-permute-start.15 = (f32[4,1,768]{2,1,0:T(1,128)S(1)}, f32[4,1,768]{2,1,0:T(1,128)S(1)}, u32[]{:S(2)}, u32[]{:S(2)}) collective-permute-start(f32[4,1,768]{2,1,0:T(1,128)S(1)} %add.50), channel_id=1, source_target_pairs={{0,224},{32,64},{64,32},{96,128},{128,96},{160,192},{192,160},{224... | collective-permute-start | bytes 36872 | tf_op jit(solution)/shard_map/ppermute | solution.py:31
  109.5 1.9 %collective-permute-done.15 = f32[4,1,768]{2,1,0:T(1,128)S(1)} collective-permute-done((f32[4,1,768]{2,1,0:T(1,128)S(1)}, f32[4,1,768]{2,1,0:T(1,128)S(1)}, u32[]{:S(2)}, u32[]{:S(2)}) %collective-permute-start.15) | collective-permute-done | bytes 12320 | tf_op jit(solution)/shard_map/ppermute | solution.py:31
  111.4 5.4 %collective-permute-start.16 = (f32[4,1,768]{2,1,0:T(1,128)S(1)}, f32[4,1,768]{2,1,0:T(1,128)S(1)}, u32[]{:S(2)}, u32[]{:S(2)}) collective-permute-start(f32[4,1,768]{2,1,0:T(1,128)S(1)} %add.51), channel_id=1, source_target_pairs={{0,96},{32,192},{64,160},{96,0},{128,224},{160,64},{192,32},{224,1... | collective-permute-start | bytes 36872 | tf_op jit(solution)/shard_map/ppermute | solution.py:31
  116.8 1.9 %collective-permute-done.16 = f32[4,1,768]{2,1,0:T(1,128)S(1)} collective-permute-done((f32[4,1,768]{2,1,0:T(1,128)S(1)}, f32[4,1,768]{2,1,0:T(1,128)S(1)}, u32[]{:S(2)}, u32[]{:S(2)}) %collective-permute-start.16) | collective-permute-done | bytes 12320 | tf_op jit(solution)/shard_map/ppermute | solution.py:31
  118.7 3.1 %collective-permute-start.19 = (f32[4,1,768]{2,1,0:T(1,128)S(1)}, f32[4,1,768]{2,1,0:T(1,128)S(1)}, u32[]{:S(2)}, u32[]{:S(2)}) collective-permute-start(f32[4,1,768]{2,1,0:T(1,128)S(1)} %add.52), channel_id=1, source_target_pairs={{0,24},{8,0},{16,8},{24,16},{1,25},{9,1},{17,9},{25,17},{2,26},{10... | collective-permute-start | bytes 36872 | tf_op jit(solution)/shard_map/ppermute | solution.py:27
  121.8 0.7 collective-permute-start.18
  123.2 1.0 collective-permute-start.17
  124.7 2.3 %collective-permute-done.18 = f32[4,1,768]{2,1,0:T(1,128)S(1)} collective-permute-done((f32[4,1,768]{2,1,0:T(1,128)S(1)}, f32[4,1,768]{2,1,0:T(1,128)S(1)}, u32[]{:S(2)}, u32[]{:S(2)}) %collective-permute-start.18) | collective-permute-done | bytes 12320 | tf_op jit(solution)/shard_map/ppermute | solution.py:27
  127.0 1.4 collective-permute-done.17
  129.0 1.5 copy-done
  130.5 2.9 %sum_x.1 = bf16[8,160,256]{2,1,0:T(8,128)(2,1)} custom-call(bf16[4,8,160,256]{3,2,1,0:T(8,128)(2,1)} %copy-done), custom_call_target="tpu_custom_call" | custom-call | flops 1310720 | bytes 3932160 | tf_op jit(solution)/shard_map/sum_x/pallas_call | solution.py:332
  133.5 7.6 %all-to-all-start.3 = ((bf16[8,160,256]{2,1,0:T(8,128)(2,1)}), bf16[8,160,256]{2,1,0:T(8,128)(2,1)}, u32[]{:S(2)}, u32[]{:S(2)}) async-start(bf16[8,160,256]{2,1,0:T(8,128)(2,1)} %sum_x.1), calls=%async_computation.4 | async-start | bytes 1310720 | tf_op jit(solution)/shard_map/all_to_all | solution.py:446
  141.1 0.8 copy-done.20
  141.9 3.3 %final.1 = bf16[2,256,640]{2,1,0:T(8,128)(2,1)} custom-call(bf16[512,640]{1,0:T(8,128)(2,1)} %get-tuple-element.62.u0, bf16[512,640]{1,0:T(8,128)(2,1)} %copy-done.20, bf16[512,640]{1,0:T(8,128)(2,1)} %collective-permute-done.21.u2, bf16[512,640]{1,0:T(8,128)(2,1)} %collective-permute-done.22.u3, bf16[2,256,640]{2,1,0:T(8,128)(2,1)} %h_ref.1, ...), custom_call_target="tpu_custom_call" | custom-call | flops 199999995904 | bytes 3932160 | tf_op jit(solution)/shard_map/final/pallas_call | solution.py:364
  145.3 1.5 collective-permute-start.23
  146.8 2.6 %collective-permute-start.25 = (f32[1,768]{1,0:T(1,128)S(1)}, f32[1,768]{1,0:T(1,128)S(1)}, u32[]{:S(2)}, u32[]{:S(2)}) collective-permute-start(f32[1,768]{1,0:T(1,128)S(1)} %get-tuple-element.75), channel_id=1, source_target_pairs={{0,4},{2,6},{4,0},{6,2},{1,5},{3,7},{5,1},{7,3},{8,12},{10,14},{12... | collective-permute-start | bytes 9224 | tf_op jit(solution)/shard_map/ppermute | solution.py:27
  149.4 2.5 %collective-permute-done.25 = f32[1,768]{1,0:T(1,128)S(1)} collective-permute-done((f32[1,768]{1,0:T(1,128)S(1)}, f32[1,768]{1,0:T(1,128)S(1)}, u32[]{:S(2)}, u32[]{:S(2)}) %collective-permute-start.25) | collective-permute-done | bytes 3104 | tf_op jit(solution)/shard_map/ppermute | solution.py:27
  151.9 2.3 %collective-permute-done.24 = f32[1,768]{1,0:T(1,128)S(1)} collective-permute-done((f32[1,768]{1,0:T(1,128)S(1)}, f32[1,768]{1,0:T(1,128)S(1)}, u32[]{:S(2)}, u32[]{:S(2)}) %collective-permute-start.24) | collective-permute-done | bytes 3104 | tf_op jit(solution)/shard_map/ppermute | solution.py:27
  155.4 0.9 reduce-scatter.5.cloned.1.call-done
  156.3 1.9 %join.1 = f32[160,512]{1,0:T(8,128)} custom-call(bf16[8,160,256]{2,1,0:T(8,128)(2,1)} %all-to-all-done.3.from_z, bf16[160,256]{1,0:T(8,128)(2,1)} %bitcast.30), custom_call_target="tpu_custom_call" | custom-call | flops 655360 | bytes 1310720 | tf_op jit(solution)/shard_map/join/pallas_call | solution.py:364
  (90 shorter events, 9.5 us)
Async XLA Ops:
  7.2 28.1 %copy-start.21 = (s32[4]{0:T(128)S(1)}, s32[4]{0:T(128)}, u32[]{:S(2)}) copy-start(s32[4]{0:T(128)} %constant.37.clone) | copy-start | bytes 52
  9.0 26.9 %copy-start.1 = (bf16[528,640]{1,0:T(8,128)(2,1)}, bf16[528,640]{1,0:T(8,128)(2,1)S(1)}, u32[]{:S(2)}) copy-start(bf16[528,640]{1,0:T(8,128)(2,1)S(1)} %pad_maximum_fusion.refs_0_) | copy-start | bytes 2027524
  9.0 19.1 %collective-permute-start.1 = (bf16[528,640]{1,0:T(8,128)(2,1)S(1)}, bf16[528,640]{1,0:T(8,128)(2,1)S(1)}, u32[]{:S(2)}, u32[]{:S(2)}) collective-permute-start(bf16[528,640]{1,0:T(8,128)(2,1)S(1)} %pad_maximum_fusion.refs_0_), channel_id=1, source_target_pairs={{0,6},{2,0},{4,2},{6,4},{1,7},{3,1},{5,3},{7,5},{8,14},{10,8},{12,... | collective-permute-start | bytes 2027528 | tf_op jit(solution)/shard_map/ppermute | solution.py:27
  12.1 17.8 %collective-permute-start = (bf16[528,640]{1,0:T(8,128)(2,1)S(1)}, bf16[528,640]{1,0:T(8,128)(2,1)S(1)}, u32[]{:S(2)}, u32[]{:S(2)}) collective-permute-start(bf16[528,640]{1,0:T(8,128)(2,1)S(1)} %pad_maximum_fusion.refs_0_), channel_id=1, source_target_pairs={{0,2},{2,4},{4,6},{6,0},{1,3},{3,5},{5,7},{7,1},{8,10},{10,12},{12... | collective-permute-start | bytes 2027528 | tf_op jit(solution)/shard_map/ppermute | solution.py:27
  13.4 14.7 %all-to-all-start = ((f32[8,1,128]{2,1,0:T(1,128)}), f32[8,1,128]{2,1,0:T(1,128)S(1)}, u32[]{:S(2)}, u32[]{:S(2)}) async-start(f32[8,1,128]{2,1,0:T(1,128)} %local.1), calls=%async_computation | async-start | bytes 8192 | tf_op jit(solution)/shard_map/all_to_all | solution.py:402
  22.0 13.9 %collective-permute-start.3 = (bf16[528,640]{1,0:T(8,128)(2,1)S(1)}, bf16[528,640]{1,0:T(8,128)(2,1)S(1)}, u32[]{:S(2)}, u32[]{:S(2)}) collective-permute-start(bf16[528,640]{1,0:T(8,128)(2,1)S(1)} %pad_maximum_fusion.refs_0_), channel_id=1, source_target_pairs={{0,1},{1,0},{2,3},{3,2},{4,5},{5,4},{6,7},{7,6},{8,9},{9,8},{10,11... | collective-permute-start | bytes 2027528 | tf_op jit(solution)/shard_map/ppermute | solution.py:27
  28.2 35.1 %copy-start.14 = (f32[128]{0:T(128)}, f32[128]{0:T(128)S(1)}, u32[]{:S(2)}) copy-start(f32[128]{0:T(128)S(1)} %reduce_sum.11) | copy-start | bytes 1540
  28.2 7.8 %copy-start.3 = (bf16[528,640]{1,0:T(8,128)(2,1)}, bf16[528,640]{1,0:T(8,128)(2,1)S(1)}, u32[]{:S(2)}) copy-start(bf16[528,640]{1,0:T(8,128)(2,1)S(1)} %collective-permute-done.1.refs_4_) | copy-start | bytes 2027524
  30.0 6.0 %copy-start.2 = (bf16[528,640]{1,0:T(8,128)(2,1)}, bf16[528,640]{1,0:T(8,128)(2,1)S(1)}, u32[]{:S(2)}) copy-start(bf16[528,640]{1,0:T(8,128)(2,1)S(1)} %collective-permute-done.refs_2_) | copy-start | bytes 2027524
  31.5 4.4 %collective-permute-start.4 = (bf16[528,640]{1,0:T(8,128)(2,1)S(1)}, bf16[528,640]{1,0:T(8,128)(2,1)S(1)}, u32[]{:S(2)}, u32[]{:S(2)}) collective-permute-start(bf16[528,640]{1,0:T(8,128)(2,1)S(1)} %collective-permute-done.refs_2_), channel_id=1, source_target_pairs={{0,1},{1,0},{2,3},{3,2},{4,5},{5,4},{6,7},{7,6},{8,9},{9,8},{10,11... | collective-permute-start | bytes 2027528 | tf_op jit(solution)/shard_map/ppermute | solution.py:27
  31.5 4.4 %collective-permute-start.5 = (bf16[528,640]{1,0:T(8,128)(2,1)S(1)}, bf16[528,640]{1,0:T(8,128)(2,1)}, u32[]{:S(2)}, u32[]{:S(2)}) collective-permute-start(bf16[528,640]{1,0:T(8,128)(2,1)S(1)} %collective-permute-done.1.refs_4_), channel_id=1, source_target_pairs={{0,1},{1,0},{2,3},{3,2},{4,5},{5,4},{6,7},{7,6},{8,9},{9,8},{10,11... | collective-permute-start | bytes 2027528 | tf_op jit(solution)/shard_map/ppermute | solution.py:27
  32.0 14.5 %collective-permute-start.2 = (bf16[272,640]{1,0:T(8,128)(2,1)}, bf16[272,640]{1,0:T(8,128)(2,1)}, u32[]{:S(2)}, u32[]{:S(2)}) collective-permute-start(bf16[272,640]{1,0:T(8,128)(2,1)} %slice.28), channel_id=1, source_target_pairs={{0,2},{2,4},{4,6},{6,0},{1,3},{3,5},{5,7},{7,1},{8,10},{10,12},{12... | collective-permute-start | bytes 1044488 | tf_op jit(solution)/shard_map/ppermute | solution.py:27
  32.0 14.6 %collective-permute-start.6 = (bf16[256,640]{1,0:T(8,128)(2,1)}, bf16[256,640]{1,0:T(8,128)(2,1)}, u32[]{:S(2)}, u32[]{:S(2)}) collective-permute-start(bf16[256,640]{1,0:T(8,128)(2,1)} %slice.29), channel_id=1, source_target_pairs={{0,6},{2,0},{4,2},{6,4},{1,7},{3,1},{5,3},{7,5},{8,14},{10,8},{12,... | collective-permute-start | bytes 983048 | tf_op jit(solution)/shard_map/ppermute | solution.py:27
  35.9 11.3 %copy-start.15 = (s32[2,256]{1,0:T(2,128)S(1)}, s32[2,256]{1,0:T(2,128)}, u32[]{:S(2)}) copy-start(s32[2,256]{1,0:T(2,128)} %param.12) | copy-start | bytes 6148
  35.9 0.9 copy-start.4
  35.9 1.1 copy-start.5
  46.6 2.4 %collective-permute-start.7 = (bf16[272,640]{1,0:T(8,128)(2,1)}, bf16[272,640]{1,0:T(8,128)(2,1)S(1)}, u32[]{:S(2)}, u32[]{:S(2)}) collective-permute-start(bf16[272,640]{1,0:T(8,128)(2,1)} %collective-permute-done.2.refs_0_), channel_id=1, source_target_pairs={{0,1},{1,0},{2,3},{3,2},{4,5},{5,4},{6,7},{7,6},{8,9},{9,8},{10,11... | collective-permute-start | bytes 1044488 | tf_op jit(solution)/shard_map/ppermute | solution.py:27
  46.7 2.3 %collective-permute-start.8 = (bf16[256,640]{1,0:T(8,128)(2,1)}, bf16[256,640]{1,0:T(8,128)(2,1)S(1)}, u32[]{:S(2)}, u32[]{:S(2)}) collective-permute-start(bf16[256,640]{1,0:T(8,128)(2,1)} %collective-permute-done.6.refs_1_), channel_id=1, source_target_pairs={{0,1},{1,0},{2,3},{3,2},{4,5},{5,4},{6,7},{7,6},{8,9},{9,8},{10,11... | collective-permute-start | bytes 983048 | tf_op jit(solution)/shard_map/ppermute | solution.py:27
  49.8 14.3 %copy-start.16 = (f32[2,256]{1,0:T(2,128)S(1)}, f32[2,256]{1,0:T(2,128)}, u32[]{:S(2)}) copy-start(f32[2,256]{1,0:T(2,128)} %param.14) | copy-start | bytes 6148
  56.0 30.1 %collective-permute-start.13 = (bf16[512,5120]{1,0:T(8,128)(2,1)}, bf16[512,5120]{1,0:T(8,128)(2,1)}, u32[]{:S(2)}, u32[]{:S(2)}) collective-permute-start(bf16[512,5120]{1,0:T(8,128)(2,1)} %head.1), channel_id=1, source_target_pairs={{0,1},{1,0},{2,3},{3,2},{4,5},{5,4},{6,7},{7,6},{8,9},{9,8},{10,11... | collective-permute-start | bytes 15728648 | tf_op jit(solution)/shard_map/ppermute | solution.py:27
  56.2 11.8 %all-to-all-start.1 = ((f32[8,8,512]{2,1,0:T(8,128)}), f32[8,8,512]{2,1,0:T(8,128)S(1)}, u32[]{:S(2)}, u32[]{:S(2)}) async-start(f32[8,8,512]{2,1,0:T(8,128)} %get-tuple-element.52), calls=%async_computation.1 | async-start | bytes 262144 | tf_op jit(solution)/shard_map/all_to_all | solution.py:425
  59.6 73.8 %reduce-scatter.3.cloned.1.call-start = ((), (), s32[]{:S(2)}) async-start(), calls=%async_computation.6 | async-start | bytes 2949120 | tf_op jit(solution)/shard_map/reduce_scatter | solution.py:431
  59.6 5.1 %collective-permute-start.11 = (f32[1,128]{1,0:T(1,128)S(1)}, f32[1,128]{1,0:T(1,128)S(1)}, u32[]{:S(2)}, u32[]{:S(2)}) collective-permute-start(f32[1,128]{1,0:T(1,128)S(1)} %bitcast.34), channel_id=1, source_target_pairs={{0,24},{8,0},{16,8},{24,16},{1,25},{9,1},{17,9},{25,17},{2,26},{10... | collective-permute-start | bytes 1544 | tf_op jit(solution)/shard_map/ppermute | solution.py:27
  62.5 5.0 %collective-permute-start.10 = (f32[1,128]{1,0:T(1,128)S(1)}, f32[1,128]{1,0:T(1,128)S(1)}, u32[]{:S(2)}, u32[]{:S(2)}) collective-permute-start(f32[1,128]{1,0:T(1,128)S(1)} %bitcast.35), channel_id=1, source_target_pairs={{0,16},{8,24},{16,0},{24,8},{1,17},{9,25},{17,1},{25,9},{2,18},{10... | collective-permute-start | bytes 1544 | tf_op jit(solution)/shard_map/ppermute | solution.py:27
  63.3 4.8 %collective-permute-start.9 = (f32[1,128]{1,0:T(1,128)S(1)}, f32[1,128]{1,0:T(1,128)S(1)}, u32[]{:S(2)}, u32[]{:S(2)}) collective-permute-start(f32[1,128]{1,0:T(1,128)S(1)} %bitcast.36), channel_id=1, source_target_pairs={{0,8},{8,16},{16,24},{24,0},{1,9},{9,17},{17,25},{25,1},{2,10},{10... | collective-permute-start | bytes 1544 | tf_op jit(solution)/shard_map/ppermute | solution.py:27
  64.8 3.3 %copy-start.17 = (f32[1,128]{1,0:T(1,128)}, f32[1,128]{1,0:T(1,128)S(1)}, u32[]{:S(2)}) copy-start(f32[1,128]{1,0:T(1,128)S(1)} %collective-permute-done.11.sum3) | copy-start | bytes 1540
  80.3 3.9 %copy-start.6 = (bf16[512,512]{1,0:T(8,128)(2,1)S(1)}, bf16[512,512]{1,0:T(8,128)(2,1)}, u32[]{:S(2)}) copy-start(bf16[512,512]{1,0:T(8,128)(2,1)} %get-tuple-element.58.dl) | copy-start | bytes 1572868
  80.3 48.7 %all-to-all-start.2 = ((bf16[4,8,160,256]{3,2,1,0:T(8,128)(2,1)}), bf16[4,8,160,256]{3,2,1,0:T(8,128)(2,1)S(1)}, u32[]{:S(2)}, u32[]{:S(2)}) async-start(bf16[4,8,160,256]{3,2,1,0:T(8,128)(2,1)} %get-tuple-element.57), calls=%async_computation.2 | async-start | bytes 5242880 | tf_op jit(solution)/shard_map/all_to_all | solution.py:432
  84.1 72.2 %reduce-scatter.5.cloned.1.call-start = ((), (), s32[]{:S(2)}) async-start(), calls=%async_computation.7 | async-start | bytes 409600 | tf_op jit(solution)/shard_map/reduce_scatter | solution.py:447
  84.1 2.0 %collective-permute-start.12 = (bf16[512,512]{1,0:T(8,128)(2,1)S(1)}, bf16[512,512]{1,0:T(8,128)(2,1)S(1)}, u32[]{:S(2)}, u32[]{:S(2)}) collective-permute-start(bf16[512,512]{1,0:T(8,128)(2,1)S(1)} %copy-done.6), channel_id=1, source_target_pairs={{0,1},{1,0},{2,3},{3,2},{4,5},{5,4},{6,7},{7,6},{8,9},{9,8},{10,11... | collective-permute-start | bytes 1572872 | tf_op jit(solution)/shard_map/ppermute | solution.py:27
  87.0 37.2 %copy-start.12 = (bf16[640]{0:T(1024)(128)(2,1)S(1)}, bf16[640]{0:T(1024)(128)(2,1)}, u32[]{:S(2)}) copy-start(bf16[640]{0:T(1024)(128)(2,1)} %param.10) | copy-start | bytes 3844
  96.8 44.3 %collective-permute-start.20 = (bf16[512,640]{1,0:T(8,128)(2,1)}, bf16[512,640]{1,0:T(8,128)(2,1)S(1)}, u32[]{:S(2)}, u32[]{:S(2)}) collective-permute-start(bf16[512,640]{1,0:T(8,128)(2,1)} %get-tuple-element.63), channel_id=1, source_target_pairs={{0,6},{2,0},{4,2},{6,4},{1,7},{3,1},{5,3},{7,5},{8,14},{10,8},{12,... | collective-permute-start | bytes 1966088 | tf_op jit(solution)/shard_map/ppermute | solution.py:27
  99.9 41.2 %collective-permute-start.21 = (bf16[512,640]{1,0:T(8,128)(2,1)}, bf16[512,640]{1,0:T(8,128)(2,1)}, u32[]{:S(2)}, u32[]{:S(2)}) collective-permute-start(bf16[512,640]{1,0:T(8,128)(2,1)} %get-tuple-element.64), channel_id=1, source_target_pairs={{0,2},{2,4},{4,6},{6,0},{1,3},{3,5},{5,7},{7,1},{8,10},{10,12},{12... | collective-permute-start | bytes 1966088 | tf_op jit(solution)/shard_map/ppermute | solution.py:27
  99.9 41.2 %collective-permute-start.22 = (bf16[512,640]{1,0:T(8,128)(2,1)}, bf16[512,640]{1,0:T(8,128)(2,1)}, u32[]{:S(2)}, u32[]{:S(2)}) collective-permute-start(bf16[512,640]{1,0:T(8,128)(2,1)} %get-tuple-element.65), channel_id=1, source_target_pairs={{0,4},{2,6},{4,0},{6,2},{1,5},{3,7},{5,1},{7,3},{8,12},{10,14},{12... | collective-permute-start | bytes 1966088 | tf_op jit(solution)/shard_map/ppermute | solution.py:27
  102.2 4.3 %collective-permute-start.14 = (f32[4,1,768]{2,1,0:T(1,128)}, f32[4,1,768]{2,1,0:T(1,128)S(1)}, u32[]{:S(2)}, u32[]{:S(2)}) collective-permute-start(f32[4,1,768]{2,1,0:T(1,128)} %get-tuple-element.61), channel_id=1, source_target_pairs={{0,32},{32,0},{64,96},{96,64},{128,160},{160,128},{192,224},{224,1... | collective-permute-start | bytes 36872 | tf_op jit(solution)/shard_map/ppermute | solution.py:31
  107.3 4.0 %collective-permute-start.15 = (f32[4,1,768]{2,1,0:T(1,128)S(1)}, f32[4,1,768]{2,1,0:T(1,128)S(1)}, u32[]{:S(2)}, u32[]{:S(2)}) collective-permute-start(f32[4,1,768]{2,1,0:T(1,128)S(1)} %add.50), channel_id=1, source_target_pairs={{0,224},{32,64},{64,32},{96,128},{128,96},{160,192},{192,160},{224... | collective-permute-start | bytes 36872 | tf_op jit(solution)/shard_map/ppermute | solution.py:31
  111.4 7.3 %collective-permute-start.16 = (f32[4,1,768]{2,1,0:T(1,128)S(1)}, f32[4,1,768]{2,1,0:T(1,128)S(1)}, u32[]{:S(2)}, u32[]{:S(2)}) collective-permute-start(f32[4,1,768]{2,1,0:T(1,128)S(1)} %add.51), channel_id=1, source_target_pairs={{0,96},{32,192},{64,160},{96,0},{128,224},{160,64},{192,32},{224,1... | collective-permute-start | bytes 36872 | tf_op jit(solution)/shard_map/ppermute | solution.py:31
  118.7 4.5 %collective-permute-start.19 = (f32[4,1,768]{2,1,0:T(1,128)S(1)}, f32[4,1,768]{2,1,0:T(1,128)S(1)}, u32[]{:S(2)}, u32[]{:S(2)}) collective-permute-start(f32[4,1,768]{2,1,0:T(1,128)S(1)} %add.52), channel_id=1, source_target_pairs={{0,24},{8,0},{16,8},{24,16},{1,25},{9,1},{17,9},{25,17},{2,26},{10... | collective-permute-start | bytes 36872 | tf_op jit(solution)/shard_map/ppermute | solution.py:27
  121.8 5.2 %collective-permute-start.18 = (f32[4,1,768]{2,1,0:T(1,128)S(1)}, f32[4,1,768]{2,1,0:T(1,128)S(1)}, u32[]{:S(2)}, u32[]{:S(2)}) collective-permute-start(f32[4,1,768]{2,1,0:T(1,128)S(1)} %add.52), channel_id=1, source_target_pairs={{0,16},{8,24},{16,0},{24,8},{1,17},{9,25},{17,1},{25,9},{2,18},{10... | collective-permute-start | bytes 36872 | tf_op jit(solution)/shard_map/ppermute | solution.py:27
  123.2 5.2 %collective-permute-start.17 = (f32[4,1,768]{2,1,0:T(1,128)S(1)}, f32[4,1,768]{2,1,0:T(1,128)S(1)}, u32[]{:S(2)}, u32[]{:S(2)}) collective-permute-start(f32[4,1,768]{2,1,0:T(1,128)S(1)} %add.52), channel_id=1, source_target_pairs={{0,8},{8,16},{16,24},{24,0},{1,9},{9,17},{17,25},{25,1},{2,10},{10... | collective-permute-start | bytes 36872 | tf_op jit(solution)/shard_map/ppermute | solution.py:27
  129.0 1.5 copy-start
  133.5 22.9 %all-to-all-start.3 = ((bf16[8,160,256]{2,1,0:T(8,128)(2,1)}), bf16[8,160,256]{2,1,0:T(8,128)(2,1)}, u32[]{:S(2)}, u32[]{:S(2)}) async-start(bf16[8,160,256]{2,1,0:T(8,128)(2,1)} %sum_x.1), calls=%async_computation.4 | async-start | bytes 1310720 | tf_op jit(solution)/shard_map/all_to_all | solution.py:446
  141.1 0.8 copy-start.20
  141.9 3.3 %copy-start.11 = (f32[4,1,768]{2,1,0:T(1,128)S(1)}, f32[4,1,768]{2,1,0:T(1,128)}, u32[]{:S(2)}) copy-start(f32[4,1,768]{2,1,0:T(1,128)} %add_add_fusion) | copy-start | bytes 36868
  141.9 12.8 %copy-start.13 = (bf16[640]{0:T(1024)(128)(2,1)S(1)}, bf16[640]{0:T(1024)(128)(2,1)}, u32[]{:S(2)}) copy-start(bf16[640]{0:T(1024)(128)(2,1)} %param.10) | copy-start | bytes 3844
  145.3 4.2 %collective-permute-start.23 = (f32[1,768]{1,0:T(1,128)S(1)}, f32[1,768]{1,0:T(1,128)S(1)}, u32[]{:S(2)}, u32[]{:S(2)}) collective-permute-start(f32[1,768]{1,0:T(1,128)S(1)} %get-tuple-element.74), channel_id=1, source_target_pairs={{0,6},{2,0},{4,2},{6,4},{1,7},{3,1},{5,3},{7,5},{8,14},{10,8},{12,... | collective-permute-start | bytes 9224 | tf_op jit(solution)/shard_map/ppermute | solution.py:27
  146.8 5.1 %collective-permute-start.25 = (f32[1,768]{1,0:T(1,128)S(1)}, f32[1,768]{1,0:T(1,128)S(1)}, u32[]{:S(2)}, u32[]{:S(2)}) collective-permute-start(f32[1,768]{1,0:T(1,128)S(1)} %get-tuple-element.75), channel_id=1, source_target_pairs={{0,4},{2,6},{4,0},{6,2},{1,5},{3,7},{5,1},{7,3},{8,12},{10,14},{12... | collective-permute-start | bytes 9224 | tf_op jit(solution)/shard_map/ppermute | solution.py:27
  149.4 4.8 %collective-permute-start.24 = (f32[1,768]{1,0:T(1,128)S(1)}, f32[1,768]{1,0:T(1,128)S(1)}, u32[]{:S(2)}, u32[]{:S(2)}) collective-permute-start(f32[1,768]{1,0:T(1,128)S(1)} %get-tuple-element.76), channel_id=1, source_target_pairs={{0,2},{2,4},{4,6},{6,0},{1,3},{3,5},{5,7},{7,1},{8,10},{10,12},{12... | collective-permute-start | bytes 9224 | tf_op jit(solution)/shard_map/ppermute | solution.py:27
  (6 other events, 4.1 us)
Sparse Core Ops, SparseCore 0:
  80.4 44.6 reduce-scatter.2
  133.6 22.6 reduce-scatter.4

commit v8 on v7

--- a/solution.py
+++ b/solution.py
@@ -433,12 +433,13 @@
     u0, u1, u2, u3, lines = back_of(
         at, after(dl, to_x), dl_o, early, late, small, head, head_o, cols
     )
+    tail = lines[0] + shift(lines[1], "y", -1) + shift(lines[2], "y", 1) + shift(lines[3], "y", 2)
+    u1, u2, u3, tail = lax.optimization_barrier((u1, u2, u3, tail))
     u1, u2, u3 = shift(u1, "y", -1), shift(u2, "y", 1), shift(u3, "y", 2)
 
     for step in (1, -1, 3):
-        lines = lines + turn(lines, step)
-    lines = lines + shift(lines, "x", 1) + shift(lines, "x", 2) + shift(lines, "x", -1)
-    from_x = after(from_x, lines)
+        tail = tail + turn(tail, step)
+    from_x = after(from_x, tail)
 
     to_z = sum_first(from_x, "sum_x")
     half_z = after(half_z, to_z)
@@ -454,8 +455,8 @@
         "final",
         200 * 10**9,
     )
-    lines = after(lines, grad_hidden)
-    tail = lines[0] + shift(lines[1], "y", -1) + shift(lines[2], "y", 1) + shift(lines[3], "y", 2)
+    tail = after(tail, grad_hidden)
+    tail = tail + shift(tail, "x", 1) + shift(tail, "x", 2) + shift(tail, "x", -1)
     (grad_head_t,) = simple(
         join_kernel,
         [like((part, 2 * half), f32)],

time: 167 us -> 165 us (0.988)
    ppermute x3, waiting for transfers between devices: 8.09 us -> 6.11 us  [turn(): lax.ppermute(value, 'z', [(i, (i + (step if i % 2 == 0 else -step)) % 8)...]
  transfers between devices with their start and end apart: 32 -> 32, of which waited for: 15 -> 15; matrix products, arithmetic and copies ran while one was open for 4% -> 4% of each run, Pallas kernels for 23% -> 24%
where the time goes in v8:
time: 165 us; the launch traced here: 163 us
  starting transfers between devices  56.8 us (34%)
  Pallas kernels  46.6 us (28%)
  waiting for transfers between devices  31.1 us (19%)
  between operations  14.3 us (9%)
  local copies, waits for them, and re-layouts  11.5 us (7%)
  other arithmetic  3.08 us (2%)
    ppermute x23, starting transfers between devices, shift(): return lax.ppermute(value, axis, [(i, (i + step) % n) for i in range(n)])  25.3 us
    ppermute x23, waiting for transfers between devices, shift(): return lax.ppermute(value, axis, [(i, (i + step) % n) for i in range(n)])  16.2 us
    pallas_call x2, Pallas kernels, logits_of(): pl.pallas_call(functools.partial(logits_kernel, count, per, last), out_sh...  15.7 us
    pallas_call x1, Pallas kernels, back_of(): pl.pallas_call(back_kernel, out_shape=shapes, grid_spec=pltpu.PrefetchSca...  9.87 us
    pallas_call x1, Pallas kernels, heads_of(): pl.pallas_call(heads_kernel, out_shape=shapes, grid_spec=pltpu.PrefetchSc...  8.8 us
    all_to_all x1, starting transfers between devices, body(): over_z = lax.all_to_all(local, 'z', 0, 0, tiled=True).sum(axis=0)  8.57 us
    ppermute x3, starting transfers between devices, turn(): lax.ppermute(value, 'z', [(i, (i + (step if i % 2 == 0 else -step)) % 8)...  7.86 us
    all_to_all x1, starting transfers between devices, body(): from_z = lax.all_to_all(to_z, 'z', 0, 0, tiled=True)  7.8 us
  transfers between devices with their start and end apart: 32, of which 15 were waited for; matrix products, arithmetic and copies ran while one was open for 4% of the time, Pallas kernels for 24%

profile of v8, /device:TPU:32, one launch (start us, length us, event | category | flops | bytes accessed | tf_op | source)
XLA Modules:
  0.0 163.3 jit_solution(4961220216059903025)
XLA Ops:
  7.9 1.1 pad_maximum_fusion.refs_0_
  9.0 3.1 %collective-permute-start.1 = (bf16[528,640]{1,0:T(8,128)(2,1)S(1)}, bf16[528,640]{1,0:T(8,128)(2,1)S(1)}, u32[]{:S(2)}, u32[]{:S(2)}) collective-permute-start(bf16[528,640]{1,0:T(8,128)(2,1)S(1)} %pad_maximum_fusion.refs_0_), channel_id=1, source_target_pairs={{0,6},{2,0},{4,2},{6,4},{1,7},{3,1},{5,3},{7,5},{8,14},{10,8},{12,... | collective-permute-start | bytes 2027528 | tf_op jit(solution)/shard_map/ppermute | solution.py:27
  12.1 1.3 local.1
  13.4 8.6 %all-to-all-start = ((f32[8,1,128]{2,1,0:T(1,128)}), f32[8,1,128]{2,1,0:T(1,128)S(1)}, u32[]{:S(2)}, u32[]{:S(2)}) async-start(f32[8,1,128]{2,1,0:T(1,128)} %local.1), calls=%async_computation | async-start | bytes 8192 | tf_op jit(solution)/shard_map/all_to_all | solution.py:402
  22.0 6.1 %all-to-all-done = f32[8,1,128]{2,1,0:T(1,128)S(1)} async-done(((f32[8,1,128]{2,1,0:T(1,128)}), f32[8,1,128]{2,1,0:T(1,128)S(1)}, u32[]{:S(2)}, u32[]{:S(2)}) %all-to-all-start) | async-done | bytes 4128 | tf_op jit(solution)/shard_map/all_to_all | solution.py:402
  28.2 1.8 %collective-permute-done.refs_2_ = bf16[528,640]{1,0:T(8,128)(2,1)S(1)} collective-permute-done((bf16[528,640]{1,0:T(8,128)(2,1)S(1)}, bf16[528,640]{1,0:T(8,128)(2,1)S(1)}, u32[]{:S(2)}, u32[]{:S(2)}) %collective-permute-start) | collective-permute-done | bytes 675872 | tf_op jit(solution)/shard_map/ppermute | solution.py:27
  30.0 0.8 slice.29
  30.8 0.8 slice.28
  32.0 3.2 %collective-permute-start.6 = (bf16[256,640]{1,0:T(8,128)(2,1)}, bf16[256,640]{1,0:T(8,128)(2,1)}, u32[]{:S(2)}, u32[]{:S(2)}) collective-permute-start(bf16[256,640]{1,0:T(8,128)(2,1)} %slice.29), channel_id=1, source_target_pairs={{0,6},{2,0},{4,2},{6,4},{1,7},{3,1},{5,3},{7,5},{8,14},{10,8},{12,... | collective-permute-start | bytes 983048 | tf_op jit(solution)/shard_map/ppermute | solution.py:27
  36.0 0.8 copy-done.4
  37.0 9.5 %logits_first.1 = (bf16[3,512,1280]{2,1,0:T(8,128)(2,1)}, f32[512,512]{1,0:T(8,128)}, f32[8,512]{1,0:T(8,128)}) custom-call(s32[12]{0:T(128)} %concatenate.6.at, bf16[528,640]{1,0:T(8,128)(2,1)} %copy-done.1, bf16[528,640]{1,0:T(8,128)(2,1)} %copy-done.4, bf16[528,640]{1,0:T(8,128)(2,1)} %copy-done.2, bf16[528,640]{1,0:T(8,128)(2,1)} %copy-done.5, ...), custom_call_target="tpu_custom_call" | custom-call | flops 1000 | bytes 1000 | tf_op jit(solution)/shard_map/logits_first/pallas_call | solution.py:163
  47.8 1.2 collective-permute-done.8.refs_3_
  49.0 0.7 copy-done.10
  49.8 6.1 %logits_last.1 = (bf16[1,512,1280]{2,1,0:T(8,128)(2,1)}, f32[512,512]{1,0:T(8,128)}, f32[8,8,512]{2,1,0:T(8,128)}, f32[8,512]{1,0:T(8,128)}) custom-call(s32[12]{0:T(128)} %concatenate.6.at, bf16[272,640]{1,0:T(8,128)(2,1)} %collective-permute-done.2.refs_0_, bf16[256,640]{1,0:T(8,128)(2,1)} %collective-permute-done.6.refs_1_, bf16[272,640]{1,0:T(8,128)(2,1)} %copy-done.9, ...), custom_call_target="tpu_custom_call" | custom-call | flops 1000 | bytes 1000 | tf_op jit(solution)/shard_map/logits_last/pallas_call | solution.py:163
  56.2 3.4 %all-to-all-start.1 = ((f32[8,8,512]{2,1,0:T(8,128)}), f32[8,8,512]{2,1,0:T(8,128)S(1)}, u32[]{:S(2)}, u32[]{:S(2)}) async-start(f32[8,8,512]{2,1,0:T(8,128)} %get-tuple-element.56), calls=%async_computation.1 | async-start | bytes 262144 | tf_op jit(solution)/shard_map/all_to_all | solution.py:425
  59.6 2.8 %collective-permute-start.11 = (f32[1,128]{1,0:T(1,128)S(1)}, f32[1,128]{1,0:T(1,128)S(1)}, u32[]{:S(2)}, u32[]{:S(2)}) collective-permute-start(f32[1,128]{1,0:T(1,128)S(1)} %bitcast.34), channel_id=1, source_target_pairs={{0,24},{8,0},{16,8},{24,16},{1,25},{9,1},{17,9},{25,17},{2,26},{10... | collective-permute-start | bytes 1544 | tf_op jit(solution)/shard_map/ppermute | solution.py:27
  62.5 0.8 collective-permute-start.10
  63.3 0.9 collective-permute-start.9
  64.8 2.8 %collective-permute-done.10.sum2 = f32[1,128]{1,0:T(1,128)S(1)} collective-permute-done((f32[1,128]{1,0:T(1,128)S(1)}, f32[1,128]{1,0:T(1,128)S(1)}, u32[]{:S(2)}, u32[]{:S(2)}) %collective-permute-start.10) | collective-permute-done | bytes 544 | tf_op jit(solution)/shard_map/ppermute | solution.py:27
  68.7 2.7 %policy.1 = (bf16[512,512]{1,0:T(8,128)(2,1)}, f32[8,512]{1,0:T(8,128)}) custom-call(s32[12]{0:T(128)} %concatenate.6.at, f32[2]{0:T(128)} %rewards.3, s32[2]{0:T(128)} %lengths.3, s32[2]{0:T(128)} %slots.3, f32[1,128]{1,0:T(1,128)} %bitcast.37, f32[1,128]{1,0:T(1,128)} %copy-done.19, f32[1,128]{1,0:T(1,128)} %copy-done.18, f32[1,128]{1,0:T(1,128)} %copy-done.17, ...), custom_call_target="tpu_custom_call" | custom-call | flops 2097152 | bytes 1572864 | tf_op jit(solution)/shard_map/policy/pallas_call | solution.py:230
  71.4 8.8 %heads.1 = (bf16[4,8,160,256]{3,2,1,0:T(8,128)(2,1)}, bf16[8,4,160,256]{3,2,1,0:T(8,128)(2,1)}) custom-call(s32[12]{0:T(128)} %concatenate.6.at, bf16[3,512,1280]{2,1,0:T(8,128)(2,1)} %get-tuple-element.59.early, bf16[1,512,1280]{2,1,0:T(8,128)(2,1)} %get-tuple-element.60.late, bf16[512,512]{1,0:T(8,128)(2,1)} %get-tuple-element.62.dl), custom_call_target="tpu_custom_call" | custom-call | flops 2684354560 | bytes 15728640 | tf_op jit(solution)/shard_map/heads/pallas_call | solution.py:304
  80.3 3.8 %all-to-all-start.2 = ((bf16[4,8,160,256]{3,2,1,0:T(8,128)(2,1)}), bf16[4,8,160,256]{3,2,1,0:T(8,128)(2,1)S(1)}, u32[]{:S(2)}, u32[]{:S(2)}) async-start(bf16[4,8,160,256]{3,2,1,0:T(8,128)(2,1)} %get-tuple-element.61), calls=%async_computation.2 | async-start | bytes 5242880 | tf_op jit(solution)/shard_map/all_to_all | solution.py:432
  84.2 1.9 %collective-permute-done.12.dl_o = bf16[512,512]{1,0:T(8,128)(2,1)S(1)} collective-permute-done((bf16[512,512]{1,0:T(8,128)(2,1)S(1)}, bf16[512,512]{1,0:T(8,128)(2,1)S(1)}, u32[]{:S(2)}, u32[]{:S(2)}) %collective-permute-start.12) | collective-permute-done | bytes 524320 | tf_op jit(solution)/shard_map/ppermute | solution.py:27
  86.2 0.8 copy-done.7
  87.0 9.9 %back.1 = (bf16[512,640]{1,0:T(8,128)(2,1)}, bf16[512,640]{1,0:T(8,128)(2,1)}, bf16[512,640]{1,0:T(8,128)(2,1)}, bf16[512,640]{1,0:T(8,128)(2,1)}, f32[4,1,768]{2,1,0:T(1,128)}) custom-call(s32[12]{0:T(128)} %concatenate.6.at, bf16[512,512]{1,0:T(8,128)(2,1)} %get-tuple-element.62.dl, bf16[512,512]{1,0:T(8,128)(2,1)} %copy-done.7, ...), custom_call_target="tpu_custom_call" | custom-call | flops 2684354560 | bytes 10485760 | tf_op jit(solution)/shard_map/back/pallas_call | solution.py:262
  96.8 0.7 slice_bitcast_fusion.2
  97.6 3.1 %collective-permute-start.14 = (f32[1,768]{1,0:T(1,128)S(1)}, f32[1,768]{1,0:T(1,128)S(1)}, u32[]{:S(2)}, u32[]{:S(2)}) collective-permute-start(f32[1,768]{1,0:T(1,128)S(1)} %get-tuple-element.82), channel_id=1, source_target_pairs={{0,6},{2,0},{4,2},{6,4},{1,7},{3,1},{5,3},{7,5},{8,14},{10,8},{12,... | collective-permute-start | bytes 9224 | tf_op jit(solution)/shard_map/ppermute | solution.py:27
  100.7 0.8 collective-permute-start.16
  101.5 0.9 collective-permute-start.15
  102.4 3.4 %collective-permute-done.16 = f32[1,768]{1,0:T(1,128)S(1)} collective-permute-done((f32[1,768]{1,0:T(1,128)S(1)}, f32[1,768]{1,0:T(1,128)S(1)}, u32[]{:S(2)}, u32[]{:S(2)}) %collective-permute-start.16) | collective-permute-done | bytes 3104 | tf_op jit(solution)/shard_map/ppermute | solution.py:27
  107.3 1.7 %collective-permute-start.21 = (bf16[512,640]{1,0:T(8,128)(2,1)}, bf16[512,640]{1,0:T(8,128)(2,1)}, u32[]{:S(2)}, u32[]{:S(2)}) collective-permute-start(bf16[512,640]{1,0:T(8,128)(2,1)} %get-tuple-element.72), channel_id=1, source_target_pairs={{0,2},{2,4},{4,6},{6,0},{1,3},{3,5},{5,7},{7,1},{8,10},{10,12},{12... | collective-permute-start | bytes 1966088 | tf_op jit(solution)/shard_map/ppermute | solution.py:27
  109.0 1.5 collective-permute-start.22
  110.6 3.5 %collective-permute-done.17 = f32[1,768]{1,0:T(1,128)S(1)} collective-permute-done((f32[1,768]{1,0:T(1,128)S(1)}, f32[1,768]{1,0:T(1,128)S(1)}, u32[]{:S(2)}, u32[]{:S(2)}) %collective-permute-start.17) | collective-permute-done | bytes 3104 | tf_op jit(solution)/shard_map/ppermute | solution.py:31
  114.1 2.1 %collective-permute-start.18 = (f32[1,768]{1,0:T(1,128)S(1)}, f32[1,768]{1,0:T(1,128)S(1)}, u32[]{:S(2)}, u32[]{:S(2)}) collective-permute-start(f32[1,768]{1,0:T(1,128)S(1)} %add.53), channel_id=1, source_target_pairs={{0,224},{32,64},{64,32},{96,128},{128,96},{160,192},{192,160},{224... | collective-permute-start | bytes 9224 | tf_op jit(solution)/shard_map/ppermute | solution.py:31
  116.2 1.6 collective-permute-done.18
  117.8 5.7 %collective-permute-start.19 = (f32[1,768]{1,0:T(1,128)S(1)}, f32[1,768]{1,0:T(1,128)S(1)}, u32[]{:S(2)}, u32[]{:S(2)}) collective-permute-start(f32[1,768]{1,0:T(1,128)S(1)} %add.54), channel_id=1, source_target_pairs={{0,96},{32,192},{64,160},{96,0},{128,224},{160,64},{192,32},{224,1... | collective-permute-start | bytes 9224 | tf_op jit(solution)/shard_map/ppermute | solution.py:31
  124.1 1.0 collective-permute-done.19
  125.7 1.5 copy-done
  127.1 2.9 %sum_x.1 = bf16[8,160,256]{2,1,0:T(8,128)(2,1)} custom-call(bf16[4,8,160,256]{3,2,1,0:T(8,128)(2,1)} %copy-done), custom_call_target="tpu_custom_call" | custom-call | flops 1310720 | bytes 3932160 | tf_op jit(solution)/shard_map/sum_x/pallas_call | solution.py:332
  130.1 7.8 %all-to-all-start.3 = ((bf16[8,160,256]{2,1,0:T(8,128)(2,1)}), bf16[8,160,256]{2,1,0:T(8,128)(2,1)}, u32[]{:S(2)}, u32[]{:S(2)}) async-start(bf16[8,160,256]{2,1,0:T(8,128)(2,1)} %sum_x.1), calls=%async_computation.4 | async-start | bytes 1310720 | tf_op jit(solution)/shard_map/all_to_all | solution.py:447
  138.1 0.7 copy-done.20
  138.8 3.3 %final.1 = bf16[2,256,640]{2,1,0:T(8,128)(2,1)} custom-call(bf16[512,640]{1,0:T(8,128)(2,1)} %get-tuple-element.70.u0, bf16[512,640]{1,0:T(8,128)(2,1)} %copy-done.20, bf16[512,640]{1,0:T(8,128)(2,1)} %collective-permute-done.21.u2, bf16[512,640]{1,0:T(8,128)(2,1)} %collective-permute-done.22.u3, bf16[2,256,640]{2,1,0:T(8,128)(2,1)} %h_ref.1, ...), custom_call_target="tpu_custom_call" | custom-call | flops 199999995904 | bytes 3932160 | tf_op jit(solution)/shard_map/final/pallas_call | solution.py:364
  142.1 3.0 %collective-permute-start.25 = (f32[1,768]{1,0:T(1,128)S(1)}, f32[1,768]{1,0:T(1,128)S(1)}, u32[]{:S(2)}, u32[]{:S(2)}) collective-permute-start(f32[1,768]{1,0:T(1,128)S(1)} %copy-done.13), channel_id=1, source_target_pairs={{0,24},{8,0},{16,8},{24,16},{1,25},{9,1},{17,9},{25,17},{2,26},{10... | collective-permute-start | bytes 9224 | tf_op jit(solution)/shard_map/ppermute | solution.py:27
  145.1 0.8 collective-permute-start.24
  146.0 0.9 collective-permute-start.23
  146.9 3.4 %collective-permute-done.24 = f32[1,768]{1,0:T(1,128)S(1)} collective-permute-done((f32[1,768]{1,0:T(1,128)S(1)}, f32[1,768]{1,0:T(1,128)S(1)}, u32[]{:S(2)}, u32[]{:S(2)}) %collective-permute-start.24) | collective-permute-done | bytes 3104 | tf_op jit(solution)/shard_map/ppermute | solution.py:27
  152.0 2.6 %reduce-scatter.5.cloned.1.call-done = bf16[1,160,256]{2,1,0:T(8,128)(2,1)} async-done(((bf16[4,160,256]{2,1,0:T(8,128)(2,1)}), bf16[1,160,256]{2,1,0:T(8,128)(2,1)}) %reduce-scatter.5.cloned.1.call-update) | async-done | bytes 81936 | tf_op jit(solution)/shard_map/reduce_scatter | solution.py:448
  154.5 1.9 %join.1 = f32[160,512]{1,0:T(8,128)} custom-call(bf16[8,160,256]{2,1,0:T(8,128)(2,1)} %all-to-all-done.3.from_z, bf16[160,256]{1,0:T(8,128)(2,1)} %bitcast.30), custom_call_target="tpu_custom_call" | custom-call | flops 655360 | bytes 1310720 | tf_op jit(solution)/shard_map/join/pallas_call | solution.py:364
  (90 shorter events, 10.2 us)
Async XLA Ops:
  7.2 28.1 %copy-start.21 = (s32[4]{0:T(128)S(1)}, s32[4]{0:T(128)}, u32[]{:S(2)}) copy-start(s32[4]{0:T(128)} %constant.37.clone) | copy-start | bytes 52
  9.0 26.9 %copy-start.1 = (bf16[528,640]{1,0:T(8,128)(2,1)}, bf16[528,640]{1,0:T(8,128)(2,1)S(1)}, u32[]{:S(2)}) copy-start(bf16[528,640]{1,0:T(8,128)(2,1)S(1)} %pad_maximum_fusion.refs_0_) | copy-start | bytes 2027524
  9.0 19.1 %collective-permute-start.1 = (bf16[528,640]{1,0:T(8,128)(2,1)S(1)}, bf16[528,640]{1,0:T(8,128)(2,1)S(1)}, u32[]{:S(2)}, u32[]{:S(2)}) collective-permute-start(bf16[528,640]{1,0:T(8,128)(2,1)S(1)} %pad_maximum_fusion.refs_0_), channel_id=1, source_target_pairs={{0,6},{2,0},{4,2},{6,4},{1,7},{3,1},{5,3},{7,5},{8,14},{10,8},{12,... | collective-permute-start | bytes 2027528 | tf_op jit(solution)/shard_map/ppermute | solution.py:27
  12.1 17.8 %collective-permute-start = (bf16[528,640]{1,0:T(8,128)(2,1)S(1)}, bf16[528,640]{1,0:T(8,128)(2,1)S(1)}, u32[]{:S(2)}, u32[]{:S(2)}) collective-permute-start(bf16[528,640]{1,0:T(8,128)(2,1)S(1)} %pad_maximum_fusion.refs_0_), channel_id=1, source_target_pairs={{0,2},{2,4},{4,6},{6,0},{1,3},{3,5},{5,7},{7,1},{8,10},{10,12},{12... | collective-permute-start | bytes 2027528 | tf_op jit(solution)/shard_map/ppermute | solution.py:27
  13.4 14.7 %all-to-all-start = ((f32[8,1,128]{2,1,0:T(1,128)}), f32[8,1,128]{2,1,0:T(1,128)S(1)}, u32[]{:S(2)}, u32[]{:S(2)}) async-start(f32[8,1,128]{2,1,0:T(1,128)} %local.1), calls=%async_computation | async-start | bytes 8192 | tf_op jit(solution)/shard_map/all_to_all | solution.py:402
  22.0 13.9 %collective-permute-start.3 = (bf16[528,640]{1,0:T(8,128)(2,1)S(1)}, bf16[528,640]{1,0:T(8,128)(2,1)S(1)}, u32[]{:S(2)}, u32[]{:S(2)}) collective-permute-start(bf16[528,640]{1,0:T(8,128)(2,1)S(1)} %pad_maximum_fusion.refs_0_), channel_id=1, source_target_pairs={{0,1},{1,0},{2,3},{3,2},{4,5},{5,4},{6,7},{7,6},{8,9},{9,8},{10,11... | collective-permute-start | bytes 2027528 | tf_op jit(solution)/shard_map/ppermute | solution.py:27
  28.2 35.1 %copy-start.14 = (f32[128]{0:T(128)}, f32[128]{0:T(128)S(1)}, u32[]{:S(2)}) copy-start(f32[128]{0:T(128)S(1)} %reduce_sum.11) | copy-start | bytes 1540
  28.2 7.8 %copy-start.3 = (bf16[528,640]{1,0:T(8,128)(2,1)}, bf16[528,640]{1,0:T(8,128)(2,1)S(1)}, u32[]{:S(2)}) copy-start(bf16[528,640]{1,0:T(8,128)(2,1)S(1)} %collective-permute-done.1.refs_4_) | copy-start | bytes 2027524
  30.0 6.0 %copy-start.2 = (bf16[528,640]{1,0:T(8,128)(2,1)}, bf16[528,640]{1,0:T(8,128)(2,1)S(1)}, u32[]{:S(2)}) copy-start(bf16[528,640]{1,0:T(8,128)(2,1)S(1)} %collective-permute-done.refs_2_) | copy-start | bytes 2027524
  31.5 4.4 %collective-permute-start.4 = (bf16[528,640]{1,0:T(8,128)(2,1)S(1)}, bf16[528,640]{1,0:T(8,128)(2,1)S(1)}, u32[]{:S(2)}, u32[]{:S(2)}) collective-permute-start(bf16[528,640]{1,0:T(8,128)(2,1)S(1)} %collective-permute-done.refs_2_), channel_id=1, source_target_pairs={{0,1},{1,0},{2,3},{3,2},{4,5},{5,4},{6,7},{7,6},{8,9},{9,8},{10,11... | collective-permute-start | bytes 2027528 | tf_op jit(solution)/shard_map/ppermute | solution.py:27
  31.5 4.4 %collective-permute-start.5 = (bf16[528,640]{1,0:T(8,128)(2,1)S(1)}, bf16[528,640]{1,0:T(8,128)(2,1)}, u32[]{:S(2)}, u32[]{:S(2)}) collective-permute-start(bf16[528,640]{1,0:T(8,128)(2,1)S(1)} %collective-permute-done.1.refs_4_), channel_id=1, source_target_pairs={{0,1},{1,0},{2,3},{3,2},{4,5},{5,4},{6,7},{7,6},{8,9},{9,8},{10,11... | collective-permute-start | bytes 2027528 | tf_op jit(solution)/shard_map/ppermute | solution.py:27
  32.0 14.5 %collective-permute-start.2 = (bf16[272,640]{1,0:T(8,128)(2,1)}, bf16[272,640]{1,0:T(8,128)(2,1)}, u32[]{:S(2)}, u32[]{:S(2)}) collective-permute-start(bf16[272,640]{1,0:T(8,128)(2,1)} %slice.28), channel_id=1, source_target_pairs={{0,2},{2,4},{4,6},{6,0},{1,3},{3,5},{5,7},{7,1},{8,10},{10,12},{12... | collective-permute-start | bytes 1044488 | tf_op jit(solution)/shard_map/ppermute | solution.py:27
  32.0 14.6 %collective-permute-start.6 = (bf16[256,640]{1,0:T(8,128)(2,1)}, bf16[256,640]{1,0:T(8,128)(2,1)}, u32[]{:S(2)}, u32[]{:S(2)}) collective-permute-start(bf16[256,640]{1,0:T(8,128)(2,1)} %slice.29), channel_id=1, source_target_pairs={{0,6},{2,0},{4,2},{6,4},{1,7},{3,1},{5,3},{7,5},{8,14},{10,8},{12,... | collective-permute-start | bytes 983048 | tf_op jit(solution)/shard_map/ppermute | solution.py:27
  35.9 11.3 %copy-start.15 = (s32[2,256]{1,0:T(2,128)S(1)}, s32[2,256]{1,0:T(2,128)}, u32[]{:S(2)}) copy-start(s32[2,256]{1,0:T(2,128)} %param.12) | copy-start | bytes 6148
  35.9 0.9 copy-start.4
  35.9 1.1 copy-start.5
  46.6 2.4 %collective-permute-start.7 = (bf16[272,640]{1,0:T(8,128)(2,1)}, bf16[272,640]{1,0:T(8,128)(2,1)S(1)}, u32[]{:S(2)}, u32[]{:S(2)}) collective-permute-start(bf16[272,640]{1,0:T(8,128)(2,1)} %collective-permute-done.2.refs_0_), channel_id=1, source_target_pairs={{0,1},{1,0},{2,3},{3,2},{4,5},{5,4},{6,7},{7,6},{8,9},{9,8},{10,11... | collective-permute-start | bytes 1044488 | tf_op jit(solution)/shard_map/ppermute | solution.py:27
  46.7 2.3 %collective-permute-start.8 = (bf16[256,640]{1,0:T(8,128)(2,1)}, bf16[256,640]{1,0:T(8,128)(2,1)S(1)}, u32[]{:S(2)}, u32[]{:S(2)}) collective-permute-start(bf16[256,640]{1,0:T(8,128)(2,1)} %collective-permute-done.6.refs_1_), channel_id=1, source_target_pairs={{0,1},{1,0},{2,3},{3,2},{4,5},{5,4},{6,7},{7,6},{8,9},{9,8},{10,11... | collective-permute-start | bytes 983048 | tf_op jit(solution)/shard_map/ppermute | solution.py:27
  49.8 14.3 %copy-start.16 = (f32[2,256]{1,0:T(2,128)S(1)}, f32[2,256]{1,0:T(2,128)}, u32[]{:S(2)}) copy-start(f32[2,256]{1,0:T(2,128)} %param.14) | copy-start | bytes 6148
  56.0 30.1 %collective-permute-start.13 = (bf16[512,5120]{1,0:T(8,128)(2,1)}, bf16[512,5120]{1,0:T(8,128)(2,1)}, u32[]{:S(2)}, u32[]{:S(2)}) collective-permute-start(bf16[512,5120]{1,0:T(8,128)(2,1)} %head.1), channel_id=1, source_target_pairs={{0,1},{1,0},{2,3},{3,2},{4,5},{5,4},{6,7},{7,6},{8,9},{9,8},{10,11... | collective-permute-start | bytes 15728648 | tf_op jit(solution)/shard_map/ppermute | solution.py:27
  56.2 11.8 %all-to-all-start.1 = ((f32[8,8,512]{2,1,0:T(8,128)}), f32[8,8,512]{2,1,0:T(8,128)S(1)}, u32[]{:S(2)}, u32[]{:S(2)}) async-start(f32[8,8,512]{2,1,0:T(8,128)} %get-tuple-element.56), calls=%async_computation.1 | async-start | bytes 262144 | tf_op jit(solution)/shard_map/all_to_all | solution.py:425
  59.6 70.5 %reduce-scatter.3.cloned.1.call-start = ((), (), s32[]{:S(2)}) async-start(), calls=%async_computation.6 | async-start | bytes 2949120 | tf_op jit(solution)/shard_map/reduce_scatter | solution.py:431
  59.6 5.1 %collective-permute-start.11 = (f32[1,128]{1,0:T(1,128)S(1)}, f32[1,128]{1,0:T(1,128)S(1)}, u32[]{:S(2)}, u32[]{:S(2)}) collective-permute-start(f32[1,128]{1,0:T(1,128)S(1)} %bitcast.34), channel_id=1, source_target_pairs={{0,24},{8,0},{16,8},{24,16},{1,25},{9,1},{17,9},{25,17},{2,26},{10... | collective-permute-start | bytes 1544 | tf_op jit(solution)/shard_map/ppermute | solution.py:27
  62.5 5.0 %collective-permute-start.10 = (f32[1,128]{1,0:T(1,128)S(1)}, f32[1,128]{1,0:T(1,128)S(1)}, u32[]{:S(2)}, u32[]{:S(2)}) collective-permute-start(f32[1,128]{1,0:T(1,128)S(1)} %bitcast.35), channel_id=1, source_target_pairs={{0,16},{8,24},{16,0},{24,8},{1,17},{9,25},{17,1},{25,9},{2,18},{10... | collective-permute-start | bytes 1544 | tf_op jit(solution)/shard_map/ppermute | solution.py:27
  63.3 4.8 %collective-permute-start.9 = (f32[1,128]{1,0:T(1,128)S(1)}, f32[1,128]{1,0:T(1,128)S(1)}, u32[]{:S(2)}, u32[]{:S(2)}) collective-permute-start(f32[1,128]{1,0:T(1,128)S(1)} %bitcast.36), channel_id=1, source_target_pairs={{0,8},{8,16},{16,24},{24,0},{1,9},{9,17},{17,25},{25,1},{2,10},{10... | collective-permute-start | bytes 1544 | tf_op jit(solution)/shard_map/ppermute | solution.py:27
  64.8 3.3 %copy-start.17 = (f32[1,128]{1,0:T(1,128)}, f32[1,128]{1,0:T(1,128)S(1)}, u32[]{:S(2)}) copy-start(f32[1,128]{1,0:T(1,128)S(1)} %collective-permute-done.11.sum3) | copy-start | bytes 1540
  80.3 3.9 %copy-start.6 = (bf16[512,512]{1,0:T(8,128)(2,1)S(1)}, bf16[512,512]{1,0:T(8,128)(2,1)}, u32[]{:S(2)}) copy-start(bf16[512,512]{1,0:T(8,128)(2,1)} %get-tuple-element.62.dl) | copy-start | bytes 1572868
  80.3 45.4 %all-to-all-start.2 = ((bf16[4,8,160,256]{3,2,1,0:T(8,128)(2,1)}), bf16[4,8,160,256]{3,2,1,0:T(8,128)(2,1)S(1)}, u32[]{:S(2)}, u32[]{:S(2)}) async-start(bf16[4,8,160,256]{3,2,1,0:T(8,128)(2,1)} %get-tuple-element.61), calls=%async_computation.2 | async-start | bytes 5242880 | tf_op jit(solution)/shard_map/all_to_all | solution.py:432
  84.1 70.4 %reduce-scatter.5.cloned.1.call-start = ((), (), s32[]{:S(2)}) async-start(), calls=%async_computation.7 | async-start | bytes 409600 | tf_op jit(solution)/shard_map/reduce_scatter | solution.py:448
  84.1 2.0 %collective-permute-start.12 = (bf16[512,512]{1,0:T(8,128)(2,1)S(1)}, bf16[512,512]{1,0:T(8,128)(2,1)S(1)}, u32[]{:S(2)}, u32[]{:S(2)}) collective-permute-start(bf16[512,512]{1,0:T(8,128)(2,1)S(1)} %copy-done.6), channel_id=1, source_target_pairs={{0,1},{1,0},{2,3},{3,2},{4,5},{5,4},{6,7},{7,6},{8,9},{9,8},{10,11... | collective-permute-start | bytes 1572872 | tf_op jit(solution)/shard_map/ppermute | solution.py:27
  87.0 36.5 %copy-start.11 = (bf16[640]{0:T(1024)(128)(2,1)S(1)}, bf16[640]{0:T(1024)(128)(2,1)}, u32[]{:S(2)}) copy-start(bf16[640]{0:T(1024)(128)(2,1)} %param.10) | copy-start | bytes 3844
  97.6 4.8 %collective-permute-start.14 = (f32[1,768]{1,0:T(1,128)S(1)}, f32[1,768]{1,0:T(1,128)S(1)}, u32[]{:S(2)}, u32[]{:S(2)}) collective-permute-start(f32[1,768]{1,0:T(1,128)S(1)} %get-tuple-element.82), channel_id=1, source_target_pairs={{0,6},{2,0},{4,2},{6,4},{1,7},{3,1},{5,3},{7,5},{8,14},{10,8},{12,... | collective-permute-start | bytes 9224 | tf_op jit(solution)/shard_map/ppermute | solution.py:27
  100.7 5.1 %collective-permute-start.16 = (f32[1,768]{1,0:T(1,128)S(1)}, f32[1,768]{1,0:T(1,128)S(1)}, u32[]{:S(2)}, u32[]{:S(2)}) collective-permute-start(f32[1,768]{1,0:T(1,128)S(1)} %get-tuple-element.83), channel_id=1, source_target_pairs={{0,4},{2,6},{4,0},{6,2},{1,5},{3,7},{5,1},{7,3},{8,12},{10,14},{12... | collective-permute-start | bytes 9224 | tf_op jit(solution)/shard_map/ppermute | solution.py:27
  101.5 4.8 %collective-permute-start.15 = (f32[1,768]{1,0:T(1,128)S(1)}, f32[1,768]{1,0:T(1,128)S(1)}, u32[]{:S(2)}, u32[]{:S(2)}) collective-permute-start(f32[1,768]{1,0:T(1,128)S(1)} %get-tuple-element.84), channel_id=1, source_target_pairs={{0,2},{2,4},{4,6},{6,0},{1,3},{3,5},{5,7},{7,1},{8,10},{10,12},{12... | collective-permute-start | bytes 9224 | tf_op jit(solution)/shard_map/ppermute | solution.py:27
  107.0 30.9 %collective-permute-start.20 = (bf16[512,640]{1,0:T(8,128)(2,1)}, bf16[512,640]{1,0:T(8,128)(2,1)S(1)}, u32[]{:S(2)}, u32[]{:S(2)}) collective-permute-start(bf16[512,640]{1,0:T(8,128)(2,1)} %get-tuple-element.71), channel_id=1, source_target_pairs={{0,6},{2,0},{4,2},{6,4},{1,7},{3,1},{5,3},{7,5},{8,14},{10,8},{12,... | collective-permute-start | bytes 1966088 | tf_op jit(solution)/shard_map/ppermute | solution.py:27
  107.3 30.6 %collective-permute-start.21 = (bf16[512,640]{1,0:T(8,128)(2,1)}, bf16[512,640]{1,0:T(8,128)(2,1)}, u32[]{:S(2)}, u32[]{:S(2)}) collective-permute-start(bf16[512,640]{1,0:T(8,128)(2,1)} %get-tuple-element.72), channel_id=1, source_target_pairs={{0,2},{2,4},{4,6},{6,0},{1,3},{3,5},{5,7},{7,1},{8,10},{10,12},{12... | collective-permute-start | bytes 1966088 | tf_op jit(solution)/shard_map/ppermute | solution.py:27
  109.0 29.0 %collective-permute-start.22 = (bf16[512,640]{1,0:T(8,128)(2,1)}, bf16[512,640]{1,0:T(8,128)(2,1)}, u32[]{:S(2)}, u32[]{:S(2)}) collective-permute-start(bf16[512,640]{1,0:T(8,128)(2,1)} %get-tuple-element.73), channel_id=1, source_target_pairs={{0,4},{2,6},{4,0},{6,2},{1,5},{3,7},{5,1},{7,3},{8,12},{10,14},{12... | collective-permute-start | bytes 1966088 | tf_op jit(solution)/shard_map/ppermute | solution.py:27
  110.5 3.6 %collective-permute-start.17 = (f32[1,768]{1,0:T(1,128)S(1)}, f32[1,768]{1,0:T(1,128)S(1)}, u32[]{:S(2)}, u32[]{:S(2)}) collective-permute-start(f32[1,768]{1,0:T(1,128)S(1)} %fusion.1), channel_id=1, source_target_pairs={{0,32},{32,0},{64,96},{96,64},{128,160},{160,128},{192,224},{224,1... | collective-permute-start | bytes 9224 | tf_op jit(solution)/shard_map/ppermute | solution.py:31
  114.1 3.6 %collective-permute-start.18 = (f32[1,768]{1,0:T(1,128)S(1)}, f32[1,768]{1,0:T(1,128)S(1)}, u32[]{:S(2)}, u32[]{:S(2)}) collective-permute-start(f32[1,768]{1,0:T(1,128)S(1)} %add.53), channel_id=1, source_target_pairs={{0,224},{32,64},{64,32},{96,128},{128,96},{160,192},{192,160},{224... | collective-permute-start | bytes 9224 | tf_op jit(solution)/shard_map/ppermute | solution.py:31
  117.8 7.3 %collective-permute-start.19 = (f32[1,768]{1,0:T(1,128)S(1)}, f32[1,768]{1,0:T(1,128)S(1)}, u32[]{:S(2)}, u32[]{:S(2)}) collective-permute-start(f32[1,768]{1,0:T(1,128)S(1)} %add.54), channel_id=1, source_target_pairs={{0,96},{32,192},{64,160},{96,0},{128,224},{160,64},{192,32},{224,1... | collective-permute-start | bytes 9224 | tf_op jit(solution)/shard_map/ppermute | solution.py:31
  125.7 1.5 copy-start
  130.1 24.4 %all-to-all-start.3 = ((bf16[8,160,256]{2,1,0:T(8,128)(2,1)}), bf16[8,160,256]{2,1,0:T(8,128)(2,1)}, u32[]{:S(2)}, u32[]{:S(2)}) async-start(bf16[8,160,256]{2,1,0:T(8,128)(2,1)} %sum_x.1), calls=%async_computation.4 | async-start | bytes 1310720 | tf_op jit(solution)/shard_map/all_to_all | solution.py:447
  137.9 0.8 copy-start.20
  138.8 3.3 %copy-start.13 = (f32[1,768]{1,0:T(1,128)S(1)}, f32[1,768]{1,0:T(1,128)}, u32[]{:S(2)}) copy-start(f32[1,768]{1,0:T(1,128)} %add.55) | copy-start | bytes 9220
  138.8 12.6 %copy-start.12 = (bf16[640]{0:T(1024)(128)(2,1)S(1)}, bf16[640]{0:T(1024)(128)(2,1)}, u32[]{:S(2)}) copy-start(bf16[640]{0:T(1024)(128)(2,1)} %param.10) | copy-start | bytes 3844
  142.1 4.8 %collective-permute-start.25 = (f32[1,768]{1,0:T(1,128)S(1)}, f32[1,768]{1,0:T(1,128)S(1)}, u32[]{:S(2)}, u32[]{:S(2)}) collective-permute-start(f32[1,768]{1,0:T(1,128)S(1)} %copy-done.13), channel_id=1, source_target_pairs={{0,24},{8,0},{16,8},{24,16},{1,25},{9,1},{17,9},{25,17},{2,26},{10... | collective-permute-start | bytes 9224 | tf_op jit(solution)/shard_map/ppermute | solution.py:27
  145.1 5.1 %collective-permute-start.24 = (f32[1,768]{1,0:T(1,128)S(1)}, f32[1,768]{1,0:T(1,128)S(1)}, u32[]{:S(2)}, u32[]{:S(2)}) collective-permute-start(f32[1,768]{1,0:T(1,128)S(1)} %copy-done.13), channel_id=1, source_target_pairs={{0,16},{8,24},{16,0},{24,8},{1,17},{9,25},{17,1},{25,9},{2,18},{10... | collective-permute-start | bytes 9224 | tf_op jit(solution)/shard_map/ppermute | solution.py:27
  146.0 4.8 %collective-permute-start.23 = (f32[1,768]{1,0:T(1,128)S(1)}, f32[1,768]{1,0:T(1,128)S(1)}, u32[]{:S(2)}, u32[]{:S(2)}) collective-permute-start(f32[1,768]{1,0:T(1,128)S(1)} %copy-done.13), channel_id=1, source_target_pairs={{0,8},{8,16},{16,24},{24,0},{1,9},{9,17},{17,25},{25,1},{2,10},{10... | collective-permute-start | bytes 9224 | tf_op jit(solution)/shard_map/ppermute | solution.py:27
  (6 other events, 4.1 us)
Sparse Core Ops, SparseCore 0:
  80.4 44.4 reduce-scatter.2
  130.2 24.2 reduce-scatter.4

commit v9 on v6

--- a/solution.py
+++ b/solution.py
@@ -437,11 +437,9 @@
 
     for step in (1, -1, 3):
         tail = tail + turn(tail, step)
-    from_x = after(from_x, tail)
+    from_x = after(from_x, tail, half_z)
 
     to_z = sum_first(from_x, "sum_x")
-    half_z = after(half_z, to_z)
-    to_z = after(to_z, half_z)
     from_z = lax.all_to_all(to_z, "z", 0, 0, tiled=True)
     half_z = lax.psum_scatter(half_z, "x", scatter_dimension=0, tiled=False)
     u1, u2, u3, _ = lax.optimization_barrier((u1, u2, u3, to_z))

time: 162 us -> 161 us (level)
  no operation moved by 1% of the time
where the time goes in v9:
time: 161 us
  starting transfers between devices  47.8 us (30%)
  Pallas kernels  46.9 us (29%)
  waiting for transfers between devices  37.7 us (23%)
  between operations  14.3 us (9%)
  local copies, waits for them, and re-layouts  10.8 us (7%)
  other arithmetic  3.05 us (2%)
    ppermute x20, starting transfers between devices, shift(): return lax.ppermute(value, axis, [(i, (i + step) % n) for i in range(n)])  18.1 us
    ppermute x20, waiting for transfers between devices, shift(): return lax.ppermute(value, axis, [(i, (i + step) % n) for i in range(n)])  16 us
    pallas_call x2, Pallas kernels, logits_of(): pl.pallas_call(functools.partial(logits_kernel, count, per, last), out_sh...  15.7 us
    all_to_all x1, starting transfers between devices, body(): sums = lax.all_to_all(local, DP, 0, 0, tiled=True)  11.2 us
    pallas_call x1, Pallas kernels, back_of(): pl.pallas_call(back_kernel, out_shape=shapes, grid_spec=pltpu.PrefetchSca...  10.1 us
    pallas_call x1, Pallas kernels, heads_of(): pl.pallas_call(heads_kernel, out_shape=shapes, grid_spec=pltpu.PrefetchSc...  8.87 us
    all_to_all x1, waiting for transfers between devices, body(): sums = lax.all_to_all(local, DP, 0, 0, tiled=True)  8.38 us
    ppermute x3, waiting for transfers between devices, turn(): lax.ppermute(value, 'z', [(i, (i + (step if i % 2 == 0 else -step)) % 8)...  7.88 us
  transfers between devices with their start and end apart: 29, of which 13 were waited for; matrix products, arithmetic and copies ran while one was open for 4% of the time, Pallas kernels for 24%

profile of v9, /device:TPU:32, one launch (start us, length us, event | category | flops | bytes accessed | tf_op | source)
XLA Modules:
  0.0 160.6 jit_solution(1463673899607727348)
XLA Ops:
  7.2 0.7 broadcast_in_dim.8
  7.9 1.1 pad_maximum_fusion.refs_0_
  9.0 3.1 %collective-permute-start.1 = (bf16[528,640]{1,0:T(8,128)(2,1)S(1)}, bf16[528,640]{1,0:T(8,128)(2,1)S(1)}, u32[]{:S(2)}, u32[]{:S(2)}) collective-permute-start(bf16[528,640]{1,0:T(8,128)(2,1)S(1)} %pad_maximum_fusion.refs_0_), channel_id=1, source_target_pairs={{0,6},{2,0},{4,2},{6,4},{1,7},{3,1},{5,3},{7,5},{8,14},{10,8},{12,... | collective-permute-start | bytes 2027528 | tf_op jit(solution)/shard_map/ppermute | solution.py:27
  12.1 1.3 local.1
  13.4 11.2 %all-to-all-start = ((f32[32,1,128]{2,1,0:T(1,128)}), f32[32,1,128]{2,1,0:T(1,128)S(1)}, u32[]{:S(2)}, u32[]{:S(2)}) async-start(f32[32,1,128]{2,1,0:T(1,128)} %local.1), calls=%async_computation | async-start | bytes 32768 | tf_op jit(solution)/shard_map/all_to_all | solution.py:402
  24.7 8.4 %all-to-all-done.sums_ref = f32[32,1,128]{2,1,0:T(1,128)S(1)} async-done(((f32[32,1,128]{2,1,0:T(1,128)}), f32[32,1,128]{2,1,0:T(1,128)S(1)}, u32[]{:S(2)}, u32[]{:S(2)}) %all-to-all-start) | async-done | bytes 16416 | tf_op jit(solution)/shard_map/all_to_all | solution.py:402
  33.1 0.8 slice.29
  33.9 0.8 slice.28
  35.8 2.7 %collective-permute-start.6 = (bf16[256,640]{1,0:T(8,128)(2,1)}, bf16[256,640]{1,0:T(8,128)(2,1)}, u32[]{:S(2)}, u32[]{:S(2)}) collective-permute-start(bf16[256,640]{1,0:T(8,128)(2,1)} %slice.29), channel_id=1, source_target_pairs={{0,6},{2,0},{4,2},{6,4},{1,7},{3,1},{5,3},{7,5},{8,14},{10,8},{12,... | collective-permute-start | bytes 983048 | tf_op jit(solution)/shard_map/ppermute | solution.py:27
  38.5 0.7 concatenate.6.at
  39.2 0.8 copy-done.4
  40.3 9.5 %logits_first.1 = (bf16[3,512,1280]{2,1,0:T(8,128)(2,1)}, f32[512,512]{1,0:T(8,128)}, f32[8,512]{1,0:T(8,128)}) custom-call(s32[12]{0:T(128)} %concatenate.6.at, bf16[528,640]{1,0:T(8,128)(2,1)} %copy-done.1, bf16[528,640]{1,0:T(8,128)(2,1)} %copy-done.4, bf16[528,640]{1,0:T(8,128)(2,1)} %copy-done.2, bf16[528,640]{1,0:T(8,128)(2,1)} %copy-done.5, ...), custom_call_target="tpu_custom_call" | custom-call | flops 1000 | bytes 1000 | tf_op jit(solution)/shard_map/logits_first/pallas_call | solution.py:163
  51.0 1.2 collective-permute-done.8.refs_3_
  52.3 0.7 copy-done.10
  53.1 6.1 %logits_last.1 = (bf16[1,512,1280]{2,1,0:T(8,128)(2,1)}, f32[512,512]{1,0:T(8,128)}, f32[8,8,512]{2,1,0:T(8,128)}, f32[8,512]{1,0:T(8,128)}) custom-call(s32[12]{0:T(128)} %concatenate.6.at, bf16[272,640]{1,0:T(8,128)(2,1)} %collective-permute-done.2.refs_0_, bf16[256,640]{1,0:T(8,128)(2,1)} %collective-permute-done.6.refs_1_, bf16[272,640]{1,0:T(8,128)(2,1)} %copy-done.9, ...), custom_call_target="tpu_custom_call" | custom-call | flops 1000 | bytes 1000 | tf_op jit(solution)/shard_map/logits_last/pallas_call | solution.py:163
  59.5 3.4 %all-to-all-start.1 = ((f32[8,8,512]{2,1,0:T(8,128)}), f32[8,8,512]{2,1,0:T(8,128)S(1)}, u32[]{:S(2)}, u32[]{:S(2)}) async-start(f32[8,8,512]{2,1,0:T(8,128)} %get-tuple-element.51), calls=%async_computation.1 | async-start | bytes 262144 | tf_op jit(solution)/shard_map/all_to_all | solution.py:423
  63.5 5.4 %all-to-all-done.1.st = f32[8,8,512]{2,1,0:T(8,128)S(1)} async-done(((f32[8,8,512]{2,1,0:T(8,128)}), f32[8,8,512]{2,1,0:T(8,128)S(1)}, u32[]{:S(2)}, u32[]{:S(2)}) %all-to-all-start.1) | async-done | bytes 131104 | tf_op jit(solution)/shard_map/all_to_all | solution.py:423
  69.6 2.8 %policy.1 = (bf16[512,512]{1,0:T(8,128)(2,1)}, f32[8,512]{1,0:T(8,128)}) custom-call(s32[12]{0:T(128)} %concatenate.6.at, f32[2]{0:T(128)} %rewards.3, s32[2]{0:T(128)} %lengths.3, s32[2]{0:T(128)} %slots.3, f32[32,1,128]{2,1,0:T(1,128)} %copy-done.11, f32[8,8,512]{2,1,0:T(8,128)} %copy-done.8, f32[512,512]{1,0:T(8,128)} %get-tuple-element.52.lg, ...), custom_call_target="tpu_custom_call" | custom-call | flops 2097152 | bytes 1572864 | tf_op jit(solution)/shard_map/policy/pallas_call | solution.py:230
  72.4 8.9 %heads.1 = (bf16[4,8,160,256]{3,2,1,0:T(8,128)(2,1)}, bf16[8,4,160,256]{3,2,1,0:T(8,128)(2,1)}) custom-call(s32[12]{0:T(128)} %concatenate.6.at, bf16[3,512,1280]{2,1,0:T(8,128)(2,1)} %get-tuple-element.55.early, bf16[1,512,1280]{2,1,0:T(8,128)(2,1)} %get-tuple-element.56.late, bf16[512,512]{1,0:T(8,128)(2,1)} %get-tuple-element.58.dl), custom_call_target="tpu_custom_call" | custom-call | flops 2684354560 | bytes 15728640 | tf_op jit(solution)/shard_map/heads/pallas_call | solution.py:304
  81.3 3.8 %all-to-all-start.2 = ((bf16[4,8,160,256]{3,2,1,0:T(8,128)(2,1)}), bf16[4,8,160,256]{3,2,1,0:T(8,128)(2,1)S(1)}, u32[]{:S(2)}, u32[]{:S(2)}) async-start(bf16[4,8,160,256]{3,2,1,0:T(8,128)(2,1)} %get-tuple-element.57), calls=%async_computation.2 | async-start | bytes 5242880 | tf_op jit(solution)/shard_map/all_to_all | solution.py:430
  85.5 1.9 %collective-permute-done.9.dl_o = bf16[512,512]{1,0:T(8,128)(2,1)S(1)} collective-permute-done((bf16[512,512]{1,0:T(8,128)(2,1)S(1)}, bf16[512,512]{1,0:T(8,128)(2,1)S(1)}, u32[]{:S(2)}, u32[]{:S(2)}) %collective-permute-start.9) | collective-permute-done | bytes 524320 | tf_op jit(solution)/shard_map/ppermute | solution.py:27
  87.4 0.8 copy-done.7
  88.2 10.1 %back.1 = (bf16[512,640]{1,0:T(8,128)(2,1)}, bf16[512,640]{1,0:T(8,128)(2,1)}, bf16[512,640]{1,0:T(8,128)(2,1)}, bf16[512,640]{1,0:T(8,128)(2,1)}, f32[4,1,768]{2,1,0:T(1,128)}) custom-call(s32[12]{0:T(128)} %concatenate.6.at, bf16[512,512]{1,0:T(8,128)(2,1)} %get-tuple-element.58.dl, bf16[512,512]{1,0:T(8,128)(2,1)} %copy-done.7, ...), custom_call_target="tpu_custom_call" | custom-call | flops 2684354560 | bytes 10485760 | tf_op jit(solution)/shard_map/back/pallas_call | solution.py:262
  98.3 0.7 slice_bitcast_fusion.2
  99.0 1.1 collective-permute-start.11
  100.1 1.3 collective-permute-start.13
  101.4 1.2 collective-permute-done.11
  102.6 2.6 %collective-permute-done.13 = f32[1,768]{1,0:T(1,128)S(1)} collective-permute-done((f32[1,768]{1,0:T(1,128)S(1)}, f32[1,768]{1,0:T(1,128)S(1)}, u32[]{:S(2)}, u32[]{:S(2)}) %collective-permute-start.13) | collective-permute-done | bytes 3104 | tf_op jit(solution)/shard_map/ppermute | solution.py:27
  105.2 1.0 collective-permute-done.12
  106.2 0.7 fusion.1
  106.9 1.1 collective-permute-start.17
  108.0 1.0 collective-permute-start.18
  108.9 1.0 collective-permute-start.19
  109.9 1.6 %collective-permute-start.14 = (f32[1,768]{1,0:T(1,128)S(1)}, f32[1,768]{1,0:T(1,128)S(1)}, u32[]{:S(2)}, u32[]{:S(2)}) collective-permute-start(f32[1,768]{1,0:T(1,128)S(1)} %fusion.1), channel_id=1, source_target_pairs={{0,32},{32,0},{64,96},{96,64},{128,160},{160,128},{192,224},{224,1... | collective-permute-start | bytes 9224 | tf_op jit(solution)/shard_map/ppermute | solution.py:31
  111.6 2.0 %collective-permute-done.14 = f32[1,768]{1,0:T(1,128)S(1)} collective-permute-done((f32[1,768]{1,0:T(1,128)S(1)}, f32[1,768]{1,0:T(1,128)S(1)}, u32[]{:S(2)}, u32[]{:S(2)}) %collective-permute-start.14) | collective-permute-done | bytes 3104 | tf_op jit(solution)/shard_map/ppermute | solution.py:31
  114.2 3.0 %collective-permute-done.15 = f32[1,768]{1,0:T(1,128)S(1)} collective-permute-done((f32[1,768]{1,0:T(1,128)S(1)}, f32[1,768]{1,0:T(1,128)S(1)}, u32[]{:S(2)}, u32[]{:S(2)}) %collective-permute-start.15) | collective-permute-done | bytes 3104 | tf_op jit(solution)/shard_map/ppermute | solution.py:31
  117.1 3.1 %collective-permute-start.16 = (f32[1,768]{1,0:T(1,128)S(1)}, f32[1,768]{1,0:T(1,128)S(1)}, u32[]{:S(2)}, u32[]{:S(2)}) collective-permute-start(f32[1,768]{1,0:T(1,128)S(1)} %add.54), channel_id=1, source_target_pairs={{0,96},{32,192},{64,160},{96,0},{128,224},{160,64},{192,32},{224,1... | collective-permute-start | bytes 9224 | tf_op jit(solution)/shard_map/ppermute | solution.py:31
  120.8 2.9 %collective-permute-done.16 = f32[1,768]{1,0:T(1,128)S(1)} collective-permute-done((f32[1,768]{1,0:T(1,128)S(1)}, f32[1,768]{1,0:T(1,128)S(1)}, u32[]{:S(2)}, u32[]{:S(2)}) %collective-permute-start.16) | collective-permute-done | bytes 3104 | tf_op jit(solution)/shard_map/ppermute | solution.py:31
  124.4 1.5 copy-done
  125.9 2.9 %sum_x.1 = bf16[8,160,256]{2,1,0:T(8,128)(2,1)} custom-call(bf16[4,8,160,256]{3,2,1,0:T(8,128)(2,1)} %copy-done), custom_call_target="tpu_custom_call" | custom-call | flops 1310720 | bytes 3932160 | tf_op jit(solution)/shard_map/sum_x/pallas_call | solution.py:332
  128.8 5.9 %all-to-all-start.3 = ((bf16[8,160,256]{2,1,0:T(8,128)(2,1)}), bf16[8,160,256]{2,1,0:T(8,128)(2,1)}, u32[]{:S(2)}, u32[]{:S(2)}) async-start(bf16[8,160,256]{2,1,0:T(8,128)(2,1)} %sum_x.1), calls=%async_computation.4 | async-start | bytes 1310720 | tf_op jit(solution)/shard_map/all_to_all | solution.py:443
  134.7 4.0 %collective-permute-done.18.u2 = bf16[512,640]{1,0:T(8,128)(2,1)} collective-permute-done((bf16[512,640]{1,0:T(8,128)(2,1)}, bf16[512,640]{1,0:T(8,128)(2,1)}, u32[]{:S(2)}, u32[]{:S(2)}) %collective-permute-start.18) | collective-permute-done | bytes 655392 | tf_op jit(solution)/shard_map/ppermute | solution.py:27
  138.8 3.3 %final.1 = bf16[2,256,640]{2,1,0:T(8,128)(2,1)} custom-call(bf16[512,640]{1,0:T(8,128)(2,1)} %get-tuple-element.66.u0, bf16[512,640]{1,0:T(8,128)(2,1)} %copy-done.17, bf16[512,640]{1,0:T(8,128)(2,1)} %collective-permute-done.18.u2, bf16[512,640]{1,0:T(8,128)(2,1)} %collective-permute-done.19.u3, bf16[2,256,640]{2,1,0:T(8,128)(2,1)} %h_ref.1, ...), custom_call_target="tpu_custom_call" | custom-call | flops 199999995904 | bytes 3932160 | tf_op jit(solution)/shard_map/final/pallas_call | solution.py:364
  142.1 2.9 %collective-permute-start.22 = (f32[1,768]{1,0:T(1,128)S(1)}, f32[1,768]{1,0:T(1,128)S(1)}, u32[]{:S(2)}, u32[]{:S(2)}) collective-permute-start(f32[1,768]{1,0:T(1,128)S(1)} %copy-done.14), channel_id=1, source_target_pairs={{0,24},{8,0},{16,8},{24,16},{1,25},{9,1},{17,9},{25,17},{2,26},{10... | collective-permute-start | bytes 9224 | tf_op jit(solution)/shard_map/ppermute | solution.py:27
  145.0 0.9 collective-permute-start.21
  145.9 0.9 collective-permute-start.20
  146.7 3.4 %collective-permute-done.21 = f32[1,768]{1,0:T(1,128)S(1)} collective-permute-done((f32[1,768]{1,0:T(1,128)S(1)}, f32[1,768]{1,0:T(1,128)S(1)}, u32[]{:S(2)}, u32[]{:S(2)}) %collective-permute-start.21) | collective-permute-done | bytes 3104 | tf_op jit(solution)/shard_map/ppermute | solution.py:27
  151.8 1.9 %join.1 = f32[160,512]{1,0:T(8,128)} custom-call(bf16[8,160,256]{2,1,0:T(8,128)(2,1)} %all-to-all-done.3.from_z, bf16[160,256]{1,0:T(8,128)(2,1)} %bitcast.29), custom_call_target="tpu_custom_call" | custom-call | flops 655360 | bytes 1310720 | tf_op jit(solution)/shard_map/join/pallas_call | solution.py:364
  (77 shorter events, 8.2 us)
Async XLA Ops:
  7.2 31.3 %copy-start.18 = (s32[4]{0:T(128)S(1)}, s32[4]{0:T(128)}, u32[]{:S(2)}) copy-start(s32[4]{0:T(128)} %constant.35.clone) | copy-start | bytes 52
  9.0 30.2 %copy-start.1 = (bf16[528,640]{1,0:T(8,128)(2,1)}, bf16[528,640]{1,0:T(8,128)(2,1)S(1)}, u32[]{:S(2)}) copy-start(bf16[528,640]{1,0:T(8,128)(2,1)S(1)} %pad_maximum_fusion.refs_0_) | copy-start | bytes 2027524
  9.0 24.1 %collective-permute-start.1 = (bf16[528,640]{1,0:T(8,128)(2,1)S(1)}, bf16[528,640]{1,0:T(8,128)(2,1)S(1)}, u32[]{:S(2)}, u32[]{:S(2)}) collective-permute-start(bf16[528,640]{1,0:T(8,128)(2,1)S(1)} %pad_maximum_fusion.refs_0_), channel_id=1, source_target_pairs={{0,6},{2,0},{4,2},{6,4},{1,7},{3,1},{5,3},{7,5},{8,14},{10,8},{12,... | collective-permute-start | bytes 2027528 | tf_op jit(solution)/shard_map/ppermute | solution.py:27
  12.1 21.0 %collective-permute-start = (bf16[528,640]{1,0:T(8,128)(2,1)S(1)}, bf16[528,640]{1,0:T(8,128)(2,1)S(1)}, u32[]{:S(2)}, u32[]{:S(2)}) collective-permute-start(bf16[528,640]{1,0:T(8,128)(2,1)S(1)} %pad_maximum_fusion.refs_0_), channel_id=1, source_target_pairs={{0,2},{2,4},{4,6},{6,0},{1,3},{3,5},{5,7},{7,1},{8,10},{10,12},{12... | collective-permute-start | bytes 2027528 | tf_op jit(solution)/shard_map/ppermute | solution.py:27
  13.4 19.7 %all-to-all-start = ((f32[32,1,128]{2,1,0:T(1,128)}), f32[32,1,128]{2,1,0:T(1,128)S(1)}, u32[]{:S(2)}, u32[]{:S(2)}) async-start(f32[32,1,128]{2,1,0:T(1,128)} %local.1), calls=%async_computation | async-start | bytes 32768 | tf_op jit(solution)/shard_map/all_to_all | solution.py:402
  24.6 14.5 %collective-permute-start.3 = (bf16[528,640]{1,0:T(8,128)(2,1)S(1)}, bf16[528,640]{1,0:T(8,128)(2,1)S(1)}, u32[]{:S(2)}, u32[]{:S(2)}) collective-permute-start(bf16[528,640]{1,0:T(8,128)(2,1)S(1)} %pad_maximum_fusion.refs_0_), channel_id=1, source_target_pairs={{0,1},{1,0},{2,3},{3,2},{4,5},{5,4},{6,7},{7,6},{8,9},{9,8},{10,11... | collective-permute-start | bytes 2027528 | tf_op jit(solution)/shard_map/ppermute | solution.py:27
  33.1 16.7 %copy-start.11 = (f32[32,1,128]{2,1,0:T(1,128)}, f32[32,1,128]{2,1,0:T(1,128)S(1)}, u32[]{:S(2)}) copy-start(f32[32,1,128]{2,1,0:T(1,128)S(1)} %all-to-all-done.sums_ref) | copy-start | bytes 49156
  33.1 6.1 %copy-start.3 = (bf16[528,640]{1,0:T(8,128)(2,1)}, bf16[528,640]{1,0:T(8,128)(2,1)S(1)}, u32[]{:S(2)}) copy-start(bf16[528,640]{1,0:T(8,128)(2,1)S(1)} %collective-permute-done.1.refs_4_) | copy-start | bytes 2027524
  33.1 6.1 %copy-start.2 = (bf16[528,640]{1,0:T(8,128)(2,1)}, bf16[528,640]{1,0:T(8,128)(2,1)S(1)}, u32[]{:S(2)}) copy-start(bf16[528,640]{1,0:T(8,128)(2,1)S(1)} %collective-permute-done.refs_2_) | copy-start | bytes 2027524
  34.7 4.5 %collective-permute-start.4 = (bf16[528,640]{1,0:T(8,128)(2,1)S(1)}, bf16[528,640]{1,0:T(8,128)(2,1)S(1)}, u32[]{:S(2)}, u32[]{:S(2)}) collective-permute-start(bf16[528,640]{1,0:T(8,128)(2,1)S(1)} %collective-permute-done.refs_2_), channel_id=1, source_target_pairs={{0,1},{1,0},{2,3},{3,2},{4,5},{5,4},{6,7},{7,6},{8,9},{9,8},{10,11... | collective-permute-start | bytes 2027528 | tf_op jit(solution)/shard_map/ppermute | solution.py:27
  34.7 4.5 %collective-permute-start.5 = (bf16[528,640]{1,0:T(8,128)(2,1)S(1)}, bf16[528,640]{1,0:T(8,128)(2,1)}, u32[]{:S(2)}, u32[]{:S(2)}) collective-permute-start(bf16[528,640]{1,0:T(8,128)(2,1)S(1)} %collective-permute-done.1.refs_4_), channel_id=1, source_target_pairs={{0,1},{1,0},{2,3},{3,2},{4,5},{5,4},{6,7},{7,6},{8,9},{9,8},{10,11... | collective-permute-start | bytes 2027528 | tf_op jit(solution)/shard_map/ppermute | solution.py:27
  35.2 14.6 %collective-permute-start.2 = (bf16[272,640]{1,0:T(8,128)(2,1)}, bf16[272,640]{1,0:T(8,128)(2,1)}, u32[]{:S(2)}, u32[]{:S(2)}) collective-permute-start(bf16[272,640]{1,0:T(8,128)(2,1)} %slice.28), channel_id=1, source_target_pairs={{0,2},{2,4},{4,6},{6,0},{1,3},{3,5},{5,7},{7,1},{8,10},{10,12},{12... | collective-permute-start | bytes 1044488 | tf_op jit(solution)/shard_map/ppermute | solution.py:27
  35.8 14.1 %collective-permute-start.6 = (bf16[256,640]{1,0:T(8,128)(2,1)}, bf16[256,640]{1,0:T(8,128)(2,1)}, u32[]{:S(2)}, u32[]{:S(2)}) collective-permute-start(bf16[256,640]{1,0:T(8,128)(2,1)} %slice.29), channel_id=1, source_target_pairs={{0,6},{2,0},{4,2},{6,4},{1,7},{3,1},{5,3},{7,5},{8,14},{10,8},{12,... | collective-permute-start | bytes 983048 | tf_op jit(solution)/shard_map/ppermute | solution.py:27
  39.2 11.3 %copy-start.15 = (s32[2,256]{1,0:T(2,128)S(1)}, s32[2,256]{1,0:T(2,128)}, u32[]{:S(2)}) copy-start(s32[2,256]{1,0:T(2,128)} %param.12) | copy-start | bytes 6148
  39.2 0.8 copy-start.4
  39.2 1.1 copy-start.5
  49.8 2.4 %collective-permute-start.7 = (bf16[272,640]{1,0:T(8,128)(2,1)}, bf16[272,640]{1,0:T(8,128)(2,1)S(1)}, u32[]{:S(2)}, u32[]{:S(2)}) collective-permute-start(bf16[272,640]{1,0:T(8,128)(2,1)} %collective-permute-done.2.refs_0_), channel_id=1, source_target_pairs={{0,1},{1,0},{2,3},{3,2},{4,5},{5,4},{6,7},{7,6},{8,9},{9,8},{10,11... | collective-permute-start | bytes 1044488 | tf_op jit(solution)/shard_map/ppermute | solution.py:27
  50.0 2.3 %collective-permute-start.8 = (bf16[256,640]{1,0:T(8,128)(2,1)}, bf16[256,640]{1,0:T(8,128)(2,1)S(1)}, u32[]{:S(2)}, u32[]{:S(2)}) collective-permute-start(bf16[256,640]{1,0:T(8,128)(2,1)} %collective-permute-done.6.refs_1_), channel_id=1, source_target_pairs={{0,1},{1,0},{2,3},{3,2},{4,5},{5,4},{6,7},{7,6},{8,9},{9,8},{10,11... | collective-permute-start | bytes 983048 | tf_op jit(solution)/shard_map/ppermute | solution.py:27
  52.3 0.7 copy-start.10
  52.3 0.8 copy-start.9
  53.1 9.8 %copy-start.16 = (f32[2,256]{1,0:T(2,128)S(1)}, f32[2,256]{1,0:T(2,128)}, u32[]{:S(2)}) copy-start(f32[2,256]{1,0:T(2,128)} %param.14) | copy-start | bytes 6148
  59.3 28.1 %collective-permute-start.10 = (bf16[512,5120]{1,0:T(8,128)(2,1)}, bf16[512,5120]{1,0:T(8,128)(2,1)}, u32[]{:S(2)}, u32[]{:S(2)}) collective-permute-start(bf16[512,5120]{1,0:T(8,128)(2,1)} %head.1), channel_id=1, source_target_pairs={{0,1},{1,0},{2,3},{3,2},{4,5},{5,4},{6,7},{7,6},{8,9},{9,8},{10,11... | collective-permute-start | bytes 15728648 | tf_op jit(solution)/shard_map/ppermute | solution.py:27
  59.5 9.4 %all-to-all-start.1 = ((f32[8,8,512]{2,1,0:T(8,128)}), f32[8,8,512]{2,1,0:T(8,128)S(1)}, u32[]{:S(2)}, u32[]{:S(2)}) async-start(f32[8,8,512]{2,1,0:T(8,128)} %get-tuple-element.51), calls=%async_computation.1 | async-start | bytes 262144 | tf_op jit(solution)/shard_map/all_to_all | solution.py:423
  62.9 61.5 %reduce-scatter.3.cloned.1.call-start = ((), (), s32[]{:S(2)}) async-start(), calls=%async_computation.6 | async-start | bytes 2949120 | tf_op jit(solution)/shard_map/reduce_scatter | solution.py:429
  68.9 0.7 copy-start.8
  81.3 3.9 %copy-start.6 = (bf16[512,512]{1,0:T(8,128)(2,1)S(1)}, bf16[512,512]{1,0:T(8,128)(2,1)}, u32[]{:S(2)}) copy-start(bf16[512,512]{1,0:T(8,128)(2,1)} %get-tuple-element.58.dl) | copy-start | bytes 1572868
  81.3 43.0 %all-to-all-start.2 = ((bf16[4,8,160,256]{3,2,1,0:T(8,128)(2,1)}), bf16[4,8,160,256]{3,2,1,0:T(8,128)(2,1)S(1)}, u32[]{:S(2)}, u32[]{:S(2)}) async-start(bf16[4,8,160,256]{3,2,1,0:T(8,128)(2,1)} %get-tuple-element.57), calls=%async_computation.2 | async-start | bytes 5242880 | tf_op jit(solution)/shard_map/all_to_all | solution.py:430
  85.1 66.7 %reduce-scatter.5.cloned.1.call-start = ((), (), s32[]{:S(2)}) async-start(), calls=%async_computation.7 | async-start | bytes 409600 | tf_op jit(solution)/shard_map/reduce_scatter | solution.py:444
  85.2 2.2 %collective-permute-start.9 = (bf16[512,512]{1,0:T(8,128)(2,1)S(1)}, bf16[512,512]{1,0:T(8,128)(2,1)S(1)}, u32[]{:S(2)}, u32[]{:S(2)}) collective-permute-start(bf16[512,512]{1,0:T(8,128)(2,1)S(1)} %copy-done.6), channel_id=1, source_target_pairs={{0,1},{1,0},{2,3},{3,2},{4,5},{5,4},{6,7},{7,6},{8,9},{9,8},{10,11... | collective-permute-start | bytes 1572872 | tf_op jit(solution)/shard_map/ppermute | solution.py:27
  87.4 0.8 copy-start.7
  88.2 32.1 %copy-start.12 = (bf16[640]{0:T(1024)(128)(2,1)S(1)}, bf16[640]{0:T(1024)(128)(2,1)}, u32[]{:S(2)}) copy-start(bf16[640]{0:T(1024)(128)(2,1)} %param.10) | copy-start | bytes 3844
  99.0 3.6 %collective-permute-start.11 = (f32[1,768]{1,0:T(1,128)S(1)}, f32[1,768]{1,0:T(1,128)S(1)}, u32[]{:S(2)}, u32[]{:S(2)}) collective-permute-start(f32[1,768]{1,0:T(1,128)S(1)} %get-tuple-element.76), channel_id=1, source_target_pairs={{0,6},{2,0},{4,2},{6,4},{1,7},{3,1},{5,3},{7,5},{8,14},{10,8},{12,... | collective-permute-start | bytes 9224 | tf_op jit(solution)/shard_map/ppermute | solution.py:27
  100.1 5.1 %collective-permute-start.13 = (f32[1,768]{1,0:T(1,128)S(1)}, f32[1,768]{1,0:T(1,128)S(1)}, u32[]{:S(2)}, u32[]{:S(2)}) collective-permute-start(f32[1,768]{1,0:T(1,128)S(1)} %get-tuple-element.77), channel_id=1, source_target_pairs={{0,4},{2,6},{4,0},{6,2},{1,5},{3,7},{5,1},{7,3},{8,12},{10,14},{12... | collective-permute-start | bytes 9224 | tf_op jit(solution)/shard_map/ppermute | solution.py:27
  101.4 4.8 %collective-permute-start.12 = (f32[1,768]{1,0:T(1,128)S(1)}, f32[1,768]{1,0:T(1,128)S(1)}, u32[]{:S(2)}, u32[]{:S(2)}) collective-permute-start(f32[1,768]{1,0:T(1,128)S(1)} %get-tuple-element.78), channel_id=1, source_target_pairs={{0,2},{2,4},{4,6},{6,0},{1,3},{3,5},{5,7},{7,1},{8,10},{10,12},{12... | collective-permute-start | bytes 9224 | tf_op jit(solution)/shard_map/ppermute | solution.py:27
  106.9 27.8 %collective-permute-start.17 = (bf16[512,640]{1,0:T(8,128)(2,1)}, bf16[512,640]{1,0:T(8,128)(2,1)S(1)}, u32[]{:S(2)}, u32[]{:S(2)}) collective-permute-start(bf16[512,640]{1,0:T(8,128)(2,1)} %get-tuple-element.67), channel_id=1, source_target_pairs={{0,6},{2,0},{4,2},{6,4},{1,7},{3,1},{5,3},{7,5},{8,14},{10,8},{12,... | collective-permute-start | bytes 1966088 | tf_op jit(solution)/shard_map/ppermute | solution.py:27
  108.0 30.8 %collective-permute-start.18 = (bf16[512,640]{1,0:T(8,128)(2,1)}, bf16[512,640]{1,0:T(8,128)(2,1)}, u32[]{:S(2)}, u32[]{:S(2)}) collective-permute-start(bf16[512,640]{1,0:T(8,128)(2,1)} %get-tuple-element.68), channel_id=1, source_target_pairs={{0,2},{2,4},{4,6},{6,0},{1,3},{3,5},{5,7},{7,1},{8,10},{10,12},{12... | collective-permute-start | bytes 1966088 | tf_op jit(solution)/shard_map/ppermute | solution.py:27
  108.9 29.8 %collective-permute-start.19 = (bf16[512,640]{1,0:T(8,128)(2,1)}, bf16[512,640]{1,0:T(8,128)(2,1)}, u32[]{:S(2)}, u32[]{:S(2)}) collective-permute-start(bf16[512,640]{1,0:T(8,128)(2,1)} %get-tuple-element.69), channel_id=1, source_target_pairs={{0,4},{2,6},{4,0},{6,2},{1,5},{3,7},{5,1},{7,3},{8,12},{10,14},{12... | collective-permute-start | bytes 1966088 | tf_op jit(solution)/shard_map/ppermute | solution.py:27
  109.9 3.6 %collective-permute-start.14 = (f32[1,768]{1,0:T(1,128)S(1)}, f32[1,768]{1,0:T(1,128)S(1)}, u32[]{:S(2)}, u32[]{:S(2)}) collective-permute-start(f32[1,768]{1,0:T(1,128)S(1)} %fusion.1), channel_id=1, source_target_pairs={{0,32},{32,0},{64,96},{96,64},{128,160},{160,128},{192,224},{224,1... | collective-permute-start | bytes 9224 | tf_op jit(solution)/shard_map/ppermute | solution.py:31
  113.5 3.6 %collective-permute-start.15 = (f32[1,768]{1,0:T(1,128)S(1)}, f32[1,768]{1,0:T(1,128)S(1)}, u32[]{:S(2)}, u32[]{:S(2)}) collective-permute-start(f32[1,768]{1,0:T(1,128)S(1)} %add.53), channel_id=1, source_target_pairs={{0,224},{32,64},{64,32},{96,128},{128,96},{160,192},{192,160},{224... | collective-permute-start | bytes 9224 | tf_op jit(solution)/shard_map/ppermute | solution.py:31
  117.1 6.6 %collective-permute-start.16 = (f32[1,768]{1,0:T(1,128)S(1)}, f32[1,768]{1,0:T(1,128)S(1)}, u32[]{:S(2)}, u32[]{:S(2)}) collective-permute-start(f32[1,768]{1,0:T(1,128)S(1)} %add.54), channel_id=1, source_target_pairs={{0,96},{32,192},{64,160},{96,0},{128,224},{160,64},{192,32},{224,1... | collective-permute-start | bytes 9224 | tf_op jit(solution)/shard_map/ppermute | solution.py:31
  124.4 1.5 copy-start
  128.8 23.1 %all-to-all-start.3 = ((bf16[8,160,256]{2,1,0:T(8,128)(2,1)}), bf16[8,160,256]{2,1,0:T(8,128)(2,1)}, u32[]{:S(2)}, u32[]{:S(2)}) async-start(bf16[8,160,256]{2,1,0:T(8,128)(2,1)} %sum_x.1), calls=%async_computation.4 | async-start | bytes 1310720 | tf_op jit(solution)/shard_map/all_to_all | solution.py:443
  134.7 4.0 %copy-start.17 = (bf16[512,640]{1,0:T(8,128)(2,1)}, bf16[512,640]{1,0:T(8,128)(2,1)S(1)}, u32[]{:S(2)}) copy-start(bf16[512,640]{1,0:T(8,128)(2,1)S(1)} %collective-permute-done.17.u1) | copy-start | bytes 1966084
  138.8 3.3 %copy-start.14 = (f32[1,768]{1,0:T(1,128)S(1)}, f32[1,768]{1,0:T(1,128)}, u32[]{:S(2)}) copy-start(f32[1,768]{1,0:T(1,128)} %add.55) | copy-start | bytes 9220
  138.8 12.4 %copy-start.13 = (bf16[640]{0:T(1024)(128)(2,1)S(1)}, bf16[640]{0:T(1024)(128)(2,1)}, u32[]{:S(2)}) copy-start(bf16[640]{0:T(1024)(128)(2,1)} %param.10) | copy-start | bytes 3844
  142.1 4.6 %collective-permute-start.22 = (f32[1,768]{1,0:T(1,128)S(1)}, f32[1,768]{1,0:T(1,128)S(1)}, u32[]{:S(2)}, u32[]{:S(2)}) collective-permute-start(f32[1,768]{1,0:T(1,128)S(1)} %copy-done.14), channel_id=1, source_target_pairs={{0,24},{8,0},{16,8},{24,16},{1,25},{9,1},{17,9},{25,17},{2,26},{10... | collective-permute-start | bytes 9224 | tf_op jit(solution)/shard_map/ppermute | solution.py:27
  145.0 5.1 %collective-permute-start.21 = (f32[1,768]{1,0:T(1,128)S(1)}, f32[1,768]{1,0:T(1,128)S(1)}, u32[]{:S(2)}, u32[]{:S(2)}) collective-permute-start(f32[1,768]{1,0:T(1,128)S(1)} %copy-done.14), channel_id=1, source_target_pairs={{0,16},{8,24},{16,0},{24,8},{1,17},{9,25},{17,1},{25,9},{2,18},{10... | collective-permute-start | bytes 9224 | tf_op jit(solution)/shard_map/ppermute | solution.py:27
  145.9 4.8 %collective-permute-start.20 = (f32[1,768]{1,0:T(1,128)S(1)}, f32[1,768]{1,0:T(1,128)S(1)}, u32[]{:S(2)}, u32[]{:S(2)}) collective-permute-start(f32[1,768]{1,0:T(1,128)S(1)} %copy-done.14), channel_id=1, source_target_pairs={{0,8},{8,16},{16,24},{24,0},{1,9},{9,17},{17,25},{25,1},{2,10},{10... | collective-permute-start | bytes 9224 | tf_op jit(solution)/shard_map/ppermute | solution.py:27
Sparse Core Ops, SparseCore 0:
  81.4 40.3 reduce-scatter.2
  124.5 23.6 reduce-scatter.4

commit v10 on v8

--- a/solution.py
+++ b/solution.py
@@ -439,11 +439,9 @@
 
     for step in (1, -1, 3):
         tail = tail + turn(tail, step)
-    from_x = after(from_x, tail)
+    from_x = after(from_x, tail, half_z)
 
     to_z = sum_first(from_x, "sum_x")
-    half_z = after(half_z, to_z)
-    to_z = after(to_z, half_z)
     from_z = lax.all_to_all(to_z, "z", 0, 0, tiled=True)
     half_z = lax.psum_scatter(half_z, "x", scatter_dimension=0, tiled=False)
     u1, u2, u3, _ = lax.optimization_barrier((u1, u2, u3, to_z))

time: 165 us -> 164 us (level)
  waiting for transfers between devices: 31.1 us -> 29.1 us
    reduce_scatter x1, waiting for transfers between devices: 2.57 us -> 0.01 us  [body(): half_z = lax.psum_scatter(half_z, 'x', scatter_dimension=0, tiled=False)]
where the time goes in v10:
time: 164 us; the launch traced here: 161 us
  starting transfers between devices  56.8 us (35%)
  Pallas kernels  46.6 us (28%)
  waiting for transfers between devices  29.1 us (18%)
  between operations  14.3 us (9%)
  local copies, waits for them, and re-layouts  11.4 us (7%)
  other arithmetic  3.08 us (2%)
    ppermute x23, starting transfers between devices, shift(): return lax.ppermute(value, axis, [(i, (i + step) % n) for i in range(n)])  25.3 us
    ppermute x23, waiting for transfers between devices, shift(): return lax.ppermute(value, axis, [(i, (i + step) % n) for i in range(n)])  16.3 us
    pallas_call x2, Pallas kernels, logits_of(): pl.pallas_call(functools.partial(logits_kernel, count, per, last), out_sh...  15.7 us
    pallas_call x1, Pallas kernels, back_of(): pl.pallas_call(back_kernel, out_shape=shapes, grid_spec=pltpu.PrefetchSca...  9.87 us
    pallas_call x1, Pallas kernels, heads_of(): pl.pallas_call(heads_kernel, out_shape=shapes, grid_spec=pltpu.PrefetchSc...  8.9 us
    all_to_all x1, starting transfers between devices, body(): over_z = lax.all_to_all(local, 'z', 0, 0, tiled=True).sum(axis=0)  8.57 us
    ppermute x3, starting transfers between devices, turn(): lax.ppermute(value, 'z', [(i, (i + (step if i % 2 == 0 else -step)) % 8)...  7.86 us
    all_to_all x1, starting transfers between devices, body(): from_z = lax.all_to_all(to_z, 'z', 0, 0, tiled=True)  7.78 us
  transfers between devices with their start and end apart: 32, of which 15 were waited for; matrix products, arithmetic and copies ran while one was open for 4% of the time, Pallas kernels for 24%

profile of v10, /device:TPU:32, one launch (start us, length us, event | category | flops | bytes accessed | tf_op | source)
XLA Modules:
  0.0 161.3 jit_solution(7522594154567922088)
XLA Ops:
  7.2 0.7 broadcast_in_dim.8
  7.9 1.1 pad_maximum_fusion.refs_0_
  9.0 3.1 %collective-permute-start.1 = (bf16[528,640]{1,0:T(8,128)(2,1)S(1)}, bf16[528,640]{1,0:T(8,128)(2,1)S(1)}, u32[]{:S(2)}, u32[]{:S(2)}) collective-permute-start(bf16[528,640]{1,0:T(8,128)(2,1)S(1)} %pad_maximum_fusion.refs_0_), channel_id=1, source_target_pairs={{0,6},{2,0},{4,2},{6,4},{1,7},{3,1},{5,3},{7,5},{8,14},{10,8},{12,... | collective-permute-start | bytes 2027528 | tf_op jit(solution)/shard_map/ppermute | solution.py:27
  12.1 1.3 local.1
  13.4 8.6 %all-to-all-start = ((f32[8,1,128]{2,1,0:T(1,128)}), f32[8,1,128]{2,1,0:T(1,128)S(1)}, u32[]{:S(2)}, u32[]{:S(2)}) async-start(f32[8,1,128]{2,1,0:T(1,128)} %local.1), calls=%async_computation | async-start | bytes 8192 | tf_op jit(solution)/shard_map/all_to_all | solution.py:402
  22.0 6.1 %all-to-all-done = f32[8,1,128]{2,1,0:T(1,128)S(1)} async-done(((f32[8,1,128]{2,1,0:T(1,128)}), f32[8,1,128]{2,1,0:T(1,128)S(1)}, u32[]{:S(2)}, u32[]{:S(2)}) %all-to-all-start) | async-done | bytes 4128 | tf_op jit(solution)/shard_map/all_to_all | solution.py:402
  28.2 1.8 %collective-permute-done.refs_2_ = bf16[528,640]{1,0:T(8,128)(2,1)S(1)} collective-permute-done((bf16[528,640]{1,0:T(8,128)(2,1)S(1)}, bf16[528,640]{1,0:T(8,128)(2,1)S(1)}, u32[]{:S(2)}, u32[]{:S(2)}) %collective-permute-start) | collective-permute-done | bytes 675872 | tf_op jit(solution)/shard_map/ppermute | solution.py:27
  30.0 0.8 slice.29
  30.8 0.8 slice.28
  32.0 3.2 %collective-permute-start.6 = (bf16[256,640]{1,0:T(8,128)(2,1)}, bf16[256,640]{1,0:T(8,128)(2,1)}, u32[]{:S(2)}, u32[]{:S(2)}) collective-permute-start(bf16[256,640]{1,0:T(8,128)(2,1)} %slice.29), channel_id=1, source_target_pairs={{0,6},{2,0},{4,2},{6,4},{1,7},{3,1},{5,3},{7,5},{8,14},{10,8},{12,... | collective-permute-start | bytes 983048 | tf_op jit(solution)/shard_map/ppermute | solution.py:27
  36.0 0.8 copy-done.4
  37.0 9.5 %logits_first.1 = (bf16[3,512,1280]{2,1,0:T(8,128)(2,1)}, f32[512,512]{1,0:T(8,128)}, f32[8,512]{1,0:T(8,128)}) custom-call(s32[12]{0:T(128)} %concatenate.6.at, bf16[528,640]{1,0:T(8,128)(2,1)} %copy-done.1, bf16[528,640]{1,0:T(8,128)(2,1)} %copy-done.4, bf16[528,640]{1,0:T(8,128)(2,1)} %copy-done.2, bf16[528,640]{1,0:T(8,128)(2,1)} %copy-done.5, ...), custom_call_target="tpu_custom_call" | custom-call | flops 1000 | bytes 1000 | tf_op jit(solution)/shard_map/logits_first/pallas_call | solution.py:163
  47.8 1.2 collective-permute-done.8.refs_3_
  49.0 0.7 copy-done.10
  49.8 6.1 %logits_last.1 = (bf16[1,512,1280]{2,1,0:T(8,128)(2,1)}, f32[512,512]{1,0:T(8,128)}, f32[8,8,512]{2,1,0:T(8,128)}, f32[8,512]{1,0:T(8,128)}) custom-call(s32[12]{0:T(128)} %concatenate.6.at, bf16[272,640]{1,0:T(8,128)(2,1)} %collective-permute-done.2.refs_0_, bf16[256,640]{1,0:T(8,128)(2,1)} %collective-permute-done.6.refs_1_, bf16[272,640]{1,0:T(8,128)(2,1)} %copy-done.9, ...), custom_call_target="tpu_custom_call" | custom-call | flops 1000 | bytes 1000 | tf_op jit(solution)/shard_map/logits_last/pallas_call | solution.py:163
  56.2 3.4 %all-to-all-start.1 = ((f32[8,8,512]{2,1,0:T(8,128)}), f32[8,8,512]{2,1,0:T(8,128)S(1)}, u32[]{:S(2)}, u32[]{:S(2)}) async-start(f32[8,8,512]{2,1,0:T(8,128)} %get-tuple-element.54), calls=%async_computation.1 | async-start | bytes 262144 | tf_op jit(solution)/shard_map/all_to_all | solution.py:425
  59.6 2.8 %collective-permute-start.11 = (f32[1,128]{1,0:T(1,128)S(1)}, f32[1,128]{1,0:T(1,128)S(1)}, u32[]{:S(2)}, u32[]{:S(2)}) collective-permute-start(f32[1,128]{1,0:T(1,128)S(1)} %bitcast.34), channel_id=1, source_target_pairs={{0,24},{8,0},{16,8},{24,16},{1,25},{9,1},{17,9},{25,17},{2,26},{10... | collective-permute-start | bytes 1544 | tf_op jit(solution)/shard_map/ppermute | solution.py:27
  62.5 0.8 collective-permute-start.10
  63.3 0.9 collective-permute-start.9
  64.8 2.8 %collective-permute-done.10.sum2 = f32[1,128]{1,0:T(1,128)S(1)} collective-permute-done((f32[1,128]{1,0:T(1,128)S(1)}, f32[1,128]{1,0:T(1,128)S(1)}, u32[]{:S(2)}, u32[]{:S(2)}) %collective-permute-start.10) | collective-permute-done | bytes 544 | tf_op jit(solution)/shard_map/ppermute | solution.py:27
  68.7 2.7 %policy.1 = (bf16[512,512]{1,0:T(8,128)(2,1)}, f32[8,512]{1,0:T(8,128)}) custom-call(s32[12]{0:T(128)} %concatenate.6.at, f32[2]{0:T(128)} %rewards.3, s32[2]{0:T(128)} %lengths.3, s32[2]{0:T(128)} %slots.3, f32[1,128]{1,0:T(1,128)} %bitcast.37, f32[1,128]{1,0:T(1,128)} %copy-done.19, f32[1,128]{1,0:T(1,128)} %copy-done.18, f32[1,128]{1,0:T(1,128)} %copy-done.17, ...), custom_call_target="tpu_custom_call" | custom-call | flops 2097152 | bytes 1572864 | tf_op jit(solution)/shard_map/policy/pallas_call | solution.py:230
  71.4 8.9 %heads.1 = (bf16[4,8,160,256]{3,2,1,0:T(8,128)(2,1)}, bf16[8,4,160,256]{3,2,1,0:T(8,128)(2,1)}) custom-call(s32[12]{0:T(128)} %concatenate.6.at, bf16[3,512,1280]{2,1,0:T(8,128)(2,1)} %get-tuple-element.57.early, bf16[1,512,1280]{2,1,0:T(8,128)(2,1)} %get-tuple-element.58.late, bf16[512,512]{1,0:T(8,128)(2,1)} %get-tuple-element.60.dl), custom_call_target="tpu_custom_call" | custom-call | flops 2684354560 | bytes 15728640 | tf_op jit(solution)/shard_map/heads/pallas_call | solution.py:304
  80.4 3.8 %all-to-all-start.2 = ((bf16[4,8,160,256]{3,2,1,0:T(8,128)(2,1)}), bf16[4,8,160,256]{3,2,1,0:T(8,128)(2,1)S(1)}, u32[]{:S(2)}, u32[]{:S(2)}) async-start(bf16[4,8,160,256]{3,2,1,0:T(8,128)(2,1)} %get-tuple-element.59), calls=%async_computation.2 | async-start | bytes 5242880 | tf_op jit(solution)/shard_map/all_to_all | solution.py:432
  84.3 1.9 %collective-permute-done.12.dl_o = bf16[512,512]{1,0:T(8,128)(2,1)S(1)} collective-permute-done((bf16[512,512]{1,0:T(8,128)(2,1)S(1)}, bf16[512,512]{1,0:T(8,128)(2,1)S(1)}, u32[]{:S(2)}, u32[]{:S(2)}) %collective-permute-start.12) | collective-permute-done | bytes 524320 | tf_op jit(solution)/shard_map/ppermute | solution.py:27
  86.2 0.8 copy-done.7
  87.1 9.9 %back.1 = (bf16[512,640]{1,0:T(8,128)(2,1)}, bf16[512,640]{1,0:T(8,128)(2,1)}, bf16[512,640]{1,0:T(8,128)(2,1)}, bf16[512,640]{1,0:T(8,128)(2,1)}, f32[4,1,768]{2,1,0:T(1,128)}) custom-call(s32[12]{0:T(128)} %concatenate.6.at, bf16[512,512]{1,0:T(8,128)(2,1)} %get-tuple-element.60.dl, bf16[512,512]{1,0:T(8,128)(2,1)} %copy-done.7, ...), custom_call_target="tpu_custom_call" | custom-call | flops 2684354560 | bytes 10485760 | tf_op jit(solution)/shard_map/back/pallas_call | solution.py:262
  96.9 0.7 slice_bitcast_fusion.2
  97.7 3.1 %collective-permute-start.14 = (f32[1,768]{1,0:T(1,128)S(1)}, f32[1,768]{1,0:T(1,128)S(1)}, u32[]{:S(2)}, u32[]{:S(2)}) collective-permute-start(f32[1,768]{1,0:T(1,128)S(1)} %get-tuple-element.78), channel_id=1, source_target_pairs={{0,6},{2,0},{4,2},{6,4},{1,7},{3,1},{5,3},{7,5},{8,14},{10,8},{12,... | collective-permute-start | bytes 9224 | tf_op jit(solution)/shard_map/ppermute | solution.py:27
  100.8 0.8 collective-permute-start.16
  101.6 0.9 collective-permute-start.15
  102.5 3.4 %collective-permute-done.16 = f32[1,768]{1,0:T(1,128)S(1)} collective-permute-done((f32[1,768]{1,0:T(1,128)S(1)}, f32[1,768]{1,0:T(1,128)S(1)}, u32[]{:S(2)}, u32[]{:S(2)}) %collective-permute-start.16) | collective-permute-done | bytes 3104 | tf_op jit(solution)/shard_map/ppermute | solution.py:27
  106.4 0.7 fusion.1
  107.4 1.7 %collective-permute-start.21 = (bf16[512,640]{1,0:T(8,128)(2,1)}, bf16[512,640]{1,0:T(8,128)(2,1)}, u32[]{:S(2)}, u32[]{:S(2)}) collective-permute-start(bf16[512,640]{1,0:T(8,128)(2,1)} %get-tuple-element.70), channel_id=1, source_target_pairs={{0,2},{2,4},{4,6},{6,0},{1,3},{3,5},{5,7},{7,1},{8,10},{10,12},{12... | collective-permute-start | bytes 1966088 | tf_op jit(solution)/shard_map/ppermute | solution.py:27
  109.1 1.5 collective-permute-start.22
  110.7 3.5 %collective-permute-done.17 = f32[1,768]{1,0:T(1,128)S(1)} collective-permute-done((f32[1,768]{1,0:T(1,128)S(1)}, f32[1,768]{1,0:T(1,128)S(1)}, u32[]{:S(2)}, u32[]{:S(2)}) %collective-permute-start.17) | collective-permute-done | bytes 3104 | tf_op jit(solution)/shard_map/ppermute | solution.py:31
  114.2 2.1 %collective-permute-start.18 = (f32[1,768]{1,0:T(1,128)S(1)}, f32[1,768]{1,0:T(1,128)S(1)}, u32[]{:S(2)}, u32[]{:S(2)}) collective-permute-start(f32[1,768]{1,0:T(1,128)S(1)} %add.53), channel_id=1, source_target_pairs={{0,224},{32,64},{64,32},{96,128},{128,96},{160,192},{192,160},{224... | collective-permute-start | bytes 9224 | tf_op jit(solution)/shard_map/ppermute | solution.py:31
  116.3 1.6 collective-permute-done.18
  117.9 5.7 %collective-permute-start.19 = (f32[1,768]{1,0:T(1,128)S(1)}, f32[1,768]{1,0:T(1,128)S(1)}, u32[]{:S(2)}, u32[]{:S(2)}) collective-permute-start(f32[1,768]{1,0:T(1,128)S(1)} %add.54), channel_id=1, source_target_pairs={{0,96},{32,192},{64,160},{96,0},{128,224},{160,64},{192,32},{224,1... | collective-permute-start | bytes 9224 | tf_op jit(solution)/shard_map/ppermute | solution.py:31
  124.2 1.0 collective-permute-done.19
  125.8 1.5 copy-done
  127.3 2.9 %sum_x.1 = bf16[8,160,256]{2,1,0:T(8,128)(2,1)} custom-call(bf16[4,8,160,256]{3,2,1,0:T(8,128)(2,1)} %copy-done), custom_call_target="tpu_custom_call" | custom-call | flops 1310720 | bytes 3932160 | tf_op jit(solution)/shard_map/sum_x/pallas_call | solution.py:332
  130.2 7.8 %all-to-all-start.3 = ((bf16[8,160,256]{2,1,0:T(8,128)(2,1)}), bf16[8,160,256]{2,1,0:T(8,128)(2,1)}, u32[]{:S(2)}, u32[]{:S(2)}) async-start(bf16[8,160,256]{2,1,0:T(8,128)(2,1)} %sum_x.1), calls=%async_computation.4 | async-start | bytes 1310720 | tf_op jit(solution)/shard_map/all_to_all | solution.py:445
  138.8 3.4 %final.1 = bf16[2,256,640]{2,1,0:T(8,128)(2,1)} custom-call(bf16[512,640]{1,0:T(8,128)(2,1)} %get-tuple-element.68.u0, bf16[512,640]{1,0:T(8,128)(2,1)} %copy-done.20, bf16[512,640]{1,0:T(8,128)(2,1)} %collective-permute-done.21.u2, bf16[512,640]{1,0:T(8,128)(2,1)} %collective-permute-done.22.u3, bf16[2,256,640]{2,1,0:T(8,128)(2,1)} %h_ref.1, ...), custom_call_target="tpu_custom_call" | custom-call | flops 199999995904 | bytes 3932160 | tf_op jit(solution)/shard_map/final/pallas_call | solution.py:364
  142.2 3.0 %collective-permute-start.25 = (f32[1,768]{1,0:T(1,128)S(1)}, f32[1,768]{1,0:T(1,128)S(1)}, u32[]{:S(2)}, u32[]{:S(2)}) collective-permute-start(f32[1,768]{1,0:T(1,128)S(1)} %copy-done.13), channel_id=1, source_target_pairs={{0,24},{8,0},{16,8},{24,16},{1,25},{9,1},{17,9},{25,17},{2,26},{10... | collective-permute-start | bytes 9224 | tf_op jit(solution)/shard_map/ppermute | solution.py:27
  145.2 0.8 collective-permute-start.24
  146.1 0.9 collective-permute-start.23
  146.9 3.4 %collective-permute-done.24 = f32[1,768]{1,0:T(1,128)S(1)} collective-permute-done((f32[1,768]{1,0:T(1,128)S(1)}, f32[1,768]{1,0:T(1,128)S(1)}, u32[]{:S(2)}, u32[]{:S(2)}) %collective-permute-start.24) | collective-permute-done | bytes 3104 | tf_op jit(solution)/shard_map/ppermute | solution.py:27
  152.5 1.9 %join.1 = f32[160,512]{1,0:T(8,128)} custom-call(bf16[8,160,256]{2,1,0:T(8,128)(2,1)} %all-to-all-done.3.from_z, bf16[160,256]{1,0:T(8,128)(2,1)} %bitcast.30), custom_call_target="tpu_custom_call" | custom-call | flops 655360 | bytes 1310720 | tf_op jit(solution)/shard_map/join/pallas_call | solution.py:364
  (90 shorter events, 10.1 us)
Async XLA Ops:
  7.2 28.1 %copy-start.21 = (s32[4]{0:T(128)S(1)}, s32[4]{0:T(128)}, u32[]{:S(2)}) copy-start(s32[4]{0:T(128)} %constant.37.clone) | copy-start | bytes 52
  9.0 26.9 %copy-start.1 = (bf16[528,640]{1,0:T(8,128)(2,1)}, bf16[528,640]{1,0:T(8,128)(2,1)S(1)}, u32[]{:S(2)}) copy-start(bf16[528,640]{1,0:T(8,128)(2,1)S(1)} %pad_maximum_fusion.refs_0_) | copy-start | bytes 2027524
  9.0 19.1 %collective-permute-start.1 = (bf16[528,640]{1,0:T(8,128)(2,1)S(1)}, bf16[528,640]{1,0:T(8,128)(2,1)S(1)}, u32[]{:S(2)}, u32[]{:S(2)}) collective-permute-start(bf16[528,640]{1,0:T(8,128)(2,1)S(1)} %pad_maximum_fusion.refs_0_), channel_id=1, source_target_pairs={{0,6},{2,0},{4,2},{6,4},{1,7},{3,1},{5,3},{7,5},{8,14},{10,8},{12,... | collective-permute-start | bytes 2027528 | tf_op jit(solution)/shard_map/ppermute | solution.py:27
  12.1 17.8 %collective-permute-start = (bf16[528,640]{1,0:T(8,128)(2,1)S(1)}, bf16[528,640]{1,0:T(8,128)(2,1)S(1)}, u32[]{:S(2)}, u32[]{:S(2)}) collective-permute-start(bf16[528,640]{1,0:T(8,128)(2,1)S(1)} %pad_maximum_fusion.refs_0_), channel_id=1, source_target_pairs={{0,2},{2,4},{4,6},{6,0},{1,3},{3,5},{5,7},{7,1},{8,10},{10,12},{12... | collective-permute-start | bytes 2027528 | tf_op jit(solution)/shard_map/ppermute | solution.py:27
  13.4 14.7 %all-to-all-start = ((f32[8,1,128]{2,1,0:T(1,128)}), f32[8,1,128]{2,1,0:T(1,128)S(1)}, u32[]{:S(2)}, u32[]{:S(2)}) async-start(f32[8,1,128]{2,1,0:T(1,128)} %local.1), calls=%async_computation | async-start | bytes 8192 | tf_op jit(solution)/shard_map/all_to_all | solution.py:402
  22.0 13.9 %collective-permute-start.3 = (bf16[528,640]{1,0:T(8,128)(2,1)S(1)}, bf16[528,640]{1,0:T(8,128)(2,1)S(1)}, u32[]{:S(2)}, u32[]{:S(2)}) collective-permute-start(bf16[528,640]{1,0:T(8,128)(2,1)S(1)} %pad_maximum_fusion.refs_0_), channel_id=1, source_target_pairs={{0,1},{1,0},{2,3},{3,2},{4,5},{5,4},{6,7},{7,6},{8,9},{9,8},{10,11... | collective-permute-start | bytes 2027528 | tf_op jit(solution)/shard_map/ppermute | solution.py:27
  28.2 35.1 %copy-start.14 = (f32[128]{0:T(128)}, f32[128]{0:T(128)S(1)}, u32[]{:S(2)}) copy-start(f32[128]{0:T(128)S(1)} %reduce_sum.11) | copy-start | bytes 1540
  28.2 7.8 %copy-start.3 = (bf16[528,640]{1,0:T(8,128)(2,1)}, bf16[528,640]{1,0:T(8,128)(2,1)S(1)}, u32[]{:S(2)}) copy-start(bf16[528,640]{1,0:T(8,128)(2,1)S(1)} %collective-permute-done.1.refs_4_) | copy-start | bytes 2027524
  30.0 6.0 %copy-start.2 = (bf16[528,640]{1,0:T(8,128)(2,1)}, bf16[528,640]{1,0:T(8,128)(2,1)S(1)}, u32[]{:S(2)}) copy-start(bf16[528,640]{1,0:T(8,128)(2,1)S(1)} %collective-permute-done.refs_2_) | copy-start | bytes 2027524
  31.5 4.4 %collective-permute-start.4 = (bf16[528,640]{1,0:T(8,128)(2,1)S(1)}, bf16[528,640]{1,0:T(8,128)(2,1)S(1)}, u32[]{:S(2)}, u32[]{:S(2)}) collective-permute-start(bf16[528,640]{1,0:T(8,128)(2,1)S(1)} %collective-permute-done.refs_2_), channel_id=1, source_target_pairs={{0,1},{1,0},{2,3},{3,2},{4,5},{5,4},{6,7},{7,6},{8,9},{9,8},{10,11... | collective-permute-start | bytes 2027528 | tf_op jit(solution)/shard_map/ppermute | solution.py:27
  31.5 4.4 %collective-permute-start.5 = (bf16[528,640]{1,0:T(8,128)(2,1)S(1)}, bf16[528,640]{1,0:T(8,128)(2,1)}, u32[]{:S(2)}, u32[]{:S(2)}) collective-permute-start(bf16[528,640]{1,0:T(8,128)(2,1)S(1)} %collective-permute-done.1.refs_4_), channel_id=1, source_target_pairs={{0,1},{1,0},{2,3},{3,2},{4,5},{5,4},{6,7},{7,6},{8,9},{9,8},{10,11... | collective-permute-start | bytes 2027528 | tf_op jit(solution)/shard_map/ppermute | solution.py:27
  32.0 14.5 %collective-permute-start.2 = (bf16[272,640]{1,0:T(8,128)(2,1)}, bf16[272,640]{1,0:T(8,128)(2,1)}, u32[]{:S(2)}, u32[]{:S(2)}) collective-permute-start(bf16[272,640]{1,0:T(8,128)(2,1)} %slice.28), channel_id=1, source_target_pairs={{0,2},{2,4},{4,6},{6,0},{1,3},{3,5},{5,7},{7,1},{8,10},{10,12},{12... | collective-permute-start | bytes 1044488 | tf_op jit(solution)/shard_map/ppermute | solution.py:27
  32.0 14.6 %collective-permute-start.6 = (bf16[256,640]{1,0:T(8,128)(2,1)}, bf16[256,640]{1,0:T(8,128)(2,1)}, u32[]{:S(2)}, u32[]{:S(2)}) collective-permute-start(bf16[256,640]{1,0:T(8,128)(2,1)} %slice.29), channel_id=1, source_target_pairs={{0,6},{2,0},{4,2},{6,4},{1,7},{3,1},{5,3},{7,5},{8,14},{10,8},{12,... | collective-permute-start | bytes 983048 | tf_op jit(solution)/shard_map/ppermute | solution.py:27
  35.9 11.3 %copy-start.15 = (s32[2,256]{1,0:T(2,128)S(1)}, s32[2,256]{1,0:T(2,128)}, u32[]{:S(2)}) copy-start(s32[2,256]{1,0:T(2,128)} %param.12) | copy-start | bytes 6148
  35.9 0.9 copy-start.4
  35.9 1.1 copy-start.5
  46.6 2.4 %collective-permute-start.7 = (bf16[272,640]{1,0:T(8,128)(2,1)}, bf16[272,640]{1,0:T(8,128)(2,1)S(1)}, u32[]{:S(2)}, u32[]{:S(2)}) collective-permute-start(bf16[272,640]{1,0:T(8,128)(2,1)} %collective-permute-done.2.refs_0_), channel_id=1, source_target_pairs={{0,1},{1,0},{2,3},{3,2},{4,5},{5,4},{6,7},{7,6},{8,9},{9,8},{10,11... | collective-permute-start | bytes 1044488 | tf_op jit(solution)/shard_map/ppermute | solution.py:27
  46.7 2.3 %collective-permute-start.8 = (bf16[256,640]{1,0:T(8,128)(2,1)}, bf16[256,640]{1,0:T(8,128)(2,1)S(1)}, u32[]{:S(2)}, u32[]{:S(2)}) collective-permute-start(bf16[256,640]{1,0:T(8,128)(2,1)} %collective-permute-done.6.refs_1_), channel_id=1, source_target_pairs={{0,1},{1,0},{2,3},{3,2},{4,5},{5,4},{6,7},{7,6},{8,9},{9,8},{10,11... | collective-permute-start | bytes 983048 | tf_op jit(solution)/shard_map/ppermute | solution.py:27
  49.8 14.3 %copy-start.16 = (f32[2,256]{1,0:T(2,128)S(1)}, f32[2,256]{1,0:T(2,128)}, u32[]{:S(2)}) copy-start(f32[2,256]{1,0:T(2,128)} %param.14) | copy-start | bytes 6148
  56.0 30.2 %collective-permute-start.13 = (bf16[512,5120]{1,0:T(8,128)(2,1)}, bf16[512,5120]{1,0:T(8,128)(2,1)}, u32[]{:S(2)}, u32[]{:S(2)}) collective-permute-start(bf16[512,5120]{1,0:T(8,128)(2,1)} %head.1), channel_id=1, source_target_pairs={{0,1},{1,0},{2,3},{3,2},{4,5},{5,4},{6,7},{7,6},{8,9},{9,8},{10,11... | collective-permute-start | bytes 15728648 | tf_op jit(solution)/shard_map/ppermute | solution.py:27
  56.2 11.8 %all-to-all-start.1 = ((f32[8,8,512]{2,1,0:T(8,128)}), f32[8,8,512]{2,1,0:T(8,128)S(1)}, u32[]{:S(2)}, u32[]{:S(2)}) async-start(f32[8,8,512]{2,1,0:T(8,128)} %get-tuple-element.54), calls=%async_computation.1 | async-start | bytes 262144 | tf_op jit(solution)/shard_map/all_to_all | solution.py:425
  59.6 66.2 %reduce-scatter.3.cloned.1.call-start = ((), (), s32[]{:S(2)}) async-start(), calls=%async_computation.6 | async-start | bytes 2949120 | tf_op jit(solution)/shard_map/reduce_scatter | solution.py:431
  59.6 5.1 %collective-permute-start.11 = (f32[1,128]{1,0:T(1,128)S(1)}, f32[1,128]{1,0:T(1,128)S(1)}, u32[]{:S(2)}, u32[]{:S(2)}) collective-permute-start(f32[1,128]{1,0:T(1,128)S(1)} %bitcast.34), channel_id=1, source_target_pairs={{0,24},{8,0},{16,8},{24,16},{1,25},{9,1},{17,9},{25,17},{2,26},{10... | collective-permute-start | bytes 1544 | tf_op jit(solution)/shard_map/ppermute | solution.py:27
  62.5 5.0 %collective-permute-start.10 = (f32[1,128]{1,0:T(1,128)S(1)}, f32[1,128]{1,0:T(1,128)S(1)}, u32[]{:S(2)}, u32[]{:S(2)}) collective-permute-start(f32[1,128]{1,0:T(1,128)S(1)} %bitcast.35), channel_id=1, source_target_pairs={{0,16},{8,24},{16,0},{24,8},{1,17},{9,25},{17,1},{25,9},{2,18},{10... | collective-permute-start | bytes 1544 | tf_op jit(solution)/shard_map/ppermute | solution.py:27
  63.3 4.8 %collective-permute-start.9 = (f32[1,128]{1,0:T(1,128)S(1)}, f32[1,128]{1,0:T(1,128)S(1)}, u32[]{:S(2)}, u32[]{:S(2)}) collective-permute-start(f32[1,128]{1,0:T(1,128)S(1)} %bitcast.36), channel_id=1, source_target_pairs={{0,8},{8,16},{16,24},{24,0},{1,9},{9,17},{17,25},{25,1},{2,10},{10... | collective-permute-start | bytes 1544 | tf_op jit(solution)/shard_map/ppermute | solution.py:27
  64.8 3.3 %copy-start.17 = (f32[1,128]{1,0:T(1,128)}, f32[1,128]{1,0:T(1,128)S(1)}, u32[]{:S(2)}) copy-start(f32[1,128]{1,0:T(1,128)S(1)} %collective-permute-done.11.sum3) | copy-start | bytes 1540
  80.4 3.9 %copy-start.6 = (bf16[512,512]{1,0:T(8,128)(2,1)S(1)}, bf16[512,512]{1,0:T(8,128)(2,1)}, u32[]{:S(2)}) copy-start(bf16[512,512]{1,0:T(8,128)(2,1)} %get-tuple-element.60.dl) | copy-start | bytes 1572868
  80.4 45.4 %all-to-all-start.2 = ((bf16[4,8,160,256]{3,2,1,0:T(8,128)(2,1)}), bf16[4,8,160,256]{3,2,1,0:T(8,128)(2,1)S(1)}, u32[]{:S(2)}, u32[]{:S(2)}) async-start(bf16[4,8,160,256]{3,2,1,0:T(8,128)(2,1)} %get-tuple-element.59), calls=%async_computation.2 | async-start | bytes 5242880 | tf_op jit(solution)/shard_map/all_to_all | solution.py:432
  84.2 67.8 %reduce-scatter.5.cloned.1.call-start = ((), (), s32[]{:S(2)}) async-start(), calls=%async_computation.7 | async-start | bytes 409600 | tf_op jit(solution)/shard_map/reduce_scatter | solution.py:446
  84.2 2.0 %collective-permute-start.12 = (bf16[512,512]{1,0:T(8,128)(2,1)S(1)}, bf16[512,512]{1,0:T(8,128)(2,1)S(1)}, u32[]{:S(2)}, u32[]{:S(2)}) collective-permute-start(bf16[512,512]{1,0:T(8,128)(2,1)S(1)} %copy-done.6), channel_id=1, source_target_pairs={{0,1},{1,0},{2,3},{3,2},{4,5},{5,4},{6,7},{7,6},{8,9},{9,8},{10,11... | collective-permute-start | bytes 1572872 | tf_op jit(solution)/shard_map/ppermute | solution.py:27
  87.1 36.5 %copy-start.11 = (bf16[640]{0:T(1024)(128)(2,1)S(1)}, bf16[640]{0:T(1024)(128)(2,1)}, u32[]{:S(2)}) copy-start(bf16[640]{0:T(1024)(128)(2,1)} %param.10) | copy-start | bytes 3844
  97.7 4.8 %collective-permute-start.14 = (f32[1,768]{1,0:T(1,128)S(1)}, f32[1,768]{1,0:T(1,128)S(1)}, u32[]{:S(2)}, u32[]{:S(2)}) collective-permute-start(f32[1,768]{1,0:T(1,128)S(1)} %get-tuple-element.78), channel_id=1, source_target_pairs={{0,6},{2,0},{4,2},{6,4},{1,7},{3,1},{5,3},{7,5},{8,14},{10,8},{12,... | collective-permute-start | bytes 9224 | tf_op jit(solution)/shard_map/ppermute | solution.py:27
  100.8 5.1 %collective-permute-start.16 = (f32[1,768]{1,0:T(1,128)S(1)}, f32[1,768]{1,0:T(1,128)S(1)}, u32[]{:S(2)}, u32[]{:S(2)}) collective-permute-start(f32[1,768]{1,0:T(1,128)S(1)} %get-tuple-element.79), channel_id=1, source_target_pairs={{0,4},{2,6},{4,0},{6,2},{1,5},{3,7},{5,1},{7,3},{8,12},{10,14},{12... | collective-permute-start | bytes 9224 | tf_op jit(solution)/shard_map/ppermute | solution.py:27
  101.6 4.8 %collective-permute-start.15 = (f32[1,768]{1,0:T(1,128)S(1)}, f32[1,768]{1,0:T(1,128)S(1)}, u32[]{:S(2)}, u32[]{:S(2)}) collective-permute-start(f32[1,768]{1,0:T(1,128)S(1)} %get-tuple-element.80), channel_id=1, source_target_pairs={{0,2},{2,4},{4,6},{6,0},{1,3},{3,5},{5,7},{7,1},{8,10},{10,12},{12... | collective-permute-start | bytes 9224 | tf_op jit(solution)/shard_map/ppermute | solution.py:27
  107.1 30.9 %collective-permute-start.20 = (bf16[512,640]{1,0:T(8,128)(2,1)}, bf16[512,640]{1,0:T(8,128)(2,1)S(1)}, u32[]{:S(2)}, u32[]{:S(2)}) collective-permute-start(bf16[512,640]{1,0:T(8,128)(2,1)} %get-tuple-element.69), channel_id=1, source_target_pairs={{0,6},{2,0},{4,2},{6,4},{1,7},{3,1},{5,3},{7,5},{8,14},{10,8},{12,... | collective-permute-start | bytes 1966088 | tf_op jit(solution)/shard_map/ppermute | solution.py:27
  107.4 30.6 %collective-permute-start.21 = (bf16[512,640]{1,0:T(8,128)(2,1)}, bf16[512,640]{1,0:T(8,128)(2,1)}, u32[]{:S(2)}, u32[]{:S(2)}) collective-permute-start(bf16[512,640]{1,0:T(8,128)(2,1)} %get-tuple-element.70), channel_id=1, source_target_pairs={{0,2},{2,4},{4,6},{6,0},{1,3},{3,5},{5,7},{7,1},{8,10},{10,12},{12... | collective-permute-start | bytes 1966088 | tf_op jit(solution)/shard_map/ppermute | solution.py:27
  109.1 29.0 %collective-permute-start.22 = (bf16[512,640]{1,0:T(8,128)(2,1)}, bf16[512,640]{1,0:T(8,128)(2,1)}, u32[]{:S(2)}, u32[]{:S(2)}) collective-permute-start(bf16[512,640]{1,0:T(8,128)(2,1)} %get-tuple-element.71), channel_id=1, source_target_pairs={{0,4},{2,6},{4,0},{6,2},{1,5},{3,7},{5,1},{7,3},{8,12},{10,14},{12... | collective-permute-start | bytes 1966088 | tf_op jit(solution)/shard_map/ppermute | solution.py:27
  110.6 3.6 %collective-permute-start.17 = (f32[1,768]{1,0:T(1,128)S(1)}, f32[1,768]{1,0:T(1,128)S(1)}, u32[]{:S(2)}, u32[]{:S(2)}) collective-permute-start(f32[1,768]{1,0:T(1,128)S(1)} %fusion.1), channel_id=1, source_target_pairs={{0,32},{32,0},{64,96},{96,64},{128,160},{160,128},{192,224},{224,1... | collective-permute-start | bytes 9224 | tf_op jit(solution)/shard_map/ppermute | solution.py:31
  114.2 3.6 %collective-permute-start.18 = (f32[1,768]{1,0:T(1,128)S(1)}, f32[1,768]{1,0:T(1,128)S(1)}, u32[]{:S(2)}, u32[]{:S(2)}) collective-permute-start(f32[1,768]{1,0:T(1,128)S(1)} %add.53), channel_id=1, source_target_pairs={{0,224},{32,64},{64,32},{96,128},{128,96},{160,192},{192,160},{224... | collective-permute-start | bytes 9224 | tf_op jit(solution)/shard_map/ppermute | solution.py:31
  117.9 7.3 %collective-permute-start.19 = (f32[1,768]{1,0:T(1,128)S(1)}, f32[1,768]{1,0:T(1,128)S(1)}, u32[]{:S(2)}, u32[]{:S(2)}) collective-permute-start(f32[1,768]{1,0:T(1,128)S(1)} %add.54), channel_id=1, source_target_pairs={{0,96},{32,192},{64,160},{96,0},{128,224},{160,64},{192,32},{224,1... | collective-permute-start | bytes 9224 | tf_op jit(solution)/shard_map/ppermute | solution.py:31
  125.8 1.5 copy-start
  130.2 22.4 %all-to-all-start.3 = ((bf16[8,160,256]{2,1,0:T(8,128)(2,1)}), bf16[8,160,256]{2,1,0:T(8,128)(2,1)}, u32[]{:S(2)}, u32[]{:S(2)}) async-start(bf16[8,160,256]{2,1,0:T(8,128)(2,1)} %sum_x.1), calls=%async_computation.4 | async-start | bytes 1310720 | tf_op jit(solution)/shard_map/all_to_all | solution.py:445
  138.0 0.8 copy-start.20
  138.8 3.4 %copy-start.13 = (f32[1,768]{1,0:T(1,128)S(1)}, f32[1,768]{1,0:T(1,128)}, u32[]{:S(2)}) copy-start(f32[1,768]{1,0:T(1,128)} %add.55) | copy-start | bytes 9220
  138.8 12.6 %copy-start.12 = (bf16[640]{0:T(1024)(128)(2,1)S(1)}, bf16[640]{0:T(1024)(128)(2,1)}, u32[]{:S(2)}) copy-start(bf16[640]{0:T(1024)(128)(2,1)} %param.10) | copy-start | bytes 3844
  142.2 4.8 %collective-permute-start.25 = (f32[1,768]{1,0:T(1,128)S(1)}, f32[1,768]{1,0:T(1,128)S(1)}, u32[]{:S(2)}, u32[]{:S(2)}) collective-permute-start(f32[1,768]{1,0:T(1,128)S(1)} %copy-done.13), channel_id=1, source_target_pairs={{0,24},{8,0},{16,8},{24,16},{1,25},{9,1},{17,9},{25,17},{2,26},{10... | collective-permute-start | bytes 9224 | tf_op jit(solution)/shard_map/ppermute | solution.py:27
  145.2 5.1 %collective-permute-start.24 = (f32[1,768]{1,0:T(1,128)S(1)}, f32[1,768]{1,0:T(1,128)S(1)}, u32[]{:S(2)}, u32[]{:S(2)}) collective-permute-start(f32[1,768]{1,0:T(1,128)S(1)} %copy-done.13), channel_id=1, source_target_pairs={{0,16},{8,24},{16,0},{24,8},{1,17},{9,25},{17,1},{25,9},{2,18},{10... | collective-permute-start | bytes 9224 | tf_op jit(solution)/shard_map/ppermute | solution.py:27
  146.1 4.8 %collective-permute-start.23 = (f32[1,768]{1,0:T(1,128)S(1)}, f32[1,768]{1,0:T(1,128)S(1)}, u32[]{:S(2)}, u32[]{:S(2)}) collective-permute-start(f32[1,768]{1,0:T(1,128)S(1)} %copy-done.13), channel_id=1, source_target_pairs={{0,8},{8,16},{16,24},{24,0},{1,9},{9,17},{17,25},{25,1},{2,10},{10... | collective-permute-start | bytes 9224 | tf_op jit(solution)/shard_map/ppermute | solution.py:27
  (6 other events, 4.1 us)
Sparse Core Ops, SparseCore 0:
  80.5 44.4 reduce-scatter.2
  127.5 23.5 reduce-scatter.4
